TPU v7x, 128 devices: a whole 4x4x4 slice. The times are simulated.
128 devices in a mesh: dp: 16 (over x, z), tensor: 8 (over y, core).
Axes of the slice: x: 4, y: 4, z: 4, core: 2. Of those that a mesh axis runs over, the one named last changes fastest.
Arguments:
- attn_out: bfloat16 [8192, 8192], P('dp', 'tensor'), may hold values from -6 to 6
- frozen_weight: bfloat16 [8192, 8192], P('tensor', 'dp'), may hold values from -0.0625 to 0.0625
- vector_bank: float32 [256, 256], replicated, may hold values from -0.18 to 0.18
- logits_a: float32 [16, 32, 2], P(None, 'tensor'), may hold values from -2 to 2
- index_a: int32 [16, 32, 2], P(None, 'tensor'), may hold values from 0 to 255, all different within a row
- logits_b: float32 [16, 32, 2], P(None, 'tensor'), may hold values from -2 to 2
- index_b: int32 [16, 32, 2], P(None, 'tensor'), may hold values from 0 to 255, all different within a row
- out_grad: bfloat16 [8192, 8192], P('dp'), may hold values from -6 to 6
Outputs:
- layer_out: bfloat16 [8192, 8192], P('dp', 'tensor')
- attn_grad: bfloat16 [8192, 8192], P('dp', 'tensor')
- bank_grad: float32 [256, 256], replicated
- logits_a_grad: float32 [16, 32, 2], P(None, 'tensor')
- logits_b_grad: float32 [16, 32, 2], P(None, 'tensor')
Inputs may be any that keep to these rules, and one draw needn't show every extreme that they name: `index_a`: the 2 entries of one sub-vector differ. `index_b`: the 2 entries of one sub-vector differ.
All inputs are finite; a program needn't handle non-finite values.
Results may differ from a plain program's by a relative error of at most 0.014.
Values may be sent and summed in bfloat16 or wider, within the bound.
No kernel may reach another device: no remote copies, remote signals or barrier semaphores. Data moves between devices by JAX's collectives and lax.ppermute only.
A program may use at most 128 MiB of HBM per device.

v0:
```python
import functools

import jax
import jax.numpy as jnp
from jax import lax
from jax.experimental import pallas as pl
from jax.experimental.pallas import tpu as pltpu
from jax.sharding import PartitionSpec as P

adapter_scale = 2.0
SIDE = 4
BOTH = ("dp", "tensor")
LANES = [[0, 2, 4, 6], [1, 3, 5, 7]]
SWAP = [(t, t ^ 1) for t in range(8)]


def device(x, z, y, c):
    return (x * SIDE + z) * 8 + y * 2 + c


def pairs(move):
    found = []
    for x in range(SIDE):
        for z in range(SIDE):
            for y in range(SIDE):
                for c in range(2):
                    to = move(x, z, y, c)
                    if to is not None:
                        found.append((device(x, z, y, c), device(*to)))
    return found


def ring(stage, step):
    def move(x, z, y, c):
        if (stage == 0) == (c == 0):
            return ((x + step) % SIDE, z, y, c)
        return (x, (z + step) % SIDE, y, c)

    return pairs(move)


def shift(value, stage, step):
    return lax.ppermute(value, BOTH, ring(stage, step))


def ring_gather(own, stage, h):
    below = shift(own, stage, 1)
    above = shift(own, stage, -1)
    across = shift(below, stage, 1) if h == 0 else shift(above, stage, -1)
    return [own, above, across, below]


def exchange(value, axis, groups=None):
    return lax.all_to_all(
        value, axis, split_axis=0, concat_axis=0, tiled=True, axis_index_groups=groups
    )


def over_tensor(value):
    value = value + lax.ppermute(value, "tensor", SWAP)
    value = value + lax.ppermute(value, "tensor", [(t, t ^ 2) for t in range(8)])
    return value + lax.ppermute(value, "tensor", [(t, t ^ 4) for t in range(8)])


def over_dp(value):
    for bit in (1, 4, 2, 8):
        value = value + lax.ppermute(value, "dp", [(d, d ^ bit) for d in range(16)])
    return value


def after(value, *events):
    return lax.optimization_barrier((value, *events))[0]


def forward_kernel(count, near_ref, wide_ref, *refs):
    lines, out_ref, total = refs[:count], refs[count], refs[count + 1]
    step = pl.program_id(0)
    weights = jnp.concatenate([line[k] for line in lines for k in range(SIDE)], axis=1)
    product = jnp.dot(wide_ref[...], weights, preferred_element_type=jnp.float32)

    @pl.when(step == 0)
    def _():
        total[...] = product

    @pl.when(step > 0)
    def _():
        total[...] += product

    @pl.when(step == pl.num_programs(0) - 1)
    def _():
        part = out_ref.shape[2] // count
        for k in range(SIDE):
            slot = lax.rem(near_ref[0] + k, SIDE)
            for m in range(count):
                lane = (m * SIDE + k) * part
                out_ref[slot, :, m * part : (m + 1) * part] = total[:, lane : lane + part].astype(
                    out_ref.dtype
                )


def forward(near, wide, lines):
    tokens, depth = wide.shape
    part = lines[0].shape[2]
    count = len(lines)
    block = depth // 4
    return pl.pallas_call(
        functools.partial(forward_kernel, count),
        out_shape=jax.ShapeDtypeStruct((SIDE, tokens, count * part), jnp.bfloat16),
        grid_spec=pltpu.PrefetchScalarGridSpec(
            num_scalar_prefetch=1,
            grid=(4,),
            in_specs=[pl.BlockSpec((tokens, block), lambda i, n: (0, i))]
            + [pl.BlockSpec((SIDE, block, part), lambda i, n: (0, i, 0))] * count,
            out_specs=pl.BlockSpec((SIDE, tokens, count * part), lambda i, n: (0, 0, 0)),
            scratch_shapes=[pltpu.VMEM((tokens, count * SIDE * part), jnp.float32)],
        ),
        compiler_params=pltpu.CompilerParams(vmem_limit_bytes=40 << 20),
        cost_estimate=pl.CostEstimate(
            flops=2 * tokens * depth * count * SIDE * part,
            bytes_accessed=2 * depth * (tokens + count * SIDE * part),
            transcendentals=0,
        ),
        name="forward",
    )(near, wide, *lines)


def backward_kernel(count, first, spots_ref, *refs):
    lines, grads = refs[:count], refs[count : count * 5]
    weights = jnp.concatenate([line[k] for line in lines for k in range(SIDE)], axis=1)
    cols = jnp.concatenate([g[...] for g in grads], axis=1)
    product = lax.dot_general(
        cols, weights, (((1,), (1,)), ((), ())), preferred_element_type=jnp.float32
    )
    refs[-1][...] = product if first else refs[-2][...] + product


def backward(spots, grown, out_grad, lines):
    tokens = out_grad.shape[0]
    depth, part = lines[0].shape[1:]
    count = len(lines)
    block = depth // 4
    first = grown is None

    def column(j):
        return pl.BlockSpec((tokens, part), lambda i, n: (0, n[j]))

    total = pl.BlockSpec((tokens, block), lambda i, n: (0, i))
    return pl.pallas_call(
        functools.partial(backward_kernel, count, first),
        out_shape=jax.ShapeDtypeStruct((tokens, depth), jnp.float32),
        grid_spec=pltpu.PrefetchScalarGridSpec(
            num_scalar_prefetch=1,
            grid=(4,),
            in_specs=[pl.BlockSpec((SIDE, block, part), lambda i, n: (0, i, 0))] * count
            + [column(j) for j in range(count * SIDE)]
            + ([] if first else [total]),
            out_specs=total,
        ),
        compiler_params=pltpu.CompilerParams(vmem_limit_bytes=40 << 20),
        cost_estimate=pl.CostEstimate(
            flops=2 * tokens * depth * count * SIDE * part,
            bytes_accessed=2 * depth * count * SIDE * part + 8 * tokens * depth,
            transcendentals=0,
        ),
        name="backward",
    )(spots, *lines, *([out_grad] * (count * SIDE)), *([] if first else [grown]))


def compose(logits, indices, vector_bank):
    weights = jax.nn.sigmoid(logits - logits[..., ::-1])
    levels = jnp.arange(vector_bank.shape[0], dtype=jnp.int32)
    picked = (indices[..., None] == levels).astype(jnp.float32)
    mixing = jnp.sum(picked * weights[..., None], axis=2)
    blocks = jnp.einsum("rjb,bc->rjc", mixing, vector_bank, precision=lax.Precision.HIGHEST)
    return (weights, picked, mixing, blocks.reshape(blocks.shape[0], -1))


def compose_back(grad_rows, weights, picked, mixing, vector_bank):
    blocks = grad_rows.reshape(mixing.shape[0], mixing.shape[1], -1)
    bank_part = jnp.einsum("rjb,rjc->bc", mixing, blocks, precision=lax.Precision.HIGHEST)
    projected = jnp.einsum("rjc,bc->rjb", blocks, vector_bank, precision=lax.Precision.HIGHEST)
    dots = jnp.sum(picked * projected[:, :, None, :], axis=3)
    logit_grad = weights * (dots - jnp.sum(weights * dots, axis=2, keepdims=True))
    return (bank_part, logit_grad)


def settle(piece, step, z, core):
    def from_second(parity):
        def move(x, z, y, c):
            if c == 1 and y % 2 == parity:
                return (x, z, (x + step) % SIDE, y // 2)
            return None

        return lax.ppermute(piece, BOTH, pairs(move))

    def move(x, z, y, c):
        return (x, z, y, 1) if c == 0 and (z + step) % SIDE >= 2 else None

    crossed = lax.ppermute(piece, BOTH, pairs(move))
    spot = (z + step) % SIDE
    first = jnp.where(core == 0, piece, crossed)
    first = jnp.where(spot // 2 == core, first, jnp.zeros_like(first))
    return first, spot % 2, [from_second(0), from_second(1)]


def local(attn_out, frozen_weight, vector_bank, logits_a, index_a, logits_b, index_b, out_grad):
    tokens, height = attn_out.shape
    shard = frozen_weight.shape[1]
    half, part = shard // 2, shard // 4
    f32, bf16 = jnp.float32, jnp.bfloat16
    dp, tensor = lax.axis_index("dp"), lax.axis_index("tensor")
    x, z, core = dp // SIDE, dp % SIDE, tensor % 2
    near, far = jnp.where(core == 0, x, z), jnp.where(core == 0, z, x)
    spot = near.astype(jnp.int32).reshape(1)

    left, right = frozen_weight[:, :half], frozen_weight[:, half:]
    mine = jnp.where(core == 0, left, right)
    theirs = jnp.where(core == 0, right, left)
    swapped = lax.ppermute(theirs, "tensor", SWAP)
    lines = []
    for h in range(2):
        cols = slice(h * part, (h + 1) * part)
        own = jnp.concatenate([mine[:, cols], swapped[:, cols]], axis=0)
        lines.append(jnp.stack(ring_gather(own, 0, h)))
    blocks = [ring_gather(lines[h], 1, h) for h in range(2)]

    def columns(i, h):
        far_at = (far + i) % SIDE
        spots = []
        for k in range(SIDE):
            near_at = (near + k) % SIDE
            x_at = jnp.where(core == 0, near_at, far_at)
            z_at = jnp.where(core == 0, far_at, near_at)
            spots.append((x_at * SIDE + z_at) * 4 + core * 2 + h)
        return spots

    def spots_of(chunks):
        return jnp.stack([s for i, h in chunks for s in columns(i, h)]).astype(jnp.int32)

    wide = jnp.concatenate([attn_out, lax.ppermute(attn_out, "tensor", SWAP)], axis=1)

    weights_a, picked_a, mixing_a, rows_a = compose(logits_a, index_a, vector_bank)
    weights_b, picked_b, mixing_b, rows_b = compose(logits_b, index_b, vector_bank)
    down_a, up_b = rows_a.astype(bf16), rows_b.astype(bf16)
    rank = down_a.shape[0]
    grad_cols = lax.dynamic_slice_in_dim(out_grad, tensor * height, height, 1)
    cols_by_cols = (((1,), (1,)), ((), ()))
    rows_by_rows = (((0,), (0,)), ((), ()))
    low_part = lax.dot_general(down_a, attn_out, cols_by_cols, preferred_element_type=f32)
    back_part = lax.dot_general(up_b, grad_cols, cols_by_cols, preferred_element_type=f32)
    totals = jnp.concatenate([low_part, back_part], axis=0)
    totals = over_tensor(after(totals, lines[0])).astype(bf16)
    low_bf, back_bf = totals[:rank], totals[rank:]

    factor = adapter_scale / (tokens * lax.axis_size("dp"))
    grad_a = jnp.dot(back_bf, attn_out, preferred_element_type=f32)
    grad_b = jnp.dot(low_bf, grad_cols, preferred_element_type=f32)
    both = over_dp(factor * jnp.concatenate([grad_a, grad_b], axis=0))
    bank_a, logit_grad_a = compose_back(both[:rank], weights_a, picked_a, mixing_a, vector_bank)
    bank_b, logit_grad_b = compose_back(both[rank:], weights_b, picked_b, mixing_b, vector_bank)
    bank_grad = over_tensor(bank_a + bank_b)

    here = [(0, 0), (0, 1)]
    beside = [(1, 0), (3, 0), (1, 1), (3, 1)]
    across = [(2, 0), (2, 1)]

    def take(chunks):
        return [blocks[h][i] for i, h in chunks]

    piece = lax.psum_scatter(
        forward(spot, wide, take(here)),
        "tensor",
        scatter_dimension=0,
        axis_index_groups=LANES,
        tiled=True,
    )[0]
    grown = backward(spots_of(here), None, out_grad, take(here))
    arrived = exchange(forward(spot, wide, take(beside)), "tensor", LANES)
    arrived = jnp.sum(arrived.astype(f32), axis=0).astype(bf16)
    above = jnp.concatenate([arrived[:, :part], arrived[:, 2 * part : 3 * part]], axis=1)
    below = jnp.concatenate([arrived[:, part : 2 * part], arrived[:, 3 * part :]], axis=1)
    grown = backward(spots_of(beside), grown, out_grad, take(beside))

    ordered = [piece, above, jnp.zeros_like(piece), below]
    slots = []
    for s in range(SIDE):
        turn = (s - far) % SIDE
        slots.append(
            jnp.where(turn == 0, piece, jnp.where(turn == 1, above, jnp.where(turn == 3, below, 0)))
        )
    slots = jnp.stack(slots).astype(bf16)
    moved = exchange(slots, "tensor", LANES)
    crossed = lax.ppermute(jnp.where(core == 0, slots[2:], moved[:2]), "tensor", SWAP)
    firsts = jnp.where(core == 0, slots[:2], crossed)
    seconds = jnp.where(core == 0, crossed, moved[2:])

    arrived = exchange(forward(spot, wide, take(across)), "tensor", LANES)
    piece = jnp.sum(arrived.astype(f32), axis=0).astype(bf16)
    grown = backward(spots_of(across), grown, out_grad, take(across))
    first, place, second = settle(piece, 2, z, core)
    cols = []
    for s in range(2):
        cols.append(firsts[s] + jnp.where(place == s, first, jnp.zeros_like(first)))
        cols.append(seconds[s] + second[s])
    summed = jnp.concatenate(cols, axis=1)
    layer_out = (
        summed.astype(f32)
        + adapter_scale * lax.dot_general(low_bf, up_b, rows_by_rows, preferred_element_type=f32)
    ).astype(bf16)
    other = lax.ppermute(grown[:, height:].astype(bf16), "tensor", SWAP)
    attn_grad = (
        grown[:, :height]
        + other.astype(f32)
        + adapter_scale * lax.dot_general(back_bf, down_a, rows_by_rows, preferred_element_type=f32)
    ).astype(bf16)
    return (layer_out, attn_grad, bank_grad, logit_grad_a, logit_grad_b)


def solution(mesh):
    return jax.shard_map(
        local,
        mesh=mesh,
        in_specs=(
            P("dp", "tensor"),
            P("tensor", "dp"),
            P(),
            P(None, "tensor", None),
            P(None, "tensor", None),
            P(None, "tensor", None),
            P(None, "tensor", None),
            P("dp", None),
        ),
        out_specs=(
            P("dp", "tensor"),
            P("dp", "tensor"),
            P(),
            P(None, "tensor", None),
            P(None, "tensor", None),
        ),
        check_vma=False,
    )
```

profile of v0, /device:TPU:1, one launch (start us, length us, event | category | flops | bytes accessed | tf_op | source)
XLA Modules:
  0.0 224.7 jit_solution(4689374496619729977)
XLA Ops:
  8.5 1.5 collective-permute-start.1
  10.2 1.4 collective-permute-done.1
  12.5 1.7 collective-permute-start.3
  15.3 2.1 collective-permute-start.5
  17.5 1.5 collective-permute-start.2
  19.1 3.8 %collective-permute-done.3 = bf16[2048,128]{1,0:T(8,128)(2,1)S(1)} collective-permute-done((bf16[2048,128]{1,0:T(8,128)(2,1)S(1)}, bf16[2048,128]{1,0:T(8,128)(2,1)S(1)}, u32[]{:S(2)}, u32[]{:S(2)}) %collective-permute-start.3) | collective-permute-done | bytes 524320 | tf_op jit(solution)/shard_map/ppermute | solution.py:43
  24.8 1.4 collective-permute-start.7
  29.6 2.9 %collective-permute-done.4 = bf16[2048,128]{1,0:T(8,128)(2,1)S(1)} collective-permute-done((bf16[2048,128]{1,0:T(8,128)(2,1)S(1)}, bf16[2048,128]{1,0:T(8,128)(2,1)S(1)}, u32[]{:S(2)}, u32[]{:S(2)}) %collective-permute-start.4) | collective-permute-done | bytes 524320 | tf_op jit(solution)/shard_map/ppermute | solution.py:43
  33.3 1.8 pad_maximum_fusion.refs_0_
  36.1 2.0 collective-permute-start.8
  38.2 2.6 %pad_maximum_fusion.1.refs_1_ = bf16[4,2048,128]{2,1,0:T(8,128)(2,1)} fusion(bf16[1,2048,128]{2,1,0:T(8,128)(2,1)S(1)} %bitcast.117, bf16[1,2048,128]{2,1,0:T(8,128)(2,1)S(1)} %bitcast.118, bf16[1,2048,128]{2,1,0:T(8,128)(2,1)} %bitcast.6, bf16[1,2048,128]{2,1,0:T(8,128)(2,1)S(1)} %copy-done.20), kind=kLoop, calls=%fused_computation.7 | loop fusion | flops 3145728 | bytes 4194304 | tf_op jit(solution)/shard_map/stack | solution.py:224
  40.8 2.5 %collective-permute-start.10 = (bf16[4,2048,128]{2,1,0:T(8,128)(2,1)}, bf16[4,2048,128]{2,1,0:T(8,128)(2,1)}, u32[]{:S(2)}, u32[]{:S(2)}) collective-permute-start(bf16[4,2048,128]{2,1,0:T(8,128)(2,1)} %pad_maximum_fusion.1.refs_1_), channel_id=1, source_target_pairs={{0,24},{1,97},{2,26},{3,99},{4,28},{5,101},{6,30},{7,103},{8,0},{9... | collective-permute-start | bytes 6291464 | tf_op jit(solution)/shard_map/ppermute | solution.py:43
  43.3 1.6 fusion.13
  44.9 5.7 %collective-permute-start.18 = (f32[32,512]{1,0:T(8,128)S(1)}, f32[32,512]{1,0:T(8,128)S(1)}, u32[]{:S(2)}, u32[]{:S(2)}) collective-permute-start(f32[32,512]{1,0:T(8,128)S(1)} %pad_maximum_fusion.7), channel_id=1, source_target_pairs={{0,1},{1,0},{2,3},{3,2},{4,5},{5,4},{6,7},{7,6},{8,9},{9,8},{10,11... | collective-permute-start | bytes 196616 | tf_op jit(solution)/shard_map/ppermute | solution.py:60
  51.6 1.4 collective-permute-start.19
  53.0 2.2 collective-permute-done.19
  55.2 3.0 %collective-permute-start.20 = (f32[32,512]{1,0:T(8,128)S(1)}, f32[32,512]{1,0:T(8,128)S(1)}, u32[]{:S(2)}, u32[]{:S(2)}) collective-permute-start(f32[32,512]{1,0:T(8,128)S(1)} %add.386), channel_id=1, source_target_pairs={{0,4},{1,5},{2,6},{3,7},{4,0},{5,1},{6,2},{7,3},{8,12},{9,13},{10,... | collective-permute-start | bytes 196616 | tf_op jit(solution)/shard_map/ppermute | solution.py:62
  58.2 1.7 collective-permute-done.20
  60.5 2.3 %collective-permute-start = (bf16[512,1024]{1,0:T(8,128)(2,1)S(1)}, bf16[512,1024]{1,0:T(8,128)(2,1)}, u32[]{:S(2)}, u32[]{:S(2)}) collective-permute-start(bf16[512,1024]{1,0:T(8,128)(2,1)S(1)} %copy-done.8), channel_id=1, source_target_pairs={{0,1},{1,0},{2,3},{3,2},{4,5},{5,4},{6,7},{7,6},{8,9},{9,8},{10,11... | collective-permute-start | bytes 3145736 | tf_op jit(solution)/shard_map/ppermute | solution.py:240
  64.0 1.5 fusion.11
  65.8 1.3 constant_dynamic-update-slice_fusion.wide_ref
  67.2 4.3 %collective-permute-done.22 = f32[32,1024]{1,0:T(8,128)S(1)} collective-permute-done((f32[32,1024]{1,0:T(8,128)S(1)}, f32[32,1024]{1,0:T(8,128)S(1)}, u32[]{:S(2)}, u32[]{:S(2)}) %collective-permute-start.22) | collective-permute-done | bytes 131104 | tf_op jit(solution)/shard_map/ppermute | solution.py:67
  72.2 6.2 %forward.3 = bf16[4,512,256]{2,1,0:T(8,128)(2,1)} custom-call(s32[1]{0:T(128)} %bitcast.near_ref, bf16[512,2048]{1,0:T(8,128)(2,1)S(1)} %constant_dynamic-update-slice_fusion.wide_ref, bf16[4,2048,128]{2,1,0:T(8,128)(2,1)S(1)} %pad_maximum_fusion.refs_0_, bf16[4,2048,128]{2,1,0:T(8,128)(2,1)} %pad_maximum_fusion.1.refs_1_), custom_call_target="tpu_custom_call" | custom-call | flops 2147483648 | bytes 6291456 | tf_op jit(solution)/shard_map/forward/pallas_call | solution.py:106
  79.6 5.6 %collective-permute-done.23 = f32[32,1024]{1,0:T(8,128)} collective-permute-done((f32[32,1024]{1,0:T(8,128)}, f32[32,1024]{1,0:T(8,128)}, u32[]{:S(2)}, u32[]{:S(2)}) %collective-permute-start.23) | collective-permute-done | bytes 131104 | tf_op jit(solution)/shard_map/ppermute | solution.py:67
  87.3 1.6 copy-done.6
  88.9 8.7 %forward.4 = bf16[4,512,512]{2,1,0:T(8,128)(2,1)S(1)} custom-call(s32[1]{0:T(128)} %bitcast.near_ref, bf16[512,2048]{1,0:T(8,128)(2,1)S(1)} %copy-done.6, bf16[4,2048,128]{2,1,0:T(8,128)(2,1)} %collective-permute-done.8.refs_0_, bf16[4,2048,128]{2,1,0:T(8,128)(2,1)} %collective-permute-done.9.refs_1_, bf16[4,2048,128]{2,1,0:T(8,128)(2,1)} %collective-permute-done.10.refs_2_, ...), custom_call_target="tpu_custom_call" | custom-call | flops 4294967296 | bytes 10485760 | tf_op jit(solution)/shard_map/forward/pallas_call | solution.py:106
  97.7 1.4 copy-done.4
  99.0 4.4 %all-to-all-start = ((bf16[4,512,512]{2,1,0:T(8,128)(2,1)}), bf16[4,512,512]{2,1,0:T(8,128)(2,1)}, u32[]{:S(2)}, u32[]{:S(2)}) async-start(bf16[4,512,512]{2,1,0:T(8,128)(2,1)} %copy-done.4), calls=%async_computation.1 | async-start | bytes 4194304 | tf_op jit(solution)/shard_map/all_to_all | solution.py:54
  103.5 5.7 %backward.3.refs_20_ = f32[512,2048]{1,0:T(8,128)S(1)} custom-call(s32[8]{0:T(128)S(1)} %stack.193.spots_ref, bf16[4,2048,128]{2,1,0:T(8,128)(2,1)S(1)} %pad_maximum_fusion.refs_0_, bf16[4,2048,128]{2,1,0:T(8,128)(2,1)} %pad_maximum_fusion.1.refs_1_, bf16[512,8192]{1,0:T(8,128)(2,1)} %refs_9_.5, bf16[512,8192]{1,0:T(8,128)(2,1)} %refs_9_.5, ...), custom_call_target="tpu_custom_call" | custom-call | flops 2147483648 | bytes 12582912 | tf_op jit(solution)/shard_map/backward/pallas_call | solution.py:148
  109.3 2.7 %collective-permute-start.25 = (f32[32,1024]{1,0:T(8,128)S(1)}, f32[32,1024]{1,0:T(8,128)S(1)}, u32[]{:S(2)}, u32[]{:S(2)}) collective-permute-start(f32[32,1024]{1,0:T(8,128)S(1)} %add.455), channel_id=1, source_target_pairs={{0,64},{8,72},{16,80},{24,88},{32,96},{40,104},{48,112},{56,120},{... | collective-permute-start | bytes 393224 | tf_op jit(solution)/shard_map/ppermute | solution.py:67
  112.0 1.8 fusion.35
  115.2 2.2 collective-permute-start.13
  118.8 19.5 %collective-permute-start.26 = (f32[256,256]{1,0:T(8,128)S(1)}, f32[256,256]{1,0:T(8,128)S(1)}, u32[]{:S(2)}, u32[]{:S(2)}) collective-permute-start(f32[256,256]{1,0:T(8,128)S(1)} %fusion.4), channel_id=1, source_target_pairs={{0,1},{1,0},{2,3},{3,2},{4,5},{5,4},{6,7},{7,6},{8,9},{9,8},{10,11... | collective-permute-start | bytes 786440 | tf_op jit(solution)/shard_map/ppermute | solution.py:60
  140.7 1.8 collective-permute-start.27
  142.4 2.2 reduce_sum.78
  146.6 1.4 select_select_fusion.3
  149.1 4.3 %all-to-all-start.1 = ((bf16[4,512,256]{2,1,0:T(8,128)(2,1)}), bf16[4,512,256]{2,1,0:T(8,128)(2,1)}, u32[]{:S(2)}, u32[]{:S(2)}) async-start(bf16[4,512,256]{2,1,0:T(8,128)(2,1)} %pad_maximum_fusion.2), calls=%async_computation.2 | async-start | bytes 2097152 | tf_op jit(solution)/shard_map/all_to_all | solution.py:54
  153.4 9.6 %backward.4.refs_10_ = f32[512,2048]{1,0:T(8,128)S(1)} custom-call(s32[16]{0:T(128)S(1)} %stack.184.spots_ref, bf16[4,2048,128]{2,1,0:T(8,128)(2,1)} %collective-permute-done.8.refs_0_, bf16[4,2048,128]{2,1,0:T(8,128)(2,1)} %collective-permute-done.9.refs_1_, bf16[4,2048,128]{2,1,0:T(8,128)(2,1)} %collective-permute-done.10.refs_2_, ...), custom_call_target="tpu_custom_call" | custom-call | flops 4294967296 | bytes 16777216 | tf_op jit(solution)/shard_map/backward/pallas_call | solution.py:148
  162.9 5.8 %backward.5 = f32[512,2048]{1,0:T(8,128)S(1)} custom-call(s32[8]{0:T(128)S(1)} %stack.167.spots_ref, bf16[4,2048,128]{2,1,0:T(8,128)(2,1)S(1)} %collective-permute-done.13.refs_0_, bf16[4,2048,128]{2,1,0:T(8,128)(2,1)} %collective-permute-done.14.refs_1_, bf16[512,8192]{1,0:T(8,128)(2,1)} %refs_9_.5, bf16[512,8192]{1,0:T(8,128)(2,1)} %refs_9_.5, ...), custom_call_target="tpu_custom_call" | custom-call | flops 2147483648 | bytes 12582912 | tf_op jit(solution)/shard_map/backward/pallas_call | solution.py:148
  168.8 2.0 copy-done.3
  172.7 6.2 %forward.5 = bf16[4,512,256]{2,1,0:T(8,128)(2,1)} custom-call(s32[1]{0:T(128)} %bitcast.near_ref, bf16[512,2048]{1,0:T(8,128)(2,1)S(1)} %copy-done.7, bf16[4,2048,128]{2,1,0:T(8,128)(2,1)S(1)} %collective-permute-done.13.refs_0_, bf16[4,2048,128]{2,1,0:T(8,128)(2,1)} %collective-permute-done.14.refs_1_), custom_call_target="tpu_custom_call" | custom-call | flops 2147483648 | bytes 6291456 | tf_op jit(solution)/shard_map/forward/pallas_call | solution.py:106
  178.9 4.3 %all-to-all-start.2 = ((bf16[4,512,256]{2,1,0:T(8,128)(2,1)}), bf16[4,512,256]{2,1,0:T(8,128)(2,1)S(1)}, u32[]{:S(2)}, u32[]{:S(2)}) async-start(bf16[4,512,256]{2,1,0:T(8,128)(2,1)} %forward.5), calls=%async_computation.3 | async-start | bytes 2097152 | tf_op jit(solution)/shard_map/all_to_all | solution.py:54
  187.0 3.3 %collective-permute-start.28 = (f32[256,256]{1,0:T(8,128)S(1)}, f32[256,256]{1,0:T(8,128)S(1)}, u32[]{:S(2)}, u32[]{:S(2)}) collective-permute-start(f32[256,256]{1,0:T(8,128)S(1)} %add.459), channel_id=1, source_target_pairs={{0,4},{1,5},{2,6},{3,7},{4,0},{5,1},{6,2},{7,3},{8,12},{9,13},{10,... | collective-permute-start | bytes 786440 | tf_op jit(solution)/shard_map/ppermute | solution.py:62
  191.2 12.0 %collective-permute-done.28 = f32[256,256]{1,0:T(8,128)S(1)} collective-permute-done((f32[256,256]{1,0:T(8,128)S(1)}, f32[256,256]{1,0:T(8,128)S(1)}, u32[]{:S(2)}, u32[]{:S(2)}) %collective-permute-start.28) | collective-permute-done | bytes 262176 | tf_op jit(solution)/shard_map/ppermute | solution.py:62
  203.9 2.2 %maximum_select_fusion = (bf16[2,512,256]{2,1,0:T(8,128)(2,1)}, bf16[2,512,256]{2,1,0:T(8,128)(2,1)}) fusion(bf16[2,512,256]{2,1,0:T(8,128)(2,1)S(1)} %collective-permute-done.12, bf16[1,512,256]{2,1,0:T(8,128)(2,1)S(1)} %copy-done.17, bf16[1,512,256]{2,1,0:T(8,128)(2,1)S(1)} %copy-done.15, pred[]{:T(512)S(6)} %eq.93, bf16[4,512,256]{2,1,0:T(8,128)(2,1)} %all-to-all-done.1), kind=kLoop, calls=%fused_computation.29 | loop fusion | flops 786432 | bytes 2621441 | tf_op jit(solution)/shard_map/jit(_where)/select_n | solution.py:294
  206.4 3.8 %collective-permute-start.16 = (bf16[512,256]{1,0:T(8,128)(2,1)S(1)}, bf16[512,256]{1,0:T(8,128)(2,1)S(1)}, u32[]{:S(2)}, u32[]{:S(2)}) collective-permute-start(bf16[512,256]{1,0:T(8,128)(2,1)S(1)} %reduce_sum.79), channel_id=1, source_target_pairs={{1,4},{5,5},{9,12},{13,13},{17,20},{21,21},{25,28},{29,29},{33,38}... | collective-permute-start | bytes 786440 | tf_op jit(solution)/shard_map/ppermute | solution.py:194
  212.3 3.4 %fusion.3 = bf16[512,1024]{1,0:T(8,128)(2,1)} fusion(f32[512,2048]{1,0:T(8,128)} %copy-done.3, f32[512,1024]{1,0:T(8,128)S(1)} %copy-done.9, bf16[512,1024]{1,0:T(8,128)(2,1)} %collective-permute-done.21), kind=kLoop, calls=%fused_computation.5 | loop fusion | flops 2621440 | bytes 6291456 | tf_op jit(solution)/shard_map/convert_element_type | solution.py:315
  216.5 1.4 add_convert_fusion
  (176 shorter events, 36.2 us)
Async XLA Ops:
  7.2 15.8 %copy-start = (f32[256,256]{1,0:T(8,128)S(1)}, f32[256,256]{1,0:T(8,128)}, u32[]{:S(2)}) copy-start(f32[256,256]{1,0:T(8,128)} %param.10) | copy-start | bytes 786436
  7.2 137.6 %reduce-scatter.2.cloned.1.call-start = ((), (), s32[]{:S(2)}) async-start(), calls=%async_computation.4 | async-start | bytes 1310720 | tf_op jit(solution)/shard_map/reduce_scatter | solution.py:270
  8.5 3.0 %collective-permute-start.1 = (bf16[1024,256]{1,0:T(8,128)(2,1)S(1)}, bf16[1024,256]{1,0:T(8,128)(2,1)S(1)}, u32[]{:S(2)}, u32[]{:S(2)}) collective-permute-start(bf16[1024,256]{1,0:T(8,128)(2,1)S(1)} %get-tuple-element.10), channel_id=1, source_target_pairs={{0,1},{1,0},{2,3},{3,2},{4,5},{5,4},{6,7},{7,6},{8,9},{9,8},{10,11... | collective-permute-start | bytes 1572872 | tf_op jit(solution)/shard_map/ppermute | solution.py:219
  11.6 12.2 %copy-start.36 = (s32[16,4,2]{0,2,1:T(2,128)S(1)}, s32[16,4,2]{0,2,1:T(2,128)}, u32[]{:S(2)}) copy-start(s32[16,4,2]{0,2,1:T(2,128)} %param.12) | copy-start | bytes 1540
  11.6 15.8 %copy-start.8 = (bf16[512,1024]{1,0:T(8,128)(2,1)S(1)}, bf16[512,1024]{1,0:T(8,128)(2,1)}, u32[]{:S(2)}) copy-start(bf16[512,1024]{1,0:T(8,128)(2,1)} %param.8) | copy-start | bytes 3145732
  12.5 10.4 %collective-permute-start.3 = (bf16[2048,128]{1,0:T(8,128)(2,1)S(1)}, bf16[2048,128]{1,0:T(8,128)(2,1)S(1)}, u32[]{:S(2)}, u32[]{:S(2)}) collective-permute-start(bf16[2048,128]{1,0:T(8,128)(2,1)S(1)} %get-tuple-element.30), channel_id=1, source_target_pairs={{0,32},{1,9},{2,34},{3,11},{4,36},{5,13},{6,38},{7,15},{8,40},{9,1... | collective-permute-start | bytes 1572872 | tf_op jit(solution)/shard_map/ppermute | solution.py:43
  15.3 10.9 %collective-permute-start.5 = (bf16[2048,128]{1,0:T(8,128)(2,1)}, bf16[2048,128]{1,0:T(8,128)(2,1)}, u32[]{:S(2)}, u32[]{:S(2)}) collective-permute-start(bf16[2048,128]{1,0:T(8,128)(2,1)} %get-tuple-element.24), channel_id=1, source_target_pairs={{0,96},{1,25},{2,98},{3,27},{4,100},{5,29},{6,102},{7,31},{8,104},... | collective-permute-start | bytes 1572872 | tf_op jit(solution)/shard_map/ppermute | solution.py:43
  17.4 17.7 %copy-start.41 = (f32[16,4,2]{0,2,1:T(2,128)}, f32[16,4,2]{0,2,1:T(2,128)S(1)}, u32[]{:S(2)}) copy-start(f32[16,4,2]{0,2,1:T(2,128)S(1)} %add_divide_fusion.1) | copy-start | bytes 1540
  17.5 12.1 %collective-permute-start.2 = (bf16[2048,128]{1,0:T(8,128)(2,1)S(1)}, bf16[2048,128]{1,0:T(8,128)(2,1)S(1)}, u32[]{:S(2)}, u32[]{:S(2)}) collective-permute-start(bf16[2048,128]{1,0:T(8,128)(2,1)S(1)} %get-tuple-element.30), channel_id=1, source_target_pairs={{0,96},{1,25},{2,98},{3,27},{4,100},{5,29},{6,102},{7,31},{8,104},... | collective-permute-start | bytes 1572872 | tf_op jit(solution)/shard_map/ppermute | solution.py:43
  22.9 9.5 %copy-start.22 = (bf16[2048,128]{1,0:T(8,128)(2,1)}, bf16[2048,128]{1,0:T(8,128)(2,1)S(1)}, u32[]{:S(2)}) copy-start(bf16[2048,128]{1,0:T(8,128)(2,1)S(1)} %collective-permute-done.3) | copy-start | bytes 1572868
  22.9 9.5 %collective-permute-start.4 = (bf16[2048,128]{1,0:T(8,128)(2,1)S(1)}, bf16[2048,128]{1,0:T(8,128)(2,1)S(1)}, u32[]{:S(2)}, u32[]{:S(2)}) collective-permute-start(bf16[2048,128]{1,0:T(8,128)(2,1)S(1)} %collective-permute-done.3), channel_id=1, source_target_pairs={{0,32},{1,9},{2,34},{3,11},{4,36},{5,13},{6,38},{7,15},{8,40},{9,1... | collective-permute-start | bytes 1572872 | tf_op jit(solution)/shard_map/ppermute | solution.py:43
  24.8 13.4 %collective-permute-start.7 = (bf16[2048,128]{1,0:T(8,128)(2,1)}, bf16[2048,128]{1,0:T(8,128)(2,1)S(1)}, u32[]{:S(2)}, u32[]{:S(2)}) collective-permute-start(bf16[2048,128]{1,0:T(8,128)(2,1)} %get-tuple-element.24), channel_id=1, source_target_pairs={{0,32},{1,9},{2,34},{3,11},{4,36},{5,13},{6,38},{7,15},{8,40},{9,1... | collective-permute-start | bytes 1572872 | tf_op jit(solution)/shard_map/ppermute | solution.py:43
  26.1 12.0 %collective-permute-start.6 = (bf16[2048,128]{1,0:T(8,128)(2,1)}, bf16[2048,128]{1,0:T(8,128)(2,1)S(1)}, u32[]{:S(2)}, u32[]{:S(2)}) collective-permute-start(bf16[2048,128]{1,0:T(8,128)(2,1)} %collective-permute-done.5), channel_id=1, source_target_pairs={{0,96},{1,25},{2,98},{3,27},{4,100},{5,29},{6,102},{7,31},{8,104},... | collective-permute-start | bytes 1572872 | tf_op jit(solution)/shard_map/ppermute | solution.py:43
  35.1 52.2 %collective-permute-start.9 = (bf16[4,2048,128]{2,1,0:T(8,128)(2,1)S(1)}, bf16[4,2048,128]{2,1,0:T(8,128)(2,1)}, u32[]{:S(2)}, u32[]{:S(2)}) collective-permute-start(bf16[4,2048,128]{2,1,0:T(8,128)(2,1)S(1)} %pad_maximum_fusion.refs_0_), channel_id=1, source_target_pairs={{0,8},{1,33},{2,10},{3,35},{4,12},{5,37},{6,14},{7,39},{8,16},{9,4... | collective-permute-start | bytes 6291464 | tf_op jit(solution)/shard_map/ppermute | solution.py:43
  36.1 51.2 %collective-permute-start.8 = (bf16[4,2048,128]{2,1,0:T(8,128)(2,1)S(1)}, bf16[4,2048,128]{2,1,0:T(8,128)(2,1)}, u32[]{:S(2)}, u32[]{:S(2)}) collective-permute-start(bf16[4,2048,128]{2,1,0:T(8,128)(2,1)S(1)} %pad_maximum_fusion.refs_0_), channel_id=1, source_target_pairs={{0,24},{1,97},{2,26},{3,99},{4,28},{5,101},{6,30},{7,103},{8,0},{9... | collective-permute-start | bytes 6291464 | tf_op jit(solution)/shard_map/ppermute | solution.py:43
  40.8 46.5 %collective-permute-start.10 = (bf16[4,2048,128]{2,1,0:T(8,128)(2,1)}, bf16[4,2048,128]{2,1,0:T(8,128)(2,1)}, u32[]{:S(2)}, u32[]{:S(2)}) collective-permute-start(bf16[4,2048,128]{2,1,0:T(8,128)(2,1)} %pad_maximum_fusion.1.refs_1_), channel_id=1, source_target_pairs={{0,24},{1,97},{2,26},{3,99},{4,28},{5,101},{6,30},{7,103},{8,0},{9... | collective-permute-start | bytes 6291464 | tf_op jit(solution)/shard_map/ppermute | solution.py:43
  43.3 44.0 %collective-permute-start.11 = (bf16[4,2048,128]{2,1,0:T(8,128)(2,1)}, bf16[4,2048,128]{2,1,0:T(8,128)(2,1)}, u32[]{:S(2)}, u32[]{:S(2)}) collective-permute-start(bf16[4,2048,128]{2,1,0:T(8,128)(2,1)} %pad_maximum_fusion.1.refs_1_), channel_id=1, source_target_pairs={{0,8},{1,33},{2,10},{3,35},{4,12},{5,37},{6,14},{7,39},{8,16},{9,4... | collective-permute-start | bytes 6291464 | tf_op jit(solution)/shard_map/ppermute | solution.py:43
  44.9 6.6 %collective-permute-start.18 = (f32[32,512]{1,0:T(8,128)S(1)}, f32[32,512]{1,0:T(8,128)S(1)}, u32[]{:S(2)}, u32[]{:S(2)}) collective-permute-start(f32[32,512]{1,0:T(8,128)S(1)} %pad_maximum_fusion.7), channel_id=1, source_target_pairs={{0,1},{1,0},{2,3},{3,2},{4,5},{5,4},{6,7},{7,6},{8,9},{9,8},{10,11... | collective-permute-start | bytes 196616 | tf_op jit(solution)/shard_map/ppermute | solution.py:60
  51.6 3.6 %collective-permute-start.19 = (f32[32,512]{1,0:T(8,128)S(1)}, f32[32,512]{1,0:T(8,128)S(1)}, u32[]{:S(2)}, u32[]{:S(2)}) collective-permute-start(f32[32,512]{1,0:T(8,128)S(1)} %add.385), channel_id=1, source_target_pairs={{0,2},{1,3},{2,0},{3,1},{4,6},{5,7},{6,4},{7,5},{8,10},{9,11},{10,... | collective-permute-start | bytes 196616 | tf_op jit(solution)/shard_map/ppermute | solution.py:61
  55.2 4.7 %collective-permute-start.20 = (f32[32,512]{1,0:T(8,128)S(1)}, f32[32,512]{1,0:T(8,128)S(1)}, u32[]{:S(2)}, u32[]{:S(2)}) collective-permute-start(f32[32,512]{1,0:T(8,128)S(1)} %add.386), channel_id=1, source_target_pairs={{0,4},{1,5},{2,6},{3,7},{4,0},{5,1},{6,2},{7,3},{8,12},{9,13},{10,... | collective-permute-start | bytes 196616 | tf_op jit(solution)/shard_map/ppermute | solution.py:62
  60.5 5.2 %collective-permute-start = (bf16[512,1024]{1,0:T(8,128)(2,1)S(1)}, bf16[512,1024]{1,0:T(8,128)(2,1)}, u32[]{:S(2)}, u32[]{:S(2)}) collective-permute-start(bf16[512,1024]{1,0:T(8,128)(2,1)S(1)} %copy-done.8), channel_id=1, source_target_pairs={{0,1},{1,0},{2,3},{3,2},{4,5},{5,4},{6,7},{7,6},{8,9},{9,8},{10,11... | collective-permute-start | bytes 3145736 | tf_op jit(solution)/shard_map/ppermute | solution.py:240
  65.7 5.8 %collective-permute-start.22 = (f32[32,1024]{1,0:T(8,128)S(1)}, f32[32,1024]{1,0:T(8,128)S(1)}, u32[]{:S(2)}, u32[]{:S(2)}) collective-permute-start(f32[32,1024]{1,0:T(8,128)S(1)} %maximum_multiply_fusion), channel_id=1, source_target_pairs={{0,8},{8,0},{16,24},{24,16},{32,40},{40,32},{48,56},{56,48},{64,72... | collective-permute-start | bytes 393224 | tf_op jit(solution)/shard_map/ppermute | solution.py:67
  72.2 13.1 %collective-permute-start.23 = (f32[32,1024]{1,0:T(8,128)}, f32[32,1024]{1,0:T(8,128)}, u32[]{:S(2)}, u32[]{:S(2)}) collective-permute-start(f32[32,1024]{1,0:T(8,128)} %fusion.43), channel_id=1, source_target_pairs={{0,32},{8,40},{16,48},{24,56},{32,0},{40,8},{48,16},{56,24},{64,96... | collective-permute-start | bytes 393224 | tf_op jit(solution)/shard_map/ppermute | solution.py:67
  86.2 23.0 %collective-permute-start.24 = (f32[32,1024]{1,0:T(8,128)S(1)}, f32[32,1024]{1,0:T(8,128)S(1)}, u32[]{:S(2)}, u32[]{:S(2)}) collective-permute-start(f32[32,1024]{1,0:T(8,128)S(1)} %add.454), channel_id=1, source_target_pairs={{0,16},{8,24},{16,0},{24,8},{32,48},{40,56},{48,32},{56,40},{64,80... | collective-permute-start | bytes 393224 | tf_op jit(solution)/shard_map/ppermute | solution.py:67
  99.0 43.4 %all-to-all-start = ((bf16[4,512,512]{2,1,0:T(8,128)(2,1)}), bf16[4,512,512]{2,1,0:T(8,128)(2,1)}, u32[]{:S(2)}, u32[]{:S(2)}) async-start(bf16[4,512,512]{2,1,0:T(8,128)(2,1)} %copy-done.4), calls=%async_computation.1 | async-start | bytes 4194304 | tf_op jit(solution)/shard_map/all_to_all | solution.py:54
  103.5 8.5 %copy-start.25 = (bf16[4,2,8,256]{3,2,0,1:T(8,128)(2,1)S(1)}, bf16[4,2,8,256]{3,2,0,1:T(8,128)(2,1)}, u32[]{:S(2)}) copy-start(bf16[4,2,8,256]{3,2,0,1:T(8,128)(2,1)} %copy.43) | copy-start | bytes 98308
  103.5 8.5 %copy-start.30 = (bf16[32,512]{1,0:T(8,128)(2,1)S(1)}, bf16[32,512]{1,0:T(8,128)(2,1)}, u32[]{:S(2)}) copy-start(bf16[32,512]{1,0:T(8,128)(2,1)} %copy-done.29) | copy-start | bytes 98308
  109.2 9.6 %copy-start.2 = (f32[512,2048]{1,0:T(8,128)}, f32[512,2048]{1,0:T(8,128)S(1)}, u32[]{:S(2)}) copy-start(f32[512,2048]{1,0:T(8,128)S(1)} %backward.3.refs_20_) | copy-start | bytes 12582916
  109.3 5.4 %collective-permute-start.25 = (f32[32,1024]{1,0:T(8,128)S(1)}, f32[32,1024]{1,0:T(8,128)S(1)}, u32[]{:S(2)}, u32[]{:S(2)}) collective-permute-start(f32[32,1024]{1,0:T(8,128)S(1)} %add.455), channel_id=1, source_target_pairs={{0,64},{8,72},{16,80},{24,88},{32,96},{40,104},{48,112},{56,120},{... | collective-permute-start | bytes 393224 | tf_op jit(solution)/shard_map/ppermute | solution.py:67
  115.2 47.8 %collective-permute-start.13 = (bf16[4,2048,128]{2,1,0:T(8,128)(2,1)}, bf16[4,2048,128]{2,1,0:T(8,128)(2,1)S(1)}, u32[]{:S(2)}, u32[]{:S(2)}) collective-permute-start(bf16[4,2048,128]{2,1,0:T(8,128)(2,1)} %collective-permute-done.9.refs_1_), channel_id=1, source_target_pairs={{0,8},{1,33},{2,10},{3,35},{4,12},{5,37},{6,14},{7,39},{8,16},{9,4... | collective-permute-start | bytes 6291464 | tf_op jit(solution)/shard_map/ppermute | solution.py:43
  117.4 45.6 %collective-permute-start.14 = (bf16[4,2048,128]{2,1,0:T(8,128)(2,1)}, bf16[4,2048,128]{2,1,0:T(8,128)(2,1)}, u32[]{:S(2)}, u32[]{:S(2)}) collective-permute-start(bf16[4,2048,128]{2,1,0:T(8,128)(2,1)} %collective-permute-done.10.refs_2_), channel_id=1, source_target_pairs={{0,24},{1,97},{2,26},{3,99},{4,28},{5,101},{6,30},{7,103},{8,0},{9... | collective-permute-start | bytes 6291464 | tf_op jit(solution)/shard_map/ppermute | solution.py:43
  118.8 21.1 %collective-permute-start.26 = (f32[256,256]{1,0:T(8,128)S(1)}, f32[256,256]{1,0:T(8,128)S(1)}, u32[]{:S(2)}, u32[]{:S(2)}) collective-permute-start(f32[256,256]{1,0:T(8,128)S(1)} %fusion.4), channel_id=1, source_target_pairs={{0,1},{1,0},{2,3},{3,2},{4,5},{5,4},{6,7},{7,6},{8,9},{9,8},{10,11... | collective-permute-start | bytes 786440 | tf_op jit(solution)/shard_map/ppermute | solution.py:60
  140.7 45.3 %collective-permute-start.27 = (f32[256,256]{1,0:T(8,128)}, f32[256,256]{1,0:T(8,128)}, u32[]{:S(2)}, u32[]{:S(2)}) collective-permute-start(f32[256,256]{1,0:T(8,128)} %add.458), channel_id=1, source_target_pairs={{0,2},{1,3},{2,0},{3,1},{4,6},{5,7},{6,4},{7,5},{8,10},{9,11},{10,... | collective-permute-start | bytes 786440 | tf_op jit(solution)/shard_map/ppermute | solution.py:61
  149.1 29.8 %all-to-all-start.1 = ((bf16[4,512,256]{2,1,0:T(8,128)(2,1)}), bf16[4,512,256]{2,1,0:T(8,128)(2,1)}, u32[]{:S(2)}, u32[]{:S(2)}) async-start(bf16[4,512,256]{2,1,0:T(8,128)(2,1)} %pad_maximum_fusion.2), calls=%async_computation.2 | async-start | bytes 2097152 | tf_op jit(solution)/shard_map/all_to_all | solution.py:54
  171.9 40.3 %collective-permute-start.21 = (bf16[512,1024]{1,0:T(8,128)(2,1)}, bf16[512,1024]{1,0:T(8,128)(2,1)}, u32[]{:S(2)}, u32[]{:S(2)}) collective-permute-start(bf16[512,1024]{1,0:T(8,128)(2,1)} %slice.149), channel_id=1, source_target_pairs={{0,1},{1,0},{2,3},{3,2},{4,5},{5,4},{6,7},{7,6},{8,9},{9,8},{10,11... | collective-permute-start | bytes 3145736 | tf_op jit(solution)/shard_map/ppermute | solution.py:310
  178.9 11.5 %copy-start.28 = (f32[16,4,256]{2,0,1:T(8,128)S(1)}, f32[16,4,256]{2,0,1:T(8,128)}, u32[]{:S(2)}) copy-start(f32[16,4,256]{2,0,1:T(8,128)} %fusion.19) | copy-start | bytes 196612
  178.9 11.5 %copy-start.38 = (s32[16,4,2]{0,2,1:T(2,128)S(1)}, s32[16,4,2]{0,2,1:T(2,128)}, u32[]{:S(2)}) copy-start(s32[16,4,2]{0,2,1:T(2,128)} %param.14) | copy-start | bytes 1540
  178.9 11.6 %copy-start.40 = (f32[16,4,2]{0,2,1:T(2,128)S(1)}, f32[16,4,2]{0,2,1:T(2,128)}, u32[]{:S(2)}) copy-start(f32[16,4,2]{0,2,1:T(2,128)} %copy-done.39) | copy-start | bytes 1540
  178.9 27.2 %all-to-all-start.2 = ((bf16[4,512,256]{2,1,0:T(8,128)(2,1)}), bf16[4,512,256]{2,1,0:T(8,128)(2,1)S(1)}, u32[]{:S(2)}, u32[]{:S(2)}) async-start(bf16[4,512,256]{2,1,0:T(8,128)(2,1)} %forward.5), calls=%async_computation.3 | async-start | bytes 2097152 | tf_op jit(solution)/shard_map/all_to_all | solution.py:54
  183.2 20.7 %copy-start.15 = (bf16[1,512,256]{2,1,0:T(8,128)(2,1)S(1)}, bf16[1,512,256]{2,1,0:T(8,128)(2,1)}, u32[]{:S(2)}) copy-start(bf16[1,512,256]{2,1,0:T(8,128)(2,1)} %copy-done.14) | copy-start | bytes 786436
  183.3 20.6 %copy-start.17 = (bf16[1,512,256]{2,1,0:T(8,128)(2,1)S(1)}, bf16[1,512,256]{2,1,0:T(8,128)(2,1)}, u32[]{:S(2)}) copy-start(bf16[1,512,256]{2,1,0:T(8,128)(2,1)} %copy-done.16) | copy-start | bytes 786436
  184.4 19.5 %collective-permute-start.12 = (bf16[2,512,256]{2,1,0:T(8,128)(2,1)S(1)}, bf16[2,512,256]{2,1,0:T(8,128)(2,1)S(1)}, u32[]{:S(2)}, u32[]{:S(2)}) collective-permute-start(bf16[2,512,256]{2,1,0:T(8,128)(2,1)S(1)} %slice_select_fusion.1), channel_id=1, source_target_pairs={{0,1},{1,0},{2,3},{3,2},{4,5},{5,4},{6,7},{7,6},{8,9},{9,8},{10,11... | collective-permute-start | bytes 1572872 | tf_op jit(solution)/shard_map/ppermute | solution.py:293
  187.0 16.1 %collective-permute-start.28 = (f32[256,256]{1,0:T(8,128)S(1)}, f32[256,256]{1,0:T(8,128)S(1)}, u32[]{:S(2)}, u32[]{:S(2)}) collective-permute-start(f32[256,256]{1,0:T(8,128)S(1)} %add.459), channel_id=1, source_target_pairs={{0,4},{1,5},{2,6},{3,7},{4,0},{5,1},{6,2},{7,3},{8,12},{9,13},{10,... | collective-permute-start | bytes 786440 | tf_op jit(solution)/shard_map/ppermute | solution.py:62
  206.4 9.3 %copy-start.18 = (bf16[2,512,256]{2,1,0:T(8,128)(2,1)S(1)}, bf16[2,512,256]{2,1,0:T(8,128)(2,1)}, u32[]{:S(2)}) copy-start(bf16[2,512,256]{2,1,0:T(8,128)(2,1)} %get-tuple-element.18) | copy-start | bytes 1572868
  206.4 9.4 %copy-start.19 = (bf16[2,512,256]{2,1,0:T(8,128)(2,1)S(1)}, bf16[2,512,256]{2,1,0:T(8,128)(2,1)}, u32[]{:S(2)}) copy-start(bf16[2,512,256]{2,1,0:T(8,128)(2,1)} %get-tuple-element.17) | copy-start | bytes 1572868
  206.4 9.3 %collective-permute-start.16 = (bf16[512,256]{1,0:T(8,128)(2,1)S(1)}, bf16[512,256]{1,0:T(8,128)(2,1)S(1)}, u32[]{:S(2)}, u32[]{:S(2)}) collective-permute-start(bf16[512,256]{1,0:T(8,128)(2,1)S(1)} %reduce_sum.79), channel_id=1, source_target_pairs={{1,4},{5,5},{9,12},{13,13},{17,20},{21,21},{25,28},{29,29},{33,38}... | collective-permute-start | bytes 786440 | tf_op jit(solution)/shard_map/ppermute | solution.py:194
  210.2 5.5 %collective-permute-start.17 = (bf16[512,256]{1,0:T(8,128)(2,1)S(1)}, bf16[512,256]{1,0:T(8,128)(2,1)S(1)}, u32[]{:S(2)}, u32[]{:S(2)}) collective-permute-start(bf16[512,256]{1,0:T(8,128)(2,1)S(1)} %reduce_sum.79), channel_id=1, source_target_pairs={{3,4},{7,5},{11,12},{15,13},{19,20},{23,21},{27,28},{31,29},{35,38... | collective-permute-start | bytes 786440 | tf_op jit(solution)/shard_map/ppermute | solution.py:194
  210.9 4.9 %collective-permute-start.15 = (bf16[512,256]{1,0:T(8,128)(2,1)S(1)}, bf16[512,256]{1,0:T(8,128)(2,1)S(1)}, u32[]{:S(2)}, u32[]{:S(2)}) collective-permute-start(bf16[512,256]{1,0:T(8,128)(2,1)S(1)} %reduce_sum.79), channel_id=1, source_target_pairs={{0,1},{2,3},{4,5},{6,7},{8,9},{10,11},{12,13},{14,15},{32,33},{34,... | collective-permute-start | bytes 786440 | tf_op jit(solution)/shard_map/ppermute | solution.py:199
  (30 other events, 85.8 us)
Sparse Core Ops, SparseCore 0:
  79.8 45.3 reduce-scatter.1
where the time goes:
time: 227 us; the launch traced here: 225 us
  starting transfers between devices  79.2 us (35%)
  Pallas kernels  42.2 us (19%)
  waiting for transfers between devices  36.9 us (16%)
  other arithmetic  26.8 us (12%)
  between operations  14.8 us (7%)
  local copies, waits for them, and re-layouts  14.5 us (6%)
  matrix products  10.4 us (5%)
    ppermute x2, starting transfers between devices, over_tensor(): value = value + lax.ppermute(value, 'tensor', SWAP)  25.3 us
    pallas_call x3, Pallas kernels, backward(): pl.pallas_call(functools.partial(backward_kernel, count, first), out_shap...  21.1 us
    pallas_call x3, Pallas kernels, forward(): pl.pallas_call(functools.partial(forward_kernel, count), out_shape=jax.Sh...  21.1 us
    ppermute x12, starting transfers between devices, shift(): return lax.ppermute(value, BOTH, ring(stage, step))  16.8 us
    ppermute x2, waiting for transfers between devices, over_tensor(): return value + lax.ppermute(value, 'tensor', [(t, t ^ 4) for t in range(8)])  13.7 us
    all_to_all x3, starting transfers between devices, exchange(): lax.all_to_all(value, axis, split_axis=0, concat_axis=0, tiled=True, axis...  13 us
    ppermute x4, waiting for transfers between devices, over_dp(): value = value + lax.ppermute(value, 'dp', [(d, d ^ bit) for d in range(16)])  10.9 us
    unnamed x91, local copies, waits for them, and re-layouts  10.3 us
  transfers between devices with their start and end apart: 33, of which 11 were waited for; matrix products, arithmetic and copies ran while one was open for 17% of the time, Pallas kernels for 19%

commit v1 on v0

--- a/solution.py
+++ b/solution.py
@@ -43,11 +43,18 @@
     return lax.ppermute(value, BOTH, ring(stage, step))
 
 
-def ring_gather(own, stage, h):
-    below = shift(own, stage, 1)
-    above = shift(own, stage, -1)
-    across = shift(below, stage, 1) if h == 0 else shift(above, stage, -1)
+def first_ring(own, h):
+    below = shift(own, 0, 1)
+    above = shift(own, 0, -1)
+    across = shift(below, 0, 1) if h == 0 else shift(above, 0, -1)
     return [own, above, across, below]
+
+
+def second_ring(own):
+    below = shift(own, 1, 1)
+    above = shift(own, 1, -1)
+    passed = lax.optimization_barrier((below[:SIDE], above[SIDE:]))
+    return above, below, passed, [shift(passed[0], 1, 1), shift(passed[1], 1, -1)]
 
 
 def exchange(value, axis, groups=None):
@@ -62,66 +69,118 @@
     return value + lax.ppermute(value, "tensor", [(t, t ^ 4) for t in range(8)])
 
 
-def over_dp(value):
-    for bit in (1, 4, 2, 8):
-        value = value + lax.ppermute(value, "dp", [(d, d ^ bit) for d in range(16)])
-    return value
+def over_side(value, axis):
+    def from_step(step):
+        def move(x, z, y, c):
+            if axis == 0:
+                return ((x + step) % SIDE, z, y, c)
+            return (x, (z + step) % SIDE, y, c)
+
+        return lax.ppermute(value, BOTH, pairs(move))
+
+    return [value, from_step(1), from_step(2), from_step(3)]
+
+
+def total_of(parts):
+    return (parts[0] + parts[2]) + (parts[1] + parts[3])
 
 
 def after(value, *events):
     return lax.optimization_barrier((value, *events))[0]
 
 
-def forward_kernel(count, near_ref, wide_ref, *refs):
-    lines, out_ref, total = refs[:count], refs[count], refs[count + 1]
-    step = pl.program_id(0)
-    weights = jnp.concatenate([line[k] for line in lines for k in range(SIDE)], axis=1)
-    product = jnp.dot(wide_ref[...], weights, preferred_element_type=jnp.float32)
-
-    @pl.when(step == 0)
-    def _():
-        total[...] = product
-
-    @pl.when(step > 0)
-    def _():
-        total[...] += product
-
-    @pl.when(step == pl.num_programs(0) - 1)
-    def _():
-        part = out_ref.shape[2] // count
+def forward_kernel(offsets, near_ref, wide_ref, *refs):
+    count = len(offsets)
+    lines, outs, held, sems = refs[:count], refs[count:-2], refs[-2], refs[-1]
+    copies = [
+        pltpu.make_async_copy(lines[m].at[pl.ds(offsets[m], SIDE)], held.at[m], sems.at[m])
+        for m in range(count)
+    ]
+    for copy in copies:
+        copy.start()
+    part = held.shape[3]
+    for m in range(count):
+        copies[m].wait()
+        order = [lax.rem(near_ref[0] + k, SIDE) for k in range(SIDE)]
+        weights = jnp.concatenate([held[m, k] for k in order], axis=1)
+        product = jnp.dot(wide_ref[...], weights, preferred_element_type=jnp.float32)
+        product = product.astype(jnp.bfloat16)
         for k in range(SIDE):
-            slot = lax.rem(near_ref[0] + k, SIDE)
-            for m in range(count):
-                lane = (m * SIDE + k) * part
-                out_ref[slot, :, m * part : (m + 1) * part] = total[:, lane : lane + part].astype(
-                    out_ref.dtype
-                )
-
-
-def forward(near, wide, lines):
+            piece = product[:, k * part : (k + 1) * part]
+            if len(outs) == 1:
+                outs[0][k, :, m * part : (m + 1) * part] = piece
+            else:
+                outs[k][:, m * part : (m + 1) * part] = piece
+
+
+def forward(start, wide, lines, apart=False):
     tokens, depth = wide.shape
-    part = lines[0].shape[2]
+    part = lines[0][0].shape[2]
     count = len(lines)
-    block = depth // 4
+    shape = (tokens, count * part) if apart else (SIDE, tokens, count * part)
+    outs = jax.ShapeDtypeStruct(shape, jnp.bfloat16)
+    spec = pl.BlockSpec(shape, lambda i, n: (0,) * len(shape))
     return pl.pallas_call(
-        functools.partial(forward_kernel, count),
-        out_shape=jax.ShapeDtypeStruct((SIDE, tokens, count * part), jnp.bfloat16),
+        functools.partial(forward_kernel, [offset for _, offset in lines]),
+        out_shape=[outs] * SIDE if apart else outs,
+        grid_spec=pltpu.PrefetchScalarGridSpec(
+            num_scalar_prefetch=1,
+            grid=(1,),
+            in_specs=[pl.BlockSpec((tokens, depth), lambda i, n: (0, 0))]
+            + [pl.BlockSpec(memory_space=pl.ANY)] * count,
+            out_specs=[spec] * SIDE if apart else spec,
+            scratch_shapes=[
+                pltpu.VMEM((count, SIDE, depth, part), jnp.bfloat16),
+                pltpu.SemaphoreType.DMA((count,)),
+            ],
+        ),
+        compiler_params=pltpu.CompilerParams(vmem_limit_bytes=28 << 20),
+        cost_estimate=pl.CostEstimate(
+            flops=tokens * depth * count * part,
+            bytes_accessed=depth * part * count,
+            transcendentals=0,
+        ),
+        name="forward",
+    )(start, wide, *[line for line, _ in lines])
+
+
+def arrange_kernel(far_ref, here_ref, beside_ref, out_ref):
+    part = here_ref.shape[2] // 2
+    far = far_ref[0]
+
+    def total(ref, lane):
+        parts = [ref[y, :, lane : lane + part].astype(jnp.float32) for y in range(SIDE)]
+        return (parts[0] + parts[1] + parts[2] + parts[3]).astype(out_ref.dtype)
+
+    for h in range(2):
+        lanes = slice(h * part, (h + 1) * part)
+        out_ref[far, :, lanes] = total(here_ref, h * part)
+        out_ref[lax.rem(far + 1, SIDE), :, lanes] = total(beside_ref, 2 * h * part)
+        out_ref[lax.rem(far + 3, SIDE), :, lanes] = total(beside_ref, (2 * h + 1) * part)
+        out_ref[lax.rem(far + 2, SIDE), :, lanes] = jnp.zeros_like(here_ref[0, :, lanes])
+
+
+def arrange(far, here, beside):
+    tokens = here.shape[1]
+    rows = tokens // 4
+    return pl.pallas_call(
+        arrange_kernel,
+        out_shape=jax.ShapeDtypeStruct(here.shape, here.dtype),
         grid_spec=pltpu.PrefetchScalarGridSpec(
             num_scalar_prefetch=1,
             grid=(4,),
-            in_specs=[pl.BlockSpec((tokens, block), lambda i, n: (0, i))]
-            + [pl.BlockSpec((SIDE, block, part), lambda i, n: (0, i, 0))] * count,
-            out_specs=pl.BlockSpec((SIDE, tokens, count * part), lambda i, n: (0, 0, 0)),
-            scratch_shapes=[pltpu.VMEM((tokens, count * SIDE * part), jnp.float32)],
-        ),
-        compiler_params=pltpu.CompilerParams(vmem_limit_bytes=40 << 20),
+            in_specs=[
+                pl.BlockSpec((SIDE, rows, here.shape[2]), lambda i, n: (0, i, 0)),
+                pl.BlockSpec((SIDE, rows, beside.shape[2]), lambda i, n: (0, i, 0)),
+            ],
+            out_specs=pl.BlockSpec((SIDE, rows, here.shape[2]), lambda i, n: (0, i, 0)),
+        ),
+        compiler_params=pltpu.CompilerParams(vmem_limit_bytes=16 << 20),
         cost_estimate=pl.CostEstimate(
-            flops=2 * tokens * depth * count * SIDE * part,
-            bytes_accessed=2 * depth * (tokens + count * SIDE * part),
-            transcendentals=0,
-        ),
-        name="forward",
-    )(near, wide, *lines)
+            flops=4 * here.size, bytes_accessed=2 * (2 * here.size + beside.size), transcendentals=0
+        ),
+        name="arrange",
+    )(far, here, beside)
 
 
 def backward_kernel(count, first, spots_ref, *refs):
@@ -136,10 +195,13 @@
 
 def backward(spots, grown, out_grad, lines):
     tokens = out_grad.shape[0]
-    depth, part = lines[0].shape[1:]
+    depth, part = lines[0][0].shape[1:]
     count = len(lines)
     block = depth // 4
     first = grown is None
+
+    def held(place):
+        return pl.BlockSpec((SIDE, block, part), lambda i, n: (place, i, 0))
 
     def column(j):
         return pl.BlockSpec((tokens, part), lambda i, n: (0, n[j]))
@@ -151,19 +213,19 @@
         grid_spec=pltpu.PrefetchScalarGridSpec(
             num_scalar_prefetch=1,
             grid=(4,),
-            in_specs=[pl.BlockSpec((SIDE, block, part), lambda i, n: (0, i, 0))] * count
+            in_specs=[held(offset // SIDE) for _, offset in lines]
             + [column(j) for j in range(count * SIDE)]
             + ([] if first else [total]),
             out_specs=total,
         ),
-        compiler_params=pltpu.CompilerParams(vmem_limit_bytes=40 << 20),
+        compiler_params=pltpu.CompilerParams(vmem_limit_bytes=28 << 20),
         cost_estimate=pl.CostEstimate(
-            flops=2 * tokens * depth * count * SIDE * part,
-            bytes_accessed=2 * depth * count * SIDE * part + 8 * tokens * depth,
+            flops=tokens * depth * count * part,
+            bytes_accessed=depth * part * count,
             transcendentals=0,
         ),
         name="backward",
-    )(spots, *lines, *([out_grad] * (count * SIDE)), *([] if first else [grown]))
+    )(spots, *[line for line, _ in lines], *([out_grad] * (count * SIDE)), *([] if first else [grown]))
 
 
 def compose(logits, indices, vector_bank):
@@ -211,19 +273,20 @@
     dp, tensor = lax.axis_index("dp"), lax.axis_index("tensor")
     x, z, core = dp // SIDE, dp % SIDE, tensor % 2
     near, far = jnp.where(core == 0, x, z), jnp.where(core == 0, z, x)
-    spot = near.astype(jnp.int32).reshape(1)
+    side = tensor // 2
+    turned = ((SIDE - near) % SIDE).astype(jnp.int32).reshape(1)
+    turned_here = ((SIDE - near + side) % SIDE).astype(jnp.int32).reshape(1)
 
     left, right = frozen_weight[:, :half], frozen_weight[:, half:]
     mine = jnp.where(core == 0, left, right)
     theirs = jnp.where(core == 0, right, left)
     swapped = lax.ppermute(theirs, "tensor", SWAP)
-    lines = []
+    shards = []
     for h in range(2):
         cols = slice(h * part, (h + 1) * part)
-        own = jnp.concatenate([mine[:, cols], swapped[:, cols]], axis=0)
-        lines.append(jnp.stack(ring_gather(own, 0, h)))
-    blocks = [ring_gather(lines[h], 1, h) for h in range(2)]
-
+        shards.append(jnp.concatenate([mine[:, cols], swapped[:, cols]], axis=0))
+    logits_a, logits_b, *shards = lax.optimization_barrier((logits_a, logits_b, *shards))
+    lines = first_ring(shards[0], 0) + first_ring(shards[1], 1)
     def columns(i, h):
         far_at = (far + i) % SIDE
         spots = []
@@ -249,16 +312,19 @@
     low_part = lax.dot_general(down_a, attn_out, cols_by_cols, preferred_element_type=f32)
     back_part = lax.dot_general(up_b, grad_cols, cols_by_cols, preferred_element_type=f32)
     totals = jnp.concatenate([low_part, back_part], axis=0)
-    totals = over_tensor(after(totals, lines[0])).astype(bf16)
+    own, totals = lax.optimization_barrier((jnp.stack(lines), totals))
+    above, below, passed, corner = second_ring(own)
+    blocks = [
+        [(own, h * SIDE), (above, h * SIDE), (corner[h], 0), (below, h * SIDE)] for h in range(2)
+    ]
+    totals = over_tensor(totals).astype(bf16)
     low_bf, back_bf = totals[:rank], totals[rank:]
 
     factor = adapter_scale / (tokens * lax.axis_size("dp"))
     grad_a = jnp.dot(back_bf, attn_out, preferred_element_type=f32)
     grad_b = jnp.dot(low_bf, grad_cols, preferred_element_type=f32)
-    both = over_dp(factor * jnp.concatenate([grad_a, grad_b], axis=0))
-    bank_a, logit_grad_a = compose_back(both[:rank], weights_a, picked_a, mixing_a, vector_bank)
-    bank_b, logit_grad_b = compose_back(both[rank:], weights_b, picked_b, mixing_b, vector_bank)
-    bank_grad = over_tensor(bank_a + bank_b)
+    both = factor * jnp.concatenate([grad_a, grad_b], axis=0)
+    both_parts = over_side(both, 0)
 
     here = [(0, 0), (0, 1)]
     beside = [(1, 0), (3, 0), (1, 1), (3, 1)]
@@ -267,36 +333,34 @@
     def take(chunks):
         return [blocks[h][i] for i, h in chunks]
 
-    piece = lax.psum_scatter(
-        forward(spot, wide, take(here)),
-        "tensor",
-        scatter_dimension=0,
-        axis_index_groups=LANES,
-        tiled=True,
-    )[0]
+    sent_here = forward(turned, wide, take(here))
+    slots_here = exchange(sent_here, "tensor", LANES)
     grown = backward(spots_of(here), None, out_grad, take(here))
-    arrived = exchange(forward(spot, wide, take(beside)), "tensor", LANES)
-    arrived = jnp.sum(arrived.astype(f32), axis=0).astype(bf16)
-    above = jnp.concatenate([arrived[:, :part], arrived[:, 2 * part : 3 * part]], axis=1)
-    below = jnp.concatenate([arrived[:, part : 2 * part], arrived[:, 3 * part :]], axis=1)
+    both = total_of(both_parts)
+    turned, both, *_ = lax.optimization_barrier((turned, both, sent_here, grown, *passed))
+    sent_beside = forward(turned, wide, take(beside))
+    slots_here, sent_beside = lax.optimization_barrier((slots_here, sent_beside))
+    slots_beside = exchange(sent_beside, "tensor", LANES)
+    both_parts = over_side(both, 1)
     grown = backward(spots_of(beside), grown, out_grad, take(beside))
-
-    ordered = [piece, above, jnp.zeros_like(piece), below]
-    slots = []
-    for s in range(SIDE):
-        turn = (s - far) % SIDE
-        slots.append(
-            jnp.where(turn == 0, piece, jnp.where(turn == 1, above, jnp.where(turn == 3, below, 0)))
-        )
-    slots = jnp.stack(slots).astype(bf16)
+    both = total_of(lax.optimization_barrier((*both_parts, grown))[:SIDE])
+    bank_a, logit_grad_a = compose_back(both[:rank], weights_a, picked_a, mixing_a, vector_bank)
+    bank_b, logit_grad_b = compose_back(both[rank:], weights_b, picked_b, mixing_b, vector_bank)
+
+    slots = arrange(far.astype(jnp.int32).reshape(1), slots_here, after(slots_beside, grown))
     moved = exchange(slots, "tensor", LANES)
     crossed = lax.ppermute(jnp.where(core == 0, slots[2:], moved[:2]), "tensor", SWAP)
     firsts = jnp.where(core == 0, slots[:2], crossed)
     seconds = jnp.where(core == 0, crossed, moved[2:])
 
-    arrived = exchange(forward(spot, wide, take(across)), "tensor", LANES)
-    piece = jnp.sum(arrived.astype(f32), axis=0).astype(bf16)
-    grown = backward(spots_of(across), grown, out_grad, take(across))
+    sent = forward(turned_here, wide, take(across), apart=True)
+    arrived = [sent[0]]
+    for step in range(1, SIDE):
+        turns = [(t, (t + 2 * step) % 8) for t in range(8)]
+        arrived.append(lax.ppermute(sent[step], "tensor", turns))
+    piece = total_of([a.astype(f32) for a in arrived]).astype(bf16)
+    bank_grad = over_tensor(after(bank_a + bank_b, *sent))
+    grown = backward(after(spots_of(across), *sent), grown, out_grad, take(across))
     first, place, second = settle(piece, 2, z, core)
     cols = []
     for s in range(2):

time: 227 us -> 205 us (0.903)
  local copies, waits for them, and re-layouts: 14.5 us -> 38.8 us
  starting transfers between devices: 79.2 us -> 59.7 us
  other arithmetic: 26.8 us -> 13.2 us
  between operations: 14.8 us -> 1.34 us
  Pallas kernels: 42.2 us -> 38.8 us
    ppermute x2, starting transfers between devices: 25.3 us -> 0.95 us  [over_tensor(): value = value + lax.ppermute(value, 'tensor', SWAP)]
    unnamed x91 -> x66, local copies, waits for them, and re-layouts: 10.3 us -> 29 us
    ppermute x2, waiting for transfers between devices: 13.7 us -> 0.01 us  [over_tensor(): return value + lax.ppermute(value, 'tensor', [(t, t ^ 4) for t in range(8)])]
    ppermute x2, waiting for transfers between devices: 2.22 us -> 13.3 us  [over_tensor(): lax.ppermute(value, 'tensor', [(t, t ^ 2) for t in range(8)])]
    ppermute x4 -> x9, waiting for transfers between devices: 10.9 us -> 0.02 us  [the longest x6 0.02 us: from_step(): return lax.ppermute(value, BOTH, pairs(move))]
    ppermute x12 -> x10, waiting for transfers between devices: 7.73 us -> 16 us  [shift(): return lax.ppermute(value, BOTH, ring(stage, step))]
    ppermute x4 -> x9, starting transfers between devices: 3.84 us -> 11.9 us  [the longest x3 5.95 us: local(): arrived.append(lax.ppermute(sent[step], 'tensor', turns))]
    another operation x5 -> x0, other arithmetic: 7.49 us -> none  [the longest x4 6.37 us: local(): lines.append(jnp.stack(ring_gather(own, 0, h)))]
  transfers between devices with their start and end apart: 33 -> 35, of which waited for: 11 -> 8; matrix products, arithmetic and copies ran while one was open for 17% -> 20% of each run, Pallas kernels for 19% -> 19%
where the time goes in v1:
time: 205 us; the launch traced here: 202 us
  starting transfers between devices  59.7 us (29%)
  local copies, waits for them, and re-layouts  38.8 us (19%)
  Pallas kernels  38.8 us (19%)
  waiting for transfers between devices  38.1 us (19%)
  other arithmetic  13.2 us (6%)
  matrix products  12.2 us (6%)
    unnamed x66, local copies, waits for them, and re-layouts  29 us
    pallas_call x3, Pallas kernels, backward(): pl.pallas_call(functools.partial(backward_kernel, count, first), out_shap...  19.5 us
    ppermute x10, waiting for transfers between devices, shift(): return lax.ppermute(value, BOTH, ring(stage, step))  16 us
    ppermute x10, starting transfers between devices, shift(): return lax.ppermute(value, BOTH, ring(stage, step))  15.9 us
    pallas_call x3, Pallas kernels, forward(): pl.pallas_call(functools.partial(forward_kernel, [offset for _, offset in...  15.6 us
    ppermute x2, waiting for transfers between devices, over_tensor(): lax.ppermute(value, 'tensor', [(t, t ^ 2) for t in range(8)])  13.3 us
    all_to_all x3, starting transfers between devices, exchange(): lax.all_to_all(value, axis, split_axis=0, concat_axis=0, tiled=True, axis...  12.2 us
    slice x2, local copies, waits for them, and re-layouts, second_ring(): passed = lax.optimization_barrier((below[:SIDE], above[SIDE:]))  6.15 us
  transfers between devices with their start and end apart: 35, of which 8 were waited for; matrix products, arithmetic and copies ran while one was open for 20% of the time, Pallas kernels for 19%

profile of v1, /device:TPU:1, one launch (start us, length us, event | category | flops | bytes accessed | tf_op | source)
XLA Modules:
  0.0 202.3 jit_solution(9365098605701281080)
XLA Ops:
  2.1 1.5 collective-permute-start.1
  3.6 1.6 collective-permute-done.1
  6.4 1.8 collective-permute-start.3
  8.2 2.2 %collective-permute-start.2 = (bf16[2048,128]{1,0:T(8,128)(2,1)S(1)}, bf16[2048,128]{1,0:T(8,128)(2,1)}, u32[]{:S(2)}, u32[]{:S(2)}) collective-permute-start(bf16[2048,128]{1,0:T(8,128)(2,1)S(1)} %get-tuple-element.28), channel_id=1, source_target_pairs={{0,96},{1,25},{2,98},{3,27},{4,100},{5,29},{6,102},{7,31},{8,104},... | collective-permute-start | bytes 1572872 | tf_op jit(solution)/shard_map/ppermute | solution.py:43
  10.4 2.7 %collective-permute-start.5 = (bf16[2048,128]{1,0:T(8,128)(2,1)S(1)}, bf16[2048,128]{1,0:T(8,128)(2,1)}, u32[]{:S(2)}, u32[]{:S(2)}) collective-permute-start(bf16[2048,128]{1,0:T(8,128)(2,1)S(1)} %get-tuple-element.29), channel_id=1, source_target_pairs={{0,96},{1,25},{2,98},{3,27},{4,100},{5,29},{6,102},{7,31},{8,104},... | collective-permute-start | bytes 1572872 | tf_op jit(solution)/shard_map/ppermute | solution.py:43
  15.3 1.6 fusion.13
  17.8 4.6 %collective-permute-done.5 = bf16[2048,128]{1,0:T(8,128)(2,1)} collective-permute-done((bf16[2048,128]{1,0:T(8,128)(2,1)S(1)}, bf16[2048,128]{1,0:T(8,128)(2,1)}, u32[]{:S(2)}, u32[]{:S(2)}) %collective-permute-start.5) | collective-permute-done | bytes 524320 | tf_op jit(solution)/shard_map/ppermute | solution.py:43
  22.4 3.1 %collective-permute-start.6 = (bf16[2048,128]{1,0:T(8,128)(2,1)}, bf16[2048,128]{1,0:T(8,128)(2,1)S(1)}, u32[]{:S(2)}, u32[]{:S(2)}) collective-permute-start(bf16[2048,128]{1,0:T(8,128)(2,1)} %collective-permute-done.5), channel_id=1, source_target_pairs={{0,96},{1,25},{2,98},{3,27},{4,100},{5,29},{6,102},{7,31},{8,104},... | collective-permute-start | bytes 1572872 | tf_op jit(solution)/shard_map/ppermute | solution.py:43
  25.6 1.9 bitcast_dynamic-update-slice_fusion.6
  29.1 1.9 bitcast_dynamic-update-slice_fusion.4
  31.8 1.9 bitcast_dynamic-update-slice_fusion.2
  35.4 2.7 %collective-permute-start.15 = (bf16[8,2048,128]{2,1,0:T(8,128)(2,1)}, bf16[8,2048,128]{2,1,0:T(8,128)(2,1)}, u32[]{:S(2)}, u32[]{:S(2)}) collective-permute-start(bf16[8,2048,128]{2,1,0:T(8,128)(2,1)} %bitcast_dynamic-update-slice_fusion.refs_0_.refs_1_), channel_id=1, source_target_pairs={{0,24},{1,97},{2,26},{3,99},{4,28},{5,101},{6,30},{7,103},{8,0},{9... | collective-permute-start | bytes 12582920 | tf_op jit(solution)/shard_map/ppermute | solution.py:43
  38.0 1.9 collective-permute-start
  39.9 2.2 %collective-permute-done.8 = f32[32,512]{1,0:T(8,128)S(1)} collective-permute-done((f32[32,512]{1,0:T(8,128)S(1)}, f32[32,512]{1,0:T(8,128)S(1)}, u32[]{:S(2)}, u32[]{:S(2)}) %collective-permute-start.8) | collective-permute-done | bytes 65568 | tf_op jit(solution)/shard_map/ppermute | solution.py:67
  43.7 2.2 %collective-permute-done.9 = f32[32,512]{1,0:T(8,128)} collective-permute-done((f32[32,512]{1,0:T(8,128)S(1)}, f32[32,512]{1,0:T(8,128)}, u32[]{:S(2)}, u32[]{:S(2)}) %collective-permute-start.9) | collective-permute-done | bytes 65568 | tf_op jit(solution)/shard_map/ppermute | solution.py:68
  46.7 3.0 %collective-permute-start.10 = (f32[32,512]{1,0:T(8,128)S(1)}, f32[32,512]{1,0:T(8,128)S(1)}, u32[]{:S(2)}, u32[]{:S(2)}) collective-permute-start(f32[32,512]{1,0:T(8,128)S(1)} %add.387), channel_id=1, source_target_pairs={{0,4},{1,5},{2,6},{3,7},{4,0},{5,1},{6,2},{7,3},{8,12},{9,13},{10,... | collective-permute-start | bytes 196616 | tf_op jit(solution)/shard_map/ppermute | solution.py:69
  51.1 4.1 %forward.3 = bf16[4,512,256]{2,1,0:T(8,128)(2,1)S(1)} custom-call(s32[1]{0:T(128)} %bitcast.1.near_ref, bf16[512,2048]{1,0:T(8,128)(2,1)S(1)} %constant_dynamic-update-slice_fusion.wide_ref, bf16[8,2048,128]{2,1,0:T(8,128)(2,1)} %bitcast_dynamic-update-slice_fusion.refs_0_.refs_1_, bf16[8,2048,128]{2,1,0:T(8,128)(2,1)} %bitcast_dynamic-update-slice_fusion.refs_0_.refs_1_), custom_call_target="tpu_custom_call" | custom-call | flops 268435456 | bytes 524288 | tf_op jit(solution)/shard_map/forward/pallas_call | solution.py:123
  56.1 3.5 %all-to-all-start = ((bf16[4,512,256]{2,1,0:T(8,128)(2,1)}), bf16[4,512,256]{2,1,0:T(8,128)(2,1)S(1)}, u32[]{:S(2)}, u32[]{:S(2)}) async-start(bf16[4,512,256]{2,1,0:T(8,128)(2,1)} %copy-done.9), calls=%async_computation | async-start | bytes 2097152 | tf_op jit(solution)/shard_map/all_to_all | solution.py:61
  59.7 1.5 fusion.11
  61.2 1.5 fusion.36
  63.4 2.7 %collective-permute-start.13 = (f32[32,1024]{1,0:T(8,128)}, f32[32,1024]{1,0:T(8,128)}, u32[]{:S(2)}, u32[]{:S(2)}) collective-permute-start(f32[32,1024]{1,0:T(8,128)} %maximum_multiply_fusion), channel_id=1, source_target_pairs={{0,96},{1,97},{2,98},{3,99},{4,100},{5,101},{6,102},{7,103},{8,104... | collective-permute-start | bytes 393224 | tf_op jit(solution)/shard_map/ppermute | solution.py:79
  67.1 3.4 %copy-done.1 = bf16[512,8192]{1,0:T(8,128)(2,1)S(1)} copy-done((bf16[512,8192]{1,0:T(8,128)(2,1)S(1)}, bf16[512,8192]{1,0:T(8,128)(2,1)}, u32[]{:S(2)}) %copy-start.1) | copy-done | bytes 8388632
  70.4 5.6 %backward.3.refs_20_ = f32[512,2048]{1,0:T(8,128)S(1)} custom-call(s32[8]{0:T(128)S(1)} %stack.149.spots_ref, bf16[8,2048,128]{2,1,0:T(8,128)(2,1)} %bitcast_dynamic-update-slice_fusion.refs_0_.refs_1_, bf16[8,2048,128]{2,1,0:T(8,128)(2,1)} %bitcast_dynamic-update-slice_fusion.refs_0_.refs_1_, bf16[512,8192]{1,0:T(8,128)(2,1)S(1)} %copy-done.1, ...), custom_call_target="tpu_custom_call" | custom-call | flops 268435456 | bytes 524288 | tf_op jit(solution)/shard_map/backward/pallas_call | solution.py:210
  76.1 10.5 %collective-permute-done.15.refs_0_.refs_2_ = bf16[8,2048,128]{2,1,0:T(8,128)(2,1)} collective-permute-done((bf16[8,2048,128]{2,1,0:T(8,128)(2,1)}, bf16[8,2048,128]{2,1,0:T(8,128)(2,1)}, u32[]{:S(2)}, u32[]{:S(2)}) %collective-permute-start.15) | collective-permute-done | bytes 4194336 | tf_op jit(solution)/shard_map/ppermute | solution.py:43
  86.6 3.1 %slice.96 = bf16[4,2048,128]{2,1,0:T(8,128)(2,1)} slice(bf16[8,2048,128]{2,1,0:T(8,128)(2,1)} %collective-permute-done.15.refs_0_.refs_2_), slice={[4:8], [0:2048], [0:128]} | slice | bytes 4194304 | tf_op jit(solution)/shard_map/slice | solution.py:56
  89.7 3.1 %slice.95 = bf16[4,2048,128]{2,1,0:T(8,128)(2,1)} slice(bf16[8,2048,128]{2,1,0:T(8,128)(2,1)} %collective-permute-done.14.refs_1_.refs_3_), slice={[0:4], [0:2048], [0:128]} | slice | bytes 4194304 | tf_op jit(solution)/shard_map/slice | solution.py:56
  93.4 2.8 %collective-permute-start.18 = (bf16[4,2048,128]{2,1,0:T(8,128)(2,1)}, bf16[4,2048,128]{2,1,0:T(8,128)(2,1)}, u32[]{:S(2)}, u32[]{:S(2)}) collective-permute-start(bf16[4,2048,128]{2,1,0:T(8,128)(2,1)} %slice.96), channel_id=1, source_target_pairs={{0,24},{1,97},{2,26},{3,99},{4,28},{5,101},{6,30},{7,103},{8,0},{9... | collective-permute-start | bytes 6291464 | tf_op jit(solution)/shard_map/ppermute | solution.py:43
  96.2 1.7 add_add_fusion.1
  97.9 6.6 %forward.4 = bf16[4,512,512]{2,1,0:T(8,128)(2,1)S(1)} custom-call(s32[1]{0:T(128)} %bitcast.1.near_ref, bf16[512,2048]{1,0:T(8,128)(2,1)S(1)} %constant_dynamic-update-slice_fusion.wide_ref, bf16[8,2048,128]{2,1,0:T(8,128)(2,1)} %collective-permute-done.15.refs_0_.refs_2_, bf16[8,2048,128]{2,1,0:T(8,128)(2,1)} %collective-permute-done.14.refs_1_.refs_3_, ...), custom_call_target="tpu_custom_call" | custom-call | flops 536870912 | bytes 1048576 | tf_op jit(solution)/shard_map/forward/pallas_call | solution.py:123
  105.9 4.5 %all-to-all-start.1 = ((bf16[4,512,512]{2,1,0:T(8,128)(2,1)}), bf16[4,512,512]{2,1,0:T(8,128)(2,1)}, u32[]{:S(2)}, u32[]{:S(2)}) async-start(bf16[4,512,512]{2,1,0:T(8,128)(2,1)} %copy-done.8), calls=%async_computation.1 | async-start | bytes 4194304 | tf_op jit(solution)/shard_map/all_to_all | solution.py:61
  110.4 1.6 collective-permute-start.28
  112.9 3.4 %copy-done.2 = bf16[512,8192]{1,0:T(8,128)(2,1)S(1)} copy-done((bf16[512,8192]{1,0:T(8,128)(2,1)S(1)}, bf16[512,8192]{1,0:T(8,128)(2,1)}, u32[]{:S(2)}) %copy-start.2) | copy-done | bytes 8388632
  116.3 2.2 %copy-done.5 = f32[512,2048]{1,0:T(8,128)S(1)} copy-done((f32[512,2048]{1,0:T(8,128)S(1)}, f32[512,2048]{1,0:T(8,128)}, u32[]{:S(2)}) %copy-start.5) | copy-done | bytes 4194328
  118.4 8.2 %backward.4.refs_10_ = f32[512,2048]{1,0:T(8,128)S(1)} custom-call(s32[16]{0:T(128)S(1)} %stack.166.spots_ref, bf16[8,2048,128]{2,1,0:T(8,128)(2,1)} %collective-permute-done.15.refs_0_.refs_2_, bf16[8,2048,128]{2,1,0:T(8,128)(2,1)} %collective-permute-done.14.refs_1_.refs_3_, bf16[8,2048,128]{2,1,0:T(8,128)(2,1)} %collective-permute-done.15.refs_0_.refs_2_, ...), custom_call_target="tpu_custom_call" | custom-call | flops 536870912 | bytes 1048576 | tf_op jit(solution)/shard_map/backward/pallas_call | solution.py:210
  126.7 2.0 copy-done.6
  132.0 4.9 %all-to-all-done.1.beside_ref = bf16[4,512,512]{2,1,0:T(8,128)(2,1)} async-done(((bf16[4,512,512]{2,1,0:T(8,128)(2,1)}), bf16[4,512,512]{2,1,0:T(8,128)(2,1)}, u32[]{:S(2)}, u32[]{:S(2)}) %all-to-all-start.1) | async-done | bytes 2097184 | tf_op jit(solution)/shard_map/all_to_all | solution.py:61
  136.9 3.8 %arrange.1 = bf16[4,512,256]{2,1,0:T(8,128)(2,1)} custom-call(s32[1]{0:T(128)} %bitcast.far_ref, bf16[4,512,256]{2,1,0:T(8,128)(2,1)S(1)} %all-to-all-done.here_ref, bf16[4,512,512]{2,1,0:T(8,128)(2,1)} %all-to-all-done.1.beside_ref), custom_call_target="tpu_custom_call" | custom-call | flops 2097152 | bytes 4194304 | tf_op jit(solution)/shard_map/arrange/pallas_call | solution.py:166
  140.7 4.2 %all-to-all-start.2 = ((bf16[4,512,256]{2,1,0:T(8,128)(2,1)}), bf16[4,512,256]{2,1,0:T(8,128)(2,1)}, u32[]{:S(2)}, u32[]{:S(2)}) async-start(bf16[4,512,256]{2,1,0:T(8,128)(2,1)} %arrange.1), calls=%async_computation.2 | async-start | bytes 2097152 | tf_op jit(solution)/shard_map/all_to_all | solution.py:61
  147.4 4.8 %forward.5 = (bf16[512,256]{1,0:T(8,128)(2,1)S(1)}, bf16[512,256]{1,0:T(8,128)(2,1)}, bf16[512,256]{1,0:T(8,128)(2,1)S(1)}, bf16[512,256]{1,0:T(8,128)(2,1)S(1)}) custom-call(s32[1]{0:T(128)} %bitcast.36.near_ref, bf16[512,2048]{1,0:T(8,128)(2,1)S(1)} %constant_dynamic-update-slice_fusion.wide_ref, bf16[4,2048,128]{2,1,0:T(8,128)(2,1)} %collective-permute-done.17.refs_0_, ...), custom_call_target="tpu_custom_call" | custom-call | flops 268435456 | bytes 524288 | tf_op jit(solution)/shard_map/forward/pallas_call | solution.py:123
  154.1 3.3 %collective-permute-start.19 = (bf16[512,256]{1,0:T(8,128)(2,1)S(1)}, bf16[512,256]{1,0:T(8,128)(2,1)}, u32[]{:S(2)}, u32[]{:S(2)}) collective-permute-start(bf16[512,256]{1,0:T(8,128)(2,1)S(1)} %get-tuple-element.41), channel_id=1, source_target_pairs={{0,4},{1,5},{2,6},{3,7},{4,0},{5,1},{6,2},{7,3},{8,12},{9,13},{10,... | collective-permute-start | bytes 786440 | tf_op jit(solution)/shard_map/ppermute | solution.py:360
  157.7 2.4 %collective-permute-start.21 = (bf16[512,256]{1,0:T(8,128)(2,1)S(1)}, bf16[512,256]{1,0:T(8,128)(2,1)}, u32[]{:S(2)}, u32[]{:S(2)}) collective-permute-start(bf16[512,256]{1,0:T(8,128)(2,1)S(1)} %get-tuple-element.43), channel_id=1, source_target_pairs={{0,6},{1,7},{2,0},{3,1},{4,2},{5,3},{6,4},{7,5},{8,14},{9,15},{10,... | collective-permute-start | bytes 786440 | tf_op jit(solution)/shard_map/ppermute | solution.py:360
  161.5 2.3 %collective-permute-start.16 = (bf16[2,512,256]{2,1,0:T(8,128)(2,1)S(1)}, bf16[2,512,256]{2,1,0:T(8,128)(2,1)S(1)}, u32[]{:S(2)}, u32[]{:S(2)}) collective-permute-start(bf16[2,512,256]{2,1,0:T(8,128)(2,1)S(1)} %slice_select_fusion.1), channel_id=1, source_target_pairs={{0,1},{1,0},{2,3},{3,2},{4,5},{5,4},{6,7},{7,6},{8,9},{9,8},{10,11... | collective-permute-start | bytes 1572872 | tf_op jit(solution)/shard_map/ppermute | solution.py:352
  164.6 11.0 %collective-permute-done.30 = f32[256,256]{1,0:T(8,128)S(1)} collective-permute-done((f32[256,256]{1,0:T(8,128)S(1)}, f32[256,256]{1,0:T(8,128)S(1)}, u32[]{:S(2)}, u32[]{:S(2)}) %collective-permute-start.30) | collective-permute-done | bytes 262176 | tf_op jit(solution)/shard_map/ppermute | solution.py:68
  175.7 2.4 %collective-permute-start.31 = (f32[256,256]{1,0:T(8,128)S(1)}, f32[256,256]{1,0:T(8,128)S(1)}, u32[]{:S(2)}, u32[]{:S(2)}) collective-permute-start(f32[256,256]{1,0:T(8,128)S(1)} %add.474), channel_id=1, source_target_pairs={{0,4},{1,5},{2,6},{3,7},{4,0},{5,1},{6,2},{7,3},{8,12},{9,13},{10,... | collective-permute-start | bytes 786440 | tf_op jit(solution)/shard_map/ppermute | solution.py:69
  178.0 3.4 %copy-done.3 = bf16[512,8192]{1,0:T(8,128)(2,1)S(1)} copy-done((bf16[512,8192]{1,0:T(8,128)(2,1)S(1)}, bf16[512,8192]{1,0:T(8,128)(2,1)}, u32[]{:S(2)}) %copy-start.3) | copy-done | bytes 8388632
  181.4 2.2 %copy-done.7 = f32[512,2048]{1,0:T(8,128)S(1)} copy-done((f32[512,2048]{1,0:T(8,128)S(1)}, f32[512,2048]{1,0:T(8,128)}, u32[]{:S(2)}) %copy-start.7) | copy-done | bytes 4194328
  183.6 5.7 %backward.5 = f32[512,2048]{1,0:T(8,128)S(1)} custom-call(s32[8]{0:T(128)S(1)} %stack.175.spots_ref, bf16[4,2048,128]{2,1,0:T(8,128)(2,1)} %collective-permute-done.17.refs_0_, bf16[4,2048,128]{2,1,0:T(8,128)(2,1)} %collective-permute-done.18.refs_1_, bf16[512,8192]{1,0:T(8,128)(2,1)S(1)} %copy-done.3, bf16[512,8192]{1,0:T(8,128)(2,1)S(1)} %copy-done.3, ...), custom_call_target="tpu_custom_call" | custom-call | flops 268435456 | bytes 524288 | tf_op jit(solution)/shard_map/backward/pallas_call | solution.py:210
  192.8 3.0 %collective-permute-start.23 = (bf16[512,256]{1,0:T(8,128)(2,1)S(1)}, bf16[512,256]{1,0:T(8,128)(2,1)S(1)}, u32[]{:S(2)}, u32[]{:S(2)}) collective-permute-start(bf16[512,256]{1,0:T(8,128)(2,1)S(1)} %add_convert_fusion.1), channel_id=1, source_target_pairs={{1,4},{5,5},{9,12},{13,13},{17,20},{21,21},{25,28},{29,29},{33,38}... | collective-permute-start | bytes 786440 | tf_op jit(solution)/shard_map/ppermute | solution.py:256
  (147 shorter events, 38.9 us)
Async XLA Ops:
  0.6 13.3 %copy-start = (f32[256,256]{1,0:T(8,128)S(1)}, f32[256,256]{1,0:T(8,128)}, u32[]{:S(2)}) copy-start(f32[256,256]{1,0:T(8,128)} %param.10) | copy-start | bytes 786436
  0.6 12.5 %copy-start.28 = (f32[16,4,2]{0,2,1:T(2,128)S(1)}, f32[16,4,2]{0,2,1:T(2,128)}, u32[]{:S(2)}) copy-start(f32[16,4,2]{0,2,1:T(2,128)} %param.13) | copy-start | bytes 1540
  0.7 12.4 %copy-start.27 = (f32[16,4,2]{0,2,1:T(2,128)S(1)}, f32[16,4,2]{0,2,1:T(2,128)}, u32[]{:S(2)}) copy-start(f32[16,4,2]{0,2,1:T(2,128)} %param.11) | copy-start | bytes 1540
  0.7 13.1 %copy-start.23 = (s32[16,4,2]{0,2,1:T(2,128)S(1)}, s32[16,4,2]{0,2,1:T(2,128)}, u32[]{:S(2)}) copy-start(s32[16,4,2]{0,2,1:T(2,128)} %param.14) | copy-start | bytes 1540
  0.7 13.9 %copy-start.24 = (s32[16,4,2]{0,2,1:T(2,128)S(1)}, s32[16,4,2]{0,2,1:T(2,128)}, u32[]{:S(2)}) copy-start(s32[16,4,2]{0,2,1:T(2,128)} %param.12) | copy-start | bytes 1540
  0.7 14.2 %copy-start.12 = (bf16[512,1024]{1,0:T(8,128)(2,1)S(1)}, bf16[512,1024]{1,0:T(8,128)(2,1)}, u32[]{:S(2)}) copy-start(bf16[512,1024]{1,0:T(8,128)(2,1)} %param.8) | copy-start | bytes 3145732
  2.1 3.2 %collective-permute-start.1 = (bf16[1024,256]{1,0:T(8,128)(2,1)S(1)}, bf16[1024,256]{1,0:T(8,128)(2,1)}, u32[]{:S(2)}, u32[]{:S(2)}) collective-permute-start(bf16[1024,256]{1,0:T(8,128)(2,1)S(1)} %get-tuple-element.54), channel_id=1, source_target_pairs={{0,1},{1,0},{2,3},{3,2},{4,5},{5,4},{6,7},{7,6},{8,9},{9,8},{10,11... | collective-permute-start | bytes 1572872 | tf_op jit(solution)/shard_map/ppermute | solution.py:283
  6.4 11.4 %collective-permute-start.3 = (bf16[2048,128]{1,0:T(8,128)(2,1)S(1)}, bf16[2048,128]{1,0:T(8,128)(2,1)}, u32[]{:S(2)}, u32[]{:S(2)}) collective-permute-start(bf16[2048,128]{1,0:T(8,128)(2,1)S(1)} %get-tuple-element.28), channel_id=1, source_target_pairs={{0,32},{1,9},{2,34},{3,11},{4,36},{5,13},{6,38},{7,15},{8,40},{9,1... | collective-permute-start | bytes 1572872 | tf_op jit(solution)/shard_map/ppermute | solution.py:43
  8.2 17.4 %collective-permute-start.2 = (bf16[2048,128]{1,0:T(8,128)(2,1)S(1)}, bf16[2048,128]{1,0:T(8,128)(2,1)}, u32[]{:S(2)}, u32[]{:S(2)}) collective-permute-start(bf16[2048,128]{1,0:T(8,128)(2,1)S(1)} %get-tuple-element.28), channel_id=1, source_target_pairs={{0,96},{1,25},{2,98},{3,27},{4,100},{5,29},{6,102},{7,31},{8,104},... | collective-permute-start | bytes 1572872 | tf_op jit(solution)/shard_map/ppermute | solution.py:43
  10.4 24.1 %collective-permute-start.7 = (bf16[2048,128]{1,0:T(8,128)(2,1)S(1)}, bf16[2048,128]{1,0:T(8,128)(2,1)S(1)}, u32[]{:S(2)}, u32[]{:S(2)}) collective-permute-start(bf16[2048,128]{1,0:T(8,128)(2,1)S(1)} %get-tuple-element.29), channel_id=1, source_target_pairs={{0,32},{1,9},{2,34},{3,11},{4,36},{5,13},{6,38},{7,15},{8,40},{9,1... | collective-permute-start | bytes 1572872 | tf_op jit(solution)/shard_map/ppermute | solution.py:43
  10.4 12.0 %collective-permute-start.5 = (bf16[2048,128]{1,0:T(8,128)(2,1)S(1)}, bf16[2048,128]{1,0:T(8,128)(2,1)}, u32[]{:S(2)}, u32[]{:S(2)}) collective-permute-start(bf16[2048,128]{1,0:T(8,128)(2,1)S(1)} %get-tuple-element.29), channel_id=1, source_target_pairs={{0,96},{1,25},{2,98},{3,27},{4,100},{5,29},{6,102},{7,31},{8,104},... | collective-permute-start | bytes 1572872 | tf_op jit(solution)/shard_map/ppermute | solution.py:43
  14.6 19.0 %copy-start.13 = (f32[16,4,256]{2,0,1:T(8,128)}, f32[16,4,256]{2,0,1:T(8,128)S(1)}, u32[]{:S(2)}) copy-start(f32[16,4,256]{2,0,1:T(8,128)S(1)} %select_reduce_fusion.3) | copy-start | bytes 196612
  14.9 18.8 %copy-start.17 = (bf16[4,2,8,256]{3,2,0,1:T(8,128)(2,1)}, bf16[4,2,8,256]{3,2,0,1:T(8,128)(2,1)S(1)}, u32[]{:S(2)}) copy-start(bf16[4,2,8,256]{3,2,0,1:T(8,128)(2,1)S(1)} %copy.43) | copy-start | bytes 98308
  17.8 10.5 %collective-permute-start.4 = (bf16[2048,128]{1,0:T(8,128)(2,1)}, bf16[2048,128]{1,0:T(8,128)(2,1)S(1)}, u32[]{:S(2)}, u32[]{:S(2)}) collective-permute-start(bf16[2048,128]{1,0:T(8,128)(2,1)} %collective-permute-done.3), channel_id=1, source_target_pairs={{0,32},{1,9},{2,34},{3,11},{4,36},{5,13},{6,38},{7,15},{8,40},{9,1... | collective-permute-start | bytes 1572872 | tf_op jit(solution)/shard_map/ppermute | solution.py:43
  22.4 11.3 %collective-permute-start.6 = (bf16[2048,128]{1,0:T(8,128)(2,1)}, bf16[2048,128]{1,0:T(8,128)(2,1)S(1)}, u32[]{:S(2)}, u32[]{:S(2)}) collective-permute-start(bf16[2048,128]{1,0:T(8,128)(2,1)} %collective-permute-done.5), channel_id=1, source_target_pairs={{0,96},{1,25},{2,98},{3,27},{4,100},{5,29},{6,102},{7,31},{8,104},... | collective-permute-start | bytes 1572872 | tf_op jit(solution)/shard_map/ppermute | solution.py:43
  35.4 51.2 %collective-permute-start.15 = (bf16[8,2048,128]{2,1,0:T(8,128)(2,1)}, bf16[8,2048,128]{2,1,0:T(8,128)(2,1)}, u32[]{:S(2)}, u32[]{:S(2)}) collective-permute-start(bf16[8,2048,128]{2,1,0:T(8,128)(2,1)} %bitcast_dynamic-update-slice_fusion.refs_0_.refs_1_), channel_id=1, source_target_pairs={{0,24},{1,97},{2,26},{3,99},{4,28},{5,101},{6,30},{7,103},{8,0},{9... | collective-permute-start | bytes 12582920 | tf_op jit(solution)/shard_map/ppermute | solution.py:43
  38.0 51.7 %collective-permute-start.14 = (bf16[8,2048,128]{2,1,0:T(8,128)(2,1)}, bf16[8,2048,128]{2,1,0:T(8,128)(2,1)}, u32[]{:S(2)}, u32[]{:S(2)}) collective-permute-start(bf16[8,2048,128]{2,1,0:T(8,128)(2,1)} %bitcast_dynamic-update-slice_fusion.refs_0_.refs_1_), channel_id=1, source_target_pairs={{0,8},{1,33},{2,10},{3,35},{4,12},{5,37},{6,14},{7,39},{8,16},{9,4... | collective-permute-start | bytes 12582920 | tf_op jit(solution)/shard_map/ppermute | solution.py:43
  38.0 11.7 %collective-permute-start = (bf16[512,1024]{1,0:T(8,128)(2,1)S(1)}, bf16[512,1024]{1,0:T(8,128)(2,1)}, u32[]{:S(2)}, u32[]{:S(2)}) collective-permute-start(bf16[512,1024]{1,0:T(8,128)(2,1)S(1)} %copy-done.12), channel_id=1, source_target_pairs={{0,1},{1,0},{2,3},{3,2},{4,5},{5,4},{6,7},{7,6},{8,9},{9,8},{10,11... | collective-permute-start | bytes 3145736 | tf_op jit(solution)/shard_map/ppermute | solution.py:303
  39.9 2.2 %collective-permute-start.8 = (f32[32,512]{1,0:T(8,128)S(1)}, f32[32,512]{1,0:T(8,128)S(1)}, u32[]{:S(2)}, u32[]{:S(2)}) collective-permute-start(f32[32,512]{1,0:T(8,128)S(1)} %pad_maximum_fusion.2), channel_id=1, source_target_pairs={{0,1},{1,0},{2,3},{3,2},{4,5},{5,4},{6,7},{7,6},{8,9},{9,8},{10,11... | collective-permute-start | bytes 196616 | tf_op jit(solution)/shard_map/ppermute | solution.py:67
  42.1 3.7 %collective-permute-start.9 = (f32[32,512]{1,0:T(8,128)S(1)}, f32[32,512]{1,0:T(8,128)}, u32[]{:S(2)}, u32[]{:S(2)}) collective-permute-start(f32[32,512]{1,0:T(8,128)S(1)} %add.386), channel_id=1, source_target_pairs={{0,2},{1,3},{2,0},{3,1},{4,6},{5,7},{6,4},{7,5},{8,10},{9,11},{10,... | collective-permute-start | bytes 196616 | tf_op jit(solution)/shard_map/ppermute | solution.py:68
  46.7 12.9 %collective-permute-start.10 = (f32[32,512]{1,0:T(8,128)S(1)}, f32[32,512]{1,0:T(8,128)S(1)}, u32[]{:S(2)}, u32[]{:S(2)}) collective-permute-start(f32[32,512]{1,0:T(8,128)S(1)} %add.387), channel_id=1, source_target_pairs={{0,4},{1,5},{2,6},{3,7},{4,0},{5,1},{6,2},{7,3},{8,12},{9,13},{10,... | collective-permute-start | bytes 196616 | tf_op jit(solution)/shard_map/ppermute | solution.py:69
  56.1 49.8 %all-to-all-start = ((bf16[4,512,256]{2,1,0:T(8,128)(2,1)}), bf16[4,512,256]{2,1,0:T(8,128)(2,1)S(1)}, u32[]{:S(2)}, u32[]{:S(2)}) async-start(bf16[4,512,256]{2,1,0:T(8,128)(2,1)} %copy-done.9), calls=%async_computation | async-start | bytes 2097152 | tf_op jit(solution)/shard_map/all_to_all | solution.py:61
  63.4 32.8 %collective-permute-start.12 = (f32[32,1024]{1,0:T(8,128)}, f32[32,1024]{1,0:T(8,128)}, u32[]{:S(2)}, u32[]{:S(2)}) collective-permute-start(f32[32,1024]{1,0:T(8,128)} %maximum_multiply_fusion), channel_id=1, source_target_pairs={{0,32},{1,33},{2,34},{3,35},{4,36},{5,37},{6,38},{7,39},{8,40},{9,... | collective-permute-start | bytes 393224 | tf_op jit(solution)/shard_map/ppermute | solution.py:79
  63.4 32.8 %collective-permute-start.13 = (f32[32,1024]{1,0:T(8,128)}, f32[32,1024]{1,0:T(8,128)}, u32[]{:S(2)}, u32[]{:S(2)}) collective-permute-start(f32[32,1024]{1,0:T(8,128)} %maximum_multiply_fusion), channel_id=1, source_target_pairs={{0,96},{1,97},{2,98},{3,99},{4,100},{5,101},{6,102},{7,103},{8,104... | collective-permute-start | bytes 393224 | tf_op jit(solution)/shard_map/ppermute | solution.py:79
  66.0 30.2 %collective-permute-start.11 = (f32[32,1024]{1,0:T(8,128)}, f32[32,1024]{1,0:T(8,128)}, u32[]{:S(2)}, u32[]{:S(2)}) collective-permute-start(f32[32,1024]{1,0:T(8,128)} %maximum_multiply_fusion), channel_id=1, source_target_pairs={{0,64},{1,65},{2,66},{3,67},{4,68},{5,69},{6,70},{7,71},{8,72},{9,... | collective-permute-start | bytes 393224 | tf_op jit(solution)/shard_map/ppermute | solution.py:79
  76.0 16.8 %copy-start.4 = (f32[512,2048]{1,0:T(8,128)}, f32[512,2048]{1,0:T(8,128)S(1)}, u32[]{:S(2)}) copy-start(f32[512,2048]{1,0:T(8,128)S(1)} %backward.3.refs_20_) | copy-start | bytes 12582916
  92.8 54.5 %collective-permute-start.17 = (bf16[4,2048,128]{2,1,0:T(8,128)(2,1)}, bf16[4,2048,128]{2,1,0:T(8,128)(2,1)}, u32[]{:S(2)}, u32[]{:S(2)}) collective-permute-start(bf16[4,2048,128]{2,1,0:T(8,128)(2,1)} %slice.95), channel_id=1, source_target_pairs={{0,8},{1,33},{2,10},{3,35},{4,12},{5,37},{6,14},{7,39},{8,16},{9,4... | collective-permute-start | bytes 6291464 | tf_op jit(solution)/shard_map/ppermute | solution.py:43
  93.4 54.0 %collective-permute-start.18 = (bf16[4,2048,128]{2,1,0:T(8,128)(2,1)}, bf16[4,2048,128]{2,1,0:T(8,128)(2,1)}, u32[]{:S(2)}, u32[]{:S(2)}) collective-permute-start(bf16[4,2048,128]{2,1,0:T(8,128)(2,1)} %slice.96), channel_id=1, source_target_pairs={{0,24},{1,97},{2,26},{3,99},{4,28},{5,101},{6,30},{7,103},{8,0},{9... | collective-permute-start | bytes 6291464 | tf_op jit(solution)/shard_map/ppermute | solution.py:43
  105.9 31.0 %all-to-all-start.1 = ((bf16[4,512,512]{2,1,0:T(8,128)(2,1)}), bf16[4,512,512]{2,1,0:T(8,128)(2,1)}, u32[]{:S(2)}, u32[]{:S(2)}) async-start(bf16[4,512,512]{2,1,0:T(8,128)(2,1)} %copy-done.8), calls=%async_computation.1 | async-start | bytes 4194304 | tf_op jit(solution)/shard_map/all_to_all | solution.py:61
  110.4 18.3 %collective-permute-start.28 = (f32[32,1024]{1,0:T(8,128)}, f32[32,1024]{1,0:T(8,128)}, u32[]{:S(2)}, u32[]{:S(2)}) collective-permute-start(f32[32,1024]{1,0:T(8,128)} %add_add_fusion.1), channel_id=1, source_target_pairs={{0,24},{1,25},{2,26},{3,27},{4,28},{5,29},{6,30},{7,31},{8,0},{9,1... | collective-permute-start | bytes 393224 | tf_op jit(solution)/shard_map/ppermute | solution.py:79
  112.0 16.6 %collective-permute-start.27 = (f32[32,1024]{1,0:T(8,128)}, f32[32,1024]{1,0:T(8,128)}, u32[]{:S(2)}, u32[]{:S(2)}) collective-permute-start(f32[32,1024]{1,0:T(8,128)} %add_add_fusion.1), channel_id=1, source_target_pairs={{0,16},{1,17},{2,18},{3,19},{4,20},{5,21},{6,22},{7,23},{8,24},{9,... | collective-permute-start | bytes 393224 | tf_op jit(solution)/shard_map/ppermute | solution.py:79
  112.0 16.6 %collective-permute-start.26 = (f32[32,1024]{1,0:T(8,128)}, f32[32,1024]{1,0:T(8,128)}, u32[]{:S(2)}, u32[]{:S(2)}) collective-permute-start(f32[32,1024]{1,0:T(8,128)} %add_add_fusion.1), channel_id=1, source_target_pairs={{0,8},{1,9},{2,10},{3,11},{4,12},{5,13},{6,14},{7,15},{8,16},{9,17... | collective-permute-start | bytes 393224 | tf_op jit(solution)/shard_map/ppermute | solution.py:79
  118.4 11.4 %copy-start.16 = (f32[16,4,256]{2,0,1:T(8,128)S(1)}, f32[16,4,256]{2,0,1:T(8,128)}, u32[]{:S(2)}) copy-start(f32[16,4,256]{2,0,1:T(8,128)} %copy-done.15) | copy-start | bytes 196612
  128.6 17.3 %copy-start.14 = (f32[16,4,256]{2,0,1:T(8,128)S(1)}, f32[16,4,256]{2,0,1:T(8,128)}, u32[]{:S(2)}) copy-start(f32[16,4,256]{2,0,1:T(8,128)} %copy-done.13) | copy-start | bytes 196612
  140.7 19.6 %all-to-all-start.2 = ((bf16[4,512,256]{2,1,0:T(8,128)(2,1)}), bf16[4,512,256]{2,1,0:T(8,128)(2,1)}, u32[]{:S(2)}, u32[]{:S(2)}) async-start(bf16[4,512,256]{2,1,0:T(8,128)(2,1)} %arrange.1), calls=%async_computation.2 | async-start | bytes 2097152 | tf_op jit(solution)/shard_map/all_to_all | solution.py:61
  152.2 23.5 %copy-start.10 = (bf16[512,256]{1,0:T(8,128)(2,1)}, bf16[512,256]{1,0:T(8,128)(2,1)S(1)}, u32[]{:S(2)}) copy-start(bf16[512,256]{1,0:T(8,128)(2,1)S(1)} %get-tuple-element.40) | copy-start | bytes 786436
  152.2 7.9 %collective-permute-start.29 = (f32[256,256]{1,0:T(8,128)S(1)}, f32[256,256]{1,0:T(8,128)S(1)}, u32[]{:S(2)}, u32[]{:S(2)}) collective-permute-start(f32[256,256]{1,0:T(8,128)S(1)} %fusion.4), channel_id=1, source_target_pairs={{0,1},{1,0},{2,3},{3,2},{4,5},{5,4},{6,7},{7,6},{8,9},{9,8},{10,11... | collective-permute-start | bytes 786440 | tf_op jit(solution)/shard_map/ppermute | solution.py:67
  154.1 35.4 %collective-permute-start.19 = (bf16[512,256]{1,0:T(8,128)(2,1)S(1)}, bf16[512,256]{1,0:T(8,128)(2,1)}, u32[]{:S(2)}, u32[]{:S(2)}) collective-permute-start(bf16[512,256]{1,0:T(8,128)(2,1)S(1)} %get-tuple-element.41), channel_id=1, source_target_pairs={{0,4},{1,5},{2,6},{3,7},{4,0},{5,1},{6,2},{7,3},{8,12},{9,13},{10,... | collective-permute-start | bytes 786440 | tf_op jit(solution)/shard_map/ppermute | solution.py:360
  157.4 33.5 %collective-permute-start.20 = (bf16[512,256]{1,0:T(8,128)(2,1)}, bf16[512,256]{1,0:T(8,128)(2,1)}, u32[]{:S(2)}, u32[]{:S(2)}) collective-permute-start(bf16[512,256]{1,0:T(8,128)(2,1)} %get-tuple-element.42), channel_id=1, source_target_pairs={{0,2},{1,3},{2,4},{3,5},{4,6},{5,7},{6,0},{7,1},{8,10},{9,11},{10,... | collective-permute-start | bytes 786440 | tf_op jit(solution)/shard_map/ppermute | solution.py:360
  157.7 33.2 %collective-permute-start.21 = (bf16[512,256]{1,0:T(8,128)(2,1)S(1)}, bf16[512,256]{1,0:T(8,128)(2,1)}, u32[]{:S(2)}, u32[]{:S(2)}) collective-permute-start(bf16[512,256]{1,0:T(8,128)(2,1)S(1)} %get-tuple-element.43), channel_id=1, source_target_pairs={{0,6},{1,7},{2,0},{3,1},{4,2},{5,3},{6,4},{7,5},{8,14},{9,15},{10,... | collective-permute-start | bytes 786440 | tf_op jit(solution)/shard_map/ppermute | solution.py:360
  160.1 15.5 %collective-permute-start.30 = (f32[256,256]{1,0:T(8,128)S(1)}, f32[256,256]{1,0:T(8,128)S(1)}, u32[]{:S(2)}, u32[]{:S(2)}) collective-permute-start(f32[256,256]{1,0:T(8,128)S(1)} %add.473), channel_id=1, source_target_pairs={{0,2},{1,3},{2,0},{3,1},{4,6},{5,7},{6,4},{7,5},{8,10},{9,11},{10,... | collective-permute-start | bytes 786440 | tf_op jit(solution)/shard_map/ppermute | solution.py:68
  161.5 36.4 %collective-permute-start.16 = (bf16[2,512,256]{2,1,0:T(8,128)(2,1)S(1)}, bf16[2,512,256]{2,1,0:T(8,128)(2,1)S(1)}, u32[]{:S(2)}, u32[]{:S(2)}) collective-permute-start(bf16[2,512,256]{2,1,0:T(8,128)(2,1)S(1)} %slice_select_fusion.1), channel_id=1, source_target_pairs={{0,1},{1,0},{2,3},{3,2},{4,5},{5,4},{6,7},{7,6},{8,9},{9,8},{10,11... | collective-permute-start | bytes 1572872 | tf_op jit(solution)/shard_map/ppermute | solution.py:352
  175.7 20.2 %collective-permute-start.31 = (f32[256,256]{1,0:T(8,128)S(1)}, f32[256,256]{1,0:T(8,128)S(1)}, u32[]{:S(2)}, u32[]{:S(2)}) collective-permute-start(f32[256,256]{1,0:T(8,128)S(1)} %add.474), channel_id=1, source_target_pairs={{0,4},{1,5},{2,6},{3,7},{4,0},{5,1},{6,2},{7,3},{8,12},{9,13},{10,... | collective-permute-start | bytes 786440 | tf_op jit(solution)/shard_map/ppermute | solution.py:69
  189.5 9.9 %copy-start.20 = (bf16[32,512]{1,0:T(8,128)(2,1)S(1)}, bf16[32,512]{1,0:T(8,128)(2,1)}, u32[]{:S(2)}) copy-start(bf16[32,512]{1,0:T(8,128)(2,1)} %copy-done.19) | copy-start | bytes 98308
  189.5 11.3 %collective-permute-start.25 = (bf16[512,1024]{1,0:T(8,128)(2,1)S(1)}, bf16[512,1024]{1,0:T(8,128)(2,1)S(1)}, u32[]{:S(2)}, u32[]{:S(2)}) collective-permute-start(bf16[512,1024]{1,0:T(8,128)(2,1)S(1)} %slice.143), channel_id=1, source_target_pairs={{0,1},{1,0},{2,3},{3,2},{4,5},{5,4},{6,7},{7,6},{8,9},{9,8},{10,11... | collective-permute-start | bytes 3145736 | tf_op jit(solution)/shard_map/ppermute | solution.py:374
  192.1 7.1 %collective-permute-start.24 = (bf16[512,256]{1,0:T(8,128)(2,1)S(1)}, bf16[512,256]{1,0:T(8,128)(2,1)S(1)}, u32[]{:S(2)}, u32[]{:S(2)}) collective-permute-start(bf16[512,256]{1,0:T(8,128)(2,1)S(1)} %add_convert_fusion.1), channel_id=1, source_target_pairs={{3,4},{7,5},{11,12},{15,13},{19,20},{23,21},{27,28},{31,29},{35,38... | collective-permute-start | bytes 786440 | tf_op jit(solution)/shard_map/ppermute | solution.py:256
  192.8 6.4 %collective-permute-start.23 = (bf16[512,256]{1,0:T(8,128)(2,1)S(1)}, bf16[512,256]{1,0:T(8,128)(2,1)S(1)}, u32[]{:S(2)}, u32[]{:S(2)}) collective-permute-start(bf16[512,256]{1,0:T(8,128)(2,1)S(1)} %add_convert_fusion.1), channel_id=1, source_target_pairs={{1,4},{5,5},{9,12},{13,13},{17,20},{21,21},{25,28},{29,29},{33,38}... | collective-permute-start | bytes 786440 | tf_op jit(solution)/shard_map/ppermute | solution.py:256
  195.9 3.4 %collective-permute-start.22 = (bf16[512,256]{1,0:T(8,128)(2,1)S(1)}, bf16[512,256]{1,0:T(8,128)(2,1)S(1)}, u32[]{:S(2)}, u32[]{:S(2)}) collective-permute-start(bf16[512,256]{1,0:T(8,128)(2,1)S(1)} %add_convert_fusion.1), channel_id=1, source_target_pairs={{0,1},{2,3},{4,5},{6,7},{8,9},{10,11},{12,13},{14,15},{32,33},{34,... | collective-permute-start | bytes 786440 | tf_op jit(solution)/shard_map/ppermute | solution.py:261
  (16 other events, 51.9 us)

commit v2 on v1

--- a/solution.py
+++ b/solution.py
@@ -43,18 +43,11 @@
     return lax.ppermute(value, BOTH, ring(stage, step))
 
 
-def first_ring(own, h):
-    below = shift(own, 0, 1)
-    above = shift(own, 0, -1)
-    across = shift(below, 0, 1) if h == 0 else shift(above, 0, -1)
+def ring_gather(own, stage, h):
+    below = shift(own, stage, 1)
+    above = shift(own, stage, -1)
+    across = shift(below, stage, 1) if h == 0 else shift(above, stage, -1)
     return [own, above, across, below]
-
-
-def second_ring(own):
-    below = shift(own, 1, 1)
-    above = shift(own, 1, -1)
-    passed = lax.optimization_barrier((below[:SIDE], above[SIDE:]))
-    return above, below, passed, [shift(passed[0], 1, 1), shift(passed[1], 1, -1)]
 
 
 def exchange(value, axis, groups=None):
@@ -89,19 +82,16 @@
     return lax.optimization_barrier((value, *events))[0]
 
 
-def forward_kernel(offsets, near_ref, wide_ref, *refs):
-    count = len(offsets)
-    lines, outs, held, sems = refs[:count], refs[count:-2], refs[-2], refs[-1]
-    copies = [
-        pltpu.make_async_copy(lines[m].at[pl.ds(offsets[m], SIDE)], held.at[m], sems.at[m])
-        for m in range(count)
-    ]
+def forward_kernel(count, start_ref, wide_ref, *refs):
+    lines, outs, held, sems = refs[:count], refs[-6:-2], refs[-2], refs[-1]
+    outs = refs[-3:-2] if len(refs) < count + 6 else outs
+    copies = [pltpu.make_async_copy(lines[m], held.at[m], sems.at[m]) for m in range(count)]
     for copy in copies:
         copy.start()
     part = held.shape[3]
+    order = [lax.rem(start_ref[0] + k, SIDE) for k in range(SIDE)]
     for m in range(count):
         copies[m].wait()
-        order = [lax.rem(near_ref[0] + k, SIDE) for k in range(SIDE)]
         weights = jnp.concatenate([held[m, k] for k in order], axis=1)
         product = jnp.dot(wide_ref[...], weights, preferred_element_type=jnp.float32)
         product = product.astype(jnp.bfloat16)
@@ -113,27 +103,34 @@
                 outs[k][:, m * part : (m + 1) * part] = piece
 
 
-def forward(start, wide, lines, apart=False):
+def forward(start, wide, lines, apart=False, places=1, into=None):
     tokens, depth = wide.shape
-    part = lines[0][0].shape[2]
+    part = lines[0].shape[2]
     count = len(lines)
-    shape = (tokens, count * part) if apart else (SIDE, tokens, count * part)
-    outs = jax.ShapeDtypeStruct(shape, jnp.bfloat16)
-    spec = pl.BlockSpec(shape, lambda i, n: (0,) * len(shape))
+    cols = count * part
+    if apart:
+        outs = [pltpu.HBM((tokens, cols), jnp.bfloat16)] * SIDE
+        specs = [pl.BlockSpec((tokens, cols), lambda i, n: (0, 0))] * SIDE
+    else:
+        place = 0 if into is None else 1
+        outs = pltpu.HBM((SIDE, tokens, places * cols), jnp.bfloat16)
+        specs = pl.BlockSpec((SIDE, tokens, cols), lambda i, n: (0, 0, place))
+    extra = [] if into is None else [into]
     return pl.pallas_call(
-        functools.partial(forward_kernel, [offset for _, offset in lines]),
-        out_shape=[outs] * SIDE if apart else outs,
+        functools.partial(forward_kernel, count),
+        out_shape=outs,
         grid_spec=pltpu.PrefetchScalarGridSpec(
             num_scalar_prefetch=1,
             grid=(1,),
             in_specs=[pl.BlockSpec((tokens, depth), lambda i, n: (0, 0))]
-            + [pl.BlockSpec(memory_space=pl.ANY)] * count,
-            out_specs=[spec] * SIDE if apart else spec,
+            + [pl.BlockSpec(memory_space=pl.ANY)] * (count + len(extra)),
+            out_specs=specs,
             scratch_shapes=[
                 pltpu.VMEM((count, SIDE, depth, part), jnp.bfloat16),
                 pltpu.SemaphoreType.DMA((count,)),
             ],
         ),
+        input_output_aliases={} if into is None else {count + 2: 0},
         compiler_params=pltpu.CompilerParams(vmem_limit_bytes=28 << 20),
         cost_estimate=pl.CostEstimate(
             flops=tokens * depth * count * part,
@@ -141,7 +138,7 @@
             transcendentals=0,
         ),
         name="forward",
-    )(start, wide, *[line for line, _ in lines])
+    )(start, wide, *lines, *extra)
 
 
 def arrange_kernel(far_ref, here_ref, beside_ref, out_ref):
@@ -195,13 +192,10 @@
 
 def backward(spots, grown, out_grad, lines):
     tokens = out_grad.shape[0]
-    depth, part = lines[0][0].shape[1:]
+    depth, part = lines[0].shape[1:]
     count = len(lines)
-    block = depth // 4
+    block = depth // 2
     first = grown is None
-
-    def held(place):
-        return pl.BlockSpec((SIDE, block, part), lambda i, n: (place, i, 0))
 
     def column(j):
         return pl.BlockSpec((tokens, part), lambda i, n: (0, n[j]))
@@ -209,23 +203,24 @@
     total = pl.BlockSpec((tokens, block), lambda i, n: (0, i))
     return pl.pallas_call(
         functools.partial(backward_kernel, count, first),
-        out_shape=jax.ShapeDtypeStruct((tokens, depth), jnp.float32),
+        out_shape=pltpu.HBM((tokens, depth), jnp.float32),
         grid_spec=pltpu.PrefetchScalarGridSpec(
             num_scalar_prefetch=1,
-            grid=(4,),
-            in_specs=[held(offset // SIDE) for _, offset in lines]
+            grid=(2,),
+            in_specs=[pl.BlockSpec((SIDE, block, part), lambda i, n: (0, i, 0))] * count
             + [column(j) for j in range(count * SIDE)]
             + ([] if first else [total]),
             out_specs=total,
         ),
-        compiler_params=pltpu.CompilerParams(vmem_limit_bytes=28 << 20),
+        input_output_aliases={} if first else {5 * count + 1: 0},
+        compiler_params=pltpu.CompilerParams(vmem_limit_bytes=36 << 20),
         cost_estimate=pl.CostEstimate(
             flops=tokens * depth * count * part,
             bytes_accessed=depth * part * count,
             transcendentals=0,
         ),
         name="backward",
-    )(spots, *[line for line, _ in lines], *([out_grad] * (count * SIDE)), *([] if first else [grown]))
+    )(spots, *lines, *([pltpu.with_memory_space_constraint(out_grad, pltpu.HBM)] * (count * SIDE)), *([] if first else [grown]))
 
 
 def compose(logits, indices, vector_bank):
@@ -286,7 +281,7 @@
         cols = slice(h * part, (h + 1) * part)
         shards.append(jnp.concatenate([mine[:, cols], swapped[:, cols]], axis=0))
     logits_a, logits_b, *shards = lax.optimization_barrier((logits_a, logits_b, *shards))
-    lines = first_ring(shards[0], 0) + first_ring(shards[1], 1)
+    lines = [jnp.stack(ring_gather(shards[h], 0, h)) for h in range(2)]
     def columns(i, h):
         far_at = (far + i) % SIDE
         spots = []
@@ -312,11 +307,8 @@
     low_part = lax.dot_general(down_a, attn_out, cols_by_cols, preferred_element_type=f32)
     back_part = lax.dot_general(up_b, grad_cols, cols_by_cols, preferred_element_type=f32)
     totals = jnp.concatenate([low_part, back_part], axis=0)
-    own, totals = lax.optimization_barrier((jnp.stack(lines), totals))
-    above, below, passed, corner = second_ring(own)
-    blocks = [
-        [(own, h * SIDE), (above, h * SIDE), (corner[h], 0), (below, h * SIDE)] for h in range(2)
-    ]
+    lines[1], totals = lax.optimization_barrier((lines[1], totals))
+    blocks = [ring_gather(lines[h], 1, h) for h in range(2)]
     totals = over_tensor(totals).astype(bf16)
     low_bf, back_bf = totals[:rank], totals[rank:]
 
@@ -335,32 +327,34 @@
 
     sent_here = forward(turned, wide, take(here))
     slots_here = exchange(sent_here, "tensor", LANES)
-    grown = backward(spots_of(here), None, out_grad, take(here))
+    grown = backward(after(spots_of(here), sent_here), None, out_grad, take(here))
+    sent_beside = forward(after(turned, grown), wide, take(beside[:2]), places=2)
+    sent_beside = forward(turned, wide, take(beside[2:]), places=2, into=sent_beside)
+    slots_here, sent_beside, *both_parts = lax.optimization_barrier(
+        (slots_here, sent_beside, *both_parts)
+    )
+    slots_beside = exchange(sent_beside, "tensor", LANES)
+    both_parts = over_side(total_of(both_parts), 1)
+    grown = backward(after(spots_of(beside), sent_beside), grown, out_grad, take(beside))
+    sent = forward(after(turned_here, grown), wide, take(across), apart=True)
+    slots_beside, *both_parts = lax.optimization_barrier((slots_beside, *both_parts, *sent))[:5]
     both = total_of(both_parts)
-    turned, both, *_ = lax.optimization_barrier((turned, both, sent_here, grown, *passed))
-    sent_beside = forward(turned, wide, take(beside))
-    slots_here, sent_beside = lax.optimization_barrier((slots_here, sent_beside))
-    slots_beside = exchange(sent_beside, "tensor", LANES)
-    both_parts = over_side(both, 1)
-    grown = backward(spots_of(beside), grown, out_grad, take(beside))
-    both = total_of(lax.optimization_barrier((*both_parts, grown))[:SIDE])
     bank_a, logit_grad_a = compose_back(both[:rank], weights_a, picked_a, mixing_a, vector_bank)
     bank_b, logit_grad_b = compose_back(both[rank:], weights_b, picked_b, mixing_b, vector_bank)
 
-    slots = arrange(far.astype(jnp.int32).reshape(1), slots_here, after(slots_beside, grown))
+    slots = arrange(far.astype(jnp.int32).reshape(1), slots_here, slots_beside)
     moved = exchange(slots, "tensor", LANES)
     crossed = lax.ppermute(jnp.where(core == 0, slots[2:], moved[:2]), "tensor", SWAP)
     firsts = jnp.where(core == 0, slots[:2], crossed)
     seconds = jnp.where(core == 0, crossed, moved[2:])
 
-    sent = forward(turned_here, wide, take(across), apart=True)
     arrived = [sent[0]]
     for step in range(1, SIDE):
         turns = [(t, (t + 2 * step) % 8) for t in range(8)]
         arrived.append(lax.ppermute(sent[step], "tensor", turns))
     piece = total_of([a.astype(f32) for a in arrived]).astype(bf16)
-    bank_grad = over_tensor(after(bank_a + bank_b, *sent))
-    grown = backward(after(spots_of(across), *sent), grown, out_grad, take(across))
+    bank_grad = over_tensor(bank_a + bank_b)
+    grown = backward(after(spots_of(across), slots), grown, out_grad, take(across))
     first, place, second = settle(piece, 2, z, core)
     cols = []
     for s in range(2):

time: 205 us -> 201 us (0.980)
  local copies, waits for them, and re-layouts: 38.8 us -> 6.67 us
  waiting for transfers between devices: 38.1 us -> 48.4 us
  other arithmetic: 13.2 us -> 22.8 us
  Pallas kernels: 38.8 us -> 48.1 us
    unnamed x66 -> x51, local copies, waits for them, and re-layouts: 29 us -> 2.18 us
    ppermute x10 -> x12, waiting for transfers between devices: 16 us -> 30.1 us  [shift(): return lax.ppermute(value, BOTH, ring(stage, step))]
    ppermute x6, waiting for transfers between devices: 0.02 us -> 8.47 us  [from_step(): return lax.ppermute(value, BOTH, pairs(move))]
    ppermute x2, waiting for transfers between devices: 13.3 us -> 5.67 us  [over_tensor(): lax.ppermute(value, 'tensor', [(t, t ^ 2) for t in range(8)])]
    slice x2 -> x0, local copies, waits for them, and re-layouts: 6.15 us -> none  [second_ring(): passed = lax.optimization_barrier((below[:SIDE], above[SIDE:]))]
    another operation x0 -> x2, other arithmetic: none -> 5.46 us  [local(): lines = [jnp.stack(ring_gather(shards[h], 0, h)) for h in range(2)]]
    all_to_all x3, waiting for transfers between devices: 4.92 us -> 0.01 us  [exchange(): lax.all_to_all(value, axis, split_axis=0, concat_axis=0, tiled=True, axis...]
    pallas_call x3 -> x4, Pallas kernels: 15.6 us -> 20.4 us  [forward(): pl.pallas_call(functools.partial(forward_kernel, count), out_shape=outs,...]
  transfers between devices with their start and end apart: 35 -> 37, of which waited for: 8 -> 11; matrix products, arithmetic and copies ran while one was open for 20% -> 17% of each run, Pallas kernels for 19% -> 24%
where the time goes in v2:
time: 201 us; the launch traced here: 200 us
  starting transfers between devices  59.9 us (30%)
  waiting for transfers between devices  48.4 us (24%)
  Pallas kernels  48.1 us (24%)
  other arithmetic  22.8 us (11%)
  matrix products  12.4 us (6%)
  local copies, waits for them, and re-layouts  6.67 us (3%)
    ppermute x12, waiting for transfers between devices, shift(): return lax.ppermute(value, BOTH, ring(stage, step))  30.1 us
    pallas_call x3, Pallas kernels, backward(): pl.pallas_call(functools.partial(backward_kernel, count, first), out_shap...  23.9 us
    pallas_call x4, Pallas kernels, forward(): pl.pallas_call(functools.partial(forward_kernel, count), out_shape=outs,...  20.4 us
    ppermute x12, starting transfers between devices, shift(): return lax.ppermute(value, BOTH, ring(stage, step))  18 us
    all_to_all x3, starting transfers between devices, exchange(): lax.all_to_all(value, axis, split_axis=0, concat_axis=0, tiled=True, axis...  11.7 us
    ppermute x6, waiting for transfers between devices, from_step(): return lax.ppermute(value, BOTH, pairs(move))  8.47 us
    ppermute x6, starting transfers between devices, from_step(): return lax.ppermute(value, BOTH, pairs(move))  6.01 us
    ppermute x2, waiting for transfers between devices, over_tensor(): lax.ppermute(value, 'tensor', [(t, t ^ 2) for t in range(8)])  5.67 us
  transfers between devices with their start and end apart: 37, of which 11 were waited for; matrix products, arithmetic and copies ran while one was open for 17% of the time, Pallas kernels for 24%

profile of v2, /device:TPU:1, one launch (start us, length us, event | category | flops | bytes accessed | tf_op | source)
XLA Modules:
  0.0 199.8 jit_solution(5464744177802176292)
XLA Ops:
  2.0 1.5 collective-permute-start.1
  3.5 1.5 collective-permute-done.1
  5.1 1.8 collective-permute-start.3
  6.9 2.2 %collective-permute-start.2 = (bf16[2048,128]{1,0:T(8,128)(2,1)S(1)}, bf16[2048,128]{1,0:T(8,128)(2,1)}, u32[]{:S(2)}, u32[]{:S(2)}) collective-permute-start(bf16[2048,128]{1,0:T(8,128)(2,1)S(1)} %get-tuple-element.31), channel_id=1, source_target_pairs={{0,96},{1,25},{2,98},{3,27},{4,100},{5,29},{6,102},{7,31},{8,104},... | collective-permute-start | bytes 1572872 | tf_op jit(solution)/shard_map/ppermute | solution.py:43
  9.1 2.7 %collective-permute-start.5 = (bf16[2048,128]{1,0:T(8,128)(2,1)S(1)}, bf16[2048,128]{1,0:T(8,128)(2,1)}, u32[]{:S(2)}, u32[]{:S(2)}) collective-permute-start(bf16[2048,128]{1,0:T(8,128)(2,1)S(1)} %get-tuple-element.32), channel_id=1, source_target_pairs={{0,96},{1,25},{2,98},{3,27},{4,100},{5,29},{6,102},{7,31},{8,104},... | collective-permute-start | bytes 1572872 | tf_op jit(solution)/shard_map/ppermute | solution.py:43
  12.7 8.4 %collective-permute-done.5 = bf16[2048,128]{1,0:T(8,128)(2,1)} collective-permute-done((bf16[2048,128]{1,0:T(8,128)(2,1)S(1)}, bf16[2048,128]{1,0:T(8,128)(2,1)}, u32[]{:S(2)}, u32[]{:S(2)}) %collective-permute-start.5) | collective-permute-done | bytes 524320 | tf_op jit(solution)/shard_map/ppermute | solution.py:43
  21.1 3.2 %collective-permute-start.6 = (bf16[2048,128]{1,0:T(8,128)(2,1)}, bf16[2048,128]{1,0:T(8,128)(2,1)S(1)}, u32[]{:S(2)}, u32[]{:S(2)}) collective-permute-start(bf16[2048,128]{1,0:T(8,128)(2,1)} %collective-permute-done.5), channel_id=1, source_target_pairs={{0,96},{1,25},{2,98},{3,27},{4,100},{5,29},{6,102},{7,31},{8,104},... | collective-permute-start | bytes 1572872 | tf_op jit(solution)/shard_map/ppermute | solution.py:43
  24.8 1.6 fusion.13
  26.4 4.4 %collective-permute-done.6 = bf16[2048,128]{1,0:T(8,128)(2,1)S(1)} collective-permute-done((bf16[2048,128]{1,0:T(8,128)(2,1)}, bf16[2048,128]{1,0:T(8,128)(2,1)S(1)}, u32[]{:S(2)}, u32[]{:S(2)}) %collective-permute-start.6) | collective-permute-done | bytes 524320 | tf_op jit(solution)/shard_map/ppermute | solution.py:43
  30.8 2.8 %pad_maximum_fusion.1.refs_1_ = bf16[4,2048,128]{2,1,0:T(8,128)(2,1)} fusion(bf16[1,2048,128]{2,1,0:T(8,128)(2,1)} %bitcast.9, bf16[1,2048,128]{2,1,0:T(8,128)(2,1)S(1)} %bitcast.110, bf16[1,2048,128]{2,1,0:T(8,128)(2,1)} %bitcast.7, bf16[1,2048,128]{2,1,0:T(8,128)(2,1)S(1)} %bitcast.103), kind=kLoop, calls=%fused_computation.7 | loop fusion | flops 3145728 | bytes 4194304 | tf_op jit(solution)/shard_map/stack | solution.py:284
  34.3 2.7 %pad_maximum_fusion.refs_0_ = bf16[4,2048,128]{2,1,0:T(8,128)(2,1)} fusion(bf16[1,2048,128]{2,1,0:T(8,128)(2,1)S(1)} %bitcast.108, bf16[1,2048,128]{2,1,0:T(8,128)(2,1)S(1)} %bitcast.109, bf16[1,2048,128]{2,1,0:T(8,128)(2,1)} %bitcast.3, bf16[1,2048,128]{2,1,0:T(8,128)(2,1)S(1)} %bitcast.102), kind=kLoop, calls=%fused_computation.6 | loop fusion | flops 3145728 | bytes 4194304 | tf_op jit(solution)/shard_map/stack | solution.py:284
  37.6 2.1 %collective-permute-start.8 = (bf16[4,2048,128]{2,1,0:T(8,128)(2,1)}, bf16[4,2048,128]{2,1,0:T(8,128)(2,1)}, u32[]{:S(2)}, u32[]{:S(2)}) collective-permute-start(bf16[4,2048,128]{2,1,0:T(8,128)(2,1)} %pad_maximum_fusion.1.refs_1_), channel_id=1, source_target_pairs={{0,24},{1,97},{2,26},{3,99},{4,28},{5,101},{6,30},{7,103},{8,0},{9... | collective-permute-start | bytes 6291464 | tf_op jit(solution)/shard_map/ppermute | solution.py:43
  39.7 2.8 %collective-permute-start.12 = (f32[32,512]{1,0:T(8,128)S(1)}, f32[32,512]{1,0:T(8,128)S(1)}, u32[]{:S(2)}, u32[]{:S(2)}) collective-permute-start(f32[32,512]{1,0:T(8,128)S(1)} %pad_maximum_fusion.4), channel_id=1, source_target_pairs={{0,1},{1,0},{2,3},{3,2},{4,5},{5,4},{6,7},{7,6},{8,9},{9,8},{10,11... | collective-permute-start | bytes 196616 | tf_op jit(solution)/shard_map/ppermute | solution.py:60
  43.4 1.4 collective-permute-start.13
  44.8 2.7 %collective-permute-start.10 = (bf16[4,2048,128]{2,1,0:T(8,128)(2,1)}, bf16[4,2048,128]{2,1,0:T(8,128)(2,1)}, u32[]{:S(2)}, u32[]{:S(2)}) collective-permute-start(bf16[4,2048,128]{2,1,0:T(8,128)(2,1)} %pad_maximum_fusion.refs_0_), channel_id=1, source_target_pairs={{0,24},{1,97},{2,26},{3,99},{4,28},{5,101},{6,30},{7,103},{8,0},{9... | collective-permute-start | bytes 6291464 | tf_op jit(solution)/shard_map/ppermute | solution.py:43
  51.1 2.6 %collective-permute-start.14 = (f32[32,512]{1,0:T(8,128)}, f32[32,512]{1,0:T(8,128)}, u32[]{:S(2)}, u32[]{:S(2)}) collective-permute-start(f32[32,512]{1,0:T(8,128)} %add.407), channel_id=1, source_target_pairs={{0,4},{1,5},{2,6},{3,7},{4,0},{5,1},{6,2},{7,3},{8,12},{9,13},{10,... | collective-permute-start | bytes 196616 | tf_op jit(solution)/shard_map/ppermute | solution.py:62
  55.0 5.1 %forward.4 = bf16[4,512,256]{2,1,0:T(8,128)(2,1)} custom-call(s32[1]{0:T(128)} %bitcast.1.start_ref, bf16[512,2048]{1,0:T(8,128)(2,1)S(1)} %constant_dynamic-update-slice_fusion.wide_ref, bf16[4,2048,128]{2,1,0:T(8,128)(2,1)} %pad_maximum_fusion.refs_0_, bf16[4,2048,128]{2,1,0:T(8,128)(2,1)} %pad_maximum_fusion.1.refs_1_), custom_call_target="tpu_custom_call" | custom-call | flops 268435456 | bytes 524288 | tf_op jit(solution)/shard_map/forward/pallas_call | solution.py:119
  60.1 3.5 %all-to-all-start = ((bf16[4,512,256]{2,1,0:T(8,128)(2,1)}), bf16[4,512,256]{2,1,0:T(8,128)(2,1)S(1)}, u32[]{:S(2)}, u32[]{:S(2)}) async-start(bf16[4,512,256]{2,1,0:T(8,128)(2,1)} %forward.4), calls=%async_computation | async-start | bytes 2097152 | tf_op jit(solution)/shard_map/all_to_all | solution.py:54
  64.7 2.7 %collective-permute-start.22 = (bf16[4,2048,128]{2,1,0:T(8,128)(2,1)}, bf16[4,2048,128]{2,1,0:T(8,128)(2,1)}, u32[]{:S(2)}, u32[]{:S(2)}) collective-permute-start(bf16[4,2048,128]{2,1,0:T(8,128)(2,1)} %collective-permute-done.8.refs_0_.refs_2_), channel_id=1, source_target_pairs={{0,24},{1,97},{2,26},{3,99},{4,28},{5,101},{6,30},{7,103},{8,0},{9... | collective-permute-start | bytes 6291464 | tf_op jit(solution)/shard_map/ppermute | solution.py:43
  67.3 1.5 fusion.11
  68.8 1.5 fusion.37
  71.0 16.6 %collective-permute-done.9.refs_1_.refs_3_ = bf16[4,2048,128]{2,1,0:T(8,128)(2,1)} collective-permute-done((bf16[4,2048,128]{2,1,0:T(8,128)(2,1)}, bf16[4,2048,128]{2,1,0:T(8,128)(2,1)}, u32[]{:S(2)}, u32[]{:S(2)}) %collective-permute-start.9) | collective-permute-done | bytes 2097184 | tf_op jit(solution)/shard_map/ppermute | solution.py:43
  89.4 6.5 %backward.3.refs_20_ = f32[512,2048]{1,0:T(8,128)} custom-call(s32[8]{0:T(128)S(1)} %stack.153.spots_ref, bf16[4,2048,128]{2,1,0:T(8,128)(2,1)} %pad_maximum_fusion.refs_0_, bf16[4,2048,128]{2,1,0:T(8,128)(2,1)} %pad_maximum_fusion.1.refs_1_, bf16[512,8192]{1,0:T(8,128)(2,1)} %refs_9_.5, bf16[512,8192]{1,0:T(8,128)(2,1)} %refs_9_.5, ...), custom_call_target="tpu_custom_call" | custom-call | flops 268435456 | bytes 524288 | tf_op jit(solution)/shard_map/backward/pallas_call | solution.py:204
  95.9 5.1 %forward.5.refs_2_ = bf16[4,512,512]{2,1,0:T(8,128)(2,1)} custom-call(s32[1]{0:T(128)} %bitcast.1.start_ref, bf16[512,2048]{1,0:T(8,128)(2,1)S(1)} %constant_dynamic-update-slice_fusion.wide_ref, bf16[4,2048,128]{2,1,0:T(8,128)(2,1)} %collective-permute-done.10.refs_0_, bf16[4,2048,128]{2,1,0:T(8,128)(2,1)} %collective-permute-done.11.refs_1_), custom_call_target="tpu_custom_call" | custom-call | flops 268435456 | bytes 524288 | tf_op jit(solution)/shard_map/forward/pallas_call | solution.py:119
  101.0 5.1 %forward.6 = bf16[4,512,512]{2,1,0:T(8,128)(2,1)} custom-call(s32[1]{0:T(128)} %bitcast.1.start_ref, bf16[512,2048]{1,0:T(8,128)(2,1)S(1)} %constant_dynamic-update-slice_fusion.wide_ref, bf16[4,2048,128]{2,1,0:T(8,128)(2,1)} %collective-permute-done.8.refs_0_.refs_2_, ...), custom_call_target="tpu_custom_call", output_to_operand_aliasing={{}: (4, {})} | custom-call | flops 268435456 | bytes 524288 | tf_op jit(solution)/shard_map/forward/pallas_call | solution.py:119
  106.2 6.4 %collective-permute-done.15 = f32[32,1024]{1,0:T(8,128)} collective-permute-done((f32[32,1024]{1,0:T(8,128)}, f32[32,1024]{1,0:T(8,128)}, u32[]{:S(2)}, u32[]{:S(2)}) %collective-permute-start.15) | collective-permute-done | bytes 131104 | tf_op jit(solution)/shard_map/ppermute | solution.py:72
  112.5 2.1 %collective-permute-done.16 = f32[32,1024]{1,0:T(8,128)} collective-permute-done((f32[32,1024]{1,0:T(8,128)}, f32[32,1024]{1,0:T(8,128)}, u32[]{:S(2)}, u32[]{:S(2)}) %collective-permute-start.16) | collective-permute-done | bytes 131104 | tf_op jit(solution)/shard_map/ppermute | solution.py:72
  114.6 4.5 %all-to-all-start.1 = ((bf16[4,512,512]{2,1,0:T(8,128)(2,1)}), bf16[4,512,512]{2,1,0:T(8,128)(2,1)}, u32[]{:S(2)}, u32[]{:S(2)}) async-start(bf16[4,512,512]{2,1,0:T(8,128)(2,1)} %forward.6), calls=%async_computation.1 | async-start | bytes 4194304 | tf_op jit(solution)/shard_map/all_to_all | solution.py:54
  120.8 4.1 %collective-permute-start.19 = (f32[32,1024]{1,0:T(8,128)S(1)}, f32[32,1024]{1,0:T(8,128)S(1)}, u32[]{:S(2)}, u32[]{:S(2)}) collective-permute-start(f32[32,1024]{1,0:T(8,128)S(1)} %add_add_fusion.1), channel_id=1, source_target_pairs={{0,16},{1,17},{2,18},{3,19},{4,20},{5,21},{6,22},{7,23},{8,24},{9,... | collective-permute-start | bytes 393224 | tf_op jit(solution)/shard_map/ppermute | solution.py:72
  124.9 1.8 fusion.35
  126.7 10.3 %backward.4.refs_10_ = f32[512,2048]{1,0:T(8,128)} custom-call(s32[16]{0:T(128)S(1)} %stack.170.spots_ref, bf16[4,2048,128]{2,1,0:T(8,128)(2,1)} %collective-permute-done.10.refs_0_, bf16[4,2048,128]{2,1,0:T(8,128)(2,1)} %collective-permute-done.11.refs_1_, ...), custom_call_target="tpu_custom_call", output_to_operand_aliasing={{}: (21, {})} | custom-call | flops 536870912 | bytes 1048576 | tf_op jit(solution)/shard_map/backward/pallas_call | solution.py:204
  137.1 5.1 %forward.7 = (bf16[512,256]{1,0:T(8,128)(2,1)}, bf16[512,256]{1,0:T(8,128)(2,1)}, bf16[512,256]{1,0:T(8,128)(2,1)}, bf16[512,256]{1,0:T(8,128)(2,1)}) custom-call(s32[1]{0:T(128)} %bitcast.19.start_ref, bf16[512,2048]{1,0:T(8,128)(2,1)S(1)} %constant_dynamic-update-slice_fusion.wide_ref, bf16[4,2048,128]{2,1,0:T(8,128)(2,1)} %collective-permute-done.21.refs_0_, ...), custom_call_target="tpu_custom_call" | custom-call | flops 268435456 | bytes 524288 | tf_op jit(solution)/shard_map/forward/pallas_call | solution.py:119
  142.2 2.8 %collective-permute-start.26 = (bf16[512,256]{1,0:T(8,128)(2,1)}, bf16[512,256]{1,0:T(8,128)(2,1)}, u32[]{:S(2)}, u32[]{:S(2)}) collective-permute-start(bf16[512,256]{1,0:T(8,128)(2,1)} %get-tuple-element.50), channel_id=1, source_target_pairs={{0,6},{1,7},{2,0},{3,1},{4,2},{5,3},{6,4},{7,5},{8,14},{9,15},{10,... | collective-permute-start | bytes 786440 | tf_op jit(solution)/shard_map/ppermute | solution.py:354
  145.0 1.6 collective-permute-start.24
  148.4 2.0 convolution_bitcast_fusion
  151.4 3.8 %arrange.1 = bf16[4,512,256]{2,1,0:T(8,128)(2,1)} custom-call(s32[1]{0:T(128)} %bitcast.far_ref, bf16[4,512,256]{2,1,0:T(8,128)(2,1)S(1)} %all-to-all-done.here_ref, bf16[4,512,512]{2,1,0:T(8,128)(2,1)} %all-to-all-done.1.beside_ref), custom_call_target="tpu_custom_call" | custom-call | flops 2097152 | bytes 4194304 | tf_op jit(solution)/shard_map/arrange/pallas_call | solution.py:163
  155.2 3.7 %all-to-all-start.2 = ((bf16[4,512,256]{2,1,0:T(8,128)(2,1)}), bf16[4,512,256]{2,1,0:T(8,128)(2,1)S(1)}, u32[]{:S(2)}, u32[]{:S(2)}) async-start(bf16[4,512,256]{2,1,0:T(8,128)(2,1)} %arrange.1), calls=%async_computation.2 | async-start | bytes 2097152 | tf_op jit(solution)/shard_map/all_to_all | solution.py:54
  158.9 7.1 %backward.5 = f32[512,2048]{1,0:T(8,128)} custom-call(s32[8]{0:T(128)S(1)} %stack.179.spots_ref, bf16[4,2048,128]{2,1,0:T(8,128)(2,1)} %collective-permute-done.21.refs_0_, bf16[4,2048,128]{2,1,0:T(8,128)(2,1)} %collective-permute-done.22.refs_1_, bf16[512,8192]{1,0:T(8,128)(2,1)} %refs_9_.5, ...), custom_call_target="tpu_custom_call", output_to_operand_aliasing={{}: (11, {})} | custom-call | flops 268435456 | bytes 524288 | tf_op jit(solution)/shard_map/backward/pallas_call | solution.py:204
  166.1 2.8 %slice.133 = bf16[512,1024]{1,0:T(8,128)(2,1)} slice(f32[512,2048]{1,0:T(8,128)} %backward.5), slice={[0:512], [1024:2048]} | slice | bytes 2097152 | tf_op jit(solution)/shard_map/slice | solution.py:368
  171.9 1.7 collective-permute-start.32
  174.4 5.7 %collective-permute-done.32 = f32[256,256]{1,0:T(8,128)S(1)} collective-permute-done((f32[256,256]{1,0:T(8,128)S(1)}, f32[256,256]{1,0:T(8,128)S(1)}, u32[]{:S(2)}, u32[]{:S(2)}) %collective-permute-start.32) | collective-permute-done | bytes 262176 | tf_op jit(solution)/shard_map/ppermute | solution.py:61
  180.8 2.4 %collective-permute-start.33 = (f32[256,256]{1,0:T(8,128)}, f32[256,256]{1,0:T(8,128)}, u32[]{:S(2)}, u32[]{:S(2)}) collective-permute-start(f32[256,256]{1,0:T(8,128)} %add.474), channel_id=1, source_target_pairs={{0,4},{1,5},{2,6},{3,7},{4,0},{5,1},{6,2},{7,3},{8,12},{9,13},{10,... | collective-permute-start | bytes 786440 | tf_op jit(solution)/shard_map/ppermute | solution.py:62
  184.3 1.3 collective-permute-start.23
  185.6 1.3 add_convert_fusion.1
  186.9 2.2 %collective-permute-start.28 = (bf16[512,256]{1,0:T(8,128)(2,1)S(1)}, bf16[512,256]{1,0:T(8,128)(2,1)S(1)}, u32[]{:S(2)}, u32[]{:S(2)}) collective-permute-start(bf16[512,256]{1,0:T(8,128)(2,1)S(1)} %add_convert_fusion.1), channel_id=1, source_target_pairs={{1,4},{5,5},{9,12},{13,13},{17,20},{21,21},{25,28},{29,29},{33,38}... | collective-permute-start | bytes 786440 | tf_op jit(solution)/shard_map/ppermute | solution.py:251
  191.2 1.8 add.475
  193.0 3.4 %fusion.3 = bf16[512,1024]{1,0:T(8,128)(2,1)} fusion(f32[512,2048]{1,0:T(8,128)} %backward.5, f32[512,1024]{1,0:T(8,128)S(1)} %copy-done.2, bf16[512,1024]{1,0:T(8,128)(2,1)} %collective-permute-done.30), kind=kLoop, calls=%fused_computation.5 | loop fusion | flops 2621440 | bytes 6291456 | tf_op jit(solution)/shard_map/convert_element_type | solution.py:373
  198.3 1.4 add_convert_fusion
  (137 shorter events, 27.1 us)
Async XLA Ops:
  0.6 11.4 %copy-start = (f32[256,256]{1,0:T(8,128)S(1)}, f32[256,256]{1,0:T(8,128)}, u32[]{:S(2)}) copy-start(f32[256,256]{1,0:T(8,128)} %param.10) | copy-start | bytes 786436
  2.0 3.0 %collective-permute-start.1 = (bf16[1024,256]{1,0:T(8,128)(2,1)S(1)}, bf16[1024,256]{1,0:T(8,128)(2,1)S(1)}, u32[]{:S(2)}, u32[]{:S(2)}) collective-permute-start(bf16[1024,256]{1,0:T(8,128)(2,1)S(1)} %get-tuple-element.60), channel_id=1, source_target_pairs={{0,1},{1,0},{2,3},{3,2},{4,5},{5,4},{6,7},{7,6},{8,9},{9,8},{10,11... | collective-permute-start | bytes 1572872 | tf_op jit(solution)/shard_map/ppermute | solution.py:278
  3.5 8.4 %copy-start.18 = (s32[16,4,2]{0,2,1:T(2,128)S(1)}, s32[16,4,2]{0,2,1:T(2,128)}, u32[]{:S(2)}) copy-start(s32[16,4,2]{0,2,1:T(2,128)} %param.14) | copy-start | bytes 1540
  3.5 8.8 %copy-start.17 = (s32[16,4,2]{0,2,1:T(2,128)S(1)}, s32[16,4,2]{0,2,1:T(2,128)}, u32[]{:S(2)}) copy-start(s32[16,4,2]{0,2,1:T(2,128)} %param.12) | copy-start | bytes 1540
  3.5 20.9 %copy-start.1 = (bf16[512,1024]{1,0:T(8,128)(2,1)S(1)}, bf16[512,1024]{1,0:T(8,128)(2,1)}, u32[]{:S(2)}) copy-start(bf16[512,1024]{1,0:T(8,128)(2,1)} %param.8) | copy-start | bytes 3145732
  5.1 19.6 %collective-permute-start.3 = (bf16[2048,128]{1,0:T(8,128)(2,1)S(1)}, bf16[2048,128]{1,0:T(8,128)(2,1)S(1)}, u32[]{:S(2)}, u32[]{:S(2)}) collective-permute-start(bf16[2048,128]{1,0:T(8,128)(2,1)S(1)} %get-tuple-element.31), channel_id=1, source_target_pairs={{0,32},{1,9},{2,34},{3,11},{4,36},{5,13},{6,38},{7,15},{8,40},{9,1... | collective-permute-start | bytes 1572872 | tf_op jit(solution)/shard_map/ppermute | solution.py:43
  6.9 26.7 %collective-permute-start.2 = (bf16[2048,128]{1,0:T(8,128)(2,1)S(1)}, bf16[2048,128]{1,0:T(8,128)(2,1)}, u32[]{:S(2)}, u32[]{:S(2)}) collective-permute-start(bf16[2048,128]{1,0:T(8,128)(2,1)S(1)} %get-tuple-element.31), channel_id=1, source_target_pairs={{0,96},{1,25},{2,98},{3,27},{4,100},{5,29},{6,102},{7,31},{8,104},... | collective-permute-start | bytes 1572872 | tf_op jit(solution)/shard_map/ppermute | solution.py:43
  9.1 17.3 %collective-permute-start.7 = (bf16[2048,128]{1,0:T(8,128)(2,1)S(1)}, bf16[2048,128]{1,0:T(8,128)(2,1)}, u32[]{:S(2)}, u32[]{:S(2)}) collective-permute-start(bf16[2048,128]{1,0:T(8,128)(2,1)S(1)} %get-tuple-element.32), channel_id=1, source_target_pairs={{0,32},{1,9},{2,34},{3,11},{4,36},{5,13},{6,38},{7,15},{8,40},{9,1... | collective-permute-start | bytes 1572872 | tf_op jit(solution)/shard_map/ppermute | solution.py:43
  9.1 12.0 %collective-permute-start.5 = (bf16[2048,128]{1,0:T(8,128)(2,1)S(1)}, bf16[2048,128]{1,0:T(8,128)(2,1)}, u32[]{:S(2)}, u32[]{:S(2)}) collective-permute-start(bf16[2048,128]{1,0:T(8,128)(2,1)S(1)} %get-tuple-element.32), channel_id=1, source_target_pairs={{0,96},{1,25},{2,98},{3,27},{4,100},{5,29},{6,102},{7,31},{8,104},... | collective-permute-start | bytes 1572872 | tf_op jit(solution)/shard_map/ppermute | solution.py:43
  11.9 21.8 %copy-start.19 = (f32[16,4,2]{0,2,1:T(2,128)}, f32[16,4,2]{0,2,1:T(2,128)S(1)}, u32[]{:S(2)}) copy-start(f32[16,4,2]{0,2,1:T(2,128)S(1)} %add_divide_fusion) | copy-start | bytes 1540
  11.9 21.7 %copy-start.21 = (f32[16,4,2]{0,2,1:T(2,128)}, f32[16,4,2]{0,2,1:T(2,128)S(1)}, u32[]{:S(2)}) copy-start(f32[16,4,2]{0,2,1:T(2,128)S(1)} %add_divide_fusion.1) | copy-start | bytes 1540
  12.1 21.6 %copy-start.4 = (f32[16,4,256]{2,0,1:T(8,128)}, f32[16,4,256]{2,0,1:T(8,128)S(1)}, u32[]{:S(2)}) copy-start(f32[16,4,256]{2,0,1:T(8,128)S(1)} %select_reduce_fusion.2) | copy-start | bytes 196612
  12.3 12.4 %copy-start.13 = (bf16[4,2,8,256]{3,2,0,1:T(8,128)(2,1)}, bf16[4,2,8,256]{3,2,0,1:T(8,128)(2,1)S(1)}, u32[]{:S(2)}) copy-start(bf16[4,2,8,256]{3,2,0,1:T(8,128)(2,1)S(1)} %copy.47) | copy-start | bytes 98308
  21.1 9.7 %collective-permute-start.6 = (bf16[2048,128]{1,0:T(8,128)(2,1)}, bf16[2048,128]{1,0:T(8,128)(2,1)S(1)}, u32[]{:S(2)}, u32[]{:S(2)}) collective-permute-start(bf16[2048,128]{1,0:T(8,128)(2,1)} %collective-permute-done.5), channel_id=1, source_target_pairs={{0,96},{1,25},{2,98},{3,27},{4,100},{5,29},{6,102},{7,31},{8,104},... | collective-permute-start | bytes 1572872 | tf_op jit(solution)/shard_map/ppermute | solution.py:43
  24.8 9.6 %collective-permute-start.4 = (bf16[2048,128]{1,0:T(8,128)(2,1)S(1)}, bf16[2048,128]{1,0:T(8,128)(2,1)S(1)}, u32[]{:S(2)}, u32[]{:S(2)}) collective-permute-start(bf16[2048,128]{1,0:T(8,128)(2,1)S(1)} %collective-permute-done.3), channel_id=1, source_target_pairs={{0,32},{1,9},{2,34},{3,11},{4,36},{5,13},{6,38},{7,15},{8,40},{9,1... | collective-permute-start | bytes 1572872 | tf_op jit(solution)/shard_map/ppermute | solution.py:43
  37.0 27.6 %collective-permute-start.11 = (bf16[4,2048,128]{2,1,0:T(8,128)(2,1)}, bf16[4,2048,128]{2,1,0:T(8,128)(2,1)}, u32[]{:S(2)}, u32[]{:S(2)}) collective-permute-start(bf16[4,2048,128]{2,1,0:T(8,128)(2,1)} %pad_maximum_fusion.refs_0_), channel_id=1, source_target_pairs={{0,8},{1,33},{2,10},{3,35},{4,12},{5,37},{6,14},{7,39},{8,16},{9,4... | collective-permute-start | bytes 6291464 | tf_op jit(solution)/shard_map/ppermute | solution.py:43
  37.6 27.1 %collective-permute-start.8 = (bf16[4,2048,128]{2,1,0:T(8,128)(2,1)}, bf16[4,2048,128]{2,1,0:T(8,128)(2,1)}, u32[]{:S(2)}, u32[]{:S(2)}) collective-permute-start(bf16[4,2048,128]{2,1,0:T(8,128)(2,1)} %pad_maximum_fusion.1.refs_1_), channel_id=1, source_target_pairs={{0,24},{1,97},{2,26},{3,99},{4,28},{5,101},{6,30},{7,103},{8,0},{9... | collective-permute-start | bytes 6291464 | tf_op jit(solution)/shard_map/ppermute | solution.py:43
  39.7 3.7 %collective-permute-start.12 = (f32[32,512]{1,0:T(8,128)S(1)}, f32[32,512]{1,0:T(8,128)S(1)}, u32[]{:S(2)}, u32[]{:S(2)}) collective-permute-start(f32[32,512]{1,0:T(8,128)S(1)} %pad_maximum_fusion.4), channel_id=1, source_target_pairs={{0,1},{1,0},{2,3},{3,2},{4,5},{5,4},{6,7},{7,6},{8,9},{9,8},{10,11... | collective-permute-start | bytes 196616 | tf_op jit(solution)/shard_map/ppermute | solution.py:60
  43.4 4.1 %collective-permute-start.13 = (f32[32,512]{1,0:T(8,128)S(1)}, f32[32,512]{1,0:T(8,128)S(1)}, u32[]{:S(2)}, u32[]{:S(2)}) collective-permute-start(f32[32,512]{1,0:T(8,128)S(1)} %add.406), channel_id=1, source_target_pairs={{0,2},{1,3},{2,0},{3,1},{4,6},{5,7},{6,4},{7,5},{8,10},{9,11},{10,... | collective-permute-start | bytes 196616 | tf_op jit(solution)/shard_map/ppermute | solution.py:61
  44.8 42.8 %collective-permute-start.9 = (bf16[4,2048,128]{2,1,0:T(8,128)(2,1)}, bf16[4,2048,128]{2,1,0:T(8,128)(2,1)}, u32[]{:S(2)}, u32[]{:S(2)}) collective-permute-start(bf16[4,2048,128]{2,1,0:T(8,128)(2,1)} %pad_maximum_fusion.1.refs_1_), channel_id=1, source_target_pairs={{0,8},{1,33},{2,10},{3,35},{4,12},{5,37},{6,14},{7,39},{8,16},{9,4... | collective-permute-start | bytes 6291464 | tf_op jit(solution)/shard_map/ppermute | solution.py:43
  44.8 43.7 %collective-permute-start.10 = (bf16[4,2048,128]{2,1,0:T(8,128)(2,1)}, bf16[4,2048,128]{2,1,0:T(8,128)(2,1)}, u32[]{:S(2)}, u32[]{:S(2)}) collective-permute-start(bf16[4,2048,128]{2,1,0:T(8,128)(2,1)} %pad_maximum_fusion.refs_0_), channel_id=1, source_target_pairs={{0,24},{1,97},{2,26},{3,99},{4,28},{5,101},{6,30},{7,103},{8,0},{9... | collective-permute-start | bytes 6291464 | tf_op jit(solution)/shard_map/ppermute | solution.py:43
  47.5 3.6 %collective-permute-start = (bf16[512,1024]{1,0:T(8,128)(2,1)S(1)}, bf16[512,1024]{1,0:T(8,128)(2,1)}, u32[]{:S(2)}, u32[]{:S(2)}) collective-permute-start(bf16[512,1024]{1,0:T(8,128)(2,1)S(1)} %copy-done.1), channel_id=1, source_target_pairs={{0,1},{1,0},{2,3},{3,2},{4,5},{5,4},{6,7},{7,6},{8,9},{9,8},{10,11... | collective-permute-start | bytes 3145736 | tf_op jit(solution)/shard_map/ppermute | solution.py:298
  51.1 12.6 %collective-permute-start.14 = (f32[32,512]{1,0:T(8,128)}, f32[32,512]{1,0:T(8,128)}, u32[]{:S(2)}, u32[]{:S(2)}) collective-permute-start(f32[32,512]{1,0:T(8,128)} %add.407), channel_id=1, source_target_pairs={{0,4},{1,5},{2,6},{3,7},{4,0},{5,1},{6,2},{7,3},{8,12},{9,13},{10,... | collective-permute-start | bytes 196616 | tf_op jit(solution)/shard_map/ppermute | solution.py:62
  60.1 54.5 %all-to-all-start = ((bf16[4,512,256]{2,1,0:T(8,128)(2,1)}), bf16[4,512,256]{2,1,0:T(8,128)(2,1)S(1)}, u32[]{:S(2)}, u32[]{:S(2)}) async-start(bf16[4,512,256]{2,1,0:T(8,128)(2,1)} %forward.4), calls=%async_computation | async-start | bytes 2097152 | tf_op jit(solution)/shard_map/all_to_all | solution.py:54
  64.6 60.4 %copy-start.9 = (bf16[32,512]{1,0:T(8,128)(2,1)}, bf16[32,512]{1,0:T(8,128)(2,1)S(1)}, u32[]{:S(2)}) copy-start(bf16[32,512]{1,0:T(8,128)(2,1)S(1)} %add_convert_fusion.2) | copy-start | bytes 98308
  64.6 72.5 %collective-permute-start.21 = (bf16[4,2048,128]{2,1,0:T(8,128)(2,1)}, bf16[4,2048,128]{2,1,0:T(8,128)(2,1)}, u32[]{:S(2)}, u32[]{:S(2)}) collective-permute-start(bf16[4,2048,128]{2,1,0:T(8,128)(2,1)} %collective-permute-done.11.refs_1_), channel_id=1, source_target_pairs={{0,8},{1,33},{2,10},{3,35},{4,12},{5,37},{6,14},{7,39},{8,16},{9,4... | collective-permute-start | bytes 6291464 | tf_op jit(solution)/shard_map/ppermute | solution.py:43
  64.7 72.4 %collective-permute-start.22 = (bf16[4,2048,128]{2,1,0:T(8,128)(2,1)}, bf16[4,2048,128]{2,1,0:T(8,128)(2,1)}, u32[]{:S(2)}, u32[]{:S(2)}) collective-permute-start(bf16[4,2048,128]{2,1,0:T(8,128)(2,1)} %collective-permute-done.8.refs_0_.refs_2_), channel_id=1, source_target_pairs={{0,24},{1,97},{2,26},{3,99},{4,28},{5,101},{6,30},{7,103},{8,0},{9... | collective-permute-start | bytes 6291464 | tf_op jit(solution)/shard_map/ppermute | solution.py:43
  70.9 41.6 %collective-permute-start.15 = (f32[32,1024]{1,0:T(8,128)}, f32[32,1024]{1,0:T(8,128)}, u32[]{:S(2)}, u32[]{:S(2)}) collective-permute-start(f32[32,1024]{1,0:T(8,128)} %maximum_multiply_fusion), channel_id=1, source_target_pairs={{0,32},{1,33},{2,34},{3,35},{4,36},{5,37},{6,38},{7,39},{8,40},{9,... | collective-permute-start | bytes 393224 | tf_op jit(solution)/shard_map/ppermute | solution.py:72
  87.6 27.1 %collective-permute-start.16 = (f32[32,1024]{1,0:T(8,128)}, f32[32,1024]{1,0:T(8,128)}, u32[]{:S(2)}, u32[]{:S(2)}) collective-permute-start(f32[32,1024]{1,0:T(8,128)} %maximum_multiply_fusion), channel_id=1, source_target_pairs={{0,64},{1,65},{2,66},{3,67},{4,68},{5,69},{6,70},{7,71},{8,72},{9,... | collective-permute-start | bytes 393224 | tf_op jit(solution)/shard_map/ppermute | solution.py:72
  88.5 26.1 %collective-permute-start.17 = (f32[32,1024]{1,0:T(8,128)}, f32[32,1024]{1,0:T(8,128)}, u32[]{:S(2)}, u32[]{:S(2)}) collective-permute-start(f32[32,1024]{1,0:T(8,128)} %maximum_multiply_fusion), channel_id=1, source_target_pairs={{0,96},{1,97},{2,98},{3,99},{4,100},{5,101},{6,102},{7,103},{8,104... | collective-permute-start | bytes 393224 | tf_op jit(solution)/shard_map/ppermute | solution.py:72
  114.6 32.6 %all-to-all-start.1 = ((bf16[4,512,512]{2,1,0:T(8,128)(2,1)}), bf16[4,512,512]{2,1,0:T(8,128)(2,1)}, u32[]{:S(2)}, u32[]{:S(2)}) async-start(bf16[4,512,512]{2,1,0:T(8,128)(2,1)} %forward.6), calls=%async_computation.1 | async-start | bytes 4194304 | tf_op jit(solution)/shard_map/all_to_all | solution.py:54
  120.7 16.4 %copy-start.5 = (f32[32,1024]{1,0:T(8,128)}, f32[32,1024]{1,0:T(8,128)S(1)}, u32[]{:S(2)}) copy-start(f32[32,1024]{1,0:T(8,128)S(1)} %add_add_fusion.1) | copy-start | bytes 393220
  120.7 24.3 %collective-permute-start.18 = (f32[32,1024]{1,0:T(8,128)S(1)}, f32[32,1024]{1,0:T(8,128)S(1)}, u32[]{:S(2)}, u32[]{:S(2)}) collective-permute-start(f32[32,1024]{1,0:T(8,128)S(1)} %add_add_fusion.1), channel_id=1, source_target_pairs={{0,8},{1,9},{2,10},{3,11},{4,12},{5,13},{6,14},{7,15},{8,16},{9,17... | collective-permute-start | bytes 393224 | tf_op jit(solution)/shard_map/ppermute | solution.py:72
  120.8 25.8 %collective-permute-start.19 = (f32[32,1024]{1,0:T(8,128)S(1)}, f32[32,1024]{1,0:T(8,128)S(1)}, u32[]{:S(2)}, u32[]{:S(2)}) collective-permute-start(f32[32,1024]{1,0:T(8,128)S(1)} %add_add_fusion.1), channel_id=1, source_target_pairs={{0,16},{1,17},{2,18},{3,19},{4,20},{5,21},{6,22},{7,23},{8,24},{9,... | collective-permute-start | bytes 393224 | tf_op jit(solution)/shard_map/ppermute | solution.py:72
  124.9 22.4 %collective-permute-start.20 = (f32[32,1024]{1,0:T(8,128)S(1)}, f32[32,1024]{1,0:T(8,128)}, u32[]{:S(2)}, u32[]{:S(2)}) collective-permute-start(f32[32,1024]{1,0:T(8,128)S(1)} %add_add_fusion.1), channel_id=1, source_target_pairs={{0,24},{1,25},{2,26},{3,27},{4,28},{5,29},{6,30},{7,31},{8,0},{9,1... | collective-permute-start | bytes 393224 | tf_op jit(solution)/shard_map/ppermute | solution.py:72
  142.2 42.1 %collective-permute-start.26 = (bf16[512,256]{1,0:T(8,128)(2,1)}, bf16[512,256]{1,0:T(8,128)(2,1)}, u32[]{:S(2)}, u32[]{:S(2)}) collective-permute-start(bf16[512,256]{1,0:T(8,128)(2,1)} %get-tuple-element.50), channel_id=1, source_target_pairs={{0,6},{1,7},{2,0},{3,1},{4,2},{5,3},{6,4},{7,5},{8,14},{9,15},{10,... | collective-permute-start | bytes 786440 | tf_op jit(solution)/shard_map/ppermute | solution.py:354
  145.0 40.7 %collective-permute-start.25 = (bf16[512,256]{1,0:T(8,128)(2,1)}, bf16[512,256]{1,0:T(8,128)(2,1)}, u32[]{:S(2)}, u32[]{:S(2)}) collective-permute-start(bf16[512,256]{1,0:T(8,128)(2,1)} %get-tuple-element.48), channel_id=1, source_target_pairs={{0,2},{1,3},{2,4},{3,5},{4,6},{5,7},{6,0},{7,1},{8,10},{9,11},{10,... | collective-permute-start | bytes 786440 | tf_op jit(solution)/shard_map/ppermute | solution.py:354
  145.0 40.7 %collective-permute-start.24 = (bf16[512,256]{1,0:T(8,128)(2,1)}, bf16[512,256]{1,0:T(8,128)(2,1)}, u32[]{:S(2)}, u32[]{:S(2)}) collective-permute-start(bf16[512,256]{1,0:T(8,128)(2,1)} %get-tuple-element.49), channel_id=1, source_target_pairs={{0,4},{1,5},{2,6},{3,7},{4,0},{5,1},{6,2},{7,3},{8,12},{9,13},{10,... | collective-permute-start | bytes 786440 | tf_op jit(solution)/shard_map/ppermute | solution.py:354
  155.2 28.0 %all-to-all-start.2 = ((bf16[4,512,256]{2,1,0:T(8,128)(2,1)}), bf16[4,512,256]{2,1,0:T(8,128)(2,1)S(1)}, u32[]{:S(2)}, u32[]{:S(2)}) async-start(bf16[4,512,256]{2,1,0:T(8,128)(2,1)} %arrange.1), calls=%async_computation.2 | async-start | bytes 2097152 | tf_op jit(solution)/shard_map/all_to_all | solution.py:54
  168.8 24.1 %collective-permute-start.30 = (bf16[512,1024]{1,0:T(8,128)(2,1)}, bf16[512,1024]{1,0:T(8,128)(2,1)}, u32[]{:S(2)}, u32[]{:S(2)}) collective-permute-start(bf16[512,1024]{1,0:T(8,128)(2,1)} %slice.133), channel_id=1, source_target_pairs={{0,1},{1,0},{2,3},{3,2},{4,5},{5,4},{6,7},{7,6},{8,9},{9,8},{10,11... | collective-permute-start | bytes 3145736 | tf_op jit(solution)/shard_map/ppermute | solution.py:368
  169.6 2.2 %collective-permute-start.31 = (f32[256,256]{1,0:T(8,128)S(1)}, f32[256,256]{1,0:T(8,128)S(1)}, u32[]{:S(2)}, u32[]{:S(2)}) collective-permute-start(f32[256,256]{1,0:T(8,128)S(1)} %fusion.4), channel_id=1, source_target_pairs={{0,1},{1,0},{2,3},{3,2},{4,5},{5,4},{6,7},{7,6},{8,9},{9,8},{10,11... | collective-permute-start | bytes 786440 | tf_op jit(solution)/shard_map/ppermute | solution.py:60
  171.9 8.2 %collective-permute-start.32 = (f32[256,256]{1,0:T(8,128)S(1)}, f32[256,256]{1,0:T(8,128)S(1)}, u32[]{:S(2)}, u32[]{:S(2)}) collective-permute-start(f32[256,256]{1,0:T(8,128)S(1)} %add.473), channel_id=1, source_target_pairs={{0,2},{1,3},{2,0},{3,1},{4,6},{5,7},{6,4},{7,5},{8,10},{9,11},{10,... | collective-permute-start | bytes 786440 | tf_op jit(solution)/shard_map/ppermute | solution.py:61
  174.4 18.6 %copy-start.2 = (f32[512,1024]{1,0:T(8,128)S(1)}, f32[512,1024]{1,0:T(8,128)}, u32[]{:S(2)}) copy-start(f32[512,1024]{1,0:T(8,128)} %fusion.35) | copy-start | bytes 6291460
  180.8 9.1 %collective-permute-start.33 = (f32[256,256]{1,0:T(8,128)}, f32[256,256]{1,0:T(8,128)}, u32[]{:S(2)}, u32[]{:S(2)}) collective-permute-start(f32[256,256]{1,0:T(8,128)} %add.474), channel_id=1, source_target_pairs={{0,4},{1,5},{2,6},{3,7},{4,0},{5,1},{6,2},{7,3},{8,12},{9,13},{10,... | collective-permute-start | bytes 786440 | tf_op jit(solution)/shard_map/ppermute | solution.py:62
  184.3 12.1 %collective-permute-start.23 = (bf16[2,512,256]{2,1,0:T(8,128)(2,1)S(1)}, bf16[2,512,256]{2,1,0:T(8,128)(2,1)S(1)}, u32[]{:S(2)}, u32[]{:S(2)}) collective-permute-start(bf16[2,512,256]{2,1,0:T(8,128)(2,1)S(1)} %slice_select_fusion.1), channel_id=1, source_target_pairs={{0,1},{1,0},{2,3},{3,2},{4,5},{5,4},{6,7},{7,6},{8,9},{9,8},{10,11... | collective-permute-start | bytes 1572872 | tf_op jit(solution)/shard_map/ppermute | solution.py:347
  186.9 10.6 %collective-permute-start.28 = (bf16[512,256]{1,0:T(8,128)(2,1)S(1)}, bf16[512,256]{1,0:T(8,128)(2,1)S(1)}, u32[]{:S(2)}, u32[]{:S(2)}) collective-permute-start(bf16[512,256]{1,0:T(8,128)(2,1)S(1)} %add_convert_fusion.1), channel_id=1, source_target_pairs={{1,4},{5,5},{9,12},{13,13},{17,20},{21,21},{25,28},{29,29},{33,38}... | collective-permute-start | bytes 786440 | tf_op jit(solution)/shard_map/ppermute | solution.py:251
  189.2 8.4 %collective-permute-start.29 = (bf16[512,256]{1,0:T(8,128)(2,1)S(1)}, bf16[512,256]{1,0:T(8,128)(2,1)S(1)}, u32[]{:S(2)}, u32[]{:S(2)}) collective-permute-start(bf16[512,256]{1,0:T(8,128)(2,1)S(1)} %add_convert_fusion.1), channel_id=1, source_target_pairs={{3,4},{7,5},{11,12},{15,13},{19,20},{23,21},{27,28},{31,29},{35,38... | collective-permute-start | bytes 786440 | tf_op jit(solution)/shard_map/ppermute | solution.py:251
  189.9 7.8 %collective-permute-start.27 = (bf16[512,256]{1,0:T(8,128)(2,1)S(1)}, bf16[512,256]{1,0:T(8,128)(2,1)S(1)}, u32[]{:S(2)}, u32[]{:S(2)}) collective-permute-start(bf16[512,256]{1,0:T(8,128)(2,1)S(1)} %add_convert_fusion.1), channel_id=1, source_target_pairs={{0,1},{2,3},{4,5},{6,7},{8,9},{10,11},{12,13},{14,15},{32,33},{34,... | collective-permute-start | bytes 786440 | tf_op jit(solution)/shard_map/ppermute | solution.py:256
  (14 other events, 51.5 us)

commit v3 on v2

--- a/solution.py
+++ b/solution.py
@@ -62,45 +62,44 @@
     return value + lax.ppermute(value, "tensor", [(t, t ^ 4) for t in range(8)])
 
 
-def over_side(value, axis):
-    def from_step(step):
-        def move(x, z, y, c):
-            if axis == 0:
-                return ((x + step) % SIDE, z, y, c)
-            return (x, (z + step) % SIDE, y, c)
-
-        return lax.ppermute(value, BOTH, pairs(move))
-
-    return [value, from_step(1), from_step(2), from_step(3)]
+def after(value, *events):
+    return lax.optimization_barrier((value, *events))[0]
+
+
+def with_partner(value, bit, *events):
+    other = lax.ppermute(value, "dp", [(d, d ^ bit) for d in range(16)])
+    return value + after(other, *events)
 
 
 def total_of(parts):
     return (parts[0] + parts[2]) + (parts[1] + parts[3])
 
 
-def after(value, *events):
-    return lax.optimization_barrier((value, *events))[0]
-
-
-def forward_kernel(count, start_ref, wide_ref, *refs):
-    lines, outs, held, sems = refs[:count], refs[-6:-2], refs[-2], refs[-1]
-    outs = refs[-3:-2] if len(refs) < count + 6 else outs
+def forward_kernel(count, many, start_ref, wide_ref, *refs):
+    lines, outs, held, sems = refs[:count], refs[-2 - many : -2], refs[-2], refs[-1]
     copies = [pltpu.make_async_copy(lines[m], held.at[m], sems.at[m]) for m in range(count)]
-    for copy in copies:
-        copy.start()
     part = held.shape[3]
     order = [lax.rem(start_ref[0] + k, SIDE) for k in range(SIDE)]
+
+    @pl.when(pl.program_id(0) == 0)
+    def _():
+        for copy in copies:
+            copy.start()
+
     for m in range(count):
-        copies[m].wait()
-        weights = jnp.concatenate([held[m, k] for k in order], axis=1)
-        product = jnp.dot(wide_ref[...], weights, preferred_element_type=jnp.float32)
-        product = product.astype(jnp.bfloat16)
-        for k in range(SIDE):
-            piece = product[:, k * part : (k + 1) * part]
-            if len(outs) == 1:
-                outs[0][k, :, m * part : (m + 1) * part] = piece
-            else:
-                outs[k][:, m * part : (m + 1) * part] = piece
+
+        @pl.when(pl.program_id(0) == m)
+        def _():
+            copies[m].wait()
+            weights = jnp.concatenate([held[m, k] for k in order], axis=1)
+            product = jnp.dot(wide_ref[...], weights, preferred_element_type=jnp.float32)
+            product = product.astype(jnp.bfloat16)
+            for k in range(SIDE):
+                piece = product[:, k * part : (k + 1) * part]
+                if many == 1:
+                    outs[0][k] = piece
+                else:
+                    outs[k][...] = piece
 
 
 def forward(start, wide, lines, apart=False, places=1, into=None):
@@ -108,21 +107,22 @@
     part = lines[0].shape[2]
     count = len(lines)
     cols = count * part
+    many = SIDE if apart else 1
     if apart:
         outs = [pltpu.HBM((tokens, cols), jnp.bfloat16)] * SIDE
-        specs = [pl.BlockSpec((tokens, cols), lambda i, n: (0, 0))] * SIDE
+        specs = [pl.BlockSpec((tokens, part), lambda i, n: (0, i))] * SIDE
     else:
-        place = 0 if into is None else 1
-        outs = pltpu.HBM((SIDE, tokens, places * cols), jnp.bfloat16)
-        specs = pl.BlockSpec((SIDE, tokens, cols), lambda i, n: (0, 0, place))
+        place = 0 if into is None else count
+        outs = [pltpu.HBM((SIDE, tokens, places * cols), jnp.bfloat16)]
+        specs = [pl.BlockSpec((SIDE, tokens, part), lambda i, n: (0, 0, place + i))]
     extra = [] if into is None else [into]
-    return pl.pallas_call(
-        functools.partial(forward_kernel, count),
+    made = pl.pallas_call(
+        functools.partial(forward_kernel, count, many),
         out_shape=outs,
         grid_spec=pltpu.PrefetchScalarGridSpec(
             num_scalar_prefetch=1,
-            grid=(1,),
-            in_specs=[pl.BlockSpec((tokens, depth), lambda i, n: (0, 0))]
+            grid=(count,),
+            in_specs=[pl.BlockSpec(memory_space=pltpu.VMEM)]
             + [pl.BlockSpec(memory_space=pl.ANY)] * (count + len(extra)),
             out_specs=specs,
             scratch_shapes=[
@@ -131,7 +131,7 @@
             ],
         ),
         input_output_aliases={} if into is None else {count + 2: 0},
-        compiler_params=pltpu.CompilerParams(vmem_limit_bytes=28 << 20),
+        compiler_params=pltpu.CompilerParams(vmem_limit_bytes=24 << 20),
         cost_estimate=pl.CostEstimate(
             flops=tokens * depth * count * part,
             bytes_accessed=depth * part * count,
@@ -139,6 +139,7 @@
         ),
         name="forward",
     )(start, wide, *lines, *extra)
+    return made if apart else made[0]
 
 
 def arrange_kernel(far_ref, here_ref, beside_ref, out_ref):
@@ -180,47 +181,72 @@
     )(far, here, beside)
 
 
-def backward_kernel(count, first, spots_ref, *refs):
+def backward_kernel(count, first, last, spots_ref, *refs):
     lines, grads = refs[:count], refs[count : count * 5]
     weights = jnp.concatenate([line[k] for line in lines for k in range(SIDE)], axis=1)
     cols = jnp.concatenate([g[...] for g in grads], axis=1)
     product = lax.dot_general(
         cols, weights, (((1,), (1,)), ((), ())), preferred_element_type=jnp.float32
     )
-    refs[-1][...] = product if first else refs[-2][...] + product
-
-
-def backward(spots, grown, out_grad, lines):
+    if first:
+        refs[-1][...] = product
+    elif not last:
+        refs[-1][...] = refs[-2][...] + product
+    else:
+        total = refs[-3][...] + product
+
+        @pl.when(pl.program_id(0) < 2)
+        def _():
+            refs[-1][...] = total.astype(jnp.bfloat16)
+
+        @pl.when(pl.program_id(0) >= 2)
+        def _():
+            refs[-2][...] = total
+
+
+def backward(spots, grown, out_grad, lines, last=False):
     tokens = out_grad.shape[0]
     depth, part = lines[0].shape[1:]
     count = len(lines)
-    block = depth // 2
+    block = depth // 4
     first = grown is None
+    out_grad = pltpu.with_memory_space_constraint(out_grad, pltpu.HBM)
 
     def column(j):
         return pl.BlockSpec((tokens, part), lambda i, n: (0, n[j]))
 
-    total = pl.BlockSpec((tokens, block), lambda i, n: (0, i))
-    return pl.pallas_call(
-        functools.partial(backward_kernel, count, first),
-        out_shape=pltpu.HBM((tokens, depth), jnp.float32),
+    total = pl.BlockSpec((tokens, block), lambda i, n: (0, (i + 2) % 4))
+    outs, specs = [pltpu.HBM((tokens, depth), jnp.float32)], [total]
+    if last:
+        outs = [
+            jax.ShapeDtypeStruct((tokens, depth // 2), jnp.float32),
+            jax.ShapeDtypeStruct((tokens, depth // 2), jnp.bfloat16),
+        ]
+        specs = [
+            pl.BlockSpec((tokens, block), lambda i, n: (0, jnp.maximum(i - 2, 0))),
+            pl.BlockSpec((tokens, block), lambda i, n: (0, jnp.minimum(i, 1))),
+        ]
+    made = pl.pallas_call(
+        functools.partial(backward_kernel, count, first, last),
+        out_shape=outs,
         grid_spec=pltpu.PrefetchScalarGridSpec(
             num_scalar_prefetch=1,
-            grid=(2,),
-            in_specs=[pl.BlockSpec((SIDE, block, part), lambda i, n: (0, i, 0))] * count
+            grid=(4,),
+            in_specs=[pl.BlockSpec((SIDE, block, part), lambda i, n: (0, (i + 2) % 4, 0))] * count
             + [column(j) for j in range(count * SIDE)]
             + ([] if first else [total]),
-            out_specs=total,
-        ),
-        input_output_aliases={} if first else {5 * count + 1: 0},
-        compiler_params=pltpu.CompilerParams(vmem_limit_bytes=36 << 20),
+            out_specs=specs,
+        ),
+        input_output_aliases={} if first or last else {5 * count + 1: 0},
+        compiler_params=pltpu.CompilerParams(vmem_limit_bytes=28 << 20),
         cost_estimate=pl.CostEstimate(
             flops=tokens * depth * count * part,
             bytes_accessed=depth * part * count,
             transcendentals=0,
         ),
         name="backward",
-    )(spots, *lines, *([pltpu.with_memory_space_constraint(out_grad, pltpu.HBM)] * (count * SIDE)), *([] if first else [grown]))
+    )(spots, *lines, *([out_grad] * (count * SIDE)), *([] if first else [pltpu.with_memory_space_constraint(grown, pltpu.HBM)]))
+    return made if last else made[0]
 
 
 def compose(logits, indices, vector_bank):
@@ -281,7 +307,10 @@
         cols = slice(h * part, (h + 1) * part)
         shards.append(jnp.concatenate([mine[:, cols], swapped[:, cols]], axis=0))
     logits_a, logits_b, *shards = lax.optimization_barrier((logits_a, logits_b, *shards))
-    lines = [jnp.stack(ring_gather(shards[h], 0, h)) for h in range(2)]
+    lines = [ring_gather(shards[h], 0, h) for h in range(2)]
+    lines[0] = jnp.stack(lines[0])
+    lines[0], *lines[1] = lax.optimization_barrier((lines[0], *lines[1]))
+    lines[1] = jnp.stack(lines[1])
     def columns(i, h):
         far_at = (far + i) % SIDE
         spots = []
@@ -316,7 +345,7 @@
     grad_a = jnp.dot(back_bf, attn_out, preferred_element_type=f32)
     grad_b = jnp.dot(low_bf, grad_cols, preferred_element_type=f32)
     both = factor * jnp.concatenate([grad_a, grad_b], axis=0)
-    both_parts = over_side(both, 0)
+    both = with_partner(both, 1)
 
     here = [(0, 0), (0, 1)]
     beside = [(1, 0), (3, 0), (1, 1), (3, 1)]
@@ -329,21 +358,22 @@
     slots_here = exchange(sent_here, "tensor", LANES)
     grown = backward(after(spots_of(here), sent_here), None, out_grad, take(here))
     sent_beside = forward(after(turned, grown), wide, take(beside[:2]), places=2)
-    sent_beside = forward(turned, wide, take(beside[2:]), places=2, into=sent_beside)
-    slots_here, sent_beside, *both_parts = lax.optimization_barrier(
-        (slots_here, sent_beside, *both_parts)
+    sent_beside = forward(
+        after(turned, both, sent_beside), wide, take(beside[2:]), places=2, into=sent_beside
     )
+    slots_here, sent_beside = lax.optimization_barrier((slots_here, sent_beside))
     slots_beside = exchange(sent_beside, "tensor", LANES)
-    both_parts = over_side(total_of(both_parts), 1)
-    grown = backward(after(spots_of(beside), sent_beside), grown, out_grad, take(beside))
-    sent = forward(after(turned_here, grown), wide, take(across), apart=True)
-    slots_beside, *both_parts = lax.optimization_barrier((slots_beside, *both_parts, *sent))[:5]
-    both = total_of(both_parts)
+    both = with_partner(both, 4, sent_beside)
+    grown = backward(after(spots_of(beside), both), grown, out_grad, take(beside))
+    both = with_partner(both, 2, grown)
+    sent = forward(after(turned_here, both), wide, take(across), apart=True)
+    both = with_partner(both, 8, *sent)
+    slots_beside = after(slots_beside, *sent)
+    slots = arrange(far.astype(jnp.int32).reshape(1), slots_here, slots_beside)
+    moved = exchange(slots, "tensor", LANES)
+    both = after(both, slots)
     bank_a, logit_grad_a = compose_back(both[:rank], weights_a, picked_a, mixing_a, vector_bank)
     bank_b, logit_grad_b = compose_back(both[rank:], weights_b, picked_b, mixing_b, vector_bank)
-
-    slots = arrange(far.astype(jnp.int32).reshape(1), slots_here, slots_beside)
-    moved = exchange(slots, "tensor", LANES)
     crossed = lax.ppermute(jnp.where(core == 0, slots[2:], moved[:2]), "tensor", SWAP)
     firsts = jnp.where(core == 0, slots[:2], crossed)
     seconds = jnp.where(core == 0, crossed, moved[2:])
@@ -354,7 +384,9 @@
         arrived.append(lax.ppermute(sent[step], "tensor", turns))
     piece = total_of([a.astype(f32) for a in arrived]).astype(bf16)
     bank_grad = over_tensor(bank_a + bank_b)
-    grown = backward(after(spots_of(across), slots), grown, out_grad, take(across))
+    grown, other = backward(
+        after(spots_of(across), slots), grown, out_grad, take(across), last=True
+    )
     first, place, second = settle(piece, 2, z, core)
     cols = []
     for s in range(2):
@@ -365,9 +397,9 @@
         summed.astype(f32)
         + adapter_scale * lax.dot_general(low_bf, up_b, rows_by_rows, preferred_element_type=f32)
     ).astype(bf16)
-    other = lax.ppermute(grown[:, height:].astype(bf16), "tensor", SWAP)
+    other = lax.ppermute(other, "tensor", SWAP)
     attn_grad = (
-        grown[:, :height]
+        grown
         + other.astype(f32)
         + adapter_scale * lax.dot_general(back_bf, down_a, rows_by_rows, preferred_element_type=f32)
     ).astype(bf16)

time: 201 us -> 215 us (1.070)
  starting transfers between devices: 59.9 us -> 88.2 us
  waiting for transfers between devices: 48.4 us -> 34.8 us
  other arithmetic: 22.8 us -> 25.2 us
  matrix products: 12.4 us -> 10.2 us
    ppermute x2, starting transfers between devices: 3.43 us -> 29.6 us  [over_tensor(): value = value + lax.ppermute(value, 'tensor', SWAP)]
    ppermute x12, waiting for transfers between devices: 30.1 us -> 15.7 us  [shift(): return lax.ppermute(value, BOTH, ring(stage, step))]
    ppermute x2, starting transfers between devices: 2.93 us -> 6.86 us  [from_second(): return lax.ppermute(piece, BOTH, pairs(move))]
    slice x1 -> x0, local copies, waits for them, and re-layouts: 2.77 us -> none  [local(): other = lax.ppermute(grown[:, height:].astype(bf16), 'tensor', SWAP)]
    add x2 -> x4, other arithmetic: 2.25 us -> 4.82 us  [with_partner(): return value + after(other, *events)]
    ppermute x2, starting transfers between devices: 5.01 us -> 2.62 us  [over_tensor(): return value + lax.ppermute(value, 'tensor', [(t, t ^ 4) for t in range(8)])]
    ppermute x7 -> x5, starting transfers between devices: 6.01 us -> 5.67 us  [the longest x4 5.35 us: with_partner(): other = lax.ppermute(value, 'dp', [(d, d ^ bit) for d in range(16)])]
    ppermute x7 -> x5, waiting for transfers between devices: 8.48 us -> 8.71 us  [the longest x4 8.7 us: with_partner(): other = lax.ppermute(value, 'dp', [(d, d ^ bit) for d in range(16)])]
  transfers between devices with their start and end apart: 37 -> 35, of which waited for: 11 -> 9; matrix products, arithmetic and copies ran while one was open for 17% -> 14% of each run, Pallas kernels for 24% -> 21%
where the time goes in v3:
time: 215 us; the launch traced here: 214 us
  starting transfers between devices  88.2 us (41%)
  Pallas kernels  48.6 us (23%)
  waiting for transfers between devices  34.8 us (16%)
  other arithmetic  25.2 us (12%)
  matrix products  10.2 us (5%)
  local copies, waits for them, and re-layouts  5.43 us (3%)
    ppermute x2, starting transfers between devices, over_tensor(): value = value + lax.ppermute(value, 'tensor', SWAP)  29.6 us
    pallas_call x3, Pallas kernels, backward(): pl.pallas_call(functools.partial(backward_kernel, count, first, last), ou...  24.8 us
    pallas_call x4, Pallas kernels, forward(): pl.pallas_call(functools.partial(forward_kernel, count, many), out_shape=...  19.9 us
    ppermute x12, starting transfers between devices, shift(): return lax.ppermute(value, BOTH, ring(stage, step))  17.2 us
    ppermute x12, waiting for transfers between devices, shift(): return lax.ppermute(value, BOTH, ring(stage, step))  15.7 us
    all_to_all x3, starting transfers between devices, exchange(): lax.all_to_all(value, axis, split_axis=0, concat_axis=0, tiled=True, axis...  12.2 us
    ppermute x4, waiting for transfers between devices, with_partner(): other = lax.ppermute(value, 'dp', [(d, d ^ bit) for d in range(16)])  8.7 us
    ppermute x2, starting transfers between devices, from_second(): return lax.ppermute(piece, BOTH, pairs(move))  6.86 us
  transfers between devices with their start and end apart: 35, of which 9 were waited for; matrix products, arithmetic and copies ran while one was open for 14% of the time, Pallas kernels for 21%

profile of v3, /device:TPU:1, one launch (start us, length us, event | category | flops | bytes accessed | tf_op | source)
XLA Modules:
  0.0 213.7 jit_solution(1039231632348968864)
XLA Ops:
  2.0 1.5 collective-permute-start.1
  3.5 1.6 collective-permute-done.1
  6.3 1.8 collective-permute-start.3
  8.1 2.2 %collective-permute-start.2 = (bf16[2048,128]{1,0:T(8,128)(2,1)S(1)}, bf16[2048,128]{1,0:T(8,128)(2,1)}, u32[]{:S(2)}, u32[]{:S(2)}) collective-permute-start(bf16[2048,128]{1,0:T(8,128)(2,1)S(1)} %get-tuple-element.35), channel_id=1, source_target_pairs={{0,96},{1,25},{2,98},{3,27},{4,100},{5,29},{6,102},{7,31},{8,104},... | collective-permute-start | bytes 1572872 | tf_op jit(solution)/shard_map/ppermute | solution.py:43
  10.3 1.4 collective-permute-start.5
  12.7 4.5 %collective-permute-done.3 = bf16[2048,128]{1,0:T(8,128)(2,1)} collective-permute-done((bf16[2048,128]{1,0:T(8,128)(2,1)S(1)}, bf16[2048,128]{1,0:T(8,128)(2,1)}, u32[]{:S(2)}, u32[]{:S(2)}) %collective-permute-start.3) | collective-permute-done | bytes 524320 | tf_op jit(solution)/shard_map/ppermute | solution.py:43
  17.6 4.8 %collective-permute-done.5 = bf16[2048,128]{1,0:T(8,128)(2,1)S(1)} collective-permute-done((bf16[2048,128]{1,0:T(8,128)(2,1)S(1)}, bf16[2048,128]{1,0:T(8,128)(2,1)S(1)}, u32[]{:S(2)}, u32[]{:S(2)}) %collective-permute-start.5) | collective-permute-done | bytes 524320 | tf_op jit(solution)/shard_map/ppermute | solution.py:43
  22.3 3.2 %collective-permute-start.6 = (bf16[2048,128]{1,0:T(8,128)(2,1)S(1)}, bf16[2048,128]{1,0:T(8,128)(2,1)S(1)}, u32[]{:S(2)}, u32[]{:S(2)}) collective-permute-start(bf16[2048,128]{1,0:T(8,128)(2,1)S(1)} %collective-permute-done.5), channel_id=1, source_target_pairs={{0,96},{1,25},{2,98},{3,27},{4,100},{5,29},{6,102},{7,31},{8,104},... | collective-permute-start | bytes 1572872 | tf_op jit(solution)/shard_map/ppermute | solution.py:43
  25.6 1.6 fusion.11
  28.0 2.8 %pad_maximum_fusion.refs_0_ = bf16[4,2048,128]{2,1,0:T(8,128)(2,1)} fusion(bf16[1,2048,128]{2,1,0:T(8,128)(2,1)} %bitcast.5, bf16[1,2048,128]{2,1,0:T(8,128)(2,1)S(1)} %bitcast.110, bf16[1,2048,128]{2,1,0:T(8,128)(2,1)} %bitcast.3, bf16[1,2048,128]{2,1,0:T(8,128)(2,1)S(1)} %bitcast.103), kind=kLoop, calls=%fused_computation.2 | loop fusion | flops 3145728 | bytes 4194304 | tf_op jit(solution)/shard_map/stack | solution.py:311
  31.7 2.7 %pad_maximum_fusion.1.refs_1_ = bf16[4,2048,128]{2,1,0:T(8,128)(2,1)} fusion(bf16[1,2048,128]{2,1,0:T(8,128)(2,1)} %bitcast.9, bf16[1,2048,128]{2,1,0:T(8,128)(2,1)S(1)} %bitcast.109, bf16[1,2048,128]{2,1,0:T(8,128)(2,1)S(1)} %bitcast.108, bf16[1,2048,128]{2,1,0:T(8,128)(2,1)S(1)} %bitcast.102), kind=kLoop, calls=%fused_computation.3 | loop fusion | flops 3145728 | bytes 4194304 | tf_op jit(solution)/shard_map/stack | solution.py:313
  34.3 2.4 %collective-permute-start.14 = (bf16[4,2048,128]{2,1,0:T(8,128)(2,1)}, bf16[4,2048,128]{2,1,0:T(8,128)(2,1)}, u32[]{:S(2)}, u32[]{:S(2)}) collective-permute-start(bf16[4,2048,128]{2,1,0:T(8,128)(2,1)} %pad_maximum_fusion.1.refs_1_), channel_id=1, source_target_pairs={{0,24},{1,97},{2,26},{3,99},{4,28},{5,101},{6,30},{7,103},{8,0},{9... | collective-permute-start | bytes 6291464 | tf_op jit(solution)/shard_map/ppermute | solution.py:43
  36.7 2.8 %collective-permute-start = (bf16[512,1024]{1,0:T(8,128)(2,1)S(1)}, bf16[512,1024]{1,0:T(8,128)(2,1)}, u32[]{:S(2)}, u32[]{:S(2)}) collective-permute-start(bf16[512,1024]{1,0:T(8,128)(2,1)S(1)} %copy-done.1), channel_id=1, source_target_pairs={{0,1},{1,0},{2,3},{3,2},{4,5},{5,4},{6,7},{7,6},{8,9},{9,8},{10,11... | collective-permute-start | bytes 3145736 | tf_op jit(solution)/shard_map/ppermute | solution.py:327
  39.5 2.2 %collective-permute-done.8 = f32[32,512]{1,0:T(8,128)S(1)} collective-permute-done((f32[32,512]{1,0:T(8,128)S(1)}, f32[32,512]{1,0:T(8,128)S(1)}, u32[]{:S(2)}, u32[]{:S(2)}) %collective-permute-start.8) | collective-permute-done | bytes 65568 | tf_op jit(solution)/shard_map/ppermute | solution.py:60
  41.7 1.4 collective-permute-start.9
  43.1 3.4 %collective-permute-start.12 = (bf16[4,2048,128]{2,1,0:T(8,128)(2,1)}, bf16[4,2048,128]{2,1,0:T(8,128)(2,1)}, u32[]{:S(2)}, u32[]{:S(2)}) collective-permute-start(bf16[4,2048,128]{2,1,0:T(8,128)(2,1)} %pad_maximum_fusion.refs_0_), channel_id=1, source_target_pairs={{0,24},{1,97},{2,26},{3,99},{4,28},{5,101},{6,30},{7,103},{8,0},{9... | collective-permute-start | bytes 6291464 | tf_op jit(solution)/shard_map/ppermute | solution.py:43
  48.6 2.6 %collective-permute-start.10 = (f32[32,512]{1,0:T(8,128)}, f32[32,512]{1,0:T(8,128)S(1)}, u32[]{:S(2)}, u32[]{:S(2)}) collective-permute-start(f32[32,512]{1,0:T(8,128)} %add.381), channel_id=1, source_target_pairs={{0,4},{1,5},{2,6},{3,7},{4,0},{5,1},{6,2},{7,3},{8,12},{9,13},{10,... | collective-permute-start | bytes 196616 | tf_op jit(solution)/shard_map/ppermute | solution.py:62
  52.6 5.0 %forward.4 = bf16[4,512,256]{2,1,0:T(8,128)(2,1)} custom-call(s32[1]{0:T(128)} %bitcast.1.start_ref, bf16[512,2048]{1,0:T(8,128)(2,1)S(1)} %constant_dynamic-update-slice_fusion.wide_ref, bf16[4,2048,128]{2,1,0:T(8,128)(2,1)} %pad_maximum_fusion.refs_0_, bf16[4,2048,128]{2,1,0:T(8,128)(2,1)} %pad_maximum_fusion.1.refs_1_), custom_call_target="tpu_custom_call" | custom-call | flops 268435456 | bytes 524288 | tf_op jit(solution)/shard_map/forward/pallas_call | solution.py:119
  57.6 3.5 %all-to-all-start = ((bf16[4,512,256]{2,1,0:T(8,128)(2,1)}), bf16[4,512,256]{2,1,0:T(8,128)(2,1)S(1)}, u32[]{:S(2)}, u32[]{:S(2)}) async-start(bf16[4,512,256]{2,1,0:T(8,128)(2,1)} %forward.4), calls=%async_computation | async-start | bytes 2097152 | tf_op jit(solution)/shard_map/all_to_all | solution.py:54
  62.0 1.5 fusion.35
  63.5 2.7 %collective-permute-start.19 = (bf16[4,2048,128]{2,1,0:T(8,128)(2,1)}, bf16[4,2048,128]{2,1,0:T(8,128)(2,1)}, u32[]{:S(2)}, u32[]{:S(2)}) collective-permute-start(bf16[4,2048,128]{2,1,0:T(8,128)(2,1)} %collective-permute-done.14.refs_0_.refs_2_), channel_id=1, source_target_pairs={{0,24},{1,97},{2,26},{3,99},{4,28},{5,101},{6,30},{7,103},{8,0},{9... | collective-permute-start | bytes 6291464 | tf_op jit(solution)/shard_map/ppermute | solution.py:43
  66.1 1.5 fusion.9
  69.0 7.1 %backward.3.refs_20_ = f32[512,2048]{1,0:T(8,128)} custom-call(s32[8]{0:T(128)S(1)} %stack.153.spots_ref, bf16[4,2048,128]{2,1,0:T(8,128)(2,1)} %pad_maximum_fusion.refs_0_, bf16[4,2048,128]{2,1,0:T(8,128)(2,1)} %pad_maximum_fusion.1.refs_1_, bf16[512,8192]{1,0:T(8,128)(2,1)} %refs_9_.5, bf16[512,8192]{1,0:T(8,128)(2,1)} %refs_9_.5, ...), custom_call_target="tpu_custom_call" | custom-call | flops 268435456 | bytes 524288 | tf_op jit(solution)/shard_map/backward/pallas_call | solution.py:229
  76.2 1.6 fusion.41
  77.7 4.7 %collective-permute-done.12.refs_0_ = bf16[4,2048,128]{2,1,0:T(8,128)(2,1)} collective-permute-done((bf16[4,2048,128]{2,1,0:T(8,128)(2,1)}, bf16[4,2048,128]{2,1,0:T(8,128)(2,1)}, u32[]{:S(2)}, u32[]{:S(2)}) %collective-permute-start.12) | collective-permute-done | bytes 2097184 | tf_op jit(solution)/shard_map/ppermute | solution.py:43
  82.5 5.0 %forward.5.refs_2_ = bf16[4,512,512]{2,1,0:T(8,128)(2,1)} custom-call(s32[1]{0:T(128)} %bitcast.1.start_ref, bf16[512,2048]{1,0:T(8,128)(2,1)S(1)} %constant_dynamic-update-slice_fusion.wide_ref, bf16[4,2048,128]{2,1,0:T(8,128)(2,1)} %collective-permute-done.12.refs_0_, bf16[4,2048,128]{2,1,0:T(8,128)(2,1)} %collective-permute-done.13.refs_1_), custom_call_target="tpu_custom_call" | custom-call | flops 268435456 | bytes 524288 | tf_op jit(solution)/shard_map/forward/pallas_call | solution.py:119
  87.5 5.0 %forward.6 = bf16[4,512,512]{2,1,0:T(8,128)(2,1)} custom-call(s32[1]{0:T(128)} %bitcast.1.start_ref, bf16[512,2048]{1,0:T(8,128)(2,1)S(1)} %constant_dynamic-update-slice_fusion.wide_ref, bf16[4,2048,128]{2,1,0:T(8,128)(2,1)} %collective-permute-done.14.refs_0_.refs_2_, ...), custom_call_target="tpu_custom_call", output_to_operand_aliasing={{}: (4, {})} | custom-call | flops 268435456 | bytes 524288 | tf_op jit(solution)/shard_map/forward/pallas_call | solution.py:119
  92.5 4.4 %all-to-all-start.1 = ((bf16[4,512,512]{2,1,0:T(8,128)(2,1)}), bf16[4,512,512]{2,1,0:T(8,128)(2,1)}, u32[]{:S(2)}, u32[]{:S(2)}) async-start(bf16[4,512,512]{2,1,0:T(8,128)(2,1)} %forward.6), calls=%async_computation.1 | async-start | bytes 4194304 | tf_op jit(solution)/shard_map/all_to_all | solution.py:54
  97.7 8.7 %collective-permute-done.16 = f32[32,1024]{1,0:T(8,128)S(1)} collective-permute-done((f32[32,1024]{1,0:T(8,128)}, f32[32,1024]{1,0:T(8,128)S(1)}, u32[]{:S(2)}, u32[]{:S(2)}) %collective-permute-start.16) | collective-permute-done | bytes 131104 | tf_op jit(solution)/shard_map/ppermute | solution.py:70
  106.4 1.6 add.406
  107.9 2.1 collective-permute-start.17
  110.2 10.7 %backward.4.refs_10_ = f32[512,2048]{1,0:T(8,128)} custom-call(s32[16]{0:T(128)S(1)} %stack.170.spots_ref, bf16[4,2048,128]{2,1,0:T(8,128)(2,1)} %collective-permute-done.12.refs_0_, bf16[4,2048,128]{2,1,0:T(8,128)(2,1)} %collective-permute-done.13.refs_1_, ...), custom_call_target="tpu_custom_call", output_to_operand_aliasing={{}: (21, {})} | custom-call | flops 536870912 | bytes 1048576 | tf_op jit(solution)/shard_map/backward/pallas_call | solution.py:229
  121.9 2.5 %collective-permute-start.28 = (f32[32,1024]{1,0:T(8,128)S(1)}, f32[32,1024]{1,0:T(8,128)S(1)}, u32[]{:S(2)}, u32[]{:S(2)}) collective-permute-start(f32[32,1024]{1,0:T(8,128)S(1)} %add.435), channel_id=1, source_target_pairs={{0,64},{8,72},{16,80},{24,88},{32,96},{40,104},{48,112},{56,120},{... | collective-permute-start | bytes 393224 | tf_op jit(solution)/shard_map/ppermute | solution.py:70
  124.4 1.8 fusion.33
  126.2 5.0 %forward.7 = (bf16[512,256]{1,0:T(8,128)(2,1)}, bf16[512,256]{1,0:T(8,128)(2,1)}, bf16[512,256]{1,0:T(8,128)(2,1)}, bf16[512,256]{1,0:T(8,128)(2,1)}) custom-call(s32[1]{0:T(128)} %bitcast.19.start_ref, bf16[512,2048]{1,0:T(8,128)(2,1)S(1)} %constant_dynamic-update-slice_fusion.wide_ref, bf16[4,2048,128]{2,1,0:T(8,128)(2,1)} %collective-permute-done.18.refs_0_, ...), custom_call_target="tpu_custom_call" | custom-call | flops 268435456 | bytes 524288 | tf_op jit(solution)/shard_map/forward/pallas_call | solution.py:119
  131.9 3.9 %arrange.1 = bf16[4,512,256]{2,1,0:T(8,128)(2,1)} custom-call(s32[1]{0:T(128)} %bitcast.far_ref, bf16[4,512,256]{2,1,0:T(8,128)(2,1)S(1)} %all-to-all-done.here_ref, bf16[4,512,512]{2,1,0:T(8,128)(2,1)} %all-to-all-done.1.beside_ref), custom_call_target="tpu_custom_call" | custom-call | flops 2097152 | bytes 4194304 | tf_op jit(solution)/shard_map/arrange/pallas_call | solution.py:164
  136.6 4.3 %all-to-all-start.2 = ((bf16[4,512,256]{2,1,0:T(8,128)(2,1)}), bf16[4,512,256]{2,1,0:T(8,128)(2,1)}, u32[]{:S(2)}, u32[]{:S(2)}) async-start(bf16[4,512,256]{2,1,0:T(8,128)(2,1)} %arrange.1), calls=%async_computation.2 | async-start | bytes 2097152 | tf_op jit(solution)/shard_map/all_to_all | solution.py:54
  140.8 3.0 %collective-permute-start.21 = (bf16[512,256]{1,0:T(8,128)(2,1)}, bf16[512,256]{1,0:T(8,128)(2,1)}, u32[]{:S(2)}, u32[]{:S(2)}) collective-permute-start(bf16[512,256]{1,0:T(8,128)(2,1)} %get-tuple-element.57), channel_id=1, source_target_pairs={{0,4},{1,5},{2,6},{3,7},{4,0},{5,1},{6,2},{7,3},{8,12},{9,13},{10,... | collective-permute-start | bytes 786440 | tf_op jit(solution)/shard_map/ppermute | solution.py:384
  144.2 2.3 %collective-permute-start.23 = (bf16[512,256]{1,0:T(8,128)(2,1)}, bf16[512,256]{1,0:T(8,128)(2,1)}, u32[]{:S(2)}, u32[]{:S(2)}) collective-permute-start(bf16[512,256]{1,0:T(8,128)(2,1)} %get-tuple-element.58), channel_id=1, source_target_pairs={{0,6},{1,7},{2,0},{3,1},{4,2},{5,3},{6,4},{7,5},{8,14},{9,15},{10,... | collective-permute-start | bytes 786440 | tf_op jit(solution)/shard_map/ppermute | solution.py:384
  147.3 29.6 %collective-permute-start.29 = (f32[256,256]{1,0:T(8,128)S(1)}, f32[256,256]{1,0:T(8,128)S(1)}, u32[]{:S(2)}, u32[]{:S(2)}) collective-permute-start(f32[256,256]{1,0:T(8,128)S(1)} %fusion.2), channel_id=1, source_target_pairs={{0,1},{1,0},{2,3},{3,2},{4,5},{5,4},{6,7},{7,6},{8,9},{9,8},{10,11... | collective-permute-start | bytes 786440 | tf_op jit(solution)/shard_map/ppermute | solution.py:60
  177.1 7.0 %backward.5 = (f32[512,1024]{1,0:T(8,128)S(1)}, bf16[512,1024]{1,0:T(8,128)(2,1)S(1)}) custom-call(s32[8]{0:T(128)S(1)} %stack.179.spots_ref, bf16[4,2048,128]{2,1,0:T(8,128)(2,1)} %collective-permute-done.18.refs_0_, bf16[4,2048,128]{2,1,0:T(8,128)(2,1)} %collective-permute-done.19.refs_1_, bf16[512,8192]{1,0:T(8,128)(2,1)} %refs_9_.5, ...), custom_call_target="tpu_custom_call" | custom-call | flops 268435456 | bytes 524288 | tf_op jit(solution)/shard_map/backward/pallas_call | solution.py:229
  185.9 6.6 %collective-permute-done.30 = f32[256,256]{1,0:T(8,128)S(1)} collective-permute-done((f32[256,256]{1,0:T(8,128)S(1)}, f32[256,256]{1,0:T(8,128)S(1)}, u32[]{:S(2)}, u32[]{:S(2)}) %collective-permute-start.30) | collective-permute-done | bytes 262176 | tf_op jit(solution)/shard_map/ppermute | solution.py:61
  193.3 1.4 slice_select_fusion.1
  194.7 1.4 collective-permute-start.20
  198.7 6.2 %collective-permute-start.25 = (bf16[512,256]{1,0:T(8,128)(2,1)S(1)}, bf16[512,256]{1,0:T(8,128)(2,1)S(1)}, u32[]{:S(2)}, u32[]{:S(2)}) collective-permute-start(bf16[512,256]{1,0:T(8,128)(2,1)S(1)} %add_convert_fusion.2), channel_id=1, source_target_pairs={{1,4},{5,5},{9,12},{13,13},{17,20},{21,21},{25,28},{29,29},{33,38}... | collective-permute-start | bytes 786440 | tf_op jit(solution)/shard_map/ppermute | solution.py:277
  205.6 1.8 add.467
  207.4 2.8 %add_convert_fusion = bf16[512,1024]{1,0:T(8,128)(2,1)} fusion(f32[512,1024]{1,0:T(8,128)S(1)} %copy-done.2, f32[512,1024]{1,0:T(8,128)S(1)} %get-tuple-element.61, bf16[512,1024]{1,0:T(8,128)(2,1)} %collective-permute-done.27), kind=kLoop, calls=%fused_computation.4 | loop fusion | flops 2621440 | bytes 6291456 | tf_op jit(solution)/shard_map/convert_element_type | solution.py:405
  212.3 1.4 add_convert_fusion.1
  (132 shorter events, 23.8 us)
Async XLA Ops:
  0.6 11.4 %copy-start = (f32[256,256]{1,0:T(8,128)S(1)}, f32[256,256]{1,0:T(8,128)}, u32[]{:S(2)}) copy-start(f32[256,256]{1,0:T(8,128)} %param.10) | copy-start | bytes 786436
  2.0 3.2 %collective-permute-start.1 = (bf16[1024,256]{1,0:T(8,128)(2,1)S(1)}, bf16[1024,256]{1,0:T(8,128)(2,1)}, u32[]{:S(2)}, u32[]{:S(2)}) collective-permute-start(bf16[1024,256]{1,0:T(8,128)(2,1)S(1)} %get-tuple-element.68), channel_id=1, source_target_pairs={{0,1},{1,0},{2,3},{3,2},{4,5},{5,4},{6,7},{7,6},{8,9},{9,8},{10,11... | collective-permute-start | bytes 1572872 | tf_op jit(solution)/shard_map/ppermute | solution.py:304
  3.5 8.3 %copy-start.23 = (f32[16,4,2]{0,2,1:T(2,128)S(1)}, f32[16,4,2]{0,2,1:T(2,128)}, u32[]{:S(2)}) copy-start(f32[16,4,2]{0,2,1:T(2,128)} %param.13) | copy-start | bytes 1540
  3.5 8.4 %copy-start.17 = (s32[16,4,2]{0,2,1:T(2,128)S(1)}, s32[16,4,2]{0,2,1:T(2,128)}, u32[]{:S(2)}) copy-start(s32[16,4,2]{0,2,1:T(2,128)} %param.12) | copy-start | bytes 1540
  3.5 8.8 %copy-start.16 = (s32[16,4,2]{0,2,1:T(2,128)S(1)}, s32[16,4,2]{0,2,1:T(2,128)}, u32[]{:S(2)}) copy-start(s32[16,4,2]{0,2,1:T(2,128)} %param.14) | copy-start | bytes 1540
  3.5 13.6 %copy-start.1 = (bf16[512,1024]{1,0:T(8,128)(2,1)S(1)}, bf16[512,1024]{1,0:T(8,128)(2,1)}, u32[]{:S(2)}) copy-start(bf16[512,1024]{1,0:T(8,128)(2,1)} %param.8) | copy-start | bytes 3145732
  6.3 10.9 %collective-permute-start.3 = (bf16[2048,128]{1,0:T(8,128)(2,1)S(1)}, bf16[2048,128]{1,0:T(8,128)(2,1)}, u32[]{:S(2)}, u32[]{:S(2)}) collective-permute-start(bf16[2048,128]{1,0:T(8,128)(2,1)S(1)} %get-tuple-element.35), channel_id=1, source_target_pairs={{0,32},{1,9},{2,34},{3,11},{4,36},{5,13},{6,38},{7,15},{8,40},{9,1... | collective-permute-start | bytes 1572872 | tf_op jit(solution)/shard_map/ppermute | solution.py:43
  8.1 19.1 %collective-permute-start.2 = (bf16[2048,128]{1,0:T(8,128)(2,1)S(1)}, bf16[2048,128]{1,0:T(8,128)(2,1)}, u32[]{:S(2)}, u32[]{:S(2)}) collective-permute-start(bf16[2048,128]{1,0:T(8,128)(2,1)S(1)} %get-tuple-element.35), channel_id=1, source_target_pairs={{0,96},{1,25},{2,98},{3,27},{4,100},{5,29},{6,102},{7,31},{8,104},... | collective-permute-start | bytes 1572872 | tf_op jit(solution)/shard_map/ppermute | solution.py:43
  10.3 12.0 %collective-permute-start.5 = (bf16[2048,128]{1,0:T(8,128)(2,1)S(1)}, bf16[2048,128]{1,0:T(8,128)(2,1)S(1)}, u32[]{:S(2)}, u32[]{:S(2)}) collective-permute-start(bf16[2048,128]{1,0:T(8,128)(2,1)S(1)} %get-tuple-element.38), channel_id=1, source_target_pairs={{0,96},{1,25},{2,98},{3,27},{4,100},{5,29},{6,102},{7,31},{8,104},... | collective-permute-start | bytes 1572872 | tf_op jit(solution)/shard_map/ppermute | solution.py:43
  11.7 19.2 %collective-permute-start.7 = (bf16[2048,128]{1,0:T(8,128)(2,1)S(1)}, bf16[2048,128]{1,0:T(8,128)(2,1)}, u32[]{:S(2)}, u32[]{:S(2)}) collective-permute-start(bf16[2048,128]{1,0:T(8,128)(2,1)S(1)} %get-tuple-element.38), channel_id=1, source_target_pairs={{0,32},{1,9},{2,34},{3,11},{4,36},{5,13},{6,38},{7,15},{8,40},{9,1... | collective-permute-start | bytes 1572872 | tf_op jit(solution)/shard_map/ppermute | solution.py:43
  11.8 19.0 %copy-start.18 = (f32[16,4,2]{0,2,1:T(2,128)}, f32[16,4,2]{0,2,1:T(2,128)S(1)}, u32[]{:S(2)}) copy-start(f32[16,4,2]{0,2,1:T(2,128)S(1)} %add_divide_fusion.1) | copy-start | bytes 1540
  11.9 18.9 %copy-start.20 = (f32[16,4,2]{0,2,1:T(2,128)}, f32[16,4,2]{0,2,1:T(2,128)S(1)}, u32[]{:S(2)}) copy-start(f32[16,4,2]{0,2,1:T(2,128)S(1)} %add_divide_fusion) | copy-start | bytes 1540
  12.3 18.5 %copy-start.8 = (bf16[4,2,8,256]{3,2,0,1:T(8,128)(2,1)}, bf16[4,2,8,256]{3,2,0,1:T(8,128)(2,1)S(1)}, u32[]{:S(2)}) copy-start(bf16[4,2,8,256]{3,2,0,1:T(8,128)(2,1)S(1)} %copy.45) | copy-start | bytes 98308
  12.4 18.4 %copy-start.5 = (f32[16,4,256]{2,0,1:T(8,128)}, f32[16,4,256]{2,0,1:T(8,128)S(1)}, u32[]{:S(2)}) copy-start(f32[16,4,256]{2,0,1:T(8,128)S(1)} %select_reduce_fusion.2) | copy-start | bytes 196612
  12.7 12.9 %copy-start.12 = (bf16[4,2,8,256]{3,2,0,1:T(8,128)(2,1)}, bf16[4,2,8,256]{3,2,0,1:T(8,128)(2,1)S(1)}, u32[]{:S(2)}) copy-start(bf16[4,2,8,256]{3,2,0,1:T(8,128)(2,1)S(1)} %copy.46) | copy-start | bytes 98308
  17.2 10.8 %collective-permute-start.4 = (bf16[2048,128]{1,0:T(8,128)(2,1)}, bf16[2048,128]{1,0:T(8,128)(2,1)S(1)}, u32[]{:S(2)}, u32[]{:S(2)}) collective-permute-start(bf16[2048,128]{1,0:T(8,128)(2,1)} %collective-permute-done.3), channel_id=1, source_target_pairs={{0,32},{1,9},{2,34},{3,11},{4,36},{5,13},{6,38},{7,15},{8,40},{9,1... | collective-permute-start | bytes 1572872 | tf_op jit(solution)/shard_map/ppermute | solution.py:43
  22.3 9.4 %collective-permute-start.6 = (bf16[2048,128]{1,0:T(8,128)(2,1)S(1)}, bf16[2048,128]{1,0:T(8,128)(2,1)S(1)}, u32[]{:S(2)}, u32[]{:S(2)}) collective-permute-start(bf16[2048,128]{1,0:T(8,128)(2,1)S(1)} %collective-permute-done.5), channel_id=1, source_target_pairs={{0,96},{1,25},{2,98},{3,27},{4,100},{5,29},{6,102},{7,31},{8,104},... | collective-permute-start | bytes 1572872 | tf_op jit(solution)/shard_map/ppermute | solution.py:43
  34.3 29.1 %collective-permute-start.14 = (bf16[4,2048,128]{2,1,0:T(8,128)(2,1)}, bf16[4,2048,128]{2,1,0:T(8,128)(2,1)}, u32[]{:S(2)}, u32[]{:S(2)}) collective-permute-start(bf16[4,2048,128]{2,1,0:T(8,128)(2,1)} %pad_maximum_fusion.1.refs_1_), channel_id=1, source_target_pairs={{0,24},{1,97},{2,26},{3,99},{4,28},{5,101},{6,30},{7,103},{8,0},{9... | collective-permute-start | bytes 6291464 | tf_op jit(solution)/shard_map/ppermute | solution.py:43
  36.7 29.4 %collective-permute-start.13 = (bf16[4,2048,128]{2,1,0:T(8,128)(2,1)}, bf16[4,2048,128]{2,1,0:T(8,128)(2,1)}, u32[]{:S(2)}, u32[]{:S(2)}) collective-permute-start(bf16[4,2048,128]{2,1,0:T(8,128)(2,1)} %pad_maximum_fusion.refs_0_), channel_id=1, source_target_pairs={{0,8},{1,33},{2,10},{3,35},{4,12},{5,37},{6,14},{7,39},{8,16},{9,4... | collective-permute-start | bytes 6291464 | tf_op jit(solution)/shard_map/ppermute | solution.py:43
  36.7 11.9 %collective-permute-start = (bf16[512,1024]{1,0:T(8,128)(2,1)S(1)}, bf16[512,1024]{1,0:T(8,128)(2,1)}, u32[]{:S(2)}, u32[]{:S(2)}) collective-permute-start(bf16[512,1024]{1,0:T(8,128)(2,1)S(1)} %copy-done.1), channel_id=1, source_target_pairs={{0,1},{1,0},{2,3},{3,2},{4,5},{5,4},{6,7},{7,6},{8,9},{9,8},{10,11... | collective-permute-start | bytes 3145736 | tf_op jit(solution)/shard_map/ppermute | solution.py:327
  39.5 2.2 %collective-permute-start.8 = (f32[32,512]{1,0:T(8,128)S(1)}, f32[32,512]{1,0:T(8,128)S(1)}, u32[]{:S(2)}, u32[]{:S(2)}) collective-permute-start(f32[32,512]{1,0:T(8,128)S(1)} %pad_maximum_fusion.4), channel_id=1, source_target_pairs={{0,1},{1,0},{2,3},{3,2},{4,5},{5,4},{6,7},{7,6},{8,9},{9,8},{10,11... | collective-permute-start | bytes 196616 | tf_op jit(solution)/shard_map/ppermute | solution.py:60
  41.7 4.8 %collective-permute-start.9 = (f32[32,512]{1,0:T(8,128)S(1)}, f32[32,512]{1,0:T(8,128)S(1)}, u32[]{:S(2)}, u32[]{:S(2)}) collective-permute-start(f32[32,512]{1,0:T(8,128)S(1)} %add.380), channel_id=1, source_target_pairs={{0,2},{1,3},{2,0},{3,1},{4,6},{5,7},{6,4},{7,5},{8,10},{9,11},{10,... | collective-permute-start | bytes 196616 | tf_op jit(solution)/shard_map/ppermute | solution.py:61
  43.1 39.4 %collective-permute-start.12 = (bf16[4,2048,128]{2,1,0:T(8,128)(2,1)}, bf16[4,2048,128]{2,1,0:T(8,128)(2,1)}, u32[]{:S(2)}, u32[]{:S(2)}) collective-permute-start(bf16[4,2048,128]{2,1,0:T(8,128)(2,1)} %pad_maximum_fusion.refs_0_), channel_id=1, source_target_pairs={{0,24},{1,97},{2,26},{3,99},{4,28},{5,101},{6,30},{7,103},{8,0},{9... | collective-permute-start | bytes 6291464 | tf_op jit(solution)/shard_map/ppermute | solution.py:43
  46.5 40.9 %collective-permute-start.15 = (bf16[4,2048,128]{2,1,0:T(8,128)(2,1)}, bf16[4,2048,128]{2,1,0:T(8,128)(2,1)}, u32[]{:S(2)}, u32[]{:S(2)}) collective-permute-start(bf16[4,2048,128]{2,1,0:T(8,128)(2,1)} %pad_maximum_fusion.1.refs_1_), channel_id=1, source_target_pairs={{0,8},{1,33},{2,10},{3,35},{4,12},{5,37},{6,14},{7,39},{8,16},{9,4... | collective-permute-start | bytes 6291464 | tf_op jit(solution)/shard_map/ppermute | solution.py:43
  48.6 12.5 %collective-permute-start.10 = (f32[32,512]{1,0:T(8,128)}, f32[32,512]{1,0:T(8,128)S(1)}, u32[]{:S(2)}, u32[]{:S(2)}) collective-permute-start(f32[32,512]{1,0:T(8,128)} %add.381), channel_id=1, source_target_pairs={{0,4},{1,5},{2,6},{3,7},{4,0},{5,1},{6,2},{7,3},{8,12},{9,13},{10,... | collective-permute-start | bytes 196616 | tf_op jit(solution)/shard_map/ppermute | solution.py:62
  57.6 34.9 %all-to-all-start = ((bf16[4,512,256]{2,1,0:T(8,128)(2,1)}), bf16[4,512,256]{2,1,0:T(8,128)(2,1)S(1)}, u32[]{:S(2)}, u32[]{:S(2)}) async-start(bf16[4,512,256]{2,1,0:T(8,128)(2,1)} %forward.4), calls=%async_computation | async-start | bytes 2097152 | tf_op jit(solution)/shard_map/all_to_all | solution.py:54
  63.5 62.7 %collective-permute-start.19 = (bf16[4,2048,128]{2,1,0:T(8,128)(2,1)}, bf16[4,2048,128]{2,1,0:T(8,128)(2,1)}, u32[]{:S(2)}, u32[]{:S(2)}) collective-permute-start(bf16[4,2048,128]{2,1,0:T(8,128)(2,1)} %collective-permute-done.14.refs_0_.refs_2_), channel_id=1, source_target_pairs={{0,24},{1,97},{2,26},{3,99},{4,28},{5,101},{6,30},{7,103},{8,0},{9... | collective-permute-start | bytes 6291464 | tf_op jit(solution)/shard_map/ppermute | solution.py:43
  66.1 60.1 %collective-permute-start.18 = (bf16[4,2048,128]{2,1,0:T(8,128)(2,1)}, bf16[4,2048,128]{2,1,0:T(8,128)(2,1)}, u32[]{:S(2)}, u32[]{:S(2)}) collective-permute-start(bf16[4,2048,128]{2,1,0:T(8,128)(2,1)} %collective-permute-done.13.refs_1_), channel_id=1, source_target_pairs={{0,8},{1,33},{2,10},{3,35},{4,12},{5,37},{6,14},{7,39},{8,16},{9,4... | collective-permute-start | bytes 6291464 | tf_op jit(solution)/shard_map/ppermute | solution.py:43
  68.9 7.2 %collective-permute-start.11 = (f32[32,1024]{1,0:T(8,128)}, f32[32,1024]{1,0:T(8,128)}, u32[]{:S(2)}, u32[]{:S(2)}) collective-permute-start(f32[32,1024]{1,0:T(8,128)} %maximum_multiply_fusion), channel_id=1, source_target_pairs={{0,8},{8,0},{16,24},{24,16},{32,40},{40,32},{48,56},{56,48},{64,72... | collective-permute-start | bytes 393224 | tf_op jit(solution)/shard_map/ppermute | solution.py:70
  92.5 39.4 %all-to-all-start.1 = ((bf16[4,512,512]{2,1,0:T(8,128)(2,1)}), bf16[4,512,512]{2,1,0:T(8,128)(2,1)}, u32[]{:S(2)}, u32[]{:S(2)}) async-start(bf16[4,512,512]{2,1,0:T(8,128)(2,1)} %forward.6), calls=%async_computation.1 | async-start | bytes 4194304 | tf_op jit(solution)/shard_map/all_to_all | solution.py:54
  96.9 9.4 %collective-permute-start.16 = (f32[32,1024]{1,0:T(8,128)}, f32[32,1024]{1,0:T(8,128)S(1)}, u32[]{:S(2)}, u32[]{:S(2)}) collective-permute-start(f32[32,1024]{1,0:T(8,128)} %fusion.41), channel_id=1, source_target_pairs={{0,32},{8,40},{16,48},{24,56},{32,0},{40,8},{48,16},{56,24},{64,96... | collective-permute-start | bytes 393224 | tf_op jit(solution)/shard_map/ppermute | solution.py:70
  107.9 13.0 %collective-permute-start.17 = (f32[32,1024]{1,0:T(8,128)}, f32[32,1024]{1,0:T(8,128)}, u32[]{:S(2)}, u32[]{:S(2)}) collective-permute-start(f32[32,1024]{1,0:T(8,128)} %add.406), channel_id=1, source_target_pairs={{0,16},{8,24},{16,0},{24,8},{32,48},{40,56},{48,32},{56,40},{64,80... | collective-permute-start | bytes 393224 | tf_op jit(solution)/shard_map/ppermute | solution.py:70
  110.2 14.2 %copy-start.9 = (bf16[4,2,8,256]{3,2,0,1:T(8,128)(2,1)S(1)}, bf16[4,2,8,256]{3,2,0,1:T(8,128)(2,1)}, u32[]{:S(2)}) copy-start(bf16[4,2,8,256]{3,2,0,1:T(8,128)(2,1)} %copy-done.8) | copy-start | bytes 98308
  110.2 14.2 %copy-start.11 = (bf16[32,512]{1,0:T(8,128)(2,1)S(1)}, bf16[32,512]{1,0:T(8,128)(2,1)}, u32[]{:S(2)}) copy-start(bf16[32,512]{1,0:T(8,128)(2,1)} %copy-done.10) | copy-start | bytes 98308
  121.9 9.3 %collective-permute-start.28 = (f32[32,1024]{1,0:T(8,128)S(1)}, f32[32,1024]{1,0:T(8,128)S(1)}, u32[]{:S(2)}, u32[]{:S(2)}) collective-permute-start(f32[32,1024]{1,0:T(8,128)S(1)} %add.435), channel_id=1, source_target_pairs={{0,64},{8,72},{16,80},{24,88},{32,96},{40,104},{48,112},{56,120},{... | collective-permute-start | bytes 393224 | tf_op jit(solution)/shard_map/ppermute | solution.py:70
  136.6 56.7 %all-to-all-start.2 = ((bf16[4,512,256]{2,1,0:T(8,128)(2,1)}), bf16[4,512,256]{2,1,0:T(8,128)(2,1)}, u32[]{:S(2)}, u32[]{:S(2)}) async-start(bf16[4,512,256]{2,1,0:T(8,128)(2,1)} %arrange.1), calls=%async_computation.2 | async-start | bytes 2097152 | tf_op jit(solution)/shard_map/all_to_all | solution.py:54
  140.8 53.8 %collective-permute-start.21 = (bf16[512,256]{1,0:T(8,128)(2,1)}, bf16[512,256]{1,0:T(8,128)(2,1)}, u32[]{:S(2)}, u32[]{:S(2)}) collective-permute-start(bf16[512,256]{1,0:T(8,128)(2,1)} %get-tuple-element.57), channel_id=1, source_target_pairs={{0,4},{1,5},{2,6},{3,7},{4,0},{5,1},{6,2},{7,3},{8,12},{9,13},{10,... | collective-permute-start | bytes 786440 | tf_op jit(solution)/shard_map/ppermute | solution.py:384
  143.8 52.3 %collective-permute-start.22 = (bf16[512,256]{1,0:T(8,128)(2,1)}, bf16[512,256]{1,0:T(8,128)(2,1)}, u32[]{:S(2)}, u32[]{:S(2)}) collective-permute-start(bf16[512,256]{1,0:T(8,128)(2,1)} %get-tuple-element.56), channel_id=1, source_target_pairs={{0,2},{1,3},{2,4},{3,5},{4,6},{5,7},{6,0},{7,1},{8,10},{9,11},{10,... | collective-permute-start | bytes 786440 | tf_op jit(solution)/shard_map/ppermute | solution.py:384
  144.2 51.9 %collective-permute-start.23 = (bf16[512,256]{1,0:T(8,128)(2,1)}, bf16[512,256]{1,0:T(8,128)(2,1)}, u32[]{:S(2)}, u32[]{:S(2)}) collective-permute-start(bf16[512,256]{1,0:T(8,128)(2,1)} %get-tuple-element.58), channel_id=1, source_target_pairs={{0,6},{1,7},{2,0},{3,1},{4,2},{5,3},{6,4},{7,5},{8,14},{9,15},{10,... | collective-permute-start | bytes 786440 | tf_op jit(solution)/shard_map/ppermute | solution.py:384
  147.3 37.7 %collective-permute-start.29 = (f32[256,256]{1,0:T(8,128)S(1)}, f32[256,256]{1,0:T(8,128)S(1)}, u32[]{:S(2)}, u32[]{:S(2)}) collective-permute-start(f32[256,256]{1,0:T(8,128)S(1)} %fusion.2), channel_id=1, source_target_pairs={{0,1},{1,0},{2,3},{3,2},{4,5},{5,4},{6,7},{7,6},{8,9},{9,8},{10,11... | collective-permute-start | bytes 786440 | tf_op jit(solution)/shard_map/ppermute | solution.py:60
  184.1 23.3 %collective-permute-start.27 = (bf16[512,1024]{1,0:T(8,128)(2,1)S(1)}, bf16[512,1024]{1,0:T(8,128)(2,1)}, u32[]{:S(2)}, u32[]{:S(2)}) collective-permute-start(bf16[512,1024]{1,0:T(8,128)(2,1)S(1)} %get-tuple-element.62), channel_id=1, source_target_pairs={{0,1},{1,0},{2,3},{3,2},{4,5},{5,4},{6,7},{7,6},{8,9},{9,8},{10,11... | collective-permute-start | bytes 3145736 | tf_op jit(solution)/shard_map/ppermute | solution.py:400
  185.0 7.5 %collective-permute-start.30 = (f32[256,256]{1,0:T(8,128)S(1)}, f32[256,256]{1,0:T(8,128)S(1)}, u32[]{:S(2)}, u32[]{:S(2)}) collective-permute-start(f32[256,256]{1,0:T(8,128)S(1)} %add.465), channel_id=1, source_target_pairs={{0,2},{1,3},{2,0},{3,1},{4,6},{5,7},{6,4},{7,5},{8,10},{9,11},{10,... | collective-permute-start | bytes 786440 | tf_op jit(solution)/shard_map/ppermute | solution.py:61
  193.2 11.7 %collective-permute-start.31 = (f32[256,256]{1,0:T(8,128)}, f32[256,256]{1,0:T(8,128)}, u32[]{:S(2)}, u32[]{:S(2)}) collective-permute-start(f32[256,256]{1,0:T(8,128)} %add.466), channel_id=1, source_target_pairs={{0,4},{1,5},{2,6},{3,7},{4,0},{5,1},{6,2},{7,3},{8,12},{9,13},{10,... | collective-permute-start | bytes 786440 | tf_op jit(solution)/shard_map/ppermute | solution.py:62
  193.3 14.1 %copy-start.2 = (f32[512,1024]{1,0:T(8,128)S(1)}, f32[512,1024]{1,0:T(8,128)}, u32[]{:S(2)}) copy-start(f32[512,1024]{1,0:T(8,128)} %fusion.33) | copy-start | bytes 6291460
  194.7 15.5 %collective-permute-start.20 = (bf16[2,512,256]{2,1,0:T(8,128)(2,1)S(1)}, bf16[2,512,256]{2,1,0:T(8,128)(2,1)S(1)}, u32[]{:S(2)}, u32[]{:S(2)}) collective-permute-start(bf16[2,512,256]{2,1,0:T(8,128)(2,1)S(1)} %slice_select_fusion.1), channel_id=1, source_target_pairs={{0,1},{1,0},{2,3},{3,2},{4,5},{5,4},{6,7},{7,6},{8,9},{9,8},{10,11... | collective-permute-start | bytes 1572872 | tf_op jit(solution)/shard_map/ppermute | solution.py:377
  197.4 14.2 %collective-permute-start.24 = (bf16[512,256]{1,0:T(8,128)(2,1)S(1)}, bf16[512,256]{1,0:T(8,128)(2,1)S(1)}, u32[]{:S(2)}, u32[]{:S(2)}) collective-permute-start(bf16[512,256]{1,0:T(8,128)(2,1)S(1)} %add_convert_fusion.2), channel_id=1, source_target_pairs={{0,1},{2,3},{4,5},{6,7},{8,9},{10,11},{12,13},{14,15},{32,33},{34,... | collective-permute-start | bytes 786440 | tf_op jit(solution)/shard_map/ppermute | solution.py:282
  198.7 12.8 %collective-permute-start.25 = (bf16[512,256]{1,0:T(8,128)(2,1)S(1)}, bf16[512,256]{1,0:T(8,128)(2,1)S(1)}, u32[]{:S(2)}, u32[]{:S(2)}) collective-permute-start(bf16[512,256]{1,0:T(8,128)(2,1)S(1)} %add_convert_fusion.2), channel_id=1, source_target_pairs={{1,4},{5,5},{9,12},{13,13},{17,20},{21,21},{25,28},{29,29},{33,38}... | collective-permute-start | bytes 786440 | tf_op jit(solution)/shard_map/ppermute | solution.py:277
  204.9 6.6 %collective-permute-start.26 = (bf16[512,256]{1,0:T(8,128)(2,1)S(1)}, bf16[512,256]{1,0:T(8,128)(2,1)S(1)}, u32[]{:S(2)}, u32[]{:S(2)}) collective-permute-start(bf16[512,256]{1,0:T(8,128)(2,1)S(1)} %add_convert_fusion.2), channel_id=1, source_target_pairs={{3,4},{7,5},{11,12},{15,13},{19,20},{23,21},{27,28},{31,29},{35,38... | collective-permute-start | bytes 786440 | tf_op jit(solution)/shard_map/ppermute | solution.py:277
  (11 other events, 48.9 us)

commit v4 on v3

--- a/solution.py
+++ b/solution.py
@@ -66,9 +66,16 @@
     return lax.optimization_barrier((value, *events))[0]
 
 
-def with_partner(value, bit, *events):
-    other = lax.ppermute(value, "dp", [(d, d ^ bit) for d in range(16)])
-    return value + after(other, *events)
+def over_side(value, axis):
+    def from_step(step):
+        def move(x, z, y, c):
+            if axis == 0:
+                return ((x + step) % SIDE, z, y, c)
+            return (x, (z + step) % SIDE, y, c)
+
+        return lax.ppermute(value, BOTH, pairs(move))
+
+    return [value, from_step(1), from_step(2), from_step(3)]
 
 
 def total_of(parts):
@@ -142,7 +149,8 @@
     return made if apart else made[0]
 
 
-def arrange_kernel(far_ref, here_ref, beside_ref, out_ref):
+def arrange_kernel(far_ref, here_ref, *refs):
+    besides, out_ref = refs[:2], refs[2]
     part = here_ref.shape[2] // 2
     far = far_ref[0]
 
@@ -153,32 +161,27 @@
     for h in range(2):
         lanes = slice(h * part, (h + 1) * part)
         out_ref[far, :, lanes] = total(here_ref, h * part)
-        out_ref[lax.rem(far + 1, SIDE), :, lanes] = total(beside_ref, 2 * h * part)
-        out_ref[lax.rem(far + 3, SIDE), :, lanes] = total(beside_ref, (2 * h + 1) * part)
+        out_ref[lax.rem(far + 1, SIDE), :, lanes] = total(besides[h], 0)
+        out_ref[lax.rem(far + 3, SIDE), :, lanes] = total(besides[h], part)
         out_ref[lax.rem(far + 2, SIDE), :, lanes] = jnp.zeros_like(here_ref[0, :, lanes])
 
 
-def arrange(far, here, beside):
-    tokens = here.shape[1]
-    rows = tokens // 4
+def arrange(far, *slots):
+    tokens, cols = slots[0].shape[1:]
+    rows = tokens // 2
+    block = pl.BlockSpec((SIDE, rows, cols), lambda i, n: (0, i, 0))
     return pl.pallas_call(
         arrange_kernel,
-        out_shape=jax.ShapeDtypeStruct(here.shape, here.dtype),
+        out_shape=pltpu.HBM(slots[0].shape, slots[0].dtype),
         grid_spec=pltpu.PrefetchScalarGridSpec(
-            num_scalar_prefetch=1,
-            grid=(4,),
-            in_specs=[
-                pl.BlockSpec((SIDE, rows, here.shape[2]), lambda i, n: (0, i, 0)),
-                pl.BlockSpec((SIDE, rows, beside.shape[2]), lambda i, n: (0, i, 0)),
-            ],
-            out_specs=pl.BlockSpec((SIDE, rows, here.shape[2]), lambda i, n: (0, i, 0)),
+            num_scalar_prefetch=1, grid=(2,), in_specs=[block] * 3, out_specs=block
         ),
         compiler_params=pltpu.CompilerParams(vmem_limit_bytes=16 << 20),
         cost_estimate=pl.CostEstimate(
-            flops=4 * here.size, bytes_accessed=2 * (2 * here.size + beside.size), transcendentals=0
+            flops=4 * slots[0].size, bytes_accessed=8 * slots[0].size, transcendentals=0
         ),
         name="arrange",
-    )(far, here, beside)
+    )(far, *slots)
 
 
 def backward_kernel(count, first, last, spots_ref, *refs):
@@ -308,6 +311,7 @@
         shards.append(jnp.concatenate([mine[:, cols], swapped[:, cols]], axis=0))
     logits_a, logits_b, *shards = lax.optimization_barrier((logits_a, logits_b, *shards))
     lines = [ring_gather(shards[h], 0, h) for h in range(2)]
+    arrivals = [lines[0][1], lines[0][3]]
     lines[0] = jnp.stack(lines[0])
     lines[0], *lines[1] = lax.optimization_barrier((lines[0], *lines[1]))
     lines[1] = jnp.stack(lines[1])
@@ -336,19 +340,21 @@
     low_part = lax.dot_general(down_a, attn_out, cols_by_cols, preferred_element_type=f32)
     back_part = lax.dot_general(up_b, grad_cols, cols_by_cols, preferred_element_type=f32)
     totals = jnp.concatenate([low_part, back_part], axis=0)
-    lines[1], totals = lax.optimization_barrier((lines[1], totals))
-    blocks = [ring_gather(lines[h], 1, h) for h in range(2)]
-    totals = over_tensor(totals).astype(bf16)
+    totals = over_tensor(after(totals, *arrivals)).astype(bf16)
     low_bf, back_bf = totals[:rank], totals[rank:]
 
     factor = adapter_scale / (tokens * lax.axis_size("dp"))
     grad_a = jnp.dot(back_bf, attn_out, preferred_element_type=f32)
     grad_b = jnp.dot(low_bf, grad_cols, preferred_element_type=f32)
     both = factor * jnp.concatenate([grad_a, grad_b], axis=0)
-    both = with_partner(both, 1)
+    lines[0], both = lax.optimization_barrier((lines[0], both))
+    both = total_of(over_side(both, 0))
+    both = total_of(over_side(both, 1))
+    lines[1], both = lax.optimization_barrier((lines[1], both))
+    blocks = [ring_gather(lines[h], 1, h) for h in range(2)]
 
     here = [(0, 0), (0, 1)]
-    beside = [(1, 0), (3, 0), (1, 1), (3, 1)]
+    beside = [[(1, 0), (3, 0)], [(1, 1), (3, 1)]]
     across = [(2, 0), (2, 1)]
 
     def take(chunks):
@@ -356,24 +362,27 @@
 
     sent_here = forward(turned, wide, take(here))
     slots_here = exchange(sent_here, "tensor", LANES)
-    grown = backward(after(spots_of(here), sent_here), None, out_grad, take(here))
-    sent_beside = forward(after(turned, grown), wide, take(beside[:2]), places=2)
-    sent_beside = forward(
-        after(turned, both, sent_beside), wide, take(beside[2:]), places=2, into=sent_beside
-    )
-    slots_here, sent_beside = lax.optimization_barrier((slots_here, sent_beside))
-    slots_beside = exchange(sent_beside, "tensor", LANES)
-    both = with_partner(both, 4, sent_beside)
-    grown = backward(after(spots_of(beside), both), grown, out_grad, take(beside))
-    both = with_partner(both, 2, grown)
-    sent = forward(after(turned_here, both), wide, take(across), apart=True)
-    both = with_partner(both, 8, *sent)
-    slots_beside = after(slots_beside, *sent)
-    slots = arrange(far.astype(jnp.int32).reshape(1), slots_here, slots_beside)
-    moved = exchange(slots, "tensor", LANES)
-    both = after(both, slots)
+    sent_first = forward(after(turned, sent_here), wide, take(beside[0]))
+    slots_here, sent_first = lax.optimization_barrier((slots_here, sent_first))
+    slots_first = exchange(sent_first, "tensor", LANES)
     bank_a, logit_grad_a = compose_back(both[:rank], weights_a, picked_a, mixing_a, vector_bank)
     bank_b, logit_grad_b = compose_back(both[rank:], weights_b, picked_b, mixing_b, vector_bank)
+    bank_part = bank_a + bank_b
+    bank_grad = over_tensor(bank_part)
+    chunks = here + beside[0]
+    grown = backward(after(spots_of(chunks), sent_first, bank_part), None, out_grad, take(chunks))
+    sent_second = forward(after(turned, grown, bank_grad), wide, take(beside[1]))
+    slots_first, sent_second = lax.optimization_barrier((slots_first, sent_second))
+    slots_second = exchange(sent_second, "tensor", LANES)
+    grown = backward(after(spots_of(beside[1]), sent_second), grown, out_grad, take(beside[1]))
+    slots = arrange(
+        far.astype(jnp.int32).reshape(1), slots_here, slots_first, after(slots_second, grown)
+    )
+    moved = exchange(slots, "tensor", LANES)
+    sent = forward(after(turned_here, slots), wide, take(across), apart=True)
+    grown, other = backward(
+        after(spots_of(across), *sent), grown, out_grad, take(across), last=True
+    )
     crossed = lax.ppermute(jnp.where(core == 0, slots[2:], moved[:2]), "tensor", SWAP)
     firsts = jnp.where(core == 0, slots[:2], crossed)
     seconds = jnp.where(core == 0, crossed, moved[2:])
@@ -383,10 +392,6 @@
         turns = [(t, (t + 2 * step) % 8) for t in range(8)]
         arrived.append(lax.ppermute(sent[step], "tensor", turns))
     piece = total_of([a.astype(f32) for a in arrived]).astype(bf16)
-    bank_grad = over_tensor(bank_a + bank_b)
-    grown, other = backward(
-        after(spots_of(across), slots), grown, out_grad, take(across), last=True
-    )
     first, place, second = settle(piece, 2, z, core)
     cols = []
     for s in range(2):

time: 215 us -> 232 us (1.079)
  waiting for transfers between devices: 34.8 us -> 56.6 us
  other arithmetic: 25.2 us -> 16 us
  starting transfers between devices: 88.2 us -> 90.9 us
    ppermute x2, waiting for transfers between devices: 6.58 us -> 16.5 us  [over_tensor(): lax.ppermute(value, 'tensor', [(t, t ^ 2) for t in range(8)])]
    all_to_all x3 -> x4, waiting for transfers between devices: 0.01 us -> 7.46 us  [exchange(): lax.all_to_all(value, axis, split_axis=0, concat_axis=0, tiled=True, axis...]
    ppermute x2, starting transfers between devices: 29.6 us -> 22.6 us  [over_tensor(): value = value + lax.ppermute(value, 'tensor', SWAP)]
    ppermute x1, starting transfers between devices: 1.41 us -> 6.4 us  [local(): lax.ppermute(jnp.where(core == 0, slots[2:], moved[:2]), 'tensor', SWAP)]
    ppermute x3, waiting for transfers between devices: 0.01 us -> 4.89 us  [local(): arrived.append(lax.ppermute(sent[step], 'tensor', turns))]
    all_to_all x3 -> x4, starting transfers between devices: 12.2 us -> 16.7 us  [exchange(): lax.all_to_all(value, axis, split_axis=0, concat_axis=0, tiled=True, axis...]
    add x4 -> x2, other arithmetic: 4.82 us -> 0.71 us  [total_of(): return parts[0] + parts[2] + (parts[1] + parts[3])]
    ppermute x12, waiting for transfers between devices: 15.7 us -> 12 us  [shift(): return lax.ppermute(value, BOTH, ring(stage, step))]
  transfers between devices with their start and end apart: 35 -> 38, of which waited for: 9 -> 16; matrix products, arithmetic and copies ran while one was open for 14% -> 12% of each run, Pallas kernels for 21% -> 21%
where the time goes in v4:
time: 232 us; the launch traced here: 229 us
  starting transfers between devices  90.9 us (39%)
  waiting for transfers between devices  56.6 us (24%)
  Pallas kernels  47.4 us (20%)
  other arithmetic  16 us (7%)
  matrix products  12.1 us (5%)
  local copies, waits for them, and re-layouts  4.65 us (2%)
    pallas_call x3, Pallas kernels, backward(): pl.pallas_call(functools.partial(backward_kernel, count, first, last), ou...  25 us
    ppermute x2, starting transfers between devices, over_tensor(): value = value + lax.ppermute(value, 'tensor', SWAP)  22.6 us
    pallas_call x4, Pallas kernels, forward(): pl.pallas_call(functools.partial(forward_kernel, count, many), out_shape=...  19.9 us
    all_to_all x4, starting transfers between devices, exchange(): lax.all_to_all(value, axis, split_axis=0, concat_axis=0, tiled=True, axis...  16.7 us
    ppermute x2, waiting for transfers between devices, over_tensor(): lax.ppermute(value, 'tensor', [(t, t ^ 2) for t in range(8)])  16.5 us
    ppermute x12, starting transfers between devices, shift(): return lax.ppermute(value, BOTH, ring(stage, step))  16.2 us
    ppermute x12, waiting for transfers between devices, shift(): return lax.ppermute(value, BOTH, ring(stage, step))  12 us
    ppermute x6, waiting for transfers between devices, from_step(): return lax.ppermute(value, BOTH, pairs(move))  10 us
  transfers between devices with their start and end apart: 38, of which 16 were waited for; matrix products, arithmetic and copies ran while one was open for 12% of the time, Pallas kernels for 21%

profile of v4, /device:TPU:1, one launch (start us, length us, event | category | flops | bytes accessed | tf_op | source)
XLA Modules:
  0.0 229.0 jit_solution(5607643795592739007)
XLA Ops:
  2.0 1.5 collective-permute-start.1
  3.6 1.6 collective-permute-done.1
  6.3 1.8 collective-permute-start.3
  8.1 2.2 collective-permute-start.2
  10.8 1.5 collective-permute-start.5
  13.0 1.6 fusion.11
  14.7 2.2 collective-permute-done.3
  19.9 2.1 collective-permute-done.9
  22.0 3.0 %collective-permute-start.10 = (f32[32,512]{1,0:T(8,128)S(1)}, f32[32,512]{1,0:T(8,128)S(1)}, u32[]{:S(2)}, u32[]{:S(2)}) collective-permute-start(f32[32,512]{1,0:T(8,128)S(1)} %add.387), channel_id=1, source_target_pairs={{0,4},{1,5},{2,6},{3,7},{4,0},{5,1},{6,2},{7,3},{8,12},{9,13},{10,... | collective-permute-start | bytes 196616 | tf_op jit(solution)/shard_map/ppermute | solution.py:62
  25.0 1.6 collective-permute-start.7
  26.6 1.6 collective-permute-start.4
  30.0 1.5 fusion.9
  31.5 9.8 %collective-permute-done.4 = bf16[2048,128]{1,0:T(8,128)(2,1)S(1)} collective-permute-done((bf16[2048,128]{1,0:T(8,128)(2,1)}, bf16[2048,128]{1,0:T(8,128)(2,1)S(1)}, u32[]{:S(2)}, u32[]{:S(2)}) %collective-permute-start.4) | collective-permute-done | bytes 524320 | tf_op jit(solution)/shard_map/ppermute | solution.py:43
  41.3 2.8 %pad_maximum_fusion.refs_0_ = bf16[4,2048,128]{2,1,0:T(8,128)(2,1)} fusion(bf16[1,2048,128]{2,1,0:T(8,128)(2,1)} %bitcast.5, bf16[1,2048,128]{2,1,0:T(8,128)(2,1)S(1)} %bitcast.111, bf16[1,2048,128]{2,1,0:T(8,128)(2,1)} %bitcast.3, bf16[1,2048,128]{2,1,0:T(8,128)(2,1)S(1)} %bitcast.103), kind=kLoop, calls=%fused_computation.2 | loop fusion | flops 3145728 | bytes 4194304 | tf_op jit(solution)/shard_map/stack | solution.py:315
  44.9 1.8 collective-permute-start.13
  49.4 3.4 %collective-permute-done.11 = f32[32,1024]{1,0:T(8,128)S(1)} collective-permute-done((f32[32,1024]{1,0:T(8,128)S(1)}, f32[32,1024]{1,0:T(8,128)S(1)}, u32[]{:S(2)}, u32[]{:S(2)}) %collective-permute-start.11) | collective-permute-done | bytes 131104 | tf_op jit(solution)/shard_map/ppermute | solution.py:76
  52.9 2.3 collective-permute-start.17
  55.1 4.1 %collective-permute-start = (bf16[512,1024]{1,0:T(8,128)(2,1)S(1)}, bf16[512,1024]{1,0:T(8,128)(2,1)}, u32[]{:S(2)}, u32[]{:S(2)}) collective-permute-start(bf16[512,1024]{1,0:T(8,128)(2,1)S(1)} %copy-done.3), channel_id=1, source_target_pairs={{0,1},{1,0},{2,3},{3,2},{4,5},{5,4},{6,7},{7,6},{8,9},{9,8},{10,11... | collective-permute-start | bytes 3145736 | tf_op jit(solution)/shard_map/ppermute | solution.py:331
  59.2 3.0 %collective-permute-start.16 = (f32[32,1024]{1,0:T(8,128)S(1)}, f32[32,1024]{1,0:T(8,128)S(1)}, u32[]{:S(2)}, u32[]{:S(2)}) collective-permute-start(f32[32,1024]{1,0:T(8,128)S(1)} %add_add_fusion.1), channel_id=1, source_target_pairs={{0,24},{1,25},{2,26},{3,27},{4,28},{5,29},{6,30},{7,31},{8,0},{9,1... | collective-permute-start | bytes 393224 | tf_op jit(solution)/shard_map/ppermute | solution.py:76
  62.5 1.6 pad_maximum_fusion.1.refs_1_
  64.1 2.7 %collective-permute-done.16 = f32[32,1024]{1,0:T(8,128)S(1)} collective-permute-done((f32[32,1024]{1,0:T(8,128)S(1)}, f32[32,1024]{1,0:T(8,128)S(1)}, u32[]{:S(2)}, u32[]{:S(2)}) %collective-permute-start.16) | collective-permute-done | bytes 131104 | tf_op jit(solution)/shard_map/ppermute | solution.py:76
  66.8 2.2 collective-permute-done.14
  72.5 5.0 %forward.4 = bf16[4,512,256]{2,1,0:T(8,128)(2,1)} custom-call(s32[1]{0:T(128)} %bitcast.1.start_ref, bf16[512,2048]{1,0:T(8,128)(2,1)S(1)} %constant_dynamic-update-slice_fusion.wide_ref, bf16[4,2048,128]{2,1,0:T(8,128)(2,1)} %pad_maximum_fusion.refs_0_, bf16[4,2048,128]{2,1,0:T(8,128)(2,1)} %pad_maximum_fusion.1.refs_1_), custom_call_target="tpu_custom_call" | custom-call | flops 268435456 | bytes 524288 | tf_op jit(solution)/shard_map/forward/pallas_call | solution.py:126
  77.5 3.7 %all-to-all-start = ((bf16[4,512,256]{2,1,0:T(8,128)(2,1)}), bf16[4,512,256]{2,1,0:T(8,128)(2,1)S(1)}, u32[]{:S(2)}, u32[]{:S(2)}) async-start(bf16[4,512,256]{2,1,0:T(8,128)(2,1)} %forward.4), calls=%async_computation | async-start | bytes 2097152 | tf_op jit(solution)/shard_map/all_to_all | solution.py:54
  84.6 21.9 %collective-permute-start.19 = (f32[256,256]{1,0:T(8,128)}, f32[256,256]{1,0:T(8,128)}, u32[]{:S(2)}, u32[]{:S(2)}) collective-permute-start(f32[256,256]{1,0:T(8,128)} %fusion.2), channel_id=1, source_target_pairs={{0,1},{1,0},{2,3},{3,2},{4,5},{5,4},{6,7},{7,6},{8,9},{9,8},{10,11... | collective-permute-start | bytes 786440 | tf_op jit(solution)/shard_map/ppermute | solution.py:60
  106.4 4.9 %forward.5 = bf16[4,512,256]{2,1,0:T(8,128)(2,1)} custom-call(s32[1]{0:T(128)} %bitcast.1.start_ref, bf16[512,2048]{1,0:T(8,128)(2,1)S(1)} %constant_dynamic-update-slice_fusion.wide_ref, bf16[4,2048,128]{2,1,0:T(8,128)(2,1)} %collective-permute-done.17.refs_0_.refs_2_, bf16[4,2048,128]{2,1,0:T(8,128)(2,1)} %collective-permute-done.18.refs_1_.refs_3_), custom_call_target="tpu_custom_call" | custom-call | flops 268435456 | bytes 524288 | tf_op jit(solution)/shard_map/forward/pallas_call | solution.py:126
  111.4 4.3 %all-to-all-start.1 = ((bf16[4,512,256]{2,1,0:T(8,128)(2,1)}), bf16[4,512,256]{2,1,0:T(8,128)(2,1)}, u32[]{:S(2)}, u32[]{:S(2)}) async-start(bf16[4,512,256]{2,1,0:T(8,128)(2,1)} %forward.5), calls=%async_computation.1 | async-start | bytes 2097152 | tf_op jit(solution)/shard_map/all_to_all | solution.py:54
  116.8 1.5 collective-permute-start.20
  118.3 14.4 %collective-permute-done.20 = f32[256,256]{1,0:T(8,128)S(1)} collective-permute-done((f32[256,256]{1,0:T(8,128)S(1)}, f32[256,256]{1,0:T(8,128)S(1)}, u32[]{:S(2)}, u32[]{:S(2)}) %collective-permute-start.20) | collective-permute-done | bytes 262176 | tf_op jit(solution)/shard_map/ppermute | solution.py:61
  133.5 2.0 collective-permute-start.21
  135.4 2.7 %collective-permute-start.26 = (bf16[4,2048,128]{2,1,0:T(8,128)(2,1)}, bf16[4,2048,128]{2,1,0:T(8,128)(2,1)}, u32[]{:S(2)}, u32[]{:S(2)}) collective-permute-start(bf16[4,2048,128]{2,1,0:T(8,128)(2,1)} %collective-permute-done.22.refs_0_), channel_id=1, source_target_pairs={{0,24},{1,97},{2,26},{3,99},{4,28},{5,101},{6,30},{7,103},{8,0},{9... | collective-permute-start | bytes 6291464 | tf_op jit(solution)/shard_map/ppermute | solution.py:43
  138.2 2.3 collective-permute-done.21
  140.5 1.8 add.438
  142.3 9.9 %backward.3.refs_10_ = f32[512,2048]{1,0:T(8,128)} custom-call(s32[16]{0:T(128)S(1)} %stack.161.spots_ref, bf16[4,2048,128]{2,1,0:T(8,128)(2,1)} %pad_maximum_fusion.refs_0_, bf16[4,2048,128]{2,1,0:T(8,128)(2,1)} %pad_maximum_fusion.1.refs_1_, bf16[4,2048,128]{2,1,0:T(8,128)(2,1)} %collective-permute-done.17.refs_0_.refs_2_, ...), custom_call_target="tpu_custom_call" | custom-call | flops 536870912 | bytes 1048576 | tf_op jit(solution)/shard_map/backward/pallas_call | solution.py:232
  152.2 5.0 %forward.6 = bf16[4,512,256]{2,1,0:T(8,128)(2,1)} custom-call(s32[1]{0:T(128)} %bitcast.1.start_ref, bf16[512,2048]{1,0:T(8,128)(2,1)S(1)} %constant_dynamic-update-slice_fusion.wide_ref, bf16[4,2048,128]{2,1,0:T(8,128)(2,1)} %collective-permute-done.22.refs_0_, bf16[4,2048,128]{2,1,0:T(8,128)(2,1)} %collective-permute-done.23.refs_1_), custom_call_target="tpu_custom_call" | custom-call | flops 268435456 | bytes 524288 | tf_op jit(solution)/shard_map/forward/pallas_call | solution.py:126
  157.2 4.3 %all-to-all-start.2 = ((bf16[4,512,256]{2,1,0:T(8,128)(2,1)}), bf16[4,512,256]{2,1,0:T(8,128)(2,1)}, u32[]{:S(2)}, u32[]{:S(2)}) async-start(bf16[4,512,256]{2,1,0:T(8,128)(2,1)} %forward.6), calls=%async_computation.2 | async-start | bytes 2097152 | tf_op jit(solution)/shard_map/all_to_all | solution.py:54
  161.7 2.5 %fusion.33 = f32[512,1024]{1,0:T(8,128)} fusion(bf16[16,1024]{1,0:T(8,128)(2,1)S(1)} %bitcast.113, bf16[32,512]{1,0:T(8,128)(2,1)} %copy-done.10), kind=kOutput, calls=%fused_computation.65 | convolution fusion | flops 16777216 | bytes 2146304 | tf_op jit(solution)/shard_map/dot_general | solution.py:409
  164.2 8.1 %backward.4.refs_10_ = f32[512,2048]{1,0:T(8,128)} custom-call(s32[8]{0:T(128)S(1)} %stack.170.spots_ref, bf16[4,2048,128]{2,1,0:T(8,128)(2,1)} %collective-permute-done.22.refs_0_, bf16[4,2048,128]{2,1,0:T(8,128)(2,1)} %collective-permute-done.23.refs_1_, bf16[512,8192]{1,0:T(8,128)(2,1)} %refs_9_.5, ...), custom_call_target="tpu_custom_call", output_to_operand_aliasing={{}: (11, {})} | custom-call | flops 268435456 | bytes 524288 | tf_op jit(solution)/shard_map/backward/pallas_call | solution.py:232
  172.3 2.6 %arrange.1 = bf16[4,512,256]{2,1,0:T(8,128)(2,1)} custom-call(s32[1]{0:T(128)} %bitcast.far_ref, bf16[4,512,256]{2,1,0:T(8,128)(2,1)S(1)} %all-to-all-done.here_ref, bf16[4,512,256]{2,1,0:T(8,128)(2,1)} %all-to-all-done.1.refs_0_, bf16[4,512,256]{2,1,0:T(8,128)(2,1)} %all-to-all-done.2.refs_1_), custom_call_target="tpu_custom_call" | custom-call | flops 2097152 | bytes 4194304 | tf_op jit(solution)/shard_map/arrange/pallas_call | solution.py:173
  174.9 4.4 %all-to-all-start.3 = ((bf16[4,512,256]{2,1,0:T(8,128)(2,1)}), bf16[4,512,256]{2,1,0:T(8,128)(2,1)}, u32[]{:S(2)}, u32[]{:S(2)}) async-start(bf16[4,512,256]{2,1,0:T(8,128)(2,1)} %arrange.1), calls=%async_computation.3 | async-start | bytes 2097152 | tf_op jit(solution)/shard_map/all_to_all | solution.py:54
  181.7 7.4 %all-to-all-done.3 = bf16[4,512,256]{2,1,0:T(8,128)(2,1)} async-done(((bf16[4,512,256]{2,1,0:T(8,128)(2,1)}), bf16[4,512,256]{2,1,0:T(8,128)(2,1)}, u32[]{:S(2)}, u32[]{:S(2)}) %all-to-all-start.3) | async-done | bytes 1048608 | tf_op jit(solution)/shard_map/all_to_all | solution.py:54
  190.3 6.4 %collective-permute-start.24 = (bf16[2,512,256]{2,1,0:T(8,128)(2,1)S(1)}, bf16[2,512,256]{2,1,0:T(8,128)(2,1)S(1)}, u32[]{:S(2)}, u32[]{:S(2)}) collective-permute-start(bf16[2,512,256]{2,1,0:T(8,128)(2,1)S(1)} %slice_select_fusion.1), channel_id=1, source_target_pairs={{0,1},{1,0},{2,3},{3,2},{4,5},{5,4},{6,7},{7,6},{8,9},{9,8},{10,11... | collective-permute-start | bytes 1572872 | tf_op jit(solution)/shard_map/ppermute | solution.py:386
  196.7 5.0 %forward.7 = (bf16[512,256]{1,0:T(8,128)(2,1)}, bf16[512,256]{1,0:T(8,128)(2,1)}, bf16[512,256]{1,0:T(8,128)(2,1)}, bf16[512,256]{1,0:T(8,128)(2,1)}) custom-call(s32[1]{0:T(128)} %bitcast.38.start_ref, bf16[512,2048]{1,0:T(8,128)(2,1)S(1)} %constant_dynamic-update-slice_fusion.wide_ref, bf16[4,2048,128]{2,1,0:T(8,128)(2,1)} %collective-permute-done.25.refs_0_, ...), custom_call_target="tpu_custom_call" | custom-call | flops 268435456 | bytes 524288 | tf_op jit(solution)/shard_map/forward/pallas_call | solution.py:126
  204.7 7.0 %backward.5 = (f32[512,1024]{1,0:T(8,128)S(1)}, bf16[512,1024]{1,0:T(8,128)(2,1)S(1)}) custom-call(s32[8]{0:T(128)S(1)} %stack.179.spots_ref, bf16[4,2048,128]{2,1,0:T(8,128)(2,1)} %collective-permute-done.25.refs_0_, bf16[4,2048,128]{2,1,0:T(8,128)(2,1)} %collective-permute-done.26.refs_1_, bf16[512,8192]{1,0:T(8,128)(2,1)} %refs_9_.5, ...), custom_call_target="tpu_custom_call" | custom-call | flops 268435456 | bytes 524288 | tf_op jit(solution)/shard_map/backward/pallas_call | solution.py:232
  212.4 4.9 %collective-permute-done.28 = bf16[512,256]{1,0:T(8,128)(2,1)S(1)} collective-permute-done((bf16[512,256]{1,0:T(8,128)(2,1)}, bf16[512,256]{1,0:T(8,128)(2,1)S(1)}, u32[]{:S(2)}, u32[]{:S(2)}) %collective-permute-start.28) | collective-permute-done | bytes 262176 | tf_op jit(solution)/shard_map/ppermute | solution.py:393
  217.4 3.8 %collective-permute-start.31 = (bf16[512,256]{1,0:T(8,128)(2,1)S(1)}, bf16[512,256]{1,0:T(8,128)(2,1)S(1)}, u32[]{:S(2)}, u32[]{:S(2)}) collective-permute-start(bf16[512,256]{1,0:T(8,128)(2,1)S(1)} %add_convert_fusion.2), channel_id=1, source_target_pairs={{1,4},{5,5},{9,12},{13,13},{17,20},{21,21},{25,28},{29,29},{33,38}... | collective-permute-start | bytes 786440 | tf_op jit(solution)/shard_map/ppermute | solution.py:280
  225.4 1.4 add_convert_fusion.1
  227.4 1.6 add_convert_fusion
  (124 shorter events, 33.3 us)
Async XLA Ops:
  0.6 9.8 %copy-start = (f32[256,256]{1,0:T(8,128)S(1)}, f32[256,256]{1,0:T(8,128)}, u32[]{:S(2)}) copy-start(f32[256,256]{1,0:T(8,128)} %param.10) | copy-start | bytes 786436
  2.0 3.2 %collective-permute-start.1 = (bf16[1024,256]{1,0:T(8,128)(2,1)S(1)}, bf16[1024,256]{1,0:T(8,128)(2,1)}, u32[]{:S(2)}, u32[]{:S(2)}) collective-permute-start(bf16[1024,256]{1,0:T(8,128)(2,1)S(1)} %get-tuple-element.70), channel_id=1, source_target_pairs={{0,1},{1,0},{2,3},{3,2},{4,5},{5,4},{6,7},{7,6},{8,9},{9,8},{10,11... | collective-permute-start | bytes 1572872 | tf_op jit(solution)/shard_map/ppermute | solution.py:307
  3.5 8.7 %copy-start.17 = (f32[16,4,2]{0,2,1:T(2,128)S(1)}, f32[16,4,2]{0,2,1:T(2,128)}, u32[]{:S(2)}) copy-start(f32[16,4,2]{0,2,1:T(2,128)} %param.11) | copy-start | bytes 1540
  3.5 8.7 %copy-start.14 = (s32[16,4,2]{0,2,1:T(2,128)S(1)}, s32[16,4,2]{0,2,1:T(2,128)}, u32[]{:S(2)}) copy-start(s32[16,4,2]{0,2,1:T(2,128)} %param.12) | copy-start | bytes 1540
  3.5 9.1 %copy-start.3 = (bf16[512,1024]{1,0:T(8,128)(2,1)S(1)}, bf16[512,1024]{1,0:T(8,128)(2,1)}, u32[]{:S(2)}) copy-start(bf16[512,1024]{1,0:T(8,128)(2,1)} %param.8) | copy-start | bytes 3145732
  6.3 10.6 %collective-permute-start.3 = (bf16[2048,128]{1,0:T(8,128)(2,1)S(1)}, bf16[2048,128]{1,0:T(8,128)(2,1)}, u32[]{:S(2)}, u32[]{:S(2)}) collective-permute-start(bf16[2048,128]{1,0:T(8,128)(2,1)S(1)} %get-tuple-element.36), channel_id=1, source_target_pairs={{0,32},{1,9},{2,34},{3,11},{4,36},{5,13},{6,38},{7,15},{8,40},{9,1... | collective-permute-start | bytes 1572872 | tf_op jit(solution)/shard_map/ppermute | solution.py:43
  8.1 8.8 %collective-permute-start.2 = (bf16[2048,128]{1,0:T(8,128)(2,1)S(1)}, bf16[2048,128]{1,0:T(8,128)(2,1)}, u32[]{:S(2)}, u32[]{:S(2)}) collective-permute-start(bf16[2048,128]{1,0:T(8,128)(2,1)S(1)} %get-tuple-element.36), channel_id=1, source_target_pairs={{0,96},{1,25},{2,98},{3,27},{4,100},{5,29},{6,102},{7,31},{8,104},... | collective-permute-start | bytes 1572872 | tf_op jit(solution)/shard_map/ppermute | solution.py:43
  10.5 19.2 %copy-start.5 = (f32[16,4,256]{2,0,1:T(8,128)}, f32[16,4,256]{2,0,1:T(8,128)S(1)}, u32[]{:S(2)}) copy-start(f32[16,4,256]{2,0,1:T(8,128)S(1)} %select_reduce_fusion.2) | copy-start | bytes 196612
  10.7 18.6 %copy-start.12 = (bf16[4,2,8,256]{3,2,0,1:T(8,128)(2,1)}, bf16[4,2,8,256]{3,2,0,1:T(8,128)(2,1)S(1)}, u32[]{:S(2)}) copy-start(bf16[4,2,8,256]{3,2,0,1:T(8,128)(2,1)S(1)} %copy.45) | copy-start | bytes 98308
  10.8 17.5 %collective-permute-start.5 = (bf16[2048,128]{1,0:T(8,128)(2,1)S(1)}, bf16[2048,128]{1,0:T(8,128)(2,1)S(1)}, u32[]{:S(2)}, u32[]{:S(2)}) collective-permute-start(bf16[2048,128]{1,0:T(8,128)(2,1)S(1)} %get-tuple-element.43), channel_id=1, source_target_pairs={{0,96},{1,25},{2,98},{3,27},{4,100},{5,29},{6,102},{7,31},{8,104},... | collective-permute-start | bytes 1572872 | tf_op jit(solution)/shard_map/ppermute | solution.py:43
  12.6 17.0 %copy-start.7 = (bf16[4,2,8,256]{3,2,0,1:T(8,128)(2,1)}, bf16[4,2,8,256]{3,2,0,1:T(8,128)(2,1)S(1)}, u32[]{:S(2)}) copy-start(bf16[4,2,8,256]{3,2,0,1:T(8,128)(2,1)S(1)} %copy.44) | copy-start | bytes 98308
  16.9 1.6 collective-permute-start.8
  18.5 3.5 %collective-permute-start.9 = (f32[32,512]{1,0:T(8,128)S(1)}, f32[32,512]{1,0:T(8,128)S(1)}, u32[]{:S(2)}, u32[]{:S(2)}) collective-permute-start(f32[32,512]{1,0:T(8,128)S(1)} %add.386), channel_id=1, source_target_pairs={{0,2},{1,3},{2,0},{3,1},{4,6},{5,7},{6,4},{7,5},{8,10},{9,11},{10,... | collective-permute-start | bytes 196616 | tf_op jit(solution)/shard_map/ppermute | solution.py:61
  22.0 7.3 %collective-permute-start.10 = (f32[32,512]{1,0:T(8,128)S(1)}, f32[32,512]{1,0:T(8,128)S(1)}, u32[]{:S(2)}, u32[]{:S(2)}) collective-permute-start(f32[32,512]{1,0:T(8,128)S(1)} %add.387), channel_id=1, source_target_pairs={{0,4},{1,5},{2,6},{3,7},{4,0},{5,1},{6,2},{7,3},{8,12},{9,13},{10,... | collective-permute-start | bytes 196616 | tf_op jit(solution)/shard_map/ppermute | solution.py:62
  25.0 19.0 %collective-permute-start.7 = (bf16[2048,128]{1,0:T(8,128)(2,1)S(1)}, bf16[2048,128]{1,0:T(8,128)(2,1)S(1)}, u32[]{:S(2)}, u32[]{:S(2)}) collective-permute-start(bf16[2048,128]{1,0:T(8,128)(2,1)S(1)} %get-tuple-element.43), channel_id=1, source_target_pairs={{0,32},{1,9},{2,34},{3,11},{4,36},{5,13},{6,38},{7,15},{8,40},{9,1... | collective-permute-start | bytes 1572872 | tf_op jit(solution)/shard_map/ppermute | solution.py:43
  26.6 14.6 %collective-permute-start.4 = (bf16[2048,128]{1,0:T(8,128)(2,1)}, bf16[2048,128]{1,0:T(8,128)(2,1)S(1)}, u32[]{:S(2)}, u32[]{:S(2)}) collective-permute-start(bf16[2048,128]{1,0:T(8,128)(2,1)} %collective-permute-done.3), channel_id=1, source_target_pairs={{0,32},{1,9},{2,34},{3,11},{4,36},{5,13},{6,38},{7,15},{8,40},{9,1... | collective-permute-start | bytes 1572872 | tf_op jit(solution)/shard_map/ppermute | solution.py:43
  28.3 15.7 %collective-permute-start.6 = (bf16[2048,128]{1,0:T(8,128)(2,1)S(1)}, bf16[2048,128]{1,0:T(8,128)(2,1)S(1)}, u32[]{:S(2)}, u32[]{:S(2)}) collective-permute-start(bf16[2048,128]{1,0:T(8,128)(2,1)S(1)} %collective-permute-done.5), channel_id=1, source_target_pairs={{0,96},{1,25},{2,98},{3,27},{4,100},{5,29},{6,102},{7,31},{8,104},... | collective-permute-start | bytes 1572872 | tf_op jit(solution)/shard_map/ppermute | solution.py:43
  44.0 5.0 %collective-permute-start.12 = (f32[32,1024]{1,0:T(8,128)S(1)}, f32[32,1024]{1,0:T(8,128)S(1)}, u32[]{:S(2)}, u32[]{:S(2)}) collective-permute-start(f32[32,1024]{1,0:T(8,128)S(1)} %maximum_multiply_fusion), channel_id=1, source_target_pairs={{0,32},{1,33},{2,34},{3,35},{4,36},{5,37},{6,38},{7,39},{8,40},{9,... | collective-permute-start | bytes 393224 | tf_op jit(solution)/shard_map/ppermute | solution.py:76
  44.9 4.4 %collective-permute-start.13 = (f32[32,1024]{1,0:T(8,128)S(1)}, f32[32,1024]{1,0:T(8,128)S(1)}, u32[]{:S(2)}, u32[]{:S(2)}) collective-permute-start(f32[32,1024]{1,0:T(8,128)S(1)} %maximum_multiply_fusion), channel_id=1, source_target_pairs={{0,96},{1,97},{2,98},{3,99},{4,100},{5,101},{6,102},{7,103},{8,104... | collective-permute-start | bytes 393224 | tf_op jit(solution)/shard_map/ppermute | solution.py:76
  46.7 6.0 %collective-permute-start.11 = (f32[32,1024]{1,0:T(8,128)S(1)}, f32[32,1024]{1,0:T(8,128)S(1)}, u32[]{:S(2)}, u32[]{:S(2)}) collective-permute-start(f32[32,1024]{1,0:T(8,128)S(1)} %maximum_multiply_fusion), channel_id=1, source_target_pairs={{0,64},{1,65},{2,66},{3,67},{4,68},{5,69},{6,70},{7,71},{8,72},{9,... | collective-permute-start | bytes 393224 | tf_op jit(solution)/shard_map/ppermute | solution.py:76
  52.8 9.4 %collective-permute-start.15 = (f32[32,1024]{1,0:T(8,128)S(1)}, f32[32,1024]{1,0:T(8,128)S(1)}, u32[]{:S(2)}, u32[]{:S(2)}) collective-permute-start(f32[32,1024]{1,0:T(8,128)S(1)} %add_add_fusion.1), channel_id=1, source_target_pairs={{0,8},{1,9},{2,10},{3,11},{4,12},{5,13},{6,14},{7,15},{8,16},{9,17... | collective-permute-start | bytes 393224 | tf_op jit(solution)/shard_map/ppermute | solution.py:76
  52.9 53.5 %collective-permute-start.17 = (bf16[4,2048,128]{2,1,0:T(8,128)(2,1)}, bf16[4,2048,128]{2,1,0:T(8,128)(2,1)}, u32[]{:S(2)}, u32[]{:S(2)}) collective-permute-start(bf16[4,2048,128]{2,1,0:T(8,128)(2,1)} %pad_maximum_fusion.refs_0_), channel_id=1, source_target_pairs={{0,24},{1,97},{2,26},{3,99},{4,28},{5,101},{6,30},{7,103},{8,0},{9... | collective-permute-start | bytes 6291464 | tf_op jit(solution)/shard_map/ppermute | solution.py:43
  55.1 51.3 %collective-permute-start.18 = (bf16[4,2048,128]{2,1,0:T(8,128)(2,1)}, bf16[4,2048,128]{2,1,0:T(8,128)(2,1)}, u32[]{:S(2)}, u32[]{:S(2)}) collective-permute-start(bf16[4,2048,128]{2,1,0:T(8,128)(2,1)} %pad_maximum_fusion.refs_0_), channel_id=1, source_target_pairs={{0,8},{1,33},{2,10},{3,35},{4,12},{5,37},{6,14},{7,39},{8,16},{9,4... | collective-permute-start | bytes 6291464 | tf_op jit(solution)/shard_map/ppermute | solution.py:43
  55.1 16.1 %collective-permute-start = (bf16[512,1024]{1,0:T(8,128)(2,1)S(1)}, bf16[512,1024]{1,0:T(8,128)(2,1)}, u32[]{:S(2)}, u32[]{:S(2)}) collective-permute-start(bf16[512,1024]{1,0:T(8,128)(2,1)S(1)} %copy-done.3), channel_id=1, source_target_pairs={{0,1},{1,0},{2,3},{3,2},{4,5},{5,4},{6,7},{7,6},{8,9},{9,8},{10,11... | collective-permute-start | bytes 3145736 | tf_op jit(solution)/shard_map/ppermute | solution.py:331
  59.2 7.6 %collective-permute-start.16 = (f32[32,1024]{1,0:T(8,128)S(1)}, f32[32,1024]{1,0:T(8,128)S(1)}, u32[]{:S(2)}, u32[]{:S(2)}) collective-permute-start(f32[32,1024]{1,0:T(8,128)S(1)} %add_add_fusion.1), channel_id=1, source_target_pairs={{0,24},{1,25},{2,26},{3,27},{4,28},{5,29},{6,30},{7,31},{8,0},{9,1... | collective-permute-start | bytes 393224 | tf_op jit(solution)/shard_map/ppermute | solution.py:76
  62.2 6.8 %collective-permute-start.14 = (f32[32,1024]{1,0:T(8,128)S(1)}, f32[32,1024]{1,0:T(8,128)S(1)}, u32[]{:S(2)}, u32[]{:S(2)}) collective-permute-start(f32[32,1024]{1,0:T(8,128)S(1)} %add_add_fusion.1), channel_id=1, source_target_pairs={{0,16},{1,17},{2,18},{3,19},{4,20},{5,21},{6,22},{7,23},{8,24},{9,... | collective-permute-start | bytes 393224 | tf_op jit(solution)/shard_map/ppermute | solution.py:76
  69.7 65.8 %collective-permute-start.22 = (bf16[4,2048,128]{2,1,0:T(8,128)(2,1)}, bf16[4,2048,128]{2,1,0:T(8,128)(2,1)}, u32[]{:S(2)}, u32[]{:S(2)}) collective-permute-start(bf16[4,2048,128]{2,1,0:T(8,128)(2,1)} %pad_maximum_fusion.1.refs_1_), channel_id=1, source_target_pairs={{0,24},{1,97},{2,26},{3,99},{4,28},{5,101},{6,30},{7,103},{8,0},{9... | collective-permute-start | bytes 6291464 | tf_op jit(solution)/shard_map/ppermute | solution.py:43
  70.7 81.4 %collective-permute-start.23 = (bf16[4,2048,128]{2,1,0:T(8,128)(2,1)}, bf16[4,2048,128]{2,1,0:T(8,128)(2,1)}, u32[]{:S(2)}, u32[]{:S(2)}) collective-permute-start(bf16[4,2048,128]{2,1,0:T(8,128)(2,1)} %pad_maximum_fusion.1.refs_1_), channel_id=1, source_target_pairs={{0,8},{1,33},{2,10},{3,35},{4,12},{5,37},{6,14},{7,39},{8,16},{9,4... | collective-permute-start | bytes 6291464 | tf_op jit(solution)/shard_map/ppermute | solution.py:43
  77.5 33.8 %all-to-all-start = ((bf16[4,512,256]{2,1,0:T(8,128)(2,1)}), bf16[4,512,256]{2,1,0:T(8,128)(2,1)S(1)}, u32[]{:S(2)}, u32[]{:S(2)}) async-start(bf16[4,512,256]{2,1,0:T(8,128)(2,1)} %forward.4), calls=%async_computation | async-start | bytes 2097152 | tf_op jit(solution)/shard_map/all_to_all | solution.py:54
  84.6 31.1 %collective-permute-start.19 = (f32[256,256]{1,0:T(8,128)}, f32[256,256]{1,0:T(8,128)}, u32[]{:S(2)}, u32[]{:S(2)}) collective-permute-start(f32[256,256]{1,0:T(8,128)} %fusion.2), channel_id=1, source_target_pairs={{0,1},{1,0},{2,3},{3,2},{4,5},{5,4},{6,7},{7,6},{8,9},{9,8},{10,11... | collective-permute-start | bytes 786440 | tf_op jit(solution)/shard_map/ppermute | solution.py:60
  111.4 45.8 %all-to-all-start.1 = ((bf16[4,512,256]{2,1,0:T(8,128)(2,1)}), bf16[4,512,256]{2,1,0:T(8,128)(2,1)}, u32[]{:S(2)}, u32[]{:S(2)}) async-start(bf16[4,512,256]{2,1,0:T(8,128)(2,1)} %forward.5), calls=%async_computation.1 | async-start | bytes 2097152 | tf_op jit(solution)/shard_map/all_to_all | solution.py:54
  116.8 16.0 %collective-permute-start.20 = (f32[256,256]{1,0:T(8,128)S(1)}, f32[256,256]{1,0:T(8,128)S(1)}, u32[]{:S(2)}, u32[]{:S(2)}) collective-permute-start(f32[256,256]{1,0:T(8,128)S(1)} %add.436), channel_id=1, source_target_pairs={{0,2},{1,3},{2,0},{3,1},{4,6},{5,7},{6,4},{7,5},{8,10},{9,11},{10,... | collective-permute-start | bytes 786440 | tf_op jit(solution)/shard_map/ppermute | solution.py:61
  133.5 7.0 %collective-permute-start.21 = (f32[256,256]{1,0:T(8,128)}, f32[256,256]{1,0:T(8,128)}, u32[]{:S(2)}, u32[]{:S(2)}) collective-permute-start(f32[256,256]{1,0:T(8,128)} %add.437), channel_id=1, source_target_pairs={{0,4},{1,5},{2,6},{3,7},{4,0},{5,1},{6,2},{7,3},{8,12},{9,13},{10,... | collective-permute-start | bytes 786440 | tf_op jit(solution)/shard_map/ppermute | solution.py:62
  135.4 61.2 %collective-permute-start.25 = (bf16[4,2048,128]{2,1,0:T(8,128)(2,1)}, bf16[4,2048,128]{2,1,0:T(8,128)(2,1)}, u32[]{:S(2)}, u32[]{:S(2)}) collective-permute-start(bf16[4,2048,128]{2,1,0:T(8,128)(2,1)} %collective-permute-done.18.refs_1_.refs_3_), channel_id=1, source_target_pairs={{0,8},{1,33},{2,10},{3,35},{4,12},{5,37},{6,14},{7,39},{8,16},{9,4... | collective-permute-start | bytes 6291464 | tf_op jit(solution)/shard_map/ppermute | solution.py:43
  135.4 61.2 %collective-permute-start.26 = (bf16[4,2048,128]{2,1,0:T(8,128)(2,1)}, bf16[4,2048,128]{2,1,0:T(8,128)(2,1)}, u32[]{:S(2)}, u32[]{:S(2)}) collective-permute-start(bf16[4,2048,128]{2,1,0:T(8,128)(2,1)} %collective-permute-done.22.refs_0_), channel_id=1, source_target_pairs={{0,24},{1,97},{2,26},{3,99},{4,28},{5,101},{6,30},{7,103},{8,0},{9... | collective-permute-start | bytes 6291464 | tf_op jit(solution)/shard_map/ppermute | solution.py:43
  157.2 15.2 %all-to-all-start.2 = ((bf16[4,512,256]{2,1,0:T(8,128)(2,1)}), bf16[4,512,256]{2,1,0:T(8,128)(2,1)}, u32[]{:S(2)}, u32[]{:S(2)}) async-start(bf16[4,512,256]{2,1,0:T(8,128)(2,1)} %forward.6), calls=%async_computation.2 | async-start | bytes 2097152 | tf_op jit(solution)/shard_map/all_to_all | solution.py:54
  174.9 14.2 %copy-start.1 = (bf16[4,512,256]{2,1,0:T(8,128)(2,1)S(1)}, bf16[4,512,256]{2,1,0:T(8,128)(2,1)}, u32[]{:S(2)}) copy-start(bf16[4,512,256]{2,1,0:T(8,128)(2,1)} %arrange.1) | copy-start | bytes 3145732
  174.9 14.2 %all-to-all-start.3 = ((bf16[4,512,256]{2,1,0:T(8,128)(2,1)}), bf16[4,512,256]{2,1,0:T(8,128)(2,1)}, u32[]{:S(2)}, u32[]{:S(2)}) async-start(bf16[4,512,256]{2,1,0:T(8,128)(2,1)} %arrange.1), calls=%async_computation.3 | async-start | bytes 2097152 | tf_op jit(solution)/shard_map/all_to_all | solution.py:54
  190.3 32.9 %collective-permute-start.24 = (bf16[2,512,256]{2,1,0:T(8,128)(2,1)S(1)}, bf16[2,512,256]{2,1,0:T(8,128)(2,1)S(1)}, u32[]{:S(2)}, u32[]{:S(2)}) collective-permute-start(bf16[2,512,256]{2,1,0:T(8,128)(2,1)S(1)} %slice_select_fusion.1), channel_id=1, source_target_pairs={{0,1},{1,0},{2,3},{3,2},{4,5},{5,4},{6,7},{7,6},{8,9},{9,8},{10,11... | collective-permute-start | bytes 1572872 | tf_op jit(solution)/shard_map/ppermute | solution.py:386
  201.7 10.7 %collective-permute-start.29 = (bf16[512,256]{1,0:T(8,128)(2,1)}, bf16[512,256]{1,0:T(8,128)(2,1)S(1)}, u32[]{:S(2)}, u32[]{:S(2)}) collective-permute-start(bf16[512,256]{1,0:T(8,128)(2,1)} %get-tuple-element.63), channel_id=1, source_target_pairs={{0,6},{1,7},{2,0},{3,1},{4,2},{5,3},{6,4},{7,5},{8,14},{9,15},{10,... | collective-permute-start | bytes 786440 | tf_op jit(solution)/shard_map/ppermute | solution.py:393
  202.6 14.6 %collective-permute-start.28 = (bf16[512,256]{1,0:T(8,128)(2,1)}, bf16[512,256]{1,0:T(8,128)(2,1)S(1)}, u32[]{:S(2)}, u32[]{:S(2)}) collective-permute-start(bf16[512,256]{1,0:T(8,128)(2,1)} %get-tuple-element.62), channel_id=1, source_target_pairs={{0,2},{1,3},{2,4},{3,5},{4,6},{5,7},{6,0},{7,1},{8,10},{9,11},{10,... | collective-permute-start | bytes 786440 | tf_op jit(solution)/shard_map/ppermute | solution.py:393
  203.2 14.0 %collective-permute-start.27 = (bf16[512,256]{1,0:T(8,128)(2,1)}, bf16[512,256]{1,0:T(8,128)(2,1)S(1)}, u32[]{:S(2)}, u32[]{:S(2)}) collective-permute-start(bf16[512,256]{1,0:T(8,128)(2,1)} %get-tuple-element.61), channel_id=1, source_target_pairs={{0,4},{1,5},{2,6},{3,7},{4,0},{5,1},{6,2},{7,3},{8,12},{9,13},{10,... | collective-permute-start | bytes 786440 | tf_op jit(solution)/shard_map/ppermute | solution.py:393
  204.7 12.6 %copy-start.9 = (bf16[512,256]{1,0:T(8,128)(2,1)S(1)}, bf16[512,256]{1,0:T(8,128)(2,1)}, u32[]{:S(2)}) copy-start(bf16[512,256]{1,0:T(8,128)(2,1)} %get-tuple-element.60) | copy-start | bytes 786436
  204.7 18.5 %copy-start.2 = (bf16[4,512,256]{2,1,0:T(8,128)(2,1)S(1)}, bf16[4,512,256]{2,1,0:T(8,128)(2,1)}, u32[]{:S(2)}) copy-start(bf16[4,512,256]{2,1,0:T(8,128)(2,1)} %arrange.1) | copy-start | bytes 3145732
  211.7 15.2 %collective-permute-start.33 = (bf16[512,1024]{1,0:T(8,128)(2,1)S(1)}, bf16[512,1024]{1,0:T(8,128)(2,1)S(1)}, u32[]{:S(2)}, u32[]{:S(2)}) collective-permute-start(bf16[512,1024]{1,0:T(8,128)(2,1)S(1)} %get-tuple-element.66), channel_id=1, source_target_pairs={{0,1},{1,0},{2,3},{3,2},{4,5},{5,4},{6,7},{7,6},{8,9},{9,8},{10,11... | collective-permute-start | bytes 3145736 | tf_op jit(solution)/shard_map/ppermute | solution.py:405
  217.4 7.2 %collective-permute-start.31 = (bf16[512,256]{1,0:T(8,128)(2,1)S(1)}, bf16[512,256]{1,0:T(8,128)(2,1)S(1)}, u32[]{:S(2)}, u32[]{:S(2)}) collective-permute-start(bf16[512,256]{1,0:T(8,128)(2,1)S(1)} %add_convert_fusion.2), channel_id=1, source_target_pairs={{1,4},{5,5},{9,12},{13,13},{17,20},{21,21},{25,28},{29,29},{33,38}... | collective-permute-start | bytes 786440 | tf_op jit(solution)/shard_map/ppermute | solution.py:280
  221.2 3.3 %collective-permute-start.32 = (bf16[512,256]{1,0:T(8,128)(2,1)S(1)}, bf16[512,256]{1,0:T(8,128)(2,1)S(1)}, u32[]{:S(2)}, u32[]{:S(2)}) collective-permute-start(bf16[512,256]{1,0:T(8,128)(2,1)S(1)} %add_convert_fusion.2), channel_id=1, source_target_pairs={{3,4},{7,5},{11,12},{15,13},{19,20},{23,21},{27,28},{31,29},{35,38... | collective-permute-start | bytes 786440 | tf_op jit(solution)/shard_map/ppermute | solution.py:280
  221.9 3.4 %collective-permute-start.30 = (bf16[512,256]{1,0:T(8,128)(2,1)S(1)}, bf16[512,256]{1,0:T(8,128)(2,1)S(1)}, u32[]{:S(2)}, u32[]{:S(2)}) collective-permute-start(bf16[512,256]{1,0:T(8,128)(2,1)S(1)} %add_convert_fusion.2), channel_id=1, source_target_pairs={{0,1},{2,3},{4,5},{6,7},{8,9},{10,11},{12,13},{14,15},{32,33},{34,... | collective-permute-start | bytes 786440 | tf_op jit(solution)/shard_map/ppermute | solution.py:285
  (8 other events, 25.4 us)

commit v5 on v3

--- a/solution.py
+++ b/solution.py
@@ -77,22 +77,31 @@
 
 def forward_kernel(count, many, start_ref, wide_ref, *refs):
     lines, outs, held, sems = refs[:count], refs[-2 - many : -2], refs[-2], refs[-1]
-    copies = [pltpu.make_async_copy(lines[m], held.at[m], sems.at[m]) for m in range(count)]
-    part = held.shape[3]
-    order = [lax.rem(start_ref[0] + k, SIDE) for k in range(SIDE)]
+    part = held.shape[2] // SIDE
+
+    def copies(m):
+        return [
+            pltpu.make_async_copy(
+                lines[m].at[lax.rem(start_ref[0] + k, SIDE)],
+                held.at[m, :, pl.ds(k * part, part)],
+                sems.at[m, k],
+            )
+            for k in range(SIDE)
+        ]
 
     @pl.when(pl.program_id(0) == 0)
     def _():
-        for copy in copies:
-            copy.start()
+        for m in range(count):
+            for copy in copies(m):
+                copy.start()
 
     for m in range(count):
 
         @pl.when(pl.program_id(0) == m)
         def _():
-            copies[m].wait()
-            weights = jnp.concatenate([held[m, k] for k in order], axis=1)
-            product = jnp.dot(wide_ref[...], weights, preferred_element_type=jnp.float32)
+            for copy in copies(m):
+                copy.wait()
+            product = jnp.dot(wide_ref[...], held[m], preferred_element_type=jnp.float32)
             product = product.astype(jnp.bfloat16)
             for k in range(SIDE):
                 piece = product[:, k * part : (k + 1) * part]
@@ -102,20 +111,17 @@
                     outs[k][...] = piece
 
 
-def forward(start, wide, lines, apart=False, places=1, into=None):
+def forward(start, wide, lines, apart=False):
     tokens, depth = wide.shape
     part = lines[0].shape[2]
     count = len(lines)
-    cols = count * part
     many = SIDE if apart else 1
     if apart:
-        outs = [pltpu.HBM((tokens, cols), jnp.bfloat16)] * SIDE
+        outs = [pltpu.HBM((tokens, count * part), jnp.bfloat16)] * SIDE
         specs = [pl.BlockSpec((tokens, part), lambda i, n: (0, i))] * SIDE
     else:
-        place = 0 if into is None else count
-        outs = [pltpu.HBM((SIDE, tokens, places * cols), jnp.bfloat16)]
-        specs = [pl.BlockSpec((SIDE, tokens, part), lambda i, n: (0, 0, place + i))]
-    extra = [] if into is None else [into]
+        outs = [pltpu.HBM((SIDE, tokens, count * part), jnp.bfloat16)]
+        specs = [pl.BlockSpec((SIDE, tokens, part), lambda i, n: (0, 0, i))]
     made = pl.pallas_call(
         functools.partial(forward_kernel, count, many),
         out_shape=outs,
@@ -123,14 +129,13 @@
             num_scalar_prefetch=1,
             grid=(count,),
             in_specs=[pl.BlockSpec(memory_space=pltpu.VMEM)]
-            + [pl.BlockSpec(memory_space=pl.ANY)] * (count + len(extra)),
+            + [pl.BlockSpec(memory_space=pl.ANY)] * count,
             out_specs=specs,
             scratch_shapes=[
-                pltpu.VMEM((count, SIDE, depth, part), jnp.bfloat16),
-                pltpu.SemaphoreType.DMA((count,)),
+                pltpu.VMEM((count, depth, SIDE * part), jnp.bfloat16),
+                pltpu.SemaphoreType.DMA((count, SIDE)),
             ],
         ),
-        input_output_aliases={} if into is None else {count + 2: 0},
         compiler_params=pltpu.CompilerParams(vmem_limit_bytes=24 << 20),
         cost_estimate=pl.CostEstimate(
             flops=tokens * depth * count * part,
@@ -138,7 +143,7 @@
             transcendentals=0,
         ),
         name="forward",
-    )(start, wide, *lines, *extra)
+    )(start, wide, *lines)
     return made if apart else made[0]
 
 
@@ -181,40 +186,79 @@
     )(far, here, beside)
 
 
-def backward_kernel(count, first, last, spots_ref, *refs):
-    lines, grads = refs[:count], refs[count : count * 5]
-    weights = jnp.concatenate([line[k] for line in lines for k in range(SIDE)], axis=1)
-    cols = jnp.concatenate([g[...] for g in grads], axis=1)
-    product = lax.dot_general(
-        cols, weights, (((1,), (1,)), ((), ())), preferred_element_type=jnp.float32
-    )
-    if first:
-        refs[-1][...] = product
-    elif not last:
-        refs[-1][...] = refs[-2][...] + product
+def backward_kernel(count, last, spots_ref, grad_ref, *refs):
+    lines, held, cols, line_sems, col_sems = refs[:count], *refs[-4:]
+    part = held.shape[2] // SIDE
+    block = held.shape[1] // 4
+    step = pl.program_id(0)
+
+    def weights(m, i):
+        rows = pl.ds(((i + 2) % 4) * block, block)
+        return [
+            pltpu.make_async_copy(
+                lines[m].at[k, rows, :],
+                held.at[m, rows, pl.ds(k * part, part)],
+                line_sems.at[i, m * SIDE + k],
+            )
+            for k in range(SIDE)
+        ]
+
+    def gradients(j):
+        start = pl.multiple_of(spots_ref[j] * part, part)
+        return pltpu.make_async_copy(
+            grad_ref.at[:, pl.ds(start, part)],
+            cols.at[:, pl.ds(j * part, part)],
+            col_sems.at[j],
+        )
+
+    @pl.when(step == 0)
+    def _():
+        for j in range(count * SIDE):
+            gradients(j).start()
+        for i in range(4):
+            for m in range(count):
+                for copy in weights(m, i):
+                    copy.start()
+        for j in range(count * SIDE):
+            gradients(j).wait()
+
+    for i in range(4):
+
+        @pl.when(step == i)
+        def _():
+            for m in range(count):
+                for copy in weights(m, i):
+                    copy.wait()
+
+    rows = pl.ds(pl.multiple_of(lax.rem(step + 2, 4) * block, block), block)
+    total = refs[count][...] if last else 0.0
+    for m in range(count):
+        lanes = slice(m * SIDE * part, (m + 1) * SIDE * part)
+        total = total + lax.dot_general(
+            cols[:, lanes],
+            held[m, rows, :],
+            (((1,), (1,)), ((), ())),
+            preferred_element_type=jnp.float32,
+        )
+    if not last:
+        refs[-5][...] = total
     else:
-        total = refs[-3][...] + product
-
-        @pl.when(pl.program_id(0) < 2)
+
+        @pl.when(step < 2)
         def _():
-            refs[-1][...] = total.astype(jnp.bfloat16)
-
-        @pl.when(pl.program_id(0) >= 2)
+            refs[-5][...] = total.astype(jnp.bfloat16)
+
+        @pl.when(step >= 2)
         def _():
-            refs[-2][...] = total
-
-
-def backward(spots, grown, out_grad, lines, last=False):
+            refs[-6][...] = total
+
+
+def backward(spots, grown, out_grad, lines):
     tokens = out_grad.shape[0]
     depth, part = lines[0].shape[1:]
     count = len(lines)
     block = depth // 4
-    first = grown is None
-    out_grad = pltpu.with_memory_space_constraint(out_grad, pltpu.HBM)
-
-    def column(j):
-        return pl.BlockSpec((tokens, part), lambda i, n: (0, n[j]))
-
+    last = grown is not None
     total = pl.BlockSpec((tokens, block), lambda i, n: (0, (i + 2) % 4))
     outs, specs = [pltpu.HBM((tokens, depth), jnp.float32)], [total]
     if last:
@@ -226,26 +270,35 @@
             pl.BlockSpec((tokens, block), lambda i, n: (0, jnp.maximum(i - 2, 0))),
             pl.BlockSpec((tokens, block), lambda i, n: (0, jnp.minimum(i, 1))),
         ]
+        grown = [pltpu.with_memory_space_constraint(grown, pltpu.HBM)]
     made = pl.pallas_call(
-        functools.partial(backward_kernel, count, first, last),
+        functools.partial(backward_kernel, count, last),
         out_shape=outs,
         grid_spec=pltpu.PrefetchScalarGridSpec(
             num_scalar_prefetch=1,
             grid=(4,),
-            in_specs=[pl.BlockSpec((SIDE, block, part), lambda i, n: (0, (i + 2) % 4, 0))] * count
-            + [column(j) for j in range(count * SIDE)]
-            + ([] if first else [total]),
+            in_specs=[pl.BlockSpec(memory_space=pl.ANY)] * (count + 1) + ([total] if last else []),
             out_specs=specs,
-        ),
-        input_output_aliases={} if first or last else {5 * count + 1: 0},
-        compiler_params=pltpu.CompilerParams(vmem_limit_bytes=28 << 20),
+            scratch_shapes=[
+                pltpu.VMEM((count, depth, SIDE * part), jnp.bfloat16),
+                pltpu.VMEM((tokens, count * SIDE * part), jnp.bfloat16),
+                pltpu.SemaphoreType.DMA((4, count * SIDE)),
+                pltpu.SemaphoreType.DMA((count * SIDE,)),
+            ],
+        ),
+        compiler_params=pltpu.CompilerParams(vmem_limit_bytes=32 << 20),
         cost_estimate=pl.CostEstimate(
             flops=tokens * depth * count * part,
             bytes_accessed=depth * part * count,
             transcendentals=0,
         ),
         name="backward",
-    )(spots, *lines, *([out_grad] * (count * SIDE)), *([] if first else [pltpu.with_memory_space_constraint(grown, pltpu.HBM)]))
+    )(
+        spots,
+        pltpu.with_memory_space_constraint(out_grad, pltpu.HBM),
+        *lines,
+        *(grown if last else []),
+    )
     return made if last else made[0]
 
 
@@ -307,10 +360,7 @@
         cols = slice(h * part, (h + 1) * part)
         shards.append(jnp.concatenate([mine[:, cols], swapped[:, cols]], axis=0))
     logits_a, logits_b, *shards = lax.optimization_barrier((logits_a, logits_b, *shards))
-    lines = [ring_gather(shards[h], 0, h) for h in range(2)]
-    lines[0] = jnp.stack(lines[0])
-    lines[0], *lines[1] = lax.optimization_barrier((lines[0], *lines[1]))
-    lines[1] = jnp.stack(lines[1])
+    lines = [jnp.stack(ring_gather(shards[h], 0, h)) for h in range(2)]
     def columns(i, h):
         far_at = (far + i) % SIDE
         spots = []
@@ -344,8 +394,16 @@
     factor = adapter_scale / (tokens * lax.axis_size("dp"))
     grad_a = jnp.dot(back_bf, attn_out, preferred_element_type=f32)
     grad_b = jnp.dot(low_bf, grad_cols, preferred_element_type=f32)
-    both = factor * jnp.concatenate([grad_a, grad_b], axis=0)
-    both = with_partner(both, 1)
+    bank_a, logit_grad_a = compose_back(
+        factor * grad_a, weights_a, picked_a, mixing_a, vector_bank
+    )
+    bank_b, logit_grad_b = compose_back(
+        factor * grad_b, weights_b, picked_b, mixing_b, vector_bank
+    )
+    levels = vector_bank.shape[0]
+    logit_grads = jnp.concatenate([logit_grad_a.ravel(), logit_grad_b.ravel()])
+    logit_grads = jnp.pad(logit_grads.reshape(-1, vector_bank.shape[1]), ((0, 7), (0, 0)))
+    small = jnp.concatenate([over_tensor(bank_a + bank_b), logit_grads], axis=0)
 
     here = [(0, 0), (0, 1)]
     beside = [(1, 0), (3, 0), (1, 1), (3, 1)]
@@ -356,37 +414,33 @@
 
     sent_here = forward(turned, wide, take(here))
     slots_here = exchange(sent_here, "tensor", LANES)
-    grown = backward(after(spots_of(here), sent_here), None, out_grad, take(here))
-    sent_beside = forward(after(turned, grown), wide, take(beside[:2]), places=2)
-    sent_beside = forward(
-        after(turned, both, sent_beside), wide, take(beside[2:]), places=2, into=sent_beside
-    )
+    sent_beside = forward(after(turned, sent_here, small), wide, take(beside))
     slots_here, sent_beside = lax.optimization_barrier((slots_here, sent_beside))
     slots_beside = exchange(sent_beside, "tensor", LANES)
-    both = with_partner(both, 4, sent_beside)
-    grown = backward(after(spots_of(beside), both), grown, out_grad, take(beside))
-    both = with_partner(both, 2, grown)
-    sent = forward(after(turned_here, both), wide, take(across), apart=True)
-    both = with_partner(both, 8, *sent)
-    slots_beside = after(slots_beside, *sent)
-    slots = arrange(far.astype(jnp.int32).reshape(1), slots_here, slots_beside)
-    moved = exchange(slots, "tensor", LANES)
-    both = after(both, slots)
-    bank_a, logit_grad_a = compose_back(both[:rank], weights_a, picked_a, mixing_a, vector_bank)
-    bank_b, logit_grad_b = compose_back(both[rank:], weights_b, picked_b, mixing_b, vector_bank)
-    crossed = lax.ppermute(jnp.where(core == 0, slots[2:], moved[:2]), "tensor", SWAP)
-    firsts = jnp.where(core == 0, slots[:2], crossed)
-    seconds = jnp.where(core == 0, crossed, moved[2:])
-
+    grown = backward(
+        after(spots_of(here + beside), sent_beside), None, out_grad, take(here + beside)
+    )
+    small = with_partner(small, 1, grown)
+    sent = forward(after(turned_here, grown), wide, take(across), apart=True)
     arrived = [sent[0]]
     for step in range(1, SIDE):
         turns = [(t, (t + 2 * step) % 8) for t in range(8)]
         arrived.append(lax.ppermute(sent[step], "tensor", turns))
     piece = total_of([a.astype(f32) for a in arrived]).astype(bf16)
-    bank_grad = over_tensor(bank_a + bank_b)
-    grown, other = backward(
-        after(spots_of(across), slots), grown, out_grad, take(across), last=True
-    )
+    small = with_partner(small, 4, *sent)
+    slots_beside = after(slots_beside, *sent)
+    slots = arrange(far.astype(jnp.int32).reshape(1), slots_here, slots_beside)
+    moved = exchange(slots, "tensor", LANES)
+    crossed = lax.ppermute(jnp.where(core == 0, slots[2:], moved[:2]), "tensor", SWAP)
+    firsts = jnp.where(core == 0, slots[:2], crossed)
+    seconds = jnp.where(core == 0, crossed, moved[2:])
+
+    small = with_partner(small, 2, slots)
+    grown, other = backward(after(spots_of(across), slots, piece), grown, out_grad, take(across))
+    small = with_partner(small, 8, grown)
+    bank_grad = small[:levels]
+    logit_grads = small[levels].reshape(2, *logits_a.shape)
+    logit_grad_a, logit_grad_b = logit_grads[0], logit_grads[1]
     first, place, second = settle(piece, 2, z, core)
     cols = []
     for s in range(2):

time: 215 us -> 216 us (level)
  waiting for transfers between devices: 34.8 us -> 53.8 us
  starting transfers between devices: 88.2 us -> 69.7 us
  other arithmetic: 25.2 us -> 28.6 us
  Pallas kernels: 48.6 us -> 45.9 us
    ppermute x2, starting transfers between devices: 29.6 us -> 4.25 us  [over_tensor(): value = value + lax.ppermute(value, 'tensor', SWAP)]
    ppermute x12, waiting for transfers between devices: 15.7 us -> 35.6 us  [shift(): return lax.ppermute(value, BOTH, ring(stage, step))]
    ppermute x2, waiting for transfers between devices: 0.01 us -> 6.76 us  [over_tensor(): return value + lax.ppermute(value, 'tensor', [(t, t ^ 4) for t in range(8)])]
    ppermute x2, waiting for transfers between devices: 6.58 us -> 0.42 us  [over_tensor(): lax.ppermute(value, 'tensor', [(t, t ^ 2) for t in range(8)])]
    ppermute x1, starting transfers between devices: 0.32 us -> 4.22 us  [local(): other = lax.ppermute(other, 'tensor', SWAP)]
    ppermute x1, starting transfers between devices: 2.76 us -> 0.1 us  [local(): lax.ppermute(attn_out, 'tensor', SWAP)]
    ppermute x4, starting transfers between devices: 5.35 us -> 8 us  [with_partner(): other = lax.ppermute(value, 'dp', [(d, d ^ bit) for d in range(16)])]
    pallas_call x4 -> x3, Pallas kernels: 19.9 us -> 17.5 us  [forward(): pl.pallas_call(functools.partial(forward_kernel, count, many), out_shape=...]
  transfers between devices with their start and end apart: 35 -> 35, of which waited for: 9 -> 11; matrix products, arithmetic and copies ran while one was open for 14% -> 18% of each run, Pallas kernels for 21% -> 21%
where the time goes in v5:
time: 216 us; the launch traced here: 215 us
  starting transfers between devices  69.7 us (32%)
  waiting for transfers between devices  53.8 us (25%)
  Pallas kernels  45.9 us (21%)
  other arithmetic  28.6 us (13%)
  matrix products  10.3 us (5%)
  local copies, waits for them, and re-layouts  5.46 us (3%)
    ppermute x12, waiting for transfers between devices, shift(): return lax.ppermute(value, BOTH, ring(stage, step))  35.6 us
    pallas_call x2, Pallas kernels, backward(): pl.pallas_call(functools.partial(backward_kernel, count, last), out_shape...  24.6 us
    ppermute x12, starting transfers between devices, shift(): return lax.ppermute(value, BOTH, ring(stage, step))  19.2 us
    pallas_call x3, Pallas kernels, forward(): pl.pallas_call(functools.partial(forward_kernel, count, many), out_shape=...  17.5 us
    all_to_all x3, starting transfers between devices, exchange(): lax.all_to_all(value, axis, split_axis=0, concat_axis=0, tiled=True, axis...  12.4 us
    ppermute x4, starting transfers between devices, with_partner(): other = lax.ppermute(value, 'dp', [(d, d ^ bit) for d in range(16)])  8 us
    ppermute x4, waiting for transfers between devices, with_partner(): other = lax.ppermute(value, 'dp', [(d, d ^ bit) for d in range(16)])  7.16 us
    ppermute x2, starting transfers between devices, from_second(): return lax.ppermute(piece, BOTH, pairs(move))  7.06 us
  transfers between devices with their start and end apart: 35, of which 11 were waited for; matrix products, arithmetic and copies ran while one was open for 18% of the time, Pallas kernels for 21%

profile of v5, /device:TPU:1, one launch (start us, length us, event | category | flops | bytes accessed | tf_op | source)
XLA Modules:
  0.0 214.9 jit_solution(17214014118431100251)
XLA Ops:
  0.7 1.4 broadcast_select_fusion.1
  2.0 1.5 collective-permute-start.1
  3.7 1.4 collective-permute-done.1
  6.0 1.7 collective-permute-start.3
  7.7 2.1 collective-permute-start.2
  9.8 2.7 %collective-permute-start.5 = (bf16[2048,128]{1,0:T(8,128)(2,1)S(1)}, bf16[2048,128]{1,0:T(8,128)(2,1)S(1)}, u32[]{:S(2)}, u32[]{:S(2)}) collective-permute-start(bf16[2048,128]{1,0:T(8,128)(2,1)S(1)} %get-tuple-element.29), channel_id=1, source_target_pairs={{0,96},{1,25},{2,98},{3,27},{4,100},{5,29},{6,102},{7,31},{8,104},... | collective-permute-start | bytes 1572872 | tf_op jit(solution)/shard_map/ppermute | solution.py:43
  13.4 8.7 %collective-permute-done.5 = bf16[2048,128]{1,0:T(8,128)(2,1)S(1)} collective-permute-done((bf16[2048,128]{1,0:T(8,128)(2,1)S(1)}, bf16[2048,128]{1,0:T(8,128)(2,1)S(1)}, u32[]{:S(2)}, u32[]{:S(2)}) %collective-permute-start.5) | collective-permute-done | bytes 524320 | tf_op jit(solution)/shard_map/ppermute | solution.py:43
  22.1 3.1 %collective-permute-start.6 = (bf16[2048,128]{1,0:T(8,128)(2,1)S(1)}, bf16[2048,128]{1,0:T(8,128)(2,1)S(1)}, u32[]{:S(2)}, u32[]{:S(2)}) collective-permute-start(bf16[2048,128]{1,0:T(8,128)(2,1)S(1)} %collective-permute-done.5), channel_id=1, source_target_pairs={{0,96},{1,25},{2,98},{3,27},{4,100},{5,29},{6,102},{7,31},{8,104},... | collective-permute-start | bytes 1572872 | tf_op jit(solution)/shard_map/ppermute | solution.py:43
  25.2 1.6 fusion.4
  27.9 3.5 %collective-permute-done.6 = bf16[2048,128]{1,0:T(8,128)(2,1)S(1)} collective-permute-done((bf16[2048,128]{1,0:T(8,128)(2,1)S(1)}, bf16[2048,128]{1,0:T(8,128)(2,1)S(1)}, u32[]{:S(2)}, u32[]{:S(2)}) %collective-permute-start.6) | collective-permute-done | bytes 524320 | tf_op jit(solution)/shard_map/ppermute | solution.py:43
  31.3 1.6 pad_maximum_fusion.1.refs_1_
  36.3 1.5 collective-permute-start.9
  40.1 3.0 %collective-permute-start.10 = (f32[32,512]{1,0:T(8,128)}, f32[32,512]{1,0:T(8,128)}, u32[]{:S(2)}, u32[]{:S(2)}) collective-permute-start(f32[32,512]{1,0:T(8,128)} %add.383), channel_id=1, source_target_pairs={{0,4},{1,5},{2,6},{3,7},{4,0},{5,1},{6,2},{7,3},{8,12},{9,13},{10,... | collective-permute-start | bytes 196616 | tf_op jit(solution)/shard_map/ppermute | solution.py:62
  43.1 3.1 %pad_maximum_fusion.refs_0_ = bf16[4,2048,128]{2,1,0:T(8,128)(2,1)} fusion(bf16[1,2048,128]{2,1,0:T(8,128)(2,1)} %bitcast.5, bf16[1,2048,128]{2,1,0:T(8,128)(2,1)} %bitcast.4, bf16[1,2048,128]{2,1,0:T(8,128)(2,1)} %bitcast.3, bf16[1,2048,128]{2,1,0:T(8,128)(2,1)} %bitcast.2), kind=kLoop, calls=%fused_computation | loop fusion | flops 3145728 | bytes 4194304 | tf_op jit(solution)/shard_map/stack | solution.py:363
  46.2 3.4 %collective-permute-start.14 = (bf16[4,2048,128]{2,1,0:T(8,128)(2,1)}, bf16[4,2048,128]{2,1,0:T(8,128)(2,1)}, u32[]{:S(2)}, u32[]{:S(2)}) collective-permute-start(bf16[4,2048,128]{2,1,0:T(8,128)(2,1)} %pad_maximum_fusion.refs_0_), channel_id=1, source_target_pairs={{0,24},{1,97},{2,26},{3,99},{4,28},{5,101},{6,30},{7,103},{8,0},{9... | collective-permute-start | bytes 6291464 | tf_op jit(solution)/shard_map/ppermute | solution.py:43
  49.6 2.7 %collective-permute-start.16 = (bf16[4,2048,128]{2,1,0:T(8,128)(2,1)}, bf16[4,2048,128]{2,1,0:T(8,128)(2,1)}, u32[]{:S(2)}, u32[]{:S(2)}) collective-permute-start(bf16[4,2048,128]{2,1,0:T(8,128)(2,1)} %pad_maximum_fusion.1.refs_1_), channel_id=1, source_target_pairs={{0,24},{1,97},{2,26},{3,99},{4,28},{5,101},{6,30},{7,103},{8,0},{9... | collective-permute-start | bytes 6291464 | tf_op jit(solution)/shard_map/ppermute | solution.py:43
  52.3 4.9 %forward.3 = bf16[4,512,256]{2,1,0:T(8,128)(2,1)} custom-call(s32[1]{0:T(128)} %bitcast.1.start_ref, bf16[512,2048]{1,0:T(8,128)(2,1)S(1)} %constant_dynamic-update-slice_fusion.wide_ref, bf16[4,2048,128]{2,1,0:T(8,128)(2,1)} %pad_maximum_fusion.refs_0_, bf16[4,2048,128]{2,1,0:T(8,128)(2,1)} %pad_maximum_fusion.1.refs_1_), custom_call_target="tpu_custom_call" | custom-call | flops 268435456 | bytes 524288 | tf_op jit(solution)/shard_map/forward/pallas_call | solution.py:125
  57.2 3.5 %all-to-all-start = ((bf16[4,512,256]{2,1,0:T(8,128)(2,1)}), bf16[4,512,256]{2,1,0:T(8,128)(2,1)S(1)}, u32[]{:S(2)}, u32[]{:S(2)}) async-start(bf16[4,512,256]{2,1,0:T(8,128)(2,1)} %forward.3), calls=%async_computation | async-start | bytes 2097152 | tf_op jit(solution)/shard_map/all_to_all | solution.py:54
  61.7 1.5 convolution_multiply_fusion
  63.6 1.5 convolution_multiply_fusion.1
  65.5 3.1 %collective-permute-start.11 = (f32[256,256]{1,0:T(8,128)S(1)}, f32[256,256]{1,0:T(8,128)S(1)}, u32[]{:S(2)}, u32[]{:S(2)}) collective-permute-start(f32[256,256]{1,0:T(8,128)S(1)} %fusion), channel_id=1, source_target_pairs={{0,1},{1,0},{2,3},{3,2},{4,5},{5,4},{6,7},{7,6},{8,9},{9,8},{10,11... | collective-permute-start | bytes 786440 | tf_op jit(solution)/shard_map/ppermute | solution.py:60
  69.8 1.8 collective-permute-start.12
  72.0 4.4 %collective-permute-done.15.refs_1_.refs_3_ = bf16[4,2048,128]{2,1,0:T(8,128)(2,1)} collective-permute-done((bf16[4,2048,128]{2,1,0:T(8,128)(2,1)}, bf16[4,2048,128]{2,1,0:T(8,128)(2,1)}, u32[]{:S(2)}, u32[]{:S(2)}) %collective-permute-start.15) | collective-permute-done | bytes 2097184 | tf_op jit(solution)/shard_map/ppermute | solution.py:43
  76.3 19.1 %collective-permute-done.16.refs_2_.refs_4_ = bf16[4,2048,128]{2,1,0:T(8,128)(2,1)} collective-permute-done((bf16[4,2048,128]{2,1,0:T(8,128)(2,1)}, bf16[4,2048,128]{2,1,0:T(8,128)(2,1)}, u32[]{:S(2)}, u32[]{:S(2)}) %collective-permute-start.16) | collective-permute-done | bytes 2097184 | tf_op jit(solution)/shard_map/ppermute | solution.py:43
  95.4 3.4 %collective-permute-start.19 = (bf16[4,2048,128]{2,1,0:T(8,128)(2,1)}, bf16[4,2048,128]{2,1,0:T(8,128)(2,1)}, u32[]{:S(2)}, u32[]{:S(2)}) collective-permute-start(bf16[4,2048,128]{2,1,0:T(8,128)(2,1)} %collective-permute-done.16.refs_2_.refs_4_), channel_id=1, source_target_pairs={{0,24},{1,97},{2,26},{3,99},{4,28},{5,101},{6,30},{7,103},{8,0},{9... | collective-permute-start | bytes 6291464 | tf_op jit(solution)/shard_map/ppermute | solution.py:43
  98.8 1.7 add.387
  100.8 6.8 %collective-permute-done.13 = f32[256,256]{1,0:T(8,128)} collective-permute-done((f32[256,256]{1,0:T(8,128)}, f32[256,256]{1,0:T(8,128)}, u32[]{:S(2)}, u32[]{:S(2)}) %collective-permute-start.13) | collective-permute-done | bytes 262176 | tf_op jit(solution)/shard_map/ppermute | solution.py:62
  110.1 7.6 %forward.4 = bf16[4,512,512]{2,1,0:T(8,128)(2,1)} custom-call(s32[1]{0:T(128)} %bitcast.1.start_ref, bf16[512,2048]{1,0:T(8,128)(2,1)S(1)} %constant_dynamic-update-slice_fusion.wide_ref, bf16[4,2048,128]{2,1,0:T(8,128)(2,1)} %collective-permute-done.14.refs_0_.refs_2_, bf16[4,2048,128]{2,1,0:T(8,128)(2,1)} %collective-permute-done.15.refs_1_.refs_3_, ...), custom_call_target="tpu_custom_call" | custom-call | flops 536870912 | bytes 1048576 | tf_op jit(solution)/shard_map/forward/pallas_call | solution.py:125
  117.7 4.5 %all-to-all-start.1 = ((bf16[4,512,512]{2,1,0:T(8,128)(2,1)}), bf16[4,512,512]{2,1,0:T(8,128)(2,1)}, u32[]{:S(2)}, u32[]{:S(2)}) async-start(bf16[4,512,512]{2,1,0:T(8,128)(2,1)} %forward.4), calls=%async_computation.1 | async-start | bytes 4194304 | tf_op jit(solution)/shard_map/all_to_all | solution.py:54
  122.2 4.2 %collective-permute-start.28 = (f32[264,256]{1,0:T(8,128)}, f32[264,256]{1,0:T(8,128)}, u32[]{:S(2)}, u32[]{:S(2)}) collective-permute-start(f32[264,256]{1,0:T(8,128)} %select_maximum_fusion), channel_id=1, source_target_pairs={{0,8},{8,0},{16,24},{24,16},{32,40},{40,32},{48,56},{56,48},{64,72... | collective-permute-start | bytes 811016 | tf_op jit(solution)/shard_map/ppermute | solution.py:70
  126.5 15.9 %backward.2.refs_2_ = f32[512,2048]{1,0:T(8,128)} custom-call(s32[24]{0:T(128)S(1)} %stack.166.spots_ref, bf16[512,8192]{1,0:T(8,128)(2,1)} %grad_ref.3, bf16[4,2048,128]{2,1,0:T(8,128)(2,1)} %pad_maximum_fusion.refs_0_, bf16[4,2048,128]{2,1,0:T(8,128)(2,1)} %pad_maximum_fusion.1.refs_1_, bf16[4,2048,128]{2,1,0:T(8,128)(2,1)} %collective-permute-done.14.refs_0_.refs_2_, ...), custom_call_target="tpu_custom_call" | custom-call | flops 805306368 | bytes 1572864 | tf_op jit(solution)/shard_map/backward/pallas_call | solution.py:274
  142.4 5.0 %forward.5 = (bf16[512,256]{1,0:T(8,128)(2,1)}, bf16[512,256]{1,0:T(8,128)(2,1)}, bf16[512,256]{1,0:T(8,128)(2,1)}, bf16[512,256]{1,0:T(8,128)(2,1)}) custom-call(s32[1]{0:T(128)} %bitcast.14.start_ref, bf16[512,2048]{1,0:T(8,128)(2,1)S(1)} %constant_dynamic-update-slice_fusion.wide_ref, bf16[4,2048,128]{2,1,0:T(8,128)(2,1)} %collective-permute-done.18.refs_0_, ...), custom_call_target="tpu_custom_call" | custom-call | flops 268435456 | bytes 524288 | tf_op jit(solution)/shard_map/forward/pallas_call | solution.py:125
  147.4 2.6 %collective-permute-start.23 = (bf16[512,256]{1,0:T(8,128)(2,1)}, bf16[512,256]{1,0:T(8,128)(2,1)S(1)}, u32[]{:S(2)}, u32[]{:S(2)}) collective-permute-start(bf16[512,256]{1,0:T(8,128)(2,1)} %get-tuple-element.42), channel_id=1, source_target_pairs={{0,6},{1,7},{2,0},{3,1},{4,2},{5,3},{6,4},{7,5},{8,14},{9,15},{10,... | collective-permute-start | bytes 786440 | tf_op jit(solution)/shard_map/ppermute | solution.py:428
  150.0 1.8 collective-permute-start.21
  151.9 3.8 %arrange.1 = bf16[4,512,256]{2,1,0:T(8,128)(2,1)} custom-call(s32[1]{0:T(128)} %bitcast.far_ref, bf16[4,512,256]{2,1,0:T(8,128)(2,1)S(1)} %all-to-all-done.here_ref, bf16[4,512,512]{2,1,0:T(8,128)(2,1)} %all-to-all-done.1.beside_ref), custom_call_target="tpu_custom_call" | custom-call | flops 2097152 | bytes 4194304 | tf_op jit(solution)/shard_map/arrange/pallas_call | solution.py:169
  155.7 4.4 %all-to-all-start.2 = ((bf16[4,512,256]{2,1,0:T(8,128)(2,1)}), bf16[4,512,256]{2,1,0:T(8,128)(2,1)}, u32[]{:S(2)}, u32[]{:S(2)}) async-start(bf16[4,512,256]{2,1,0:T(8,128)(2,1)} %arrange.1), calls=%async_computation.2 | async-start | bytes 2097152 | tf_op jit(solution)/shard_map/all_to_all | solution.py:54
  163.3 8.6 %backward.3 = (f32[512,1024]{1,0:T(8,128)S(1)}, bf16[512,1024]{1,0:T(8,128)(2,1)S(1)}) custom-call(s32[8]{0:T(128)S(1)} %stack.175.spots_ref, bf16[512,8192]{1,0:T(8,128)(2,1)} %grad_ref.3, bf16[4,2048,128]{2,1,0:T(8,128)(2,1)} %collective-permute-done.18.refs_0_, bf16[4,2048,128]{2,1,0:T(8,128)(2,1)} %collective-permute-done.19.refs_1_, ...), custom_call_target="tpu_custom_call" | custom-call | flops 268435456 | bytes 524288 | tf_op jit(solution)/shard_map/backward/pallas_call | solution.py:274
  171.9 4.2 %collective-permute-start.27 = (bf16[512,1024]{1,0:T(8,128)(2,1)S(1)}, bf16[512,1024]{1,0:T(8,128)(2,1)}, u32[]{:S(2)}, u32[]{:S(2)}) collective-permute-start(bf16[512,1024]{1,0:T(8,128)(2,1)S(1)} %get-tuple-element.46), channel_id=1, source_target_pairs={{0,1},{1,0},{2,3},{3,2},{4,5},{5,4},{6,7},{7,6},{8,9},{9,8},{10,11... | collective-permute-start | bytes 3145736 | tf_op jit(solution)/shard_map/ppermute | solution.py:454
  176.9 3.3 %collective-permute-start.30 = (f32[264,256]{1,0:T(8,128)}, f32[264,256]{1,0:T(8,128)}, u32[]{:S(2)}, u32[]{:S(2)}) collective-permute-start(f32[264,256]{1,0:T(8,128)} %add.467), channel_id=1, source_target_pairs={{0,16},{8,24},{16,0},{24,8},{32,48},{40,56},{48,32},{56,40},{64,80... | collective-permute-start | bytes 811016 | tf_op jit(solution)/shard_map/ppermute | solution.py:70
  180.2 7.1 %collective-permute-done.30 = f32[264,256]{1,0:T(8,128)} collective-permute-done((f32[264,256]{1,0:T(8,128)}, f32[264,256]{1,0:T(8,128)}, u32[]{:S(2)}, u32[]{:S(2)}) %collective-permute-start.30) | collective-permute-done | bytes 270368 | tf_op jit(solution)/shard_map/ppermute | solution.py:70
  187.4 1.8 add.468
  189.6 2.1 slice_select_fusion.1
  192.7 1.8 fusion.26
  194.5 5.7 %collective-permute-start.25 = (bf16[512,256]{1,0:T(8,128)(2,1)S(1)}, bf16[512,256]{1,0:T(8,128)(2,1)}, u32[]{:S(2)}, u32[]{:S(2)}) collective-permute-start(bf16[512,256]{1,0:T(8,128)(2,1)S(1)} %copy-done.5), channel_id=1, source_target_pairs={{1,4},{5,5},{9,12},{13,13},{17,20},{21,21},{25,28},{29,29},{33,38}... | collective-permute-start | bytes 786440 | tf_op jit(solution)/shard_map/ppermute | solution.py:330
  200.2 1.4 collective-permute-start.26
  206.4 3.4 %add_convert_fusion = bf16[512,1024]{1,0:T(8,128)(2,1)} fusion(f32[512,1024]{1,0:T(8,128)} %fusion.26, f32[512,1024]{1,0:T(8,128)S(1)} %get-tuple-element.45, bf16[512,1024]{1,0:T(8,128)(2,1)} %collective-permute-done.27), kind=kLoop, calls=%fused_computation.2 | loop fusion | flops 2621440 | bytes 6291456 | tf_op jit(solution)/shard_map/convert_element_type | solution.py:459
  209.9 1.4 slice_select_fusion.2
  213.5 1.4 add_convert_fusion.1
  (127 shorter events, 27.2 us)
Async XLA Ops:
  0.6 12.0 %copy-start = (f32[256,256]{1,0:T(8,128)S(1)}, f32[256,256]{1,0:T(8,128)}, u32[]{:S(2)}) copy-start(f32[256,256]{1,0:T(8,128)} %param.10) | copy-start | bytes 786436
  2.0 3.0 %collective-permute-start.1 = (bf16[1024,256]{1,0:T(8,128)(2,1)S(1)}, bf16[1024,256]{1,0:T(8,128)(2,1)S(1)}, u32[]{:S(2)}, u32[]{:S(2)}) collective-permute-start(bf16[1024,256]{1,0:T(8,128)(2,1)S(1)} %get-tuple-element.71), channel_id=1, source_target_pairs={{0,1},{1,0},{2,3},{3,2},{4,5},{5,4},{6,7},{7,6},{8,9},{9,8},{10,11... | collective-permute-start | bytes 1572872 | tf_op jit(solution)/shard_map/ppermute | solution.py:357
  3.6 34.2 %collective-permute-start = (bf16[512,1024]{1,0:T(8,128)(2,1)S(1)}, bf16[512,1024]{1,0:T(8,128)(2,1)}, u32[]{:S(2)}, u32[]{:S(2)}) collective-permute-start(bf16[512,1024]{1,0:T(8,128)(2,1)S(1)} %copy-done.2), channel_id=1, source_target_pairs={{0,1},{1,0},{2,3},{3,2},{4,5},{5,4},{6,7},{7,6},{8,9},{9,8},{10,11... | collective-permute-start | bytes 3145736 | tf_op jit(solution)/shard_map/ppermute | solution.py:377
  3.7 8.9 %copy-start.15 = (f32[16,4,2]{0,2,1:T(2,128)S(1)}, f32[16,4,2]{0,2,1:T(2,128)}, u32[]{:S(2)}) copy-start(f32[16,4,2]{0,2,1:T(2,128)} %param.13) | copy-start | bytes 1540
  3.7 8.9 %copy-start.13 = (s32[16,4,2]{0,2,1:T(2,128)S(1)}, s32[16,4,2]{0,2,1:T(2,128)}, u32[]{:S(2)}) copy-start(s32[16,4,2]{0,2,1:T(2,128)} %param.14) | copy-start | bytes 1540
  3.7 9.3 %copy-start.16 = (f32[16,4,2]{0,2,1:T(2,128)S(1)}, f32[16,4,2]{0,2,1:T(2,128)}, u32[]{:S(2)}) copy-start(f32[16,4,2]{0,2,1:T(2,128)} %param.11) | copy-start | bytes 1540
  3.7 9.3 %copy-start.14 = (s32[16,4,2]{0,2,1:T(2,128)S(1)}, s32[16,4,2]{0,2,1:T(2,128)}, u32[]{:S(2)}) copy-start(s32[16,4,2]{0,2,1:T(2,128)} %param.12) | copy-start | bytes 1540
  6.0 21.9 %collective-permute-start.3 = (bf16[2048,128]{1,0:T(8,128)(2,1)}, bf16[2048,128]{1,0:T(8,128)(2,1)}, u32[]{:S(2)}, u32[]{:S(2)}) collective-permute-start(bf16[2048,128]{1,0:T(8,128)(2,1)} %get-tuple-element.28), channel_id=1, source_target_pairs={{0,32},{1,9},{2,34},{3,11},{4,36},{5,13},{6,38},{7,15},{8,40},{9,1... | collective-permute-start | bytes 1572872 | tf_op jit(solution)/shard_map/ppermute | solution.py:43
  7.7 35.4 %collective-permute-start.2 = (bf16[2048,128]{1,0:T(8,128)(2,1)}, bf16[2048,128]{1,0:T(8,128)(2,1)}, u32[]{:S(2)}, u32[]{:S(2)}) collective-permute-start(bf16[2048,128]{1,0:T(8,128)(2,1)} %get-tuple-element.28), channel_id=1, source_target_pairs={{0,96},{1,25},{2,98},{3,27},{4,100},{5,29},{6,102},{7,31},{8,104},... | collective-permute-start | bytes 1572872 | tf_op jit(solution)/shard_map/ppermute | solution.py:43
  9.8 18.0 %collective-permute-start.7 = (bf16[2048,128]{1,0:T(8,128)(2,1)S(1)}, bf16[2048,128]{1,0:T(8,128)(2,1)S(1)}, u32[]{:S(2)}, u32[]{:S(2)}) collective-permute-start(bf16[2048,128]{1,0:T(8,128)(2,1)S(1)} %get-tuple-element.29), channel_id=1, source_target_pairs={{0,32},{1,9},{2,34},{3,11},{4,36},{5,13},{6,38},{7,15},{8,40},{9,1... | collective-permute-start | bytes 1572872 | tf_op jit(solution)/shard_map/ppermute | solution.py:43
  9.8 12.2 %collective-permute-start.5 = (bf16[2048,128]{1,0:T(8,128)(2,1)S(1)}, bf16[2048,128]{1,0:T(8,128)(2,1)S(1)}, u32[]{:S(2)}, u32[]{:S(2)}) collective-permute-start(bf16[2048,128]{1,0:T(8,128)(2,1)S(1)} %get-tuple-element.29), channel_id=1, source_target_pairs={{0,96},{1,25},{2,98},{3,27},{4,100},{5,29},{6,102},{7,31},{8,104},... | collective-permute-start | bytes 1572872 | tf_op jit(solution)/shard_map/ppermute | solution.py:43
  13.4 17.9 %copy-start.11 = (bf16[4,2,8,256]{3,2,0,1:T(8,128)(2,1)}, bf16[4,2,8,256]{3,2,0,1:T(8,128)(2,1)S(1)}, u32[]{:S(2)}) copy-start(bf16[4,2,8,256]{3,2,0,1:T(8,128)(2,1)S(1)} %copy.56) | copy-start | bytes 98308
  13.4 17.9 %copy-start.6 = (bf16[4,2,8,256]{3,2,0,1:T(8,128)(2,1)}, bf16[4,2,8,256]{3,2,0,1:T(8,128)(2,1)S(1)}, u32[]{:S(2)}) copy-start(bf16[4,2,8,256]{3,2,0,1:T(8,128)(2,1)S(1)} %copy.55) | copy-start | bytes 98308
  22.1 9.3 %collective-permute-start.6 = (bf16[2048,128]{1,0:T(8,128)(2,1)S(1)}, bf16[2048,128]{1,0:T(8,128)(2,1)S(1)}, u32[]{:S(2)}, u32[]{:S(2)}) collective-permute-start(bf16[2048,128]{1,0:T(8,128)(2,1)S(1)} %collective-permute-done.5), channel_id=1, source_target_pairs={{0,96},{1,25},{2,98},{3,27},{4,100},{5,29},{6,102},{7,31},{8,104},... | collective-permute-start | bytes 1572872 | tf_op jit(solution)/shard_map/ppermute | solution.py:43
  27.8 15.3 %collective-permute-start.4 = (bf16[2048,128]{1,0:T(8,128)(2,1)}, bf16[2048,128]{1,0:T(8,128)(2,1)}, u32[]{:S(2)}, u32[]{:S(2)}) collective-permute-start(bf16[2048,128]{1,0:T(8,128)(2,1)} %collective-permute-done.3), channel_id=1, source_target_pairs={{0,32},{1,9},{2,34},{3,11},{4,36},{5,13},{6,38},{7,15},{8,40},{9,1... | collective-permute-start | bytes 1572872 | tf_op jit(solution)/shard_map/ppermute | solution.py:43
  33.0 2.4 %collective-permute-start.8 = (f32[32,512]{1,0:T(8,128)}, f32[32,512]{1,0:T(8,128)}, u32[]{:S(2)}, u32[]{:S(2)}) collective-permute-start(f32[32,512]{1,0:T(8,128)} %pad_maximum_fusion.4), channel_id=1, source_target_pairs={{0,1},{1,0},{2,3},{3,2},{4,5},{5,4},{6,7},{7,6},{8,9},{9,8},{10,11... | collective-permute-start | bytes 196616 | tf_op jit(solution)/shard_map/ppermute | solution.py:60
  36.3 3.2 %collective-permute-start.9 = (f32[32,512]{1,0:T(8,128)S(1)}, f32[32,512]{1,0:T(8,128)S(1)}, u32[]{:S(2)}, u32[]{:S(2)}) collective-permute-start(f32[32,512]{1,0:T(8,128)S(1)} %add.382), channel_id=1, source_target_pairs={{0,2},{1,3},{2,0},{3,1},{4,6},{5,7},{6,4},{7,5},{8,10},{9,11},{10,... | collective-permute-start | bytes 196616 | tf_op jit(solution)/shard_map/ppermute | solution.py:61
  40.1 20.6 %collective-permute-start.10 = (f32[32,512]{1,0:T(8,128)}, f32[32,512]{1,0:T(8,128)}, u32[]{:S(2)}, u32[]{:S(2)}) collective-permute-start(f32[32,512]{1,0:T(8,128)} %add.383), channel_id=1, source_target_pairs={{0,4},{1,5},{2,6},{3,7},{4,0},{5,1},{6,2},{7,3},{8,12},{9,13},{10,... | collective-permute-start | bytes 196616 | tf_op jit(solution)/shard_map/ppermute | solution.py:62
  46.2 63.8 %collective-permute-start.14 = (bf16[4,2048,128]{2,1,0:T(8,128)(2,1)}, bf16[4,2048,128]{2,1,0:T(8,128)(2,1)}, u32[]{:S(2)}, u32[]{:S(2)}) collective-permute-start(bf16[4,2048,128]{2,1,0:T(8,128)(2,1)} %pad_maximum_fusion.refs_0_), channel_id=1, source_target_pairs={{0,24},{1,97},{2,26},{3,99},{4,28},{5,101},{6,30},{7,103},{8,0},{9... | collective-permute-start | bytes 6291464 | tf_op jit(solution)/shard_map/ppermute | solution.py:43
  49.6 26.7 %collective-permute-start.15 = (bf16[4,2048,128]{2,1,0:T(8,128)(2,1)}, bf16[4,2048,128]{2,1,0:T(8,128)(2,1)}, u32[]{:S(2)}, u32[]{:S(2)}) collective-permute-start(bf16[4,2048,128]{2,1,0:T(8,128)(2,1)} %pad_maximum_fusion.refs_0_), channel_id=1, source_target_pairs={{0,8},{1,33},{2,10},{3,35},{4,12},{5,37},{6,14},{7,39},{8,16},{9,4... | collective-permute-start | bytes 6291464 | tf_op jit(solution)/shard_map/ppermute | solution.py:43
  49.6 45.8 %collective-permute-start.16 = (bf16[4,2048,128]{2,1,0:T(8,128)(2,1)}, bf16[4,2048,128]{2,1,0:T(8,128)(2,1)}, u32[]{:S(2)}, u32[]{:S(2)}) collective-permute-start(bf16[4,2048,128]{2,1,0:T(8,128)(2,1)} %pad_maximum_fusion.1.refs_1_), channel_id=1, source_target_pairs={{0,24},{1,97},{2,26},{3,99},{4,28},{5,101},{6,30},{7,103},{8,0},{9... | collective-permute-start | bytes 6291464 | tf_op jit(solution)/shard_map/ppermute | solution.py:43
  52.3 57.8 %collective-permute-start.17 = (bf16[4,2048,128]{2,1,0:T(8,128)(2,1)}, bf16[4,2048,128]{2,1,0:T(8,128)(2,1)}, u32[]{:S(2)}, u32[]{:S(2)}) collective-permute-start(bf16[4,2048,128]{2,1,0:T(8,128)(2,1)} %pad_maximum_fusion.1.refs_1_), channel_id=1, source_target_pairs={{0,8},{1,33},{2,10},{3,35},{4,12},{5,37},{6,14},{7,39},{8,16},{9,4... | collective-permute-start | bytes 6291464 | tf_op jit(solution)/shard_map/ppermute | solution.py:43
  57.2 60.5 %all-to-all-start = ((bf16[4,512,256]{2,1,0:T(8,128)(2,1)}), bf16[4,512,256]{2,1,0:T(8,128)(2,1)S(1)}, u32[]{:S(2)}, u32[]{:S(2)}) async-start(bf16[4,512,256]{2,1,0:T(8,128)(2,1)} %forward.3), calls=%async_computation | async-start | bytes 2097152 | tf_op jit(solution)/shard_map/all_to_all | solution.py:54
  61.7 8.1 %copy-start.9 = (bf16[32,512]{1,0:T(8,128)(2,1)}, bf16[32,512]{1,0:T(8,128)(2,1)S(1)}, u32[]{:S(2)}) copy-start(bf16[32,512]{1,0:T(8,128)(2,1)S(1)} %add_convert_fusion.3) | copy-start | bytes 98308
  65.5 4.2 %collective-permute-start.11 = (f32[256,256]{1,0:T(8,128)S(1)}, f32[256,256]{1,0:T(8,128)S(1)}, u32[]{:S(2)}, u32[]{:S(2)}) collective-permute-start(f32[256,256]{1,0:T(8,128)S(1)} %fusion), channel_id=1, source_target_pairs={{0,1},{1,0},{2,3},{3,2},{4,5},{5,4},{6,7},{7,6},{8,9},{9,8},{10,11... | collective-permute-start | bytes 786440 | tf_op jit(solution)/shard_map/ppermute | solution.py:60
  69.8 29.1 %collective-permute-start.12 = (f32[256,256]{1,0:T(8,128)S(1)}, f32[256,256]{1,0:T(8,128)}, u32[]{:S(2)}, u32[]{:S(2)}) collective-permute-start(f32[256,256]{1,0:T(8,128)S(1)} %add.386), channel_id=1, source_target_pairs={{0,2},{1,3},{2,0},{3,1},{4,6},{5,7},{6,4},{7,5},{8,10},{9,11},{10,... | collective-permute-start | bytes 786440 | tf_op jit(solution)/shard_map/ppermute | solution.py:61
  76.3 66.1 %collective-permute-start.18 = (bf16[4,2048,128]{2,1,0:T(8,128)(2,1)}, bf16[4,2048,128]{2,1,0:T(8,128)(2,1)}, u32[]{:S(2)}, u32[]{:S(2)}) collective-permute-start(bf16[4,2048,128]{2,1,0:T(8,128)(2,1)} %collective-permute-done.15.refs_1_.refs_3_), channel_id=1, source_target_pairs={{0,8},{1,33},{2,10},{3,35},{4,12},{5,37},{6,14},{7,39},{8,16},{9,4... | collective-permute-start | bytes 6291464 | tf_op jit(solution)/shard_map/ppermute | solution.py:43
  95.4 47.0 %collective-permute-start.19 = (bf16[4,2048,128]{2,1,0:T(8,128)(2,1)}, bf16[4,2048,128]{2,1,0:T(8,128)(2,1)}, u32[]{:S(2)}, u32[]{:S(2)}) collective-permute-start(bf16[4,2048,128]{2,1,0:T(8,128)(2,1)} %collective-permute-done.16.refs_2_.refs_4_), channel_id=1, source_target_pairs={{0,24},{1,97},{2,26},{3,99},{4,28},{5,101},{6,30},{7,103},{8,0},{9... | collective-permute-start | bytes 6291464 | tf_op jit(solution)/shard_map/ppermute | solution.py:43
  100.5 7.0 %collective-permute-start.13 = (f32[256,256]{1,0:T(8,128)}, f32[256,256]{1,0:T(8,128)}, u32[]{:S(2)}, u32[]{:S(2)}) collective-permute-start(f32[256,256]{1,0:T(8,128)} %add.387), channel_id=1, source_target_pairs={{0,4},{1,5},{2,6},{3,7},{4,0},{5,1},{6,2},{7,3},{8,12},{9,13},{10,... | collective-permute-start | bytes 786440 | tf_op jit(solution)/shard_map/ppermute | solution.py:62
  117.7 34.2 %all-to-all-start.1 = ((bf16[4,512,512]{2,1,0:T(8,128)(2,1)}), bf16[4,512,512]{2,1,0:T(8,128)(2,1)}, u32[]{:S(2)}, u32[]{:S(2)}) async-start(bf16[4,512,512]{2,1,0:T(8,128)(2,1)} %forward.4), calls=%async_computation.1 | async-start | bytes 4194304 | tf_op jit(solution)/shard_map/all_to_all | solution.py:54
  122.2 29.7 %collective-permute-start.28 = (f32[264,256]{1,0:T(8,128)}, f32[264,256]{1,0:T(8,128)}, u32[]{:S(2)}, u32[]{:S(2)}) collective-permute-start(f32[264,256]{1,0:T(8,128)} %select_maximum_fusion), channel_id=1, source_target_pairs={{0,8},{8,0},{16,24},{24,16},{32,40},{40,32},{48,56},{56,48},{64,72... | collective-permute-start | bytes 811016 | tf_op jit(solution)/shard_map/ppermute | solution.py:70
  147.4 13.8 %collective-permute-start.23 = (bf16[512,256]{1,0:T(8,128)(2,1)}, bf16[512,256]{1,0:T(8,128)(2,1)S(1)}, u32[]{:S(2)}, u32[]{:S(2)}) collective-permute-start(bf16[512,256]{1,0:T(8,128)(2,1)} %get-tuple-element.42), channel_id=1, source_target_pairs={{0,6},{1,7},{2,0},{3,1},{4,2},{5,3},{6,4},{7,5},{8,14},{9,15},{10,... | collective-permute-start | bytes 786440 | tf_op jit(solution)/shard_map/ppermute | solution.py:428
  150.0 11.2 %collective-permute-start.22 = (bf16[512,256]{1,0:T(8,128)(2,1)}, bf16[512,256]{1,0:T(8,128)(2,1)S(1)}, u32[]{:S(2)}, u32[]{:S(2)}) collective-permute-start(bf16[512,256]{1,0:T(8,128)(2,1)} %get-tuple-element.40), channel_id=1, source_target_pairs={{0,2},{1,3},{2,4},{3,5},{4,6},{5,7},{6,0},{7,1},{8,10},{9,11},{10,... | collective-permute-start | bytes 786440 | tf_op jit(solution)/shard_map/ppermute | solution.py:428
  150.0 12.4 %collective-permute-start.21 = (bf16[512,256]{1,0:T(8,128)(2,1)}, bf16[512,256]{1,0:T(8,128)(2,1)S(1)}, u32[]{:S(2)}, u32[]{:S(2)}) collective-permute-start(bf16[512,256]{1,0:T(8,128)(2,1)} %get-tuple-element.41), channel_id=1, source_target_pairs={{0,4},{1,5},{2,6},{3,7},{4,0},{5,1},{6,2},{7,3},{8,12},{9,13},{10,... | collective-permute-start | bytes 786440 | tf_op jit(solution)/shard_map/ppermute | solution.py:428
  155.7 4.4 %copy-start.4 = (f32[256,256]{1,0:T(8,128)S(1)}, f32[256,256]{1,0:T(8,128)}, u32[]{:S(2)}) copy-start(f32[256,256]{1,0:T(8,128)} %copy-done.3) | copy-start | bytes 786436
  155.7 6.7 %copy-start.8 = (bf16[512,256]{1,0:T(8,128)(2,1)S(1)}, bf16[512,256]{1,0:T(8,128)(2,1)}, u32[]{:S(2)}) copy-start(bf16[512,256]{1,0:T(8,128)(2,1)} %get-tuple-element.39) | copy-start | bytes 786436
  155.7 33.9 %all-to-all-start.2 = ((bf16[4,512,256]{2,1,0:T(8,128)(2,1)}), bf16[4,512,256]{2,1,0:T(8,128)(2,1)}, u32[]{:S(2)}, u32[]{:S(2)}) async-start(bf16[4,512,256]{2,1,0:T(8,128)(2,1)} %arrange.1), calls=%async_computation.2 | async-start | bytes 2097152 | tf_op jit(solution)/shard_map/all_to_all | solution.py:54
  161.1 15.0 %collective-permute-start.29 = (f32[264,256]{1,0:T(8,128)S(1)}, f32[264,256]{1,0:T(8,128)S(1)}, u32[]{:S(2)}, u32[]{:S(2)}) collective-permute-start(f32[264,256]{1,0:T(8,128)S(1)} %fusion.31), channel_id=1, source_target_pairs={{0,32},{8,40},{16,48},{24,56},{32,0},{40,8},{48,16},{56,24},{64,96... | collective-permute-start | bytes 811016 | tf_op jit(solution)/shard_map/ppermute | solution.py:70
  171.9 20.8 %copy-start.7 = (bf16[4,2,8,256]{3,2,0,1:T(8,128)(2,1)S(1)}, bf16[4,2,8,256]{3,2,0,1:T(8,128)(2,1)}, u32[]{:S(2)}) copy-start(bf16[4,2,8,256]{3,2,0,1:T(8,128)(2,1)} %copy-done.6) | copy-start | bytes 98308
  171.9 20.8 %copy-start.10 = (bf16[32,512]{1,0:T(8,128)(2,1)S(1)}, bf16[32,512]{1,0:T(8,128)(2,1)}, u32[]{:S(2)}) copy-start(bf16[32,512]{1,0:T(8,128)(2,1)} %copy-done.9) | copy-start | bytes 98308
  171.9 34.5 %collective-permute-start.27 = (bf16[512,1024]{1,0:T(8,128)(2,1)S(1)}, bf16[512,1024]{1,0:T(8,128)(2,1)}, u32[]{:S(2)}, u32[]{:S(2)}) collective-permute-start(bf16[512,1024]{1,0:T(8,128)(2,1)S(1)} %get-tuple-element.46), channel_id=1, source_target_pairs={{0,1},{1,0},{2,3},{3,2},{4,5},{5,4},{6,7},{7,6},{8,9},{9,8},{10,11... | collective-permute-start | bytes 3145736 | tf_op jit(solution)/shard_map/ppermute | solution.py:454
  176.9 10.5 %collective-permute-start.30 = (f32[264,256]{1,0:T(8,128)}, f32[264,256]{1,0:T(8,128)}, u32[]{:S(2)}, u32[]{:S(2)}) collective-permute-start(f32[264,256]{1,0:T(8,128)} %add.467), channel_id=1, source_target_pairs={{0,16},{8,24},{16,0},{24,8},{32,48},{40,56},{48,32},{56,40},{64,80... | collective-permute-start | bytes 811016 | tf_op jit(solution)/shard_map/ppermute | solution.py:70
  180.2 14.3 %copy-start.5 = (bf16[512,256]{1,0:T(8,128)(2,1)S(1)}, bf16[512,256]{1,0:T(8,128)(2,1)}, u32[]{:S(2)}) copy-start(bf16[512,256]{1,0:T(8,128)(2,1)} %add_convert_fusion.2) | copy-start | bytes 786436
  189.2 12.4 %collective-permute-start.31 = (f32[264,256]{1,0:T(8,128)}, f32[264,256]{1,0:T(8,128)}, u32[]{:S(2)}, u32[]{:S(2)}) collective-permute-start(f32[264,256]{1,0:T(8,128)} %add.468), channel_id=1, source_target_pairs={{0,64},{8,72},{16,80},{24,88},{32,96},{40,104},{48,112},{56,120},{... | collective-permute-start | bytes 811016 | tf_op jit(solution)/shard_map/ppermute | solution.py:70
  191.6 18.2 %collective-permute-start.20 = (bf16[2,512,256]{2,1,0:T(8,128)(2,1)}, bf16[2,512,256]{2,1,0:T(8,128)(2,1)}, u32[]{:S(2)}, u32[]{:S(2)}) collective-permute-start(bf16[2,512,256]{2,1,0:T(8,128)(2,1)} %slice_select_fusion.1), channel_id=1, source_target_pairs={{0,1},{1,0},{2,3},{3,2},{4,5},{5,4},{6,7},{7,6},{8,9},{9,8},{10,11... | collective-permute-start | bytes 1572872 | tf_op jit(solution)/shard_map/ppermute | solution.py:434
  194.5 16.8 %collective-permute-start.25 = (bf16[512,256]{1,0:T(8,128)(2,1)S(1)}, bf16[512,256]{1,0:T(8,128)(2,1)}, u32[]{:S(2)}, u32[]{:S(2)}) collective-permute-start(bf16[512,256]{1,0:T(8,128)(2,1)S(1)} %copy-done.5), channel_id=1, source_target_pairs={{1,4},{5,5},{9,12},{13,13},{17,20},{21,21},{25,28},{29,29},{33,38}... | collective-permute-start | bytes 786440 | tf_op jit(solution)/shard_map/ppermute | solution.py:330
  200.2 11.1 %collective-permute-start.26 = (bf16[512,256]{1,0:T(8,128)(2,1)S(1)}, bf16[512,256]{1,0:T(8,128)(2,1)}, u32[]{:S(2)}, u32[]{:S(2)}) collective-permute-start(bf16[512,256]{1,0:T(8,128)(2,1)S(1)} %copy-done.5), channel_id=1, source_target_pairs={{3,4},{7,5},{11,12},{15,13},{19,20},{23,21},{27,28},{31,29},{35,38... | collective-permute-start | bytes 786440 | tf_op jit(solution)/shard_map/ppermute | solution.py:330
  201.6 10.8 %collective-permute-start.24 = (bf16[512,256]{1,0:T(8,128)(2,1)S(1)}, bf16[512,256]{1,0:T(8,128)(2,1)}, u32[]{:S(2)}, u32[]{:S(2)}) collective-permute-start(bf16[512,256]{1,0:T(8,128)(2,1)S(1)} %copy-done.5), channel_id=1, source_target_pairs={{0,1},{2,3},{4,5},{6,7},{8,9},{10,11},{12,13},{14,15},{32,33},{34,... | collective-permute-start | bytes 786440 | tf_op jit(solution)/shard_map/ppermute | solution.py:335
  (4 other events, 7.2 us)

commit v6 on v2

--- a/solution.py
+++ b/solution.py
@@ -159,13 +159,13 @@
 
 def arrange(far, here, beside):
     tokens = here.shape[1]
-    rows = tokens // 4
+    rows = tokens // 2
     return pl.pallas_call(
         arrange_kernel,
         out_shape=jax.ShapeDtypeStruct(here.shape, here.dtype),
         grid_spec=pltpu.PrefetchScalarGridSpec(
             num_scalar_prefetch=1,
-            grid=(4,),
+            grid=(2,),
             in_specs=[
                 pl.BlockSpec((SIDE, rows, here.shape[2]), lambda i, n: (0, i, 0)),
                 pl.BlockSpec((SIDE, rows, beside.shape[2]), lambda i, n: (0, i, 0)),
@@ -180,47 +180,108 @@
     )(far, here, beside)
 
 
-def backward_kernel(count, first, spots_ref, *refs):
-    lines, grads = refs[:count], refs[count : count * 5]
-    weights = jnp.concatenate([line[k] for line in lines for k in range(SIDE)], axis=1)
-    cols = jnp.concatenate([g[...] for g in grads], axis=1)
-    product = lax.dot_general(
-        cols, weights, (((1,), (1,)), ((), ())), preferred_element_type=jnp.float32
-    )
-    refs[-1][...] = product if first else refs[-2][...] + product
-
-
-def backward(spots, grown, out_grad, lines):
+def collect_kernel(spots_ref, grad_ref, out_ref, sems):
+    chunks, _, cols = out_ref.shape
+    part = cols // SIDE
+    copies = []
+    for j in range(chunks * SIDE):
+        start = pl.multiple_of(spots_ref[j] * part, part)
+        copies.append(
+            pltpu.make_async_copy(
+                grad_ref.at[:, pl.ds(start, part)],
+                out_ref.at[j // SIDE, :, pl.ds(j % SIDE * part, part)],
+                sems.at[j],
+            )
+        )
+    for copy in copies:
+        copy.start()
+    for copy in copies:
+        copy.wait()
+
+
+def collect(spots, out_grad, part):
     tokens = out_grad.shape[0]
+    count = spots.shape[0]
+    return pl.pallas_call(
+        collect_kernel,
+        out_shape=pltpu.HBM((count // SIDE, tokens, SIDE * part), out_grad.dtype),
+        grid_spec=pltpu.PrefetchScalarGridSpec(
+            num_scalar_prefetch=1,
+            grid=(1,),
+            in_specs=[pl.BlockSpec(memory_space=pl.ANY)],
+            out_specs=pl.BlockSpec(memory_space=pl.ANY),
+            scratch_shapes=[pltpu.SemaphoreType.DMA((count,))],
+        ),
+        compiler_params=pltpu.CompilerParams(vmem_limit_bytes=8 << 20),
+        cost_estimate=pl.CostEstimate(flops=0, bytes_accessed=1 << 21, transcendentals=0),
+        name="collect",
+    )(spots, pltpu.with_memory_space_constraint(out_grad, pltpu.HBM))
+
+
+def backward_kernel(count, first, last, *refs):
+    lines, grads = refs[:count], refs[count : 2 * count]
+    total = 0.0 if first else refs[2 * count][...]
+    for line, cols in zip(lines, grads):
+        weights = jnp.concatenate([line[k] for k in range(SIDE)], axis=1)
+        total = total + lax.dot_general(
+            cols[0], weights, (((1,), (1,)), ((), ())), preferred_element_type=jnp.float32
+        )
+    if not last:
+        refs[-1][...] = total
+    else:
+
+        @pl.when(pl.program_id(0) < 2)
+        def _():
+            refs[-1][...] = total.astype(jnp.bfloat16)
+
+        @pl.when(pl.program_id(0) >= 2)
+        def _():
+            refs[-2][...] = total
+
+
+def backward(places, grown, grads, lines, last=False):
+    tokens, cols = grads.shape[1:]
     depth, part = lines[0].shape[1:]
     count = len(lines)
-    block = depth // 2
+    block = depth // 4
     first = grown is None
 
-    def column(j):
-        return pl.BlockSpec((tokens, part), lambda i, n: (0, n[j]))
-
-    total = pl.BlockSpec((tokens, block), lambda i, n: (0, i))
-    return pl.pallas_call(
-        functools.partial(backward_kernel, count, first),
-        out_shape=pltpu.HBM((tokens, depth), jnp.float32),
-        grid_spec=pltpu.PrefetchScalarGridSpec(
-            num_scalar_prefetch=1,
-            grid=(2,),
-            in_specs=[pl.BlockSpec((SIDE, block, part), lambda i, n: (0, i, 0))] * count
-            + [column(j) for j in range(count * SIDE)]
-            + ([] if first else [total]),
-            out_specs=total,
-        ),
-        input_output_aliases={} if first else {5 * count + 1: 0},
-        compiler_params=pltpu.CompilerParams(vmem_limit_bytes=36 << 20),
+    def chunk(place):
+        return pl.BlockSpec((1, tokens, cols), lambda i: (place, 0, 0))
+
+    total = pl.BlockSpec((tokens, block), lambda i: (0, (i + 2) % 4))
+    outs, specs = [pltpu.HBM((tokens, depth), jnp.float32)], [total]
+    if last:
+        outs = [
+            jax.ShapeDtypeStruct((tokens, depth // 2), jnp.float32),
+            jax.ShapeDtypeStruct((tokens, depth // 2), jnp.bfloat16),
+        ]
+        specs = [
+            pl.BlockSpec((tokens, block), lambda i: (0, jnp.maximum(i - 2, 0))),
+            pl.BlockSpec((tokens, block), lambda i: (0, jnp.minimum(i, 1))),
+        ]
+    made = pl.pallas_call(
+        functools.partial(backward_kernel, count, first, last),
+        out_shape=outs,
+        grid=(4,),
+        in_specs=[pl.BlockSpec((SIDE, block, part), lambda i: (0, (i + 2) % 4, 0))] * count
+        + [chunk(place) for place in places]
+        + ([] if first else [total]),
+        out_specs=specs,
+        input_output_aliases={} if first or last else {2 * count: 0},
+        compiler_params=pltpu.CompilerParams(vmem_limit_bytes=28 << 20),
         cost_estimate=pl.CostEstimate(
             flops=tokens * depth * count * part,
             bytes_accessed=depth * part * count,
             transcendentals=0,
         ),
         name="backward",
-    )(spots, *lines, *([pltpu.with_memory_space_constraint(out_grad, pltpu.HBM)] * (count * SIDE)), *([] if first else [grown]))
+    )(
+        *lines,
+        *([pltpu.with_memory_space_constraint(grads, pltpu.HBM)] * count),
+        *([] if first else [pltpu.with_memory_space_constraint(grown, pltpu.HBM)]),
+    )
+    return made if last else made[0]
 
 
 def compose(logits, indices, vector_bank):
@@ -281,7 +342,6 @@
         cols = slice(h * part, (h + 1) * part)
         shards.append(jnp.concatenate([mine[:, cols], swapped[:, cols]], axis=0))
     logits_a, logits_b, *shards = lax.optimization_barrier((logits_a, logits_b, *shards))
-    lines = [jnp.stack(ring_gather(shards[h], 0, h)) for h in range(2)]
     def columns(i, h):
         far_at = (far + i) % SIDE
         spots = []
@@ -292,9 +352,15 @@
             spots.append((x_at * SIDE + z_at) * 4 + core * 2 + h)
         return spots
 
-    def spots_of(chunks):
-        return jnp.stack([s for i, h in chunks for s in columns(i, h)]).astype(jnp.int32)
-
+    chunks = [(i, h) for i in range(SIDE) for h in range(2)]
+    spots = jnp.stack([s for i, h in chunks for s in columns(i, h)]).astype(jnp.int32)
+    grads = collect(after(spots, *shards), out_grad, part)
+
+    def places(chunks):
+        return [i * 2 + h for i, h in chunks]
+
+    lines = [jnp.stack(ring_gather(shards[h], 0, h)) for h in range(2)]
+    lines[0], grads = lax.optimization_barrier((lines[0], grads))
     wide = jnp.concatenate([attn_out, lax.ppermute(attn_out, "tensor", SWAP)], axis=1)
 
     weights_a, picked_a, mixing_a, rows_a = compose(logits_a, index_a, vector_bank)
@@ -316,8 +382,6 @@
     grad_a = jnp.dot(back_bf, attn_out, preferred_element_type=f32)
     grad_b = jnp.dot(low_bf, grad_cols, preferred_element_type=f32)
     both = factor * jnp.concatenate([grad_a, grad_b], axis=0)
-    both_parts = over_side(both, 0)
-
     here = [(0, 0), (0, 1)]
     beside = [(1, 0), (3, 0), (1, 1), (3, 1)]
     across = [(2, 0), (2, 1)]
@@ -327,34 +391,35 @@
 
     sent_here = forward(turned, wide, take(here))
     slots_here = exchange(sent_here, "tensor", LANES)
-    grown = backward(after(spots_of(here), sent_here), None, out_grad, take(here))
+    grads, sent_here = lax.optimization_barrier((grads, sent_here))
+    grown = backward(places(here), None, grads, take(here))
     sent_beside = forward(after(turned, grown), wide, take(beside[:2]), places=2)
     sent_beside = forward(turned, wide, take(beside[2:]), places=2, into=sent_beside)
-    slots_here, sent_beside, *both_parts = lax.optimization_barrier(
-        (slots_here, sent_beside, *both_parts)
-    )
+    slots_here, sent_beside, both = lax.optimization_barrier((slots_here, sent_beside, both))
     slots_beside = exchange(sent_beside, "tensor", LANES)
-    both_parts = over_side(total_of(both_parts), 1)
-    grown = backward(after(spots_of(beside), sent_beside), grown, out_grad, take(beside))
+    both_parts = over_side(both, 0)
+    grads, sent_beside = lax.optimization_barrier((grads, sent_beside))
+    grown = backward(places(beside), grown, grads, take(beside))
     sent = forward(after(turned_here, grown), wide, take(across), apart=True)
-    slots_beside, *both_parts = lax.optimization_barrier((slots_beside, *both_parts, *sent))[:5]
-    both = total_of(both_parts)
-    bank_a, logit_grad_a = compose_back(both[:rank], weights_a, picked_a, mixing_a, vector_bank)
-    bank_b, logit_grad_b = compose_back(both[rank:], weights_b, picked_b, mixing_b, vector_bank)
-
-    slots = arrange(far.astype(jnp.int32).reshape(1), slots_here, slots_beside)
-    moved = exchange(slots, "tensor", LANES)
-    crossed = lax.ppermute(jnp.where(core == 0, slots[2:], moved[:2]), "tensor", SWAP)
-    firsts = jnp.where(core == 0, slots[:2], crossed)
-    seconds = jnp.where(core == 0, crossed, moved[2:])
-
     arrived = [sent[0]]
     for step in range(1, SIDE):
         turns = [(t, (t + 2 * step) % 8) for t in range(8)]
         arrived.append(lax.ppermute(sent[step], "tensor", turns))
     piece = total_of([a.astype(f32) for a in arrived]).astype(bf16)
+    slots_beside, *both_parts = lax.optimization_barrier((slots_beside, *both_parts, *sent))[:5]
+    both_parts = over_side(total_of(both_parts), 1)
+    slots = arrange(far.astype(jnp.int32).reshape(1), slots_here, slots_beside)
+    moved = exchange(slots, "tensor", LANES)
+    both = total_of(lax.optimization_barrier((*both_parts, slots))[:SIDE])
+    bank_a, logit_grad_a = compose_back(both[:rank], weights_a, picked_a, mixing_a, vector_bank)
+    bank_b, logit_grad_b = compose_back(both[rank:], weights_b, picked_b, mixing_b, vector_bank)
+    crossed = lax.ppermute(jnp.where(core == 0, slots[2:], moved[:2]), "tensor", SWAP)
+    firsts = jnp.where(core == 0, slots[:2], crossed)
+    seconds = jnp.where(core == 0, crossed, moved[2:])
+
     bank_grad = over_tensor(bank_a + bank_b)
-    grown = backward(after(spots_of(across), slots), grown, out_grad, take(across))
+    grads, slots, piece = lax.optimization_barrier((grads, slots, piece))
+    grown, other = backward(places(across), grown, grads, take(across), last=True)
     first, place, second = settle(piece, 2, z, core)
     cols = []
     for s in range(2):
@@ -365,9 +430,9 @@
         summed.astype(f32)
         + adapter_scale * lax.dot_general(low_bf, up_b, rows_by_rows, preferred_element_type=f32)
     ).astype(bf16)
-    other = lax.ppermute(grown[:, height:].astype(bf16), "tensor", SWAP)
+    other = lax.ppermute(other, "tensor", SWAP)
     attn_grad = (
-        grown[:, :height]
+        grown
         + other.astype(f32)
         + adapter_scale * lax.dot_general(back_bf, down_a, rows_by_rows, preferred_element_type=f32)
     ).astype(bf16)

time: 201 us -> 317 us (1.58); the launches traced: 200 us -> 312 us
  Pallas kernels: 48.1 us -> 175 us
  waiting for transfers between devices: 48.4 us -> 29.5 us
  starting transfers between devices: 59.9 us -> 71.7 us
  local copies, waits for them, and re-layouts: 6.67 us -> 2.95 us
    pallas_call x3 -> x4, Pallas kernels: 23.9 us -> 152 us  [the longest x1 129 us: collect(): pl.pallas_call(collect_kernel, out_shape=pltpu.HBM((count // SIDE, tokens...]
    ppermute x12, waiting for transfers between devices: 30.1 us -> 14.6 us  [shift(): return lax.ppermute(value, BOTH, ring(stage, step))]
    ppermute x6, waiting for transfers between devices: 8.47 us -> 0.02 us  [from_step(): return lax.ppermute(value, BOTH, pairs(move))]
    ppermute x1, starting transfers between devices: 0.01 us -> 6.76 us  [local(): other = lax.ppermute(other, 'tensor', SWAP)]
    ppermute x2, starting transfers between devices: 3.43 us -> 9.92 us  [over_tensor(): value = value + lax.ppermute(value, 'tensor', SWAP)]
    ppermute x12, starting transfers between devices: 18 us -> 13.4 us  [shift(): return lax.ppermute(value, BOTH, ring(stage, step))]
  transfers between devices with their start and end apart: 37 -> 37, of which waited for: 11 -> 10; matrix products, arithmetic and copies ran while one was open for 17% -> 9% of each run, Pallas kernels for 24% -> 56%
where the time goes in v6:
time: 317 us; the launch traced here: 312 us
  Pallas kernels  175 us (55%)
  starting transfers between devices  71.7 us (23%)
  waiting for transfers between devices  29.5 us (9%)
  other arithmetic  20 us (6%)
  matrix products  12.2 us (4%)
    pallas_call x1, Pallas kernels, collect(): pl.pallas_call(collect_kernel, out_shape=pltpu.HBM((count // SIDE, tokens...  129 us
    pallas_call x3, Pallas kernels, backward(): pl.pallas_call(functools.partial(backward_kernel, count, first, last), ou...  22.7 us
    pallas_call x4, Pallas kernels, forward(): pl.pallas_call(functools.partial(forward_kernel, count), out_shape=outs,...  20.5 us
    ppermute x12, waiting for transfers between devices, shift(): return lax.ppermute(value, BOTH, ring(stage, step))  14.6 us
    ppermute x12, starting transfers between devices, shift(): return lax.ppermute(value, BOTH, ring(stage, step))  13.4 us
    all_to_all x3, starting transfers between devices, exchange(): lax.all_to_all(value, axis, split_axis=0, concat_axis=0, tiled=True, axis...  12.4 us
    ppermute x2, starting transfers between devices, over_tensor(): value = value + lax.ppermute(value, 'tensor', SWAP)  9.92 us
    ppermute x6, starting transfers between devices, from_step(): return lax.ppermute(value, BOTH, pairs(move))  7.39 us
  transfers between devices with their start and end apart: 37, of which 10 were waited for; matrix products, arithmetic and copies ran while one was open for 9% of the time, Pallas kernels for 56%

profile of v6, /device:TPU:1, one launch (start us, length us, event | category | flops | bytes accessed | tf_op | source)
XLA Modules:
  0.0 312.3 jit_solution(13731505458654275471)
XLA Ops:
  2.0 1.5 collective-permute-start.1
  5.1 3.9 %collective-permute-start.5 = (bf16[2048,128]{1,0:T(8,128)(2,1)S(1)}, bf16[2048,128]{1,0:T(8,128)(2,1)S(1)}, u32[]{:S(2)}, u32[]{:S(2)}) collective-permute-start(bf16[2048,128]{1,0:T(8,128)(2,1)S(1)} %get-tuple-element.39), channel_id=1, source_target_pairs={{0,96},{1,25},{2,98},{3,27},{4,100},{5,29},{6,102},{7,31},{8,104},... | collective-permute-start | bytes 1572872 | tf_op jit(solution)/shard_map/ppermute | solution.py:43
  9.0 2.7 collective-permute-start.2
  12.7 129.0 %collect.1.refs_2_.refs_3_.refs_4_.refs_5_.refs_6_.refs_7_ = bf16[8,512,512]{2,1,0:T(8,128)(2,1)} custom-call(s32[32]{0:T(128)S(1)} %stack.166.spots_ref, bf16[512,8192]{1,0:T(8,128)(2,1)} %grad_ref.1), custom_call_target="tpu_custom_call" | custom-call | bytes 2097152 | tf_op jit(solution)/shard_map/collect/pallas_call | solution.py:205
  141.7 1.5 collective-permute-start.6
  143.2 1.6 fusion.44
  144.8 1.6 fusion.11
  146.5 3.6 %collective-permute-done.6 = bf16[2048,128]{1,0:T(8,128)(2,1)S(1)} collective-permute-done((bf16[2048,128]{1,0:T(8,128)(2,1)S(1)}, bf16[2048,128]{1,0:T(8,128)(2,1)S(1)}, u32[]{:S(2)}, u32[]{:S(2)}) %collective-permute-start.6) | collective-permute-done | bytes 524320 | tf_op jit(solution)/shard_map/ppermute | solution.py:43
  150.1 2.7 pad_maximum_fusion.1.refs_1_
  152.7 1.6 collective-permute-done.4
  154.3 1.7 pad_maximum_fusion.refs_0_
  156.0 2.2 collective-permute-start.8
  158.2 3.2 %collective-permute-start.12 = (f32[32,512]{1,0:T(8,128)S(1)}, f32[32,512]{1,0:T(8,128)S(1)}, u32[]{:S(2)}, u32[]{:S(2)}) collective-permute-start(f32[32,512]{1,0:T(8,128)S(1)} %pad_maximum_fusion.4), channel_id=1, source_target_pairs={{0,1},{1,0},{2,3},{3,2},{4,5},{5,4},{6,7},{7,6},{8,9},{9,8},{10,11... | collective-permute-start | bytes 196616 | tf_op jit(solution)/shard_map/ppermute | solution.py:60
  162.3 1.4 collective-permute-start.13
  166.5 1.7 collective-permute-start
  168.2 1.3 constant_dynamic-update-slice_fusion.1
  170.7 2.6 collective-permute-start.14
  173.4 5.1 %forward.4 = bf16[4,512,256]{2,1,0:T(8,128)(2,1)} custom-call(s32[1]{0:T(128)} %bitcast.1.start_ref, bf16[512,2048]{1,0:T(8,128)(2,1)S(1)} %constant_dynamic-update-slice_fusion.wide_ref, bf16[4,2048,128]{2,1,0:T(8,128)(2,1)} %pad_maximum_fusion.refs_0_, bf16[4,2048,128]{2,1,0:T(8,128)(2,1)} %pad_maximum_fusion.1.refs_1_), custom_call_target="tpu_custom_call" | custom-call | flops 268435456 | bytes 524288 | tf_op jit(solution)/shard_map/forward/pallas_call | solution.py:119
  178.5 3.5 %all-to-all-start = ((bf16[4,512,256]{2,1,0:T(8,128)(2,1)}), bf16[4,512,256]{2,1,0:T(8,128)(2,1)S(1)}, u32[]{:S(2)}, u32[]{:S(2)}) async-start(bf16[4,512,256]{2,1,0:T(8,128)(2,1)} %forward.4), calls=%async_computation | async-start | bytes 2097152 | tf_op jit(solution)/shard_map/all_to_all | solution.py:54
  182.0 6.5 %backward.3.refs_8_ = f32[512,2048]{1,0:T(8,128)} custom-call(bf16[4,2048,128]{2,1,0:T(8,128)(2,1)} %pad_maximum_fusion.refs_0_, bf16[4,2048,128]{2,1,0:T(8,128)(2,1)} %pad_maximum_fusion.1.refs_1_, bf16[8,512,512]{2,1,0:T(8,128)(2,1)} %collect.1.refs_2_.refs_3_.refs_4_.refs_5_.refs_6_.refs_7_, ...), custom_call_target="tpu_custom_call" | custom-call | flops 268435456 | bytes 524288 | tf_op jit(solution)/shard_map/backward/pallas_call | solution.py:263
  191.0 1.5 fusion.9
  192.5 1.5 fusion.35
  194.6 9.3 %collective-permute-done.10.refs_0_ = bf16[4,2048,128]{2,1,0:T(8,128)(2,1)} collective-permute-done((bf16[4,2048,128]{2,1,0:T(8,128)(2,1)}, bf16[4,2048,128]{2,1,0:T(8,128)(2,1)}, u32[]{:S(2)}, u32[]{:S(2)}) %collective-permute-start.10) | collective-permute-done | bytes 2097184 | tf_op jit(solution)/shard_map/ppermute | solution.py:43
  204.0 5.1 %forward.5.refs_2_ = bf16[4,512,512]{2,1,0:T(8,128)(2,1)} custom-call(s32[1]{0:T(128)} %bitcast.1.start_ref, bf16[512,2048]{1,0:T(8,128)(2,1)S(1)} %constant_dynamic-update-slice_fusion.wide_ref, bf16[4,2048,128]{2,1,0:T(8,128)(2,1)} %collective-permute-done.10.refs_0_, bf16[4,2048,128]{2,1,0:T(8,128)(2,1)} %collective-permute-done.11.refs_1_), custom_call_target="tpu_custom_call" | custom-call | flops 268435456 | bytes 524288 | tf_op jit(solution)/shard_map/forward/pallas_call | solution.py:119
  209.1 5.2 %forward.6 = bf16[4,512,512]{2,1,0:T(8,128)(2,1)} custom-call(s32[1]{0:T(128)} %bitcast.1.start_ref, bf16[512,2048]{1,0:T(8,128)(2,1)S(1)} %constant_dynamic-update-slice_fusion.wide_ref, bf16[4,2048,128]{2,1,0:T(8,128)(2,1)} %collective-permute-done.8.refs_0_.refs_2_, ...), custom_call_target="tpu_custom_call", output_to_operand_aliasing={{}: (4, {})} | custom-call | flops 268435456 | bytes 524288 | tf_op jit(solution)/shard_map/forward/pallas_call | solution.py:119
  214.3 4.5 %all-to-all-start.1 = ((bf16[4,512,512]{2,1,0:T(8,128)(2,1)}), bf16[4,512,512]{2,1,0:T(8,128)(2,1)}, u32[]{:S(2)}, u32[]{:S(2)}) async-start(bf16[4,512,512]{2,1,0:T(8,128)(2,1)} %forward.6), calls=%async_computation.1 | async-start | bytes 4194304 | tf_op jit(solution)/shard_map/all_to_all | solution.py:54
  219.7 3.7 %collective-permute-start.16 = (f32[32,1024]{1,0:T(8,128)}, f32[32,1024]{1,0:T(8,128)}, u32[]{:S(2)}, u32[]{:S(2)}) collective-permute-start(f32[32,1024]{1,0:T(8,128)} %maximum_multiply_fusion), channel_id=1, source_target_pairs={{0,64},{1,65},{2,66},{3,67},{4,68},{5,69},{6,70},{7,71},{8,72},{9,... | collective-permute-start | bytes 393224 | tf_op jit(solution)/shard_map/ppermute | solution.py:72
  223.4 10.0 %backward.4.refs_4_ = f32[512,2048]{1,0:T(8,128)} custom-call(bf16[4,2048,128]{2,1,0:T(8,128)(2,1)} %collective-permute-done.10.refs_0_, bf16[4,2048,128]{2,1,0:T(8,128)(2,1)} %collective-permute-done.11.refs_1_, bf16[4,2048,128]{2,1,0:T(8,128)(2,1)} %collective-permute-done.8.refs_0_.refs_2_, ...), custom_call_target="tpu_custom_call", output_to_operand_aliasing={{}: (8, {})} | custom-call | flops 536870912 | bytes 1048576 | tf_op jit(solution)/shard_map/backward/pallas_call | solution.py:263
  233.4 5.1 %forward.7 = (bf16[512,256]{1,0:T(8,128)(2,1)}, bf16[512,256]{1,0:T(8,128)(2,1)}, bf16[512,256]{1,0:T(8,128)(2,1)}, bf16[512,256]{1,0:T(8,128)(2,1)}) custom-call(s32[1]{0:T(128)} %bitcast.43.start_ref, bf16[512,2048]{1,0:T(8,128)(2,1)S(1)} %constant_dynamic-update-slice_fusion.wide_ref, bf16[4,2048,128]{2,1,0:T(8,128)(2,1)} %collective-permute-done.18.refs_0_, ...), custom_call_target="tpu_custom_call" | custom-call | flops 268435456 | bytes 524288 | tf_op jit(solution)/shard_map/forward/pallas_call | solution.py:119
  238.5 2.8 all-to-all-done.1.beside_ref
  242.7 2.5 collective-permute-start.30
  245.2 2.5 fusion.33
  249.2 2.6 arrange.1
  251.8 4.4 %all-to-all-start.2 = ((bf16[4,512,256]{2,1,0:T(8,128)(2,1)}), bf16[4,512,256]{2,1,0:T(8,128)(2,1)}, u32[]{:S(2)}, u32[]{:S(2)}) async-start(bf16[4,512,256]{2,1,0:T(8,128)(2,1)} %arrange.1), calls=%async_computation.2 | async-start | bytes 2097152 | tf_op jit(solution)/shard_map/all_to_all | solution.py:54
  256.3 2.6 collective-permute-start.23
  259.8 6.7 %collective-permute-start.31 = (f32[256,256]{1,0:T(8,128)S(1)}, f32[256,256]{1,0:T(8,128)S(1)}, u32[]{:S(2)}, u32[]{:S(2)}) collective-permute-start(f32[256,256]{1,0:T(8,128)S(1)} %fusion.2), channel_id=1, source_target_pairs={{0,1},{1,0},{2,3},{3,2},{4,5},{5,4},{6,7},{7,6},{8,9},{9,8},{10,11... | collective-permute-start | bytes 786440 | tf_op jit(solution)/shard_map/ppermute | solution.py:60
  267.1 2.7 collective-permute-done.23
  270.6 6.2 %backward.5 = (f32[512,1024]{1,0:T(8,128)S(1)}, bf16[512,1024]{1,0:T(8,128)(2,1)S(1)}) custom-call(bf16[4,2048,128]{2,1,0:T(8,128)(2,1)} %collective-permute-done.18.refs_0_, bf16[4,2048,128]{2,1,0:T(8,128)(2,1)} %collective-permute-done.19.refs_1_, bf16[8,512,512]{2,1,0:T(8,128)(2,1)} %collect.1.refs_2_.refs_3_.refs_4_.refs_5_.refs_6_.refs_7_, ...), custom_call_target="tpu_custom_call" | custom-call | flops 268435456 | bytes 524288 | tf_op jit(solution)/shard_map/backward/pallas_call | solution.py:263
  276.8 6.8 %collective-permute-start.27 = (bf16[512,1024]{1,0:T(8,128)(2,1)S(1)}, bf16[512,1024]{1,0:T(8,128)(2,1)}, u32[]{:S(2)}, u32[]{:S(2)}) collective-permute-start(bf16[512,1024]{1,0:T(8,128)(2,1)S(1)} %get-tuple-element.62), channel_id=1, source_target_pairs={{0,1},{1,0},{2,3},{3,2},{4,5},{5,4},{6,7},{7,6},{8,9},{9,8},{10,11... | collective-permute-start | bytes 3145736 | tf_op jit(solution)/shard_map/ppermute | solution.py:433
  284.0 1.8 collective-permute-start.32
  286.6 5.9 %collective-permute-done.32 = f32[256,256]{1,0:T(8,128)S(1)} collective-permute-done((f32[256,256]{1,0:T(8,128)S(1)}, f32[256,256]{1,0:T(8,128)S(1)}, u32[]{:S(2)}, u32[]{:S(2)}) %collective-permute-start.32) | collective-permute-done | bytes 262176 | tf_op jit(solution)/shard_map/ppermute | solution.py:61
  293.2 2.0 collective-permute-start.33
  295.2 1.4 slice_select_fusion.1
  299.6 3.8 %collective-permute-start.25 = (bf16[512,256]{1,0:T(8,128)(2,1)}, bf16[512,256]{1,0:T(8,128)(2,1)S(1)}, u32[]{:S(2)}, u32[]{:S(2)}) collective-permute-start(bf16[512,256]{1,0:T(8,128)(2,1)} %add_convert_fusion.2), channel_id=1, source_target_pairs={{1,4},{5,5},{9,12},{13,13},{17,20},{21,21},{25,28},{29,29},{33,38}... | collective-permute-start | bytes 786440 | tf_op jit(solution)/shard_map/ppermute | solution.py:312
  304.1 1.8 add.475
  305.9 2.8 add_convert_fusion
  308.7 1.3 slice_select_fusion.2
  310.8 1.4 add_convert_fusion.1
  (125 shorter events, 24.4 us)
Async XLA Ops:
  0.6 11.3 %copy-start = (f32[256,256]{1,0:T(8,128)S(1)}, f32[256,256]{1,0:T(8,128)}, u32[]{:S(2)}) copy-start(f32[256,256]{1,0:T(8,128)} %param.10) | copy-start | bytes 786436
  2.0 3.0 collective-permute-start.1
  3.6 8.2 %copy-start.15 = (f32[16,4,2]{0,2,1:T(2,128)S(1)}, f32[16,4,2]{0,2,1:T(2,128)}, u32[]{:S(2)}) copy-start(f32[16,4,2]{0,2,1:T(2,128)} %param.11) | copy-start | bytes 1540
  3.6 8.2 %copy-start.16 = (f32[16,4,2]{0,2,1:T(2,128)S(1)}, f32[16,4,2]{0,2,1:T(2,128)}, u32[]{:S(2)}) copy-start(f32[16,4,2]{0,2,1:T(2,128)} %param.13) | copy-start | bytes 1540
  3.6 8.3 %copy-start.14 = (s32[16,4,2]{0,2,1:T(2,128)S(1)}, s32[16,4,2]{0,2,1:T(2,128)}, u32[]{:S(2)}) copy-start(s32[16,4,2]{0,2,1:T(2,128)} %param.12) | copy-start | bytes 1540
  3.7 8.6 %copy-start.13 = (s32[16,4,2]{0,2,1:T(2,128)S(1)}, s32[16,4,2]{0,2,1:T(2,128)}, u32[]{:S(2)}) copy-start(s32[16,4,2]{0,2,1:T(2,128)} %param.14) | copy-start | bytes 1540
  5.1 136.5 %collective-permute-start.5 = (bf16[2048,128]{1,0:T(8,128)(2,1)S(1)}, bf16[2048,128]{1,0:T(8,128)(2,1)S(1)}, u32[]{:S(2)}, u32[]{:S(2)}) collective-permute-start(bf16[2048,128]{1,0:T(8,128)(2,1)S(1)} %get-tuple-element.39), channel_id=1, source_target_pairs={{0,96},{1,25},{2,98},{3,27},{4,100},{5,29},{6,102},{7,31},{8,104},... | collective-permute-start | bytes 1572872 | tf_op jit(solution)/shard_map/ppermute | solution.py:43
  9.0 137.4 %collective-permute-start.7 = (bf16[2048,128]{1,0:T(8,128)(2,1)S(1)}, bf16[2048,128]{1,0:T(8,128)(2,1)}, u32[]{:S(2)}, u32[]{:S(2)}) collective-permute-start(bf16[2048,128]{1,0:T(8,128)(2,1)S(1)} %get-tuple-element.39), channel_id=1, source_target_pairs={{0,32},{1,9},{2,34},{3,11},{4,36},{5,13},{6,38},{7,15},{8,40},{9,1... | collective-permute-start | bytes 1572872 | tf_op jit(solution)/shard_map/ppermute | solution.py:43
  9.0 135.7 %collective-permute-start.3 = (bf16[2048,128]{1,0:T(8,128)(2,1)S(1)}, bf16[2048,128]{1,0:T(8,128)(2,1)S(1)}, u32[]{:S(2)}, u32[]{:S(2)}) collective-permute-start(bf16[2048,128]{1,0:T(8,128)(2,1)S(1)} %get-tuple-element.38), channel_id=1, source_target_pairs={{0,32},{1,9},{2,34},{3,11},{4,36},{5,13},{6,38},{7,15},{8,40},{9,1... | collective-permute-start | bytes 1572872 | tf_op jit(solution)/shard_map/ppermute | solution.py:43
  9.0 143.7 %collective-permute-start.2 = (bf16[2048,128]{1,0:T(8,128)(2,1)S(1)}, bf16[2048,128]{1,0:T(8,128)(2,1)S(1)}, u32[]{:S(2)}, u32[]{:S(2)}) collective-permute-start(bf16[2048,128]{1,0:T(8,128)(2,1)S(1)} %get-tuple-element.38), channel_id=1, source_target_pairs={{0,96},{1,25},{2,98},{3,27},{4,100},{5,29},{6,102},{7,31},{8,104},... | collective-permute-start | bytes 1572872 | tf_op jit(solution)/shard_map/ppermute | solution.py:43
  12.3 130.9 %copy-start.3 = (bf16[4,2,8,256]{3,2,0,1:T(8,128)(2,1)}, bf16[4,2,8,256]{3,2,0,1:T(8,128)(2,1)S(1)}, u32[]{:S(2)}) copy-start(bf16[4,2,8,256]{3,2,0,1:T(8,128)(2,1)S(1)} %copy.45) | copy-start | bytes 98308
  12.6 132.2 %copy-start.9 = (bf16[4,2,8,256]{3,2,0,1:T(8,128)(2,1)}, bf16[4,2,8,256]{3,2,0,1:T(8,128)(2,1)S(1)}, u32[]{:S(2)}) copy-start(bf16[4,2,8,256]{3,2,0,1:T(8,128)(2,1)S(1)} %copy.46) | copy-start | bytes 98308
  141.7 8.4 %collective-permute-start.6 = (bf16[2048,128]{1,0:T(8,128)(2,1)S(1)}, bf16[2048,128]{1,0:T(8,128)(2,1)S(1)}, u32[]{:S(2)}, u32[]{:S(2)}) collective-permute-start(bf16[2048,128]{1,0:T(8,128)(2,1)S(1)} %collective-permute-done.5), channel_id=1, source_target_pairs={{0,96},{1,25},{2,98},{3,27},{4,100},{5,29},{6,102},{7,31},{8,104},... | collective-permute-start | bytes 1572872 | tf_op jit(solution)/shard_map/ppermute | solution.py:43
  144.8 9.6 %collective-permute-start.4 = (bf16[2048,128]{1,0:T(8,128)(2,1)S(1)}, bf16[2048,128]{1,0:T(8,128)(2,1)S(1)}, u32[]{:S(2)}, u32[]{:S(2)}) collective-permute-start(bf16[2048,128]{1,0:T(8,128)(2,1)S(1)} %collective-permute-done.3), channel_id=1, source_target_pairs={{0,32},{1,9},{2,34},{3,11},{4,36},{5,13},{6,38},{7,15},{8,40},{9,1... | collective-permute-start | bytes 1572872 | tf_op jit(solution)/shard_map/ppermute | solution.py:43
  156.0 33.5 %collective-permute-start.8 = (bf16[4,2048,128]{2,1,0:T(8,128)(2,1)}, bf16[4,2048,128]{2,1,0:T(8,128)(2,1)}, u32[]{:S(2)}, u32[]{:S(2)}) collective-permute-start(bf16[4,2048,128]{2,1,0:T(8,128)(2,1)} %pad_maximum_fusion.1.refs_1_), channel_id=1, source_target_pairs={{0,24},{1,97},{2,26},{3,99},{4,28},{5,101},{6,30},{7,103},{8,0},{9... | collective-permute-start | bytes 6291464 | tf_op jit(solution)/shard_map/ppermute | solution.py:43
  158.2 32.1 %collective-permute-start.11 = (bf16[4,2048,128]{2,1,0:T(8,128)(2,1)}, bf16[4,2048,128]{2,1,0:T(8,128)(2,1)}, u32[]{:S(2)}, u32[]{:S(2)}) collective-permute-start(bf16[4,2048,128]{2,1,0:T(8,128)(2,1)} %pad_maximum_fusion.refs_0_), channel_id=1, source_target_pairs={{0,8},{1,33},{2,10},{3,35},{4,12},{5,37},{6,14},{7,39},{8,16},{9,4... | collective-permute-start | bytes 6291464 | tf_op jit(solution)/shard_map/ppermute | solution.py:43
  158.2 4.1 %collective-permute-start.12 = (f32[32,512]{1,0:T(8,128)S(1)}, f32[32,512]{1,0:T(8,128)S(1)}, u32[]{:S(2)}, u32[]{:S(2)}) collective-permute-start(f32[32,512]{1,0:T(8,128)S(1)} %pad_maximum_fusion.4), channel_id=1, source_target_pairs={{0,1},{1,0},{2,3},{3,2},{4,5},{5,4},{6,7},{7,6},{8,9},{9,8},{10,11... | collective-permute-start | bytes 196616 | tf_op jit(solution)/shard_map/ppermute | solution.py:60
  162.3 3.6 %collective-permute-start.13 = (f32[32,512]{1,0:T(8,128)S(1)}, f32[32,512]{1,0:T(8,128)S(1)}, u32[]{:S(2)}, u32[]{:S(2)}) collective-permute-start(f32[32,512]{1,0:T(8,128)S(1)} %add.448), channel_id=1, source_target_pairs={{0,2},{1,3},{2,0},{3,1},{4,6},{5,7},{6,4},{7,5},{8,10},{9,11},{10,... | collective-permute-start | bytes 196616 | tf_op jit(solution)/shard_map/ppermute | solution.py:61
  163.7 40.3 %collective-permute-start.10 = (bf16[4,2048,128]{2,1,0:T(8,128)(2,1)}, bf16[4,2048,128]{2,1,0:T(8,128)(2,1)}, u32[]{:S(2)}, u32[]{:S(2)}) collective-permute-start(bf16[4,2048,128]{2,1,0:T(8,128)(2,1)} %pad_maximum_fusion.refs_0_), channel_id=1, source_target_pairs={{0,24},{1,97},{2,26},{3,99},{4,28},{5,101},{6,30},{7,103},{8,0},{9... | collective-permute-start | bytes 6291464 | tf_op jit(solution)/shard_map/ppermute | solution.py:43
  164.5 44.6 %collective-permute-start.9 = (bf16[4,2048,128]{2,1,0:T(8,128)(2,1)}, bf16[4,2048,128]{2,1,0:T(8,128)(2,1)}, u32[]{:S(2)}, u32[]{:S(2)}) collective-permute-start(bf16[4,2048,128]{2,1,0:T(8,128)(2,1)} %pad_maximum_fusion.1.refs_1_), channel_id=1, source_target_pairs={{0,8},{1,33},{2,10},{3,35},{4,12},{5,37},{6,14},{7,39},{8,16},{9,4... | collective-permute-start | bytes 6291464 | tf_op jit(solution)/shard_map/ppermute | solution.py:43
  166.5 4.2 %collective-permute-start = (bf16[512,1024]{1,0:T(8,128)(2,1)}, bf16[512,1024]{1,0:T(8,128)(2,1)S(1)}, u32[]{:S(2)}, u32[]{:S(2)}) collective-permute-start(bf16[512,1024]{1,0:T(8,128)(2,1)} %param.8), channel_id=1, source_target_pairs={{0,1},{1,0},{2,3},{3,2},{4,5},{5,4},{6,7},{7,6},{8,9},{9,8},{10,11... | collective-permute-start | bytes 3145736 | tf_op jit(solution)/shard_map/ppermute | solution.py:364
  170.7 17.9 %collective-permute-start.14 = (f32[32,512]{1,0:T(8,128)}, f32[32,512]{1,0:T(8,128)}, u32[]{:S(2)}, u32[]{:S(2)}) collective-permute-start(f32[32,512]{1,0:T(8,128)} %add.449), channel_id=1, source_target_pairs={{0,4},{1,5},{2,6},{3,7},{4,0},{5,1},{6,2},{7,3},{8,12},{9,13},{10,... | collective-permute-start | bytes 196616 | tf_op jit(solution)/shard_map/ppermute | solution.py:62
  178.5 35.8 %all-to-all-start = ((bf16[4,512,256]{2,1,0:T(8,128)(2,1)}), bf16[4,512,256]{2,1,0:T(8,128)(2,1)S(1)}, u32[]{:S(2)}, u32[]{:S(2)}) async-start(bf16[4,512,256]{2,1,0:T(8,128)(2,1)} %forward.4), calls=%async_computation | async-start | bytes 2097152 | tf_op jit(solution)/shard_map/all_to_all | solution.py:54
  189.5 43.9 %collective-permute-start.19 = (bf16[4,2048,128]{2,1,0:T(8,128)(2,1)}, bf16[4,2048,128]{2,1,0:T(8,128)(2,1)}, u32[]{:S(2)}, u32[]{:S(2)}) collective-permute-start(bf16[4,2048,128]{2,1,0:T(8,128)(2,1)} %collective-permute-done.8.refs_0_.refs_2_), channel_id=1, source_target_pairs={{0,24},{1,97},{2,26},{3,99},{4,28},{5,101},{6,30},{7,103},{8,0},{9... | collective-permute-start | bytes 6291464 | tf_op jit(solution)/shard_map/ppermute | solution.py:43
  190.3 43.0 %collective-permute-start.18 = (bf16[4,2048,128]{2,1,0:T(8,128)(2,1)}, bf16[4,2048,128]{2,1,0:T(8,128)(2,1)}, u32[]{:S(2)}, u32[]{:S(2)}) collective-permute-start(bf16[4,2048,128]{2,1,0:T(8,128)(2,1)} %collective-permute-done.11.refs_1_), channel_id=1, source_target_pairs={{0,8},{1,33},{2,10},{3,35},{4,12},{5,37},{6,14},{7,39},{8,16},{9,4... | collective-permute-start | bytes 6291464 | tf_op jit(solution)/shard_map/ppermute | solution.py:43
  214.3 27.1 %all-to-all-start.1 = ((bf16[4,512,512]{2,1,0:T(8,128)(2,1)}), bf16[4,512,512]{2,1,0:T(8,128)(2,1)}, u32[]{:S(2)}, u32[]{:S(2)}) async-start(bf16[4,512,512]{2,1,0:T(8,128)(2,1)} %forward.6), calls=%async_computation.1 | async-start | bytes 4194304 | tf_op jit(solution)/shard_map/all_to_all | solution.py:54
  218.7 19.7 %collective-permute-start.15 = (f32[32,1024]{1,0:T(8,128)}, f32[32,1024]{1,0:T(8,128)}, u32[]{:S(2)}, u32[]{:S(2)}) collective-permute-start(f32[32,1024]{1,0:T(8,128)} %maximum_multiply_fusion), channel_id=1, source_target_pairs={{0,32},{1,33},{2,34},{3,35},{4,36},{5,37},{6,38},{7,39},{8,40},{9,... | collective-permute-start | bytes 393224 | tf_op jit(solution)/shard_map/ppermute | solution.py:72
  219.7 18.8 %collective-permute-start.16 = (f32[32,1024]{1,0:T(8,128)}, f32[32,1024]{1,0:T(8,128)}, u32[]{:S(2)}, u32[]{:S(2)}) collective-permute-start(f32[32,1024]{1,0:T(8,128)} %maximum_multiply_fusion), channel_id=1, source_target_pairs={{0,64},{1,65},{2,66},{3,67},{4,68},{5,69},{6,70},{7,71},{8,72},{9,... | collective-permute-start | bytes 393224 | tf_op jit(solution)/shard_map/ppermute | solution.py:72
  223.4 15.1 %collective-permute-start.17 = (f32[32,1024]{1,0:T(8,128)}, f32[32,1024]{1,0:T(8,128)}, u32[]{:S(2)}, u32[]{:S(2)}) collective-permute-start(f32[32,1024]{1,0:T(8,128)} %maximum_multiply_fusion), channel_id=1, source_target_pairs={{0,96},{1,97},{2,98},{3,99},{4,100},{5,101},{6,102},{7,103},{8,104... | collective-permute-start | bytes 393224 | tf_op jit(solution)/shard_map/ppermute | solution.py:72
  238.5 9.3 %copy-start.19 = (bf16[512,256]{1,0:T(8,128)(2,1)S(1)}, bf16[512,256]{1,0:T(8,128)(2,1)}, u32[]{:S(2)}) copy-start(bf16[512,256]{1,0:T(8,128)(2,1)} %get-tuple-element.56) | copy-start | bytes 786436
  238.5 9.7 %copy-start.18 = (bf16[512,256]{1,0:T(8,128)(2,1)S(1)}, bf16[512,256]{1,0:T(8,128)(2,1)}, u32[]{:S(2)}) copy-start(bf16[512,256]{1,0:T(8,128)(2,1)} %get-tuple-element.55) | copy-start | bytes 786436
  242.5 13.8 %collective-permute-start.28 = (f32[32,1024]{1,0:T(8,128)S(1)}, f32[32,1024]{1,0:T(8,128)S(1)}, u32[]{:S(2)}, u32[]{:S(2)}) collective-permute-start(f32[32,1024]{1,0:T(8,128)S(1)} %add_add_fusion.1), channel_id=1, source_target_pairs={{0,8},{1,9},{2,10},{3,11},{4,12},{5,13},{6,14},{7,15},{8,16},{9,17... | collective-permute-start | bytes 393224 | tf_op jit(solution)/shard_map/ppermute | solution.py:72
  242.6 16.3 %collective-permute-start.29 = (f32[32,1024]{1,0:T(8,128)S(1)}, f32[32,1024]{1,0:T(8,128)S(1)}, u32[]{:S(2)}, u32[]{:S(2)}) collective-permute-start(f32[32,1024]{1,0:T(8,128)S(1)} %add_add_fusion.1), channel_id=1, source_target_pairs={{0,16},{1,17},{2,18},{3,19},{4,20},{5,21},{6,22},{7,23},{8,24},{9,... | collective-permute-start | bytes 393224 | tf_op jit(solution)/shard_map/ppermute | solution.py:72
  242.7 16.2 %collective-permute-start.30 = (f32[32,1024]{1,0:T(8,128)S(1)}, f32[32,1024]{1,0:T(8,128)S(1)}, u32[]{:S(2)}, u32[]{:S(2)}) collective-permute-start(f32[32,1024]{1,0:T(8,128)S(1)} %add_add_fusion.1), channel_id=1, source_target_pairs={{0,24},{1,25},{2,26},{3,27},{4,28},{5,29},{6,30},{7,31},{8,0},{9,1... | collective-permute-start | bytes 393224 | tf_op jit(solution)/shard_map/ppermute | solution.py:72
  247.8 19.3 %collective-permute-start.21 = (bf16[512,256]{1,0:T(8,128)(2,1)S(1)}, bf16[512,256]{1,0:T(8,128)(2,1)S(1)}, u32[]{:S(2)}, u32[]{:S(2)}) collective-permute-start(bf16[512,256]{1,0:T(8,128)(2,1)S(1)} %copy-done.19), channel_id=1, source_target_pairs={{0,4},{1,5},{2,6},{3,7},{4,0},{5,1},{6,2},{7,3},{8,12},{9,13},{10,... | collective-permute-start | bytes 786440 | tf_op jit(solution)/shard_map/ppermute | solution.py:407
  248.1 18.9 %collective-permute-start.22 = (bf16[512,256]{1,0:T(8,128)(2,1)S(1)}, bf16[512,256]{1,0:T(8,128)(2,1)S(1)}, u32[]{:S(2)}, u32[]{:S(2)}) collective-permute-start(bf16[512,256]{1,0:T(8,128)(2,1)S(1)} %copy-done.18), channel_id=1, source_target_pairs={{0,2},{1,3},{2,4},{3,5},{4,6},{5,7},{6,0},{7,1},{8,10},{9,11},{10,... | collective-permute-start | bytes 786440 | tf_op jit(solution)/shard_map/ppermute | solution.py:407
  251.8 17.9 %copy-start.4 = (bf16[512,256]{1,0:T(8,128)(2,1)S(1)}, bf16[512,256]{1,0:T(8,128)(2,1)}, u32[]{:S(2)}) copy-start(bf16[512,256]{1,0:T(8,128)(2,1)} %get-tuple-element.54) | copy-start | bytes 786436
  251.8 43.3 %all-to-all-start.2 = ((bf16[4,512,256]{2,1,0:T(8,128)(2,1)}), bf16[4,512,256]{2,1,0:T(8,128)(2,1)}, u32[]{:S(2)}, u32[]{:S(2)}) async-start(bf16[4,512,256]{2,1,0:T(8,128)(2,1)} %arrange.1), calls=%async_computation.2 | async-start | bytes 2097152 | tf_op jit(solution)/shard_map/all_to_all | solution.py:54
  256.3 13.5 %collective-permute-start.23 = (bf16[512,256]{1,0:T(8,128)(2,1)S(1)}, bf16[512,256]{1,0:T(8,128)(2,1)S(1)}, u32[]{:S(2)}, u32[]{:S(2)}) collective-permute-start(bf16[512,256]{1,0:T(8,128)(2,1)S(1)} %copy-done.17), channel_id=1, source_target_pairs={{0,6},{1,7},{2,0},{3,1},{4,2},{5,3},{6,4},{7,5},{8,14},{9,15},{10,... | collective-permute-start | bytes 786440 | tf_op jit(solution)/shard_map/ppermute | solution.py:407
  259.8 24.2 %collective-permute-start.31 = (f32[256,256]{1,0:T(8,128)S(1)}, f32[256,256]{1,0:T(8,128)S(1)}, u32[]{:S(2)}, u32[]{:S(2)}) collective-permute-start(f32[256,256]{1,0:T(8,128)S(1)} %fusion.2), channel_id=1, source_target_pairs={{0,1},{1,0},{2,3},{3,2},{4,5},{5,4},{6,7},{7,6},{8,9},{9,8},{10,11... | collective-permute-start | bytes 786440 | tf_op jit(solution)/shard_map/ppermute | solution.py:60
  276.8 29.0 %collective-permute-start.27 = (bf16[512,1024]{1,0:T(8,128)(2,1)S(1)}, bf16[512,1024]{1,0:T(8,128)(2,1)}, u32[]{:S(2)}, u32[]{:S(2)}) collective-permute-start(bf16[512,1024]{1,0:T(8,128)(2,1)S(1)} %get-tuple-element.62), channel_id=1, source_target_pairs={{0,1},{1,0},{2,3},{3,2},{4,5},{5,4},{6,7},{7,6},{8,9},{9,8},{10,11... | collective-permute-start | bytes 3145736 | tf_op jit(solution)/shard_map/ppermute | solution.py:433
  284.0 8.4 %collective-permute-start.32 = (f32[256,256]{1,0:T(8,128)S(1)}, f32[256,256]{1,0:T(8,128)S(1)}, u32[]{:S(2)}, u32[]{:S(2)}) collective-permute-start(f32[256,256]{1,0:T(8,128)S(1)} %add.473), channel_id=1, source_target_pairs={{0,2},{1,3},{2,0},{3,1},{4,6},{5,7},{6,4},{7,5},{8,10},{9,11},{10,... | collective-permute-start | bytes 786440 | tf_op jit(solution)/shard_map/ppermute | solution.py:61
  293.2 10.2 %collective-permute-start.33 = (f32[256,256]{1,0:T(8,128)}, f32[256,256]{1,0:T(8,128)}, u32[]{:S(2)}, u32[]{:S(2)}) collective-permute-start(f32[256,256]{1,0:T(8,128)} %add.474), channel_id=1, source_target_pairs={{0,4},{1,5},{2,6},{3,7},{4,0},{5,1},{6,2},{7,3},{8,12},{9,13},{10,... | collective-permute-start | bytes 786440 | tf_op jit(solution)/shard_map/ppermute | solution.py:62
  295.2 10.7 %copy-start.1 = (f32[512,1024]{1,0:T(8,128)S(1)}, f32[512,1024]{1,0:T(8,128)}, u32[]{:S(2)}) copy-start(f32[512,1024]{1,0:T(8,128)} %fusion.33) | copy-start | bytes 6291460
  296.6 12.1 %collective-permute-start.20 = (bf16[2,512,256]{2,1,0:T(8,128)(2,1)S(1)}, bf16[2,512,256]{2,1,0:T(8,128)(2,1)S(1)}, u32[]{:S(2)}, u32[]{:S(2)}) collective-permute-start(bf16[2,512,256]{2,1,0:T(8,128)(2,1)S(1)} %slice_select_fusion.1), channel_id=1, source_target_pairs={{0,1},{1,0},{2,3},{3,2},{4,5},{5,4},{6,7},{7,6},{8,9},{9,8},{10,11... | collective-permute-start | bytes 1572872 | tf_op jit(solution)/shard_map/ppermute | solution.py:416
  298.3 11.8 %collective-permute-start.24 = (bf16[512,256]{1,0:T(8,128)(2,1)}, bf16[512,256]{1,0:T(8,128)(2,1)S(1)}, u32[]{:S(2)}, u32[]{:S(2)}) collective-permute-start(bf16[512,256]{1,0:T(8,128)(2,1)} %add_convert_fusion.2), channel_id=1, source_target_pairs={{0,1},{2,3},{4,5},{6,7},{8,9},{10,11},{12,13},{14,15},{32,33},{34,... | collective-permute-start | bytes 786440 | tf_op jit(solution)/shard_map/ppermute | solution.py:317
  299.6 10.4 %collective-permute-start.25 = (bf16[512,256]{1,0:T(8,128)(2,1)}, bf16[512,256]{1,0:T(8,128)(2,1)S(1)}, u32[]{:S(2)}, u32[]{:S(2)}) collective-permute-start(bf16[512,256]{1,0:T(8,128)(2,1)} %add_convert_fusion.2), channel_id=1, source_target_pairs={{1,4},{5,5},{9,12},{13,13},{17,20},{21,21},{25,28},{29,29},{33,38}... | collective-permute-start | bytes 786440 | tf_op jit(solution)/shard_map/ppermute | solution.py:312
  303.4 6.7 %collective-permute-start.26 = (bf16[512,256]{1,0:T(8,128)(2,1)}, bf16[512,256]{1,0:T(8,128)(2,1)S(1)}, u32[]{:S(2)}, u32[]{:S(2)}) collective-permute-start(bf16[512,256]{1,0:T(8,128)(2,1)} %add_convert_fusion.2), channel_id=1, source_target_pairs={{3,4},{7,5},{11,12},{15,13},{19,20},{23,21},{27,28},{31,29},{35,38... | collective-permute-start | bytes 786440 | tf_op jit(solution)/shard_map/ppermute | solution.py:312
  (9 other events, 18.8 us)

commit v7 on v4

--- a/solution.py
+++ b/solution.py
@@ -62,10 +62,6 @@
     return value + lax.ppermute(value, "tensor", [(t, t ^ 4) for t in range(8)])
 
 
-def after(value, *events):
-    return lax.optimization_barrier((value, *events))[0]
-
-
 def over_side(value, axis):
     def from_step(step):
         def move(x, z, y, c):
@@ -76,6 +72,15 @@
         return lax.ppermute(value, BOTH, pairs(move))
 
     return [value, from_step(1), from_step(2), from_step(3)]
+
+
+def after(value, *events):
+    return lax.optimization_barrier((value, *events))[0]
+
+
+def with_partner(value, bit, *events):
+    other = lax.ppermute(value, "dp", [(d, d ^ bit) for d in range(16)])
+    return value + after(other, *events)
 
 
 def total_of(parts):
@@ -161,8 +166,8 @@
     for h in range(2):
         lanes = slice(h * part, (h + 1) * part)
         out_ref[far, :, lanes] = total(here_ref, h * part)
-        out_ref[lax.rem(far + 1, SIDE), :, lanes] = total(besides[h], 0)
-        out_ref[lax.rem(far + 3, SIDE), :, lanes] = total(besides[h], part)
+        out_ref[lax.rem(far + 1, SIDE), :, lanes] = total(besides[1 - h], h * part)
+        out_ref[lax.rem(far + 3, SIDE), :, lanes] = total(besides[h], h * part)
         out_ref[lax.rem(far + 2, SIDE), :, lanes] = jnp.zeros_like(here_ref[0, :, lanes])
 
 
@@ -310,11 +315,7 @@
         cols = slice(h * part, (h + 1) * part)
         shards.append(jnp.concatenate([mine[:, cols], swapped[:, cols]], axis=0))
     logits_a, logits_b, *shards = lax.optimization_barrier((logits_a, logits_b, *shards))
-    lines = [ring_gather(shards[h], 0, h) for h in range(2)]
-    arrivals = [lines[0][1], lines[0][3]]
-    lines[0] = jnp.stack(lines[0])
-    lines[0], *lines[1] = lax.optimization_barrier((lines[0], *lines[1]))
-    lines[1] = jnp.stack(lines[1])
+    lines = [jnp.stack(ring_gather(shards[h], 0, h)) for h in range(2)]
     def columns(i, h):
         far_at = (far + i) % SIDE
         spots = []
@@ -340,21 +341,17 @@
     low_part = lax.dot_general(down_a, attn_out, cols_by_cols, preferred_element_type=f32)
     back_part = lax.dot_general(up_b, grad_cols, cols_by_cols, preferred_element_type=f32)
     totals = jnp.concatenate([low_part, back_part], axis=0)
-    totals = over_tensor(after(totals, *arrivals)).astype(bf16)
+    lines[1], totals = lax.optimization_barrier((lines[1], totals))
+    blocks = [ring_gather(lines[h], 1, h) for h in range(2)]
+    totals = over_tensor(totals).astype(bf16)
     low_bf, back_bf = totals[:rank], totals[rank:]
 
     factor = adapter_scale / (tokens * lax.axis_size("dp"))
     grad_a = jnp.dot(back_bf, attn_out, preferred_element_type=f32)
     grad_b = jnp.dot(low_bf, grad_cols, preferred_element_type=f32)
     both = factor * jnp.concatenate([grad_a, grad_b], axis=0)
-    lines[0], both = lax.optimization_barrier((lines[0], both))
-    both = total_of(over_side(both, 0))
-    both = total_of(over_side(both, 1))
-    lines[1], both = lax.optimization_barrier((lines[1], both))
-    blocks = [ring_gather(lines[h], 1, h) for h in range(2)]
-
     here = [(0, 0), (0, 1)]
-    beside = [[(1, 0), (3, 0)], [(1, 1), (3, 1)]]
+    beside = [[(3, 0), (1, 1)], [(1, 0), (3, 1)]]
     across = [(2, 0), (2, 1)]
 
     def take(chunks):
@@ -362,36 +359,38 @@
 
     sent_here = forward(turned, wide, take(here))
     slots_here = exchange(sent_here, "tensor", LANES)
-    sent_first = forward(after(turned, sent_here), wide, take(beside[0]))
+    grown = backward(after(spots_of(here), sent_here), None, out_grad, take(here))
+    sent_first = forward(after(turned, grown), wide, take(beside[0]))
     slots_here, sent_first = lax.optimization_barrier((slots_here, sent_first))
     slots_first = exchange(sent_first, "tensor", LANES)
-    bank_a, logit_grad_a = compose_back(both[:rank], weights_a, picked_a, mixing_a, vector_bank)
-    bank_b, logit_grad_b = compose_back(both[rank:], weights_b, picked_b, mixing_b, vector_bank)
-    bank_part = bank_a + bank_b
-    bank_grad = over_tensor(bank_part)
-    chunks = here + beside[0]
-    grown = backward(after(spots_of(chunks), sent_first, bank_part), None, out_grad, take(chunks))
-    sent_second = forward(after(turned, grown, bank_grad), wide, take(beside[1]))
-    slots_first, sent_second = lax.optimization_barrier((slots_first, sent_second))
+    sent_second = forward(after(turned, sent_first), wide, take(beside[1]))
+    slots_first, sent_second, both = lax.optimization_barrier((slots_first, sent_second, both))
     slots_second = exchange(sent_second, "tensor", LANES)
-    grown = backward(after(spots_of(beside[1]), sent_second), grown, out_grad, take(beside[1]))
+    both_parts = over_side(both, 0)
+    chunks = beside[0] + beside[1]
+    grown = backward(after(spots_of(chunks), sent_second), grown, out_grad, take(chunks))
     slots = arrange(
         far.astype(jnp.int32).reshape(1), slots_here, slots_first, after(slots_second, grown)
     )
     moved = exchange(slots, "tensor", LANES)
     sent = forward(after(turned_here, slots), wide, take(across), apart=True)
-    grown, other = backward(
-        after(spots_of(across), *sent), grown, out_grad, take(across), last=True
-    )
-    crossed = lax.ppermute(jnp.where(core == 0, slots[2:], moved[:2]), "tensor", SWAP)
-    firsts = jnp.where(core == 0, slots[:2], crossed)
-    seconds = jnp.where(core == 0, crossed, moved[2:])
-
     arrived = [sent[0]]
     for step in range(1, SIDE):
         turns = [(t, (t + 2 * step) % 8) for t in range(8)]
         arrived.append(lax.ppermute(sent[step], "tensor", turns))
     piece = total_of([a.astype(f32) for a in arrived]).astype(bf16)
+    both = total_of(lax.optimization_barrier((*both_parts, *sent))[:SIDE])
+    grown, other = backward(
+        after(spots_of(across), *sent), grown, out_grad, take(across), last=True
+    )
+    both = with_partner(with_partner(both, 1, grown), 2)
+    bank_a, logit_grad_a = compose_back(both[:rank], weights_a, picked_a, mixing_a, vector_bank)
+    bank_b, logit_grad_b = compose_back(both[rank:], weights_b, picked_b, mixing_b, vector_bank)
+    bank_grad = over_tensor(bank_a + bank_b)
+    crossed = lax.ppermute(jnp.where(core == 0, slots[2:], moved[:2]), "tensor", SWAP)
+    firsts = jnp.where(core == 0, slots[:2], crossed)
+    seconds = jnp.where(core == 0, crossed, moved[2:])
+
     first, place, second = settle(piece, 2, z, core)
     cols = []
     for s in range(2):

time: 232 us -> 194 us (0.84)
  starting transfers between devices: 90.9 us -> 68.5 us
  waiting for transfers between devices: 56.6 us -> 39.2 us
  other arithmetic: 16 us -> 20.4 us
    ppermute x2, starting transfers between devices: 22.6 us -> 3.78 us  [over_tensor(): value = value + lax.ppermute(value, 'tensor', SWAP)]
    ppermute x2, waiting for transfers between devices: 16.5 us -> 4.99 us  [over_tensor(): lax.ppermute(value, 'tensor', [(t, t ^ 2) for t in range(8)])]
    ppermute x6 -> x3, waiting for transfers between devices: 10 us -> 0.01 us  [from_step(): return lax.ppermute(value, BOTH, pairs(move))]
    ppermute x12, waiting for transfers between devices: 12 us -> 21 us  [shift(): return lax.ppermute(value, BOTH, ring(stage, step))]
    ppermute x1, starting transfers between devices: 6.4 us -> 0.38 us  [local(): lax.ppermute(jnp.where(core == 0, slots[2:], moved[:2]), 'tensor', SWAP)]
    ppermute x3, waiting for transfers between devices: 4.89 us -> 0.01 us  [local(): arrived.append(lax.ppermute(sent[step], 'tensor', turns))]
    ppermute x1, starting transfers between devices: 0.68 us -> 5.28 us  [local(): other = lax.ppermute(other, 'tensor', SWAP)]
    ppermute x6 -> x3, starting transfers between devices: 6.95 us -> 3.59 us  [from_step(): return lax.ppermute(value, BOTH, pairs(move))]
  transfers between devices with their start and end apart: 38 -> 37, of which waited for: 16 -> 12; matrix products, arithmetic and copies ran while one was open for 12% -> 15% of each run, Pallas kernels for 21% -> 25%
where the time goes in v7:
time: 194 us; the launch traced here: 190 us
  starting transfers between devices  68.5 us (35%)
  Pallas kernels  47.3 us (24%)
  waiting for transfers between devices  39.2 us (20%)
  other arithmetic  20.4 us (11%)
  matrix products  10.2 us (5%)
  local copies, waits for them, and re-layouts  3.51 us (2%)
    pallas_call x3, Pallas kernels, backward(): pl.pallas_call(functools.partial(backward_kernel, count, first, last), ou...  24.9 us
    ppermute x12, waiting for transfers between devices, shift(): return lax.ppermute(value, BOTH, ring(stage, step))  21 us
    pallas_call x4, Pallas kernels, forward(): pl.pallas_call(functools.partial(forward_kernel, count, many), out_shape=...  19.9 us
    ppermute x12, starting transfers between devices, shift(): return lax.ppermute(value, BOTH, ring(stage, step))  17.6 us
    all_to_all x4, starting transfers between devices, exchange(): lax.all_to_all(value, axis, split_axis=0, concat_axis=0, tiled=True, axis...  17.1 us
    all_to_all x4, waiting for transfers between devices, exchange(): lax.all_to_all(value, axis, split_axis=0, concat_axis=0, tiled=True, axis...  5.96 us
    ppermute x1, starting transfers between devices, local(): other = lax.ppermute(other, 'tensor', SWAP)  5.28 us
    ppermute x2, waiting for transfers between devices, over_tensor(): lax.ppermute(value, 'tensor', [(t, t ^ 2) for t in range(8)])  4.99 us
  transfers between devices with their start and end apart: 37, of which 12 were waited for; matrix products, arithmetic and copies ran while one was open for 15% of the time, Pallas kernels for 25%

profile of v7, /device:TPU:1, one launch (start us, length us, event | category | flops | bytes accessed | tf_op | source)
XLA Modules:
  0.0 190.5 jit_solution(10611033658888426038)
XLA Ops:
  2.0 1.5 collective-permute-start.1
  3.5 1.6 collective-permute-done.1
  6.3 1.8 collective-permute-start.3
  8.1 2.2 %collective-permute-start.2 = (bf16[2048,128]{1,0:T(8,128)(2,1)S(1)}, bf16[2048,128]{1,0:T(8,128)(2,1)S(1)}, u32[]{:S(2)}, u32[]{:S(2)}) collective-permute-start(bf16[2048,128]{1,0:T(8,128)(2,1)S(1)} %get-tuple-element.34), channel_id=1, source_target_pairs={{0,96},{1,25},{2,98},{3,27},{4,100},{5,29},{6,102},{7,31},{8,104},... | collective-permute-start | bytes 1572872 | tf_op jit(solution)/shard_map/ppermute | solution.py:43
  10.3 2.7 %collective-permute-start.5 = (bf16[2048,128]{1,0:T(8,128)(2,1)S(1)}, bf16[2048,128]{1,0:T(8,128)(2,1)}, u32[]{:S(2)}, u32[]{:S(2)}) collective-permute-start(bf16[2048,128]{1,0:T(8,128)(2,1)S(1)} %get-tuple-element.35), channel_id=1, source_target_pairs={{0,96},{1,25},{2,98},{3,27},{4,100},{5,29},{6,102},{7,31},{8,104},... | collective-permute-start | bytes 1572872 | tf_op jit(solution)/shard_map/ppermute | solution.py:43
  14.1 8.2 %collective-permute-done.5 = bf16[2048,128]{1,0:T(8,128)(2,1)} collective-permute-done((bf16[2048,128]{1,0:T(8,128)(2,1)S(1)}, bf16[2048,128]{1,0:T(8,128)(2,1)}, u32[]{:S(2)}, u32[]{:S(2)}) %collective-permute-start.5) | collective-permute-done | bytes 524320 | tf_op jit(solution)/shard_map/ppermute | solution.py:43
  22.3 3.2 %collective-permute-start.6 = (bf16[2048,128]{1,0:T(8,128)(2,1)}, bf16[2048,128]{1,0:T(8,128)(2,1)S(1)}, u32[]{:S(2)}, u32[]{:S(2)}) collective-permute-start(bf16[2048,128]{1,0:T(8,128)(2,1)} %collective-permute-done.5), channel_id=1, source_target_pairs={{0,96},{1,25},{2,98},{3,27},{4,100},{5,29},{6,102},{7,31},{8,104},... | collective-permute-start | bytes 1572872 | tf_op jit(solution)/shard_map/ppermute | solution.py:43
  25.9 1.6 fusion.11
  28.2 3.8 %collective-permute-done.6 = bf16[2048,128]{1,0:T(8,128)(2,1)S(1)} collective-permute-done((bf16[2048,128]{1,0:T(8,128)(2,1)}, bf16[2048,128]{1,0:T(8,128)(2,1)S(1)}, u32[]{:S(2)}, u32[]{:S(2)}) %collective-permute-start.6) | collective-permute-done | bytes 524320 | tf_op jit(solution)/shard_map/ppermute | solution.py:43
  32.0 2.8 %pad_maximum_fusion.1.refs_1_ = bf16[4,2048,128]{2,1,0:T(8,128)(2,1)} fusion(bf16[1,2048,128]{2,1,0:T(8,128)(2,1)} %bitcast.9, bf16[1,2048,128]{2,1,0:T(8,128)(2,1)S(1)} %bitcast.111, bf16[1,2048,128]{2,1,0:T(8,128)(2,1)} %bitcast.7, bf16[1,2048,128]{2,1,0:T(8,128)(2,1)S(1)} %bitcast.103), kind=kLoop, calls=%fused_computation.3 | loop fusion | flops 3145728 | bytes 4194304 | tf_op jit(solution)/shard_map/stack | solution.py:318
  35.5 1.6 pad_maximum_fusion.refs_0_
  37.7 2.1 %collective-permute-start.9 = (bf16[4,2048,128]{2,1,0:T(8,128)(2,1)}, bf16[4,2048,128]{2,1,0:T(8,128)(2,1)}, u32[]{:S(2)}, u32[]{:S(2)}) collective-permute-start(bf16[4,2048,128]{2,1,0:T(8,128)(2,1)} %pad_maximum_fusion.1.refs_1_), channel_id=1, source_target_pairs={{0,24},{1,97},{2,26},{3,99},{4,28},{5,101},{6,30},{7,103},{8,0},{9... | collective-permute-start | bytes 6291464 | tf_op jit(solution)/shard_map/ppermute | solution.py:43
  39.8 2.8 %collective-permute-start = (bf16[512,1024]{1,0:T(8,128)(2,1)S(1)}, bf16[512,1024]{1,0:T(8,128)(2,1)}, u32[]{:S(2)}, u32[]{:S(2)}) collective-permute-start(bf16[512,1024]{1,0:T(8,128)(2,1)S(1)} %copy-done.2), channel_id=1, source_target_pairs={{0,1},{1,0},{2,3},{3,2},{4,5},{5,4},{6,7},{7,6},{8,9},{9,8},{10,11... | collective-permute-start | bytes 3145736 | tf_op jit(solution)/shard_map/ppermute | solution.py:332
  42.6 2.3 %collective-permute-start.10 = (bf16[4,2048,128]{2,1,0:T(8,128)(2,1)}, bf16[4,2048,128]{2,1,0:T(8,128)(2,1)}, u32[]{:S(2)}, u32[]{:S(2)}) collective-permute-start(bf16[4,2048,128]{2,1,0:T(8,128)(2,1)} %pad_maximum_fusion.refs_0_), channel_id=1, source_target_pairs={{0,24},{1,97},{2,26},{3,99},{4,28},{5,101},{6,30},{7,103},{8,0},{9... | collective-permute-start | bytes 6291464 | tf_op jit(solution)/shard_map/ppermute | solution.py:43
  46.4 5.0 %forward.4 = bf16[4,512,256]{2,1,0:T(8,128)(2,1)} custom-call(s32[1]{0:T(128)} %bitcast.1.start_ref, bf16[512,2048]{1,0:T(8,128)(2,1)S(1)} %constant_dynamic-update-slice_fusion.wide_ref, bf16[4,2048,128]{2,1,0:T(8,128)(2,1)} %pad_maximum_fusion.refs_0_, bf16[4,2048,128]{2,1,0:T(8,128)(2,1)} %pad_maximum_fusion.1.refs_1_), custom_call_target="tpu_custom_call" | custom-call | flops 268435456 | bytes 524288 | tf_op jit(solution)/shard_map/forward/pallas_call | solution.py:131
  51.4 4.2 %all-to-all-start = ((bf16[4,512,256]{2,1,0:T(8,128)(2,1)}), bf16[4,512,256]{2,1,0:T(8,128)(2,1)S(1)}, u32[]{:S(2)}, u32[]{:S(2)}) async-start(bf16[4,512,256]{2,1,0:T(8,128)(2,1)} %forward.4), calls=%async_computation | async-start | bytes 2097152 | tf_op jit(solution)/shard_map/all_to_all | solution.py:54
  55.6 8.2 %collective-permute-done.8.refs_0_ = bf16[4,2048,128]{2,1,0:T(8,128)(2,1)} collective-permute-done((bf16[4,2048,128]{2,1,0:T(8,128)(2,1)}, bf16[4,2048,128]{2,1,0:T(8,128)(2,1)}, u32[]{:S(2)}, u32[]{:S(2)}) %collective-permute-start.8) | collective-permute-done | bytes 2097184 | tf_op jit(solution)/shard_map/ppermute | solution.py:43
  63.8 2.7 %collective-permute-start.17 = (bf16[4,2048,128]{2,1,0:T(8,128)(2,1)}, bf16[4,2048,128]{2,1,0:T(8,128)(2,1)}, u32[]{:S(2)}, u32[]{:S(2)}) collective-permute-start(bf16[4,2048,128]{2,1,0:T(8,128)(2,1)} %collective-permute-done.9.refs_1_), channel_id=1, source_target_pairs={{0,24},{1,97},{2,26},{3,99},{4,28},{5,101},{6,30},{7,103},{8,0},{9... | collective-permute-start | bytes 6291464 | tf_op jit(solution)/shard_map/ppermute | solution.py:43
  66.5 3.7 %collective-permute-start.12 = (f32[32,512]{1,0:T(8,128)}, f32[32,512]{1,0:T(8,128)S(1)}, u32[]{:S(2)}, u32[]{:S(2)}) collective-permute-start(f32[32,512]{1,0:T(8,128)} %pad_maximum_fusion.4), channel_id=1, source_target_pairs={{0,1},{1,0},{2,3},{3,2},{4,5},{5,4},{6,7},{7,6},{8,9},{9,8},{10,11... | collective-permute-start | bytes 196616 | tf_op jit(solution)/shard_map/ppermute | solution.py:60
  72.1 1.4 collective-permute-start.13
  73.5 2.2 %collective-permute-done.13 = f32[32,512]{1,0:T(8,128)S(1)} collective-permute-done((f32[32,512]{1,0:T(8,128)S(1)}, f32[32,512]{1,0:T(8,128)S(1)}, u32[]{:S(2)}, u32[]{:S(2)}) %collective-permute-start.13) | collective-permute-done | bytes 65568 | tf_op jit(solution)/shard_map/ppermute | solution.py:61
  76.4 2.9 %collective-permute-start.14 = (f32[32,512]{1,0:T(8,128)}, f32[32,512]{1,0:T(8,128)}, u32[]{:S(2)}, u32[]{:S(2)}) collective-permute-start(f32[32,512]{1,0:T(8,128)} %add.404), channel_id=1, source_target_pairs={{0,4},{1,5},{2,6},{3,7},{4,0},{5,1},{6,2},{7,3},{8,12},{9,13},{10,... | collective-permute-start | bytes 196616 | tf_op jit(solution)/shard_map/ppermute | solution.py:62
  79.4 7.2 %backward.3.refs_20_ = f32[512,2048]{1,0:T(8,128)} custom-call(s32[8]{0:T(128)S(1)} %stack.153.spots_ref, bf16[4,2048,128]{2,1,0:T(8,128)(2,1)} %pad_maximum_fusion.refs_0_, bf16[4,2048,128]{2,1,0:T(8,128)(2,1)} %pad_maximum_fusion.1.refs_1_, bf16[512,8192]{1,0:T(8,128)(2,1)} %refs_9_.5, bf16[512,8192]{1,0:T(8,128)(2,1)} %refs_9_.5, ...), custom_call_target="tpu_custom_call" | custom-call | flops 268435456 | bytes 524288 | tf_op jit(solution)/shard_map/backward/pallas_call | solution.py:237
  86.5 4.9 %forward.5 = bf16[4,512,256]{2,1,0:T(8,128)(2,1)} custom-call(s32[1]{0:T(128)} %bitcast.1.start_ref, bf16[512,2048]{1,0:T(8,128)(2,1)S(1)} %constant_dynamic-update-slice_fusion.wide_ref, bf16[4,2048,128]{2,1,0:T(8,128)(2,1)} %collective-permute-done.8.refs_0_, bf16[4,2048,128]{2,1,0:T(8,128)(2,1)} %collective-permute-done.9.refs_1_), custom_call_target="tpu_custom_call" | custom-call | flops 268435456 | bytes 524288 | tf_op jit(solution)/shard_map/forward/pallas_call | solution.py:131
  91.5 4.3 %all-to-all-start.1 = ((bf16[4,512,256]{2,1,0:T(8,128)(2,1)}), bf16[4,512,256]{2,1,0:T(8,128)(2,1)}, u32[]{:S(2)}, u32[]{:S(2)}) async-start(bf16[4,512,256]{2,1,0:T(8,128)(2,1)} %forward.5), calls=%async_computation.1 | async-start | bytes 2097152 | tf_op jit(solution)/shard_map/all_to_all | solution.py:54
  96.7 1.5 fusion.9
  98.2 1.5 fusion.35
  100.3 5.0 %forward.6 = bf16[4,512,256]{2,1,0:T(8,128)(2,1)} custom-call(s32[1]{0:T(128)} %bitcast.1.start_ref, bf16[512,2048]{1,0:T(8,128)(2,1)S(1)} %constant_dynamic-update-slice_fusion.wide_ref, bf16[4,2048,128]{2,1,0:T(8,128)(2,1)} %collective-permute-done.10.refs_0_.refs_2_, bf16[4,2048,128]{2,1,0:T(8,128)(2,1)} %collective-permute-done.11.refs_1_.refs_3_), custom_call_target="tpu_custom_call" | custom-call | flops 268435456 | bytes 524288 | tf_op jit(solution)/shard_map/forward/pallas_call | solution.py:131
  105.3 4.3 %all-to-all-done.1.refs_0_ = bf16[4,512,256]{2,1,0:T(8,128)(2,1)} async-done(((bf16[4,512,256]{2,1,0:T(8,128)(2,1)}), bf16[4,512,256]{2,1,0:T(8,128)(2,1)}, u32[]{:S(2)}, u32[]{:S(2)}) %all-to-all-start.1) | async-done | bytes 1048608 | tf_op jit(solution)/shard_map/all_to_all | solution.py:54
  109.6 4.2 %all-to-all-start.2 = ((bf16[4,512,256]{2,1,0:T(8,128)(2,1)}), bf16[4,512,256]{2,1,0:T(8,128)(2,1)}, u32[]{:S(2)}, u32[]{:S(2)}) async-start(bf16[4,512,256]{2,1,0:T(8,128)(2,1)} %forward.6), calls=%async_computation.2 | async-start | bytes 2097152 | tf_op jit(solution)/shard_map/all_to_all | solution.py:54
  114.0 10.7 %backward.4.refs_10_ = f32[512,2048]{1,0:T(8,128)} custom-call(s32[16]{0:T(128)S(1)} %stack.170.spots_ref, bf16[4,2048,128]{2,1,0:T(8,128)(2,1)} %collective-permute-done.8.refs_0_, bf16[4,2048,128]{2,1,0:T(8,128)(2,1)} %collective-permute-done.9.refs_1_, ...), custom_call_target="tpu_custom_call", output_to_operand_aliasing={{}: (21, {})} | custom-call | flops 536870912 | bytes 1048576 | tf_op jit(solution)/shard_map/backward/pallas_call | solution.py:237
  124.7 1.7 all-to-all-done.2.refs_1_
  126.4 2.6 %arrange.1 = bf16[4,512,256]{2,1,0:T(8,128)(2,1)} custom-call(s32[1]{0:T(128)} %bitcast.far_ref, bf16[4,512,256]{2,1,0:T(8,128)(2,1)S(1)} %all-to-all-done.here_ref, bf16[4,512,256]{2,1,0:T(8,128)(2,1)} %all-to-all-done.1.refs_0_, bf16[4,512,256]{2,1,0:T(8,128)(2,1)} %all-to-all-done.2.refs_1_), custom_call_target="tpu_custom_call" | custom-call | flops 2097152 | bytes 4194304 | tf_op jit(solution)/shard_map/arrange/pallas_call | solution.py:178
  129.0 4.4 %all-to-all-start.3 = ((bf16[4,512,256]{2,1,0:T(8,128)(2,1)}), bf16[4,512,256]{2,1,0:T(8,128)(2,1)}, u32[]{:S(2)}, u32[]{:S(2)}) async-start(bf16[4,512,256]{2,1,0:T(8,128)(2,1)} %arrange.1), calls=%async_computation.3 | async-start | bytes 2097152 | tf_op jit(solution)/shard_map/all_to_all | solution.py:54
  133.5 3.5 %collective-permute-start.26 = (f32[32,1024]{1,0:T(8,128)S(1)}, f32[32,1024]{1,0:T(8,128)S(1)}, u32[]{:S(2)}, u32[]{:S(2)}) collective-permute-start(f32[32,1024]{1,0:T(8,128)S(1)} %copy-done.4), channel_id=1, source_target_pairs={{0,64},{1,65},{2,66},{3,67},{4,68},{5,69},{6,70},{7,71},{8,72},{9,... | collective-permute-start | bytes 393224 | tf_op jit(solution)/shard_map/ppermute | solution.py:72
  137.1 5.0 %forward.7 = (bf16[512,256]{1,0:T(8,128)(2,1)}, bf16[512,256]{1,0:T(8,128)(2,1)}, bf16[512,256]{1,0:T(8,128)(2,1)}, bf16[512,256]{1,0:T(8,128)(2,1)}) custom-call(s32[1]{0:T(128)} %bitcast.36.start_ref, bf16[512,2048]{1,0:T(8,128)(2,1)S(1)} %constant_dynamic-update-slice_fusion.wide_ref, bf16[4,2048,128]{2,1,0:T(8,128)(2,1)} %collective-permute-done.16.refs_0_, ...), custom_call_target="tpu_custom_call" | custom-call | flops 268435456 | bytes 524288 | tf_op jit(solution)/shard_map/forward/pallas_call | solution.py:131
  142.3 1.8 fusion.33
  144.1 2.6 %collective-permute-start.20 = (bf16[512,256]{1,0:T(8,128)(2,1)}, bf16[512,256]{1,0:T(8,128)(2,1)}, u32[]{:S(2)}, u32[]{:S(2)}) collective-permute-start(bf16[512,256]{1,0:T(8,128)(2,1)} %get-tuple-element.53), channel_id=1, source_target_pairs={{0,6},{1,7},{2,0},{3,1},{4,2},{5,3},{6,4},{7,5},{8,14},{9,15},{10,... | collective-permute-start | bytes 786440 | tf_op jit(solution)/shard_map/ppermute | solution.py:380
  146.6 1.8 collective-permute-start.18
  148.4 7.0 %backward.5 = (f32[512,1024]{1,0:T(8,128)S(1)}, bf16[512,1024]{1,0:T(8,128)(2,1)S(1)}) custom-call(s32[8]{0:T(128)S(1)} %stack.179.spots_ref, bf16[4,2048,128]{2,1,0:T(8,128)(2,1)} %collective-permute-done.16.refs_0_, bf16[4,2048,128]{2,1,0:T(8,128)(2,1)} %collective-permute-done.17.refs_1_, bf16[512,8192]{1,0:T(8,128)(2,1)} %refs_9_.5, ...), custom_call_target="tpu_custom_call" | custom-call | flops 268435456 | bytes 524288 | tf_op jit(solution)/shard_map/backward/pallas_call | solution.py:237
  155.4 5.3 %collective-permute-start.24 = (bf16[512,1024]{1,0:T(8,128)(2,1)S(1)}, bf16[512,1024]{1,0:T(8,128)(2,1)}, u32[]{:S(2)}, u32[]{:S(2)}) collective-permute-start(bf16[512,1024]{1,0:T(8,128)(2,1)S(1)} %get-tuple-element.56), channel_id=1, source_target_pairs={{0,1},{1,0},{2,3},{3,2},{4,5},{5,4},{6,7},{7,6},{8,9},{9,8},{10,11... | collective-permute-start | bytes 3145736 | tf_op jit(solution)/shard_map/ppermute | solution.py:404
  161.3 2.0 %collective-permute-start.29 = (f32[32,1024]{1,0:T(8,128)}, f32[32,1024]{1,0:T(8,128)}, u32[]{:S(2)}, u32[]{:S(2)}) collective-permute-start(f32[32,1024]{1,0:T(8,128)} %add.466), channel_id=1, source_target_pairs={{0,16},{8,24},{16,0},{24,8},{32,48},{40,56},{48,32},{56,40},{64,80... | collective-permute-start | bytes 393224 | tf_op jit(solution)/shard_map/ppermute | solution.py:82
  165.0 1.3 add_convert_fusion.2
  166.3 3.0 %collective-permute-start.22 = (bf16[512,256]{1,0:T(8,128)(2,1)S(1)}, bf16[512,256]{1,0:T(8,128)(2,1)S(1)}, u32[]{:S(2)}, u32[]{:S(2)}) collective-permute-start(bf16[512,256]{1,0:T(8,128)(2,1)S(1)} %add_convert_fusion.2), channel_id=1, source_target_pairs={{1,4},{5,5},{9,12},{13,13},{17,20},{21,21},{25,28},{29,29},{33,38}... | collective-permute-start | bytes 786440 | tf_op jit(solution)/shard_map/ppermute | solution.py:285
  178.2 1.4 add_convert_fusion.1
  179.6 2.8 %collective-permute-done.31 = f32[256,256]{1,0:T(8,128)S(1)} collective-permute-done((f32[256,256]{1,0:T(8,128)S(1)}, f32[256,256]{1,0:T(8,128)S(1)}, u32[]{:S(2)}, u32[]{:S(2)}) %collective-permute-start.31) | collective-permute-done | bytes 262176 | tf_op jit(solution)/shard_map/ppermute | solution.py:61
  182.6 2.8 %add_convert_fusion = bf16[512,1024]{1,0:T(8,128)(2,1)} fusion(f32[512,1024]{1,0:T(8,128)S(1)} %copy-done.3, f32[512,1024]{1,0:T(8,128)S(1)} %get-tuple-element.55, bf16[512,1024]{1,0:T(8,128)(2,1)} %collective-permute-done.24), kind=kLoop, calls=%fused_computation.4 | loop fusion | flops 2621440 | bytes 6291456 | tf_op jit(solution)/shard_map/convert_element_type | solution.py:409
  185.4 4.3 %collective-permute-done.32 = f32[256,256]{1,0:T(8,128)S(1)} collective-permute-done((f32[256,256]{1,0:T(8,128)S(1)}, f32[256,256]{1,0:T(8,128)S(1)}, u32[]{:S(2)}, u32[]{:S(2)}) %collective-permute-start.32) | collective-permute-done | bytes 262176 | tf_op jit(solution)/shard_map/ppermute | solution.py:62
  (123 shorter events, 23.9 us)
Async XLA Ops:
  0.6 12.6 %copy-start = (f32[256,256]{1,0:T(8,128)S(1)}, f32[256,256]{1,0:T(8,128)}, u32[]{:S(2)}) copy-start(f32[256,256]{1,0:T(8,128)} %param.10) | copy-start | bytes 786436
  2.0 3.2 %collective-permute-start.1 = (bf16[1024,256]{1,0:T(8,128)(2,1)S(1)}, bf16[1024,256]{1,0:T(8,128)(2,1)}, u32[]{:S(2)}, u32[]{:S(2)}) collective-permute-start(bf16[1024,256]{1,0:T(8,128)(2,1)S(1)} %get-tuple-element.66), channel_id=1, source_target_pairs={{0,1},{1,0},{2,3},{3,2},{4,5},{5,4},{6,7},{7,6},{8,9},{9,8},{10,11... | collective-permute-start | bytes 1572872 | tf_op jit(solution)/shard_map/ppermute | solution.py:312
  3.5 9.5 %copy-start.16 = (f32[16,4,2]{0,2,1:T(2,128)S(1)}, f32[16,4,2]{0,2,1:T(2,128)}, u32[]{:S(2)}) copy-start(f32[16,4,2]{0,2,1:T(2,128)} %param.13) | copy-start | bytes 1540
  3.5 9.5 %copy-start.17 = (f32[16,4,2]{0,2,1:T(2,128)S(1)}, f32[16,4,2]{0,2,1:T(2,128)}, u32[]{:S(2)}) copy-start(f32[16,4,2]{0,2,1:T(2,128)} %param.11) | copy-start | bytes 1540
  3.5 9.6 %copy-start.13 = (s32[16,4,2]{0,2,1:T(2,128)S(1)}, s32[16,4,2]{0,2,1:T(2,128)}, u32[]{:S(2)}) copy-start(s32[16,4,2]{0,2,1:T(2,128)} %param.14) | copy-start | bytes 1540
  3.5 10.2 %copy-start.12 = (s32[16,4,2]{0,2,1:T(2,128)S(1)}, s32[16,4,2]{0,2,1:T(2,128)}, u32[]{:S(2)}) copy-start(s32[16,4,2]{0,2,1:T(2,128)} %param.12) | copy-start | bytes 1540
  3.5 22.0 %copy-start.2 = (bf16[512,1024]{1,0:T(8,128)(2,1)S(1)}, bf16[512,1024]{1,0:T(8,128)(2,1)}, u32[]{:S(2)}) copy-start(bf16[512,1024]{1,0:T(8,128)(2,1)} %param.8) | copy-start | bytes 3145732
  6.3 19.6 %collective-permute-start.3 = (bf16[2048,128]{1,0:T(8,128)(2,1)S(1)}, bf16[2048,128]{1,0:T(8,128)(2,1)S(1)}, u32[]{:S(2)}, u32[]{:S(2)}) collective-permute-start(bf16[2048,128]{1,0:T(8,128)(2,1)S(1)} %get-tuple-element.34), channel_id=1, source_target_pairs={{0,32},{1,9},{2,34},{3,11},{4,36},{5,13},{6,38},{7,15},{8,40},{9,1... | collective-permute-start | bytes 1572872 | tf_op jit(solution)/shard_map/ppermute | solution.py:43
  8.1 26.7 %collective-permute-start.2 = (bf16[2048,128]{1,0:T(8,128)(2,1)S(1)}, bf16[2048,128]{1,0:T(8,128)(2,1)S(1)}, u32[]{:S(2)}, u32[]{:S(2)}) collective-permute-start(bf16[2048,128]{1,0:T(8,128)(2,1)S(1)} %get-tuple-element.34), channel_id=1, source_target_pairs={{0,96},{1,25},{2,98},{3,27},{4,100},{5,29},{6,102},{7,31},{8,104},... | collective-permute-start | bytes 1572872 | tf_op jit(solution)/shard_map/ppermute | solution.py:43
  10.3 17.9 %collective-permute-start.7 = (bf16[2048,128]{1,0:T(8,128)(2,1)S(1)}, bf16[2048,128]{1,0:T(8,128)(2,1)}, u32[]{:S(2)}, u32[]{:S(2)}) collective-permute-start(bf16[2048,128]{1,0:T(8,128)(2,1)S(1)} %get-tuple-element.35), channel_id=1, source_target_pairs={{0,32},{1,9},{2,34},{3,11},{4,36},{5,13},{6,38},{7,15},{8,40},{9,1... | collective-permute-start | bytes 1572872 | tf_op jit(solution)/shard_map/ppermute | solution.py:43
  10.3 12.0 %collective-permute-start.5 = (bf16[2048,128]{1,0:T(8,128)(2,1)S(1)}, bf16[2048,128]{1,0:T(8,128)(2,1)}, u32[]{:S(2)}, u32[]{:S(2)}) collective-permute-start(bf16[2048,128]{1,0:T(8,128)(2,1)S(1)} %get-tuple-element.35), channel_id=1, source_target_pairs={{0,96},{1,25},{2,98},{3,27},{4,100},{5,29},{6,102},{7,31},{8,104},... | collective-permute-start | bytes 1572872 | tf_op jit(solution)/shard_map/ppermute | solution.py:43
  13.7 18.3 %copy-start.10 = (bf16[4,2,8,256]{3,2,0,1:T(8,128)(2,1)}, bf16[4,2,8,256]{3,2,0,1:T(8,128)(2,1)S(1)}, u32[]{:S(2)}) copy-start(bf16[4,2,8,256]{3,2,0,1:T(8,128)(2,1)S(1)} %copy.45) | copy-start | bytes 98308
  14.1 17.9 %copy-start.5 = (bf16[4,2,8,256]{3,2,0,1:T(8,128)(2,1)}, bf16[4,2,8,256]{3,2,0,1:T(8,128)(2,1)S(1)}, u32[]{:S(2)}) copy-start(bf16[4,2,8,256]{3,2,0,1:T(8,128)(2,1)S(1)} %copy.44) | copy-start | bytes 98308
  22.3 9.7 %collective-permute-start.6 = (bf16[2048,128]{1,0:T(8,128)(2,1)}, bf16[2048,128]{1,0:T(8,128)(2,1)S(1)}, u32[]{:S(2)}, u32[]{:S(2)}) collective-permute-start(bf16[2048,128]{1,0:T(8,128)(2,1)} %collective-permute-done.5), channel_id=1, source_target_pairs={{0,96},{1,25},{2,98},{3,27},{4,100},{5,29},{6,102},{7,31},{8,104},... | collective-permute-start | bytes 1572872 | tf_op jit(solution)/shard_map/ppermute | solution.py:43
  25.9 9.6 %collective-permute-start.4 = (bf16[2048,128]{1,0:T(8,128)(2,1)S(1)}, bf16[2048,128]{1,0:T(8,128)(2,1)S(1)}, u32[]{:S(2)}, u32[]{:S(2)}) collective-permute-start(bf16[2048,128]{1,0:T(8,128)(2,1)S(1)} %collective-permute-done.3), channel_id=1, source_target_pairs={{0,32},{1,9},{2,34},{3,11},{4,36},{5,13},{6,38},{7,15},{8,40},{9,1... | collective-permute-start | bytes 1572872 | tf_op jit(solution)/shard_map/ppermute | solution.py:43
  37.1 26.7 %collective-permute-start.8 = (bf16[4,2048,128]{2,1,0:T(8,128)(2,1)}, bf16[4,2048,128]{2,1,0:T(8,128)(2,1)}, u32[]{:S(2)}, u32[]{:S(2)}) collective-permute-start(bf16[4,2048,128]{2,1,0:T(8,128)(2,1)} %pad_maximum_fusion.refs_0_), channel_id=1, source_target_pairs={{0,8},{1,33},{2,10},{3,35},{4,12},{5,37},{6,14},{7,39},{8,16},{9,4... | collective-permute-start | bytes 6291464 | tf_op jit(solution)/shard_map/ppermute | solution.py:43
  37.7 26.1 %collective-permute-start.9 = (bf16[4,2048,128]{2,1,0:T(8,128)(2,1)}, bf16[4,2048,128]{2,1,0:T(8,128)(2,1)}, u32[]{:S(2)}, u32[]{:S(2)}) collective-permute-start(bf16[4,2048,128]{2,1,0:T(8,128)(2,1)} %pad_maximum_fusion.1.refs_1_), channel_id=1, source_target_pairs={{0,24},{1,97},{2,26},{3,99},{4,28},{5,101},{6,30},{7,103},{8,0},{9... | collective-permute-start | bytes 6291464 | tf_op jit(solution)/shard_map/ppermute | solution.py:43
  39.8 5.3 %collective-permute-start = (bf16[512,1024]{1,0:T(8,128)(2,1)S(1)}, bf16[512,1024]{1,0:T(8,128)(2,1)}, u32[]{:S(2)}, u32[]{:S(2)}) collective-permute-start(bf16[512,1024]{1,0:T(8,128)(2,1)S(1)} %copy-done.2), channel_id=1, source_target_pairs={{0,1},{1,0},{2,3},{3,2},{4,5},{5,4},{6,7},{7,6},{8,9},{9,8},{10,11... | collective-permute-start | bytes 3145736 | tf_op jit(solution)/shard_map/ppermute | solution.py:332
  42.6 57.7 %collective-permute-start.10 = (bf16[4,2048,128]{2,1,0:T(8,128)(2,1)}, bf16[4,2048,128]{2,1,0:T(8,128)(2,1)}, u32[]{:S(2)}, u32[]{:S(2)}) collective-permute-start(bf16[4,2048,128]{2,1,0:T(8,128)(2,1)} %pad_maximum_fusion.refs_0_), channel_id=1, source_target_pairs={{0,24},{1,97},{2,26},{3,99},{4,28},{5,101},{6,30},{7,103},{8,0},{9... | collective-permute-start | bytes 6291464 | tf_op jit(solution)/shard_map/ppermute | solution.py:43
  45.0 55.4 %collective-permute-start.11 = (bf16[4,2048,128]{2,1,0:T(8,128)(2,1)}, bf16[4,2048,128]{2,1,0:T(8,128)(2,1)}, u32[]{:S(2)}, u32[]{:S(2)}) collective-permute-start(bf16[4,2048,128]{2,1,0:T(8,128)(2,1)} %pad_maximum_fusion.1.refs_1_), channel_id=1, source_target_pairs={{0,8},{1,33},{2,10},{3,35},{4,12},{5,37},{6,14},{7,39},{8,16},{9,4... | collective-permute-start | bytes 6291464 | tf_op jit(solution)/shard_map/ppermute | solution.py:43
  51.4 40.1 %all-to-all-start = ((bf16[4,512,256]{2,1,0:T(8,128)(2,1)}), bf16[4,512,256]{2,1,0:T(8,128)(2,1)S(1)}, u32[]{:S(2)}, u32[]{:S(2)}) async-start(bf16[4,512,256]{2,1,0:T(8,128)(2,1)} %forward.4), calls=%async_computation | async-start | bytes 2097152 | tf_op jit(solution)/shard_map/all_to_all | solution.py:54
  63.8 73.3 %collective-permute-start.16 = (bf16[4,2048,128]{2,1,0:T(8,128)(2,1)}, bf16[4,2048,128]{2,1,0:T(8,128)(2,1)}, u32[]{:S(2)}, u32[]{:S(2)}) collective-permute-start(bf16[4,2048,128]{2,1,0:T(8,128)(2,1)} %collective-permute-done.8.refs_0_), channel_id=1, source_target_pairs={{0,8},{1,33},{2,10},{3,35},{4,12},{5,37},{6,14},{7,39},{8,16},{9,4... | collective-permute-start | bytes 6291464 | tf_op jit(solution)/shard_map/ppermute | solution.py:43
  63.8 73.3 %collective-permute-start.17 = (bf16[4,2048,128]{2,1,0:T(8,128)(2,1)}, bf16[4,2048,128]{2,1,0:T(8,128)(2,1)}, u32[]{:S(2)}, u32[]{:S(2)}) collective-permute-start(bf16[4,2048,128]{2,1,0:T(8,128)(2,1)} %collective-permute-done.9.refs_1_), channel_id=1, source_target_pairs={{0,24},{1,97},{2,26},{3,99},{4,28},{5,101},{6,30},{7,103},{8,0},{9... | collective-permute-start | bytes 6291464 | tf_op jit(solution)/shard_map/ppermute | solution.py:43
  66.5 4.8 %collective-permute-start.12 = (f32[32,512]{1,0:T(8,128)}, f32[32,512]{1,0:T(8,128)S(1)}, u32[]{:S(2)}, u32[]{:S(2)}) collective-permute-start(f32[32,512]{1,0:T(8,128)} %pad_maximum_fusion.4), channel_id=1, source_target_pairs={{0,1},{1,0},{2,3},{3,2},{4,5},{5,4},{6,7},{7,6},{8,9},{9,8},{10,11... | collective-permute-start | bytes 196616 | tf_op jit(solution)/shard_map/ppermute | solution.py:60
  72.1 3.6 %collective-permute-start.13 = (f32[32,512]{1,0:T(8,128)S(1)}, f32[32,512]{1,0:T(8,128)S(1)}, u32[]{:S(2)}, u32[]{:S(2)}) collective-permute-start(f32[32,512]{1,0:T(8,128)S(1)} %add.403), channel_id=1, source_target_pairs={{0,2},{1,3},{2,0},{3,1},{4,6},{5,7},{6,4},{7,5},{8,10},{9,11},{10,... | collective-permute-start | bytes 196616 | tf_op jit(solution)/shard_map/ppermute | solution.py:61
  76.4 19.4 %collective-permute-start.14 = (f32[32,512]{1,0:T(8,128)}, f32[32,512]{1,0:T(8,128)}, u32[]{:S(2)}, u32[]{:S(2)}) collective-permute-start(f32[32,512]{1,0:T(8,128)} %add.404), channel_id=1, source_target_pairs={{0,4},{1,5},{2,6},{3,7},{4,0},{5,1},{6,2},{7,3},{8,12},{9,13},{10,... | collective-permute-start | bytes 196616 | tf_op jit(solution)/shard_map/ppermute | solution.py:62
  91.5 18.1 %all-to-all-start.1 = ((bf16[4,512,256]{2,1,0:T(8,128)(2,1)}), bf16[4,512,256]{2,1,0:T(8,128)(2,1)}, u32[]{:S(2)}, u32[]{:S(2)}) async-start(bf16[4,512,256]{2,1,0:T(8,128)(2,1)} %forward.5), calls=%async_computation.1 | async-start | bytes 2097152 | tf_op jit(solution)/shard_map/all_to_all | solution.py:54
  109.6 16.8 %all-to-all-start.2 = ((bf16[4,512,256]{2,1,0:T(8,128)(2,1)}), bf16[4,512,256]{2,1,0:T(8,128)(2,1)}, u32[]{:S(2)}, u32[]{:S(2)}) async-start(bf16[4,512,256]{2,1,0:T(8,128)(2,1)} %forward.6), calls=%async_computation.2 | async-start | bytes 2097152 | tf_op jit(solution)/shard_map/all_to_all | solution.py:54
  129.0 34.3 %all-to-all-start.3 = ((bf16[4,512,256]{2,1,0:T(8,128)(2,1)}), bf16[4,512,256]{2,1,0:T(8,128)(2,1)}, u32[]{:S(2)}, u32[]{:S(2)}) async-start(bf16[4,512,256]{2,1,0:T(8,128)(2,1)} %arrange.1), calls=%async_computation.3 | async-start | bytes 2097152 | tf_op jit(solution)/shard_map/all_to_all | solution.py:54
  133.4 8.7 %collective-permute-start.25 = (f32[32,1024]{1,0:T(8,128)S(1)}, f32[32,1024]{1,0:T(8,128)S(1)}, u32[]{:S(2)}, u32[]{:S(2)}) collective-permute-start(f32[32,1024]{1,0:T(8,128)S(1)} %copy-done.4), channel_id=1, source_target_pairs={{0,32},{1,33},{2,34},{3,35},{4,36},{5,37},{6,38},{7,39},{8,40},{9,... | collective-permute-start | bytes 393224 | tf_op jit(solution)/shard_map/ppermute | solution.py:72
  133.5 8.7 %collective-permute-start.26 = (f32[32,1024]{1,0:T(8,128)S(1)}, f32[32,1024]{1,0:T(8,128)S(1)}, u32[]{:S(2)}, u32[]{:S(2)}) collective-permute-start(f32[32,1024]{1,0:T(8,128)S(1)} %copy-done.4), channel_id=1, source_target_pairs={{0,64},{1,65},{2,66},{3,67},{4,68},{5,69},{6,70},{7,71},{8,72},{9,... | collective-permute-start | bytes 393224 | tf_op jit(solution)/shard_map/ppermute | solution.py:72
  137.0 5.2 %collective-permute-start.27 = (f32[32,1024]{1,0:T(8,128)S(1)}, f32[32,1024]{1,0:T(8,128)S(1)}, u32[]{:S(2)}, u32[]{:S(2)}) collective-permute-start(f32[32,1024]{1,0:T(8,128)S(1)} %copy-done.4), channel_id=1, source_target_pairs={{0,96},{1,97},{2,98},{3,99},{4,100},{5,101},{6,102},{7,103},{8,104... | collective-permute-start | bytes 393224 | tf_op jit(solution)/shard_map/ppermute | solution.py:72
  137.1 5.2 %copy-start.8 = (bf16[32,512]{1,0:T(8,128)(2,1)S(1)}, bf16[32,512]{1,0:T(8,128)(2,1)}, u32[]{:S(2)}) copy-start(bf16[32,512]{1,0:T(8,128)(2,1)} %copy-done.7) | copy-start | bytes 98308
  142.2 18.5 %collective-permute-start.28 = (f32[32,1024]{1,0:T(8,128)S(1)}, f32[32,1024]{1,0:T(8,128)S(1)}, u32[]{:S(2)}, u32[]{:S(2)}) collective-permute-start(f32[32,1024]{1,0:T(8,128)S(1)} %add_add_fusion), channel_id=1, source_target_pairs={{0,8},{8,0},{16,24},{24,16},{32,40},{40,32},{48,56},{56,48},{64,72... | collective-permute-start | bytes 393224 | tf_op jit(solution)/shard_map/ppermute | solution.py:82
  144.1 20.5 %collective-permute-start.20 = (bf16[512,256]{1,0:T(8,128)(2,1)}, bf16[512,256]{1,0:T(8,128)(2,1)}, u32[]{:S(2)}, u32[]{:S(2)}) collective-permute-start(bf16[512,256]{1,0:T(8,128)(2,1)} %get-tuple-element.53), channel_id=1, source_target_pairs={{0,6},{1,7},{2,0},{3,1},{4,2},{5,3},{6,4},{7,5},{8,14},{9,15},{10,... | collective-permute-start | bytes 786440 | tf_op jit(solution)/shard_map/ppermute | solution.py:380
  146.6 18.4 %collective-permute-start.19 = (bf16[512,256]{1,0:T(8,128)(2,1)}, bf16[512,256]{1,0:T(8,128)(2,1)}, u32[]{:S(2)}, u32[]{:S(2)}) collective-permute-start(bf16[512,256]{1,0:T(8,128)(2,1)} %get-tuple-element.52), channel_id=1, source_target_pairs={{0,2},{1,3},{2,4},{3,5},{4,6},{5,7},{6,0},{7,1},{8,10},{9,11},{10,... | collective-permute-start | bytes 786440 | tf_op jit(solution)/shard_map/ppermute | solution.py:380
  146.6 18.4 %collective-permute-start.18 = (bf16[512,256]{1,0:T(8,128)(2,1)}, bf16[512,256]{1,0:T(8,128)(2,1)}, u32[]{:S(2)}, u32[]{:S(2)}) collective-permute-start(bf16[512,256]{1,0:T(8,128)(2,1)} %get-tuple-element.51), channel_id=1, source_target_pairs={{0,4},{1,5},{2,6},{3,7},{4,0},{5,1},{6,2},{7,3},{8,12},{9,13},{10,... | collective-permute-start | bytes 786440 | tf_op jit(solution)/shard_map/ppermute | solution.py:380
  155.4 27.2 %collective-permute-start.24 = (bf16[512,1024]{1,0:T(8,128)(2,1)S(1)}, bf16[512,1024]{1,0:T(8,128)(2,1)}, u32[]{:S(2)}, u32[]{:S(2)}) collective-permute-start(bf16[512,1024]{1,0:T(8,128)(2,1)S(1)} %get-tuple-element.56), channel_id=1, source_target_pairs={{0,1},{1,0},{2,3},{3,2},{4,5},{5,4},{6,7},{7,6},{8,9},{9,8},{10,11... | collective-permute-start | bytes 3145736 | tf_op jit(solution)/shard_map/ppermute | solution.py:404
  161.3 8.7 %collective-permute-start.29 = (f32[32,1024]{1,0:T(8,128)}, f32[32,1024]{1,0:T(8,128)}, u32[]{:S(2)}, u32[]{:S(2)}) collective-permute-start(f32[32,1024]{1,0:T(8,128)} %add.466), channel_id=1, source_target_pairs={{0,16},{8,24},{16,0},{24,8},{32,48},{40,56},{48,32},{56,40},{64,80... | collective-permute-start | bytes 393224 | tf_op jit(solution)/shard_map/ppermute | solution.py:82
  164.6 8.3 %copy-start.15 = (f32[16,4,2]{0,2,1:T(2,128)S(1)}, f32[16,4,2]{0,2,1:T(2,128)}, u32[]{:S(2)}) copy-start(f32[16,4,2]{0,2,1:T(2,128)} %copy-done.14) | copy-start | bytes 1540
  164.6 11.7 %copy-start.1 = (bf16[4,512,256]{2,1,0:T(8,128)(2,1)S(1)}, bf16[4,512,256]{2,1,0:T(8,128)(2,1)}, u32[]{:S(2)}) copy-start(bf16[4,512,256]{2,1,0:T(8,128)(2,1)} %arrange.1) | copy-start | bytes 3145732
  164.6 11.0 %collective-permute-start.15 = (bf16[2,512,256]{2,1,0:T(8,128)(2,1)S(1)}, bf16[2,512,256]{2,1,0:T(8,128)(2,1)S(1)}, u32[]{:S(2)}, u32[]{:S(2)}) collective-permute-start(bf16[2,512,256]{2,1,0:T(8,128)(2,1)S(1)} %slice_select_fusion.1), channel_id=1, source_target_pairs={{0,1},{1,0},{2,3},{3,2},{4,5},{5,4},{6,7},{7,6},{8,9},{9,8},{10,11... | collective-permute-start | bytes 1572872 | tf_op jit(solution)/shard_map/ppermute | solution.py:390
  166.3 11.1 %collective-permute-start.22 = (bf16[512,256]{1,0:T(8,128)(2,1)S(1)}, bf16[512,256]{1,0:T(8,128)(2,1)S(1)}, u32[]{:S(2)}, u32[]{:S(2)}) collective-permute-start(bf16[512,256]{1,0:T(8,128)(2,1)S(1)} %add_convert_fusion.2), channel_id=1, source_target_pairs={{1,4},{5,5},{9,12},{13,13},{17,20},{21,21},{25,28},{29,29},{33,38}... | collective-permute-start | bytes 786440 | tf_op jit(solution)/shard_map/ppermute | solution.py:285
  169.3 8.1 %collective-permute-start.23 = (bf16[512,256]{1,0:T(8,128)(2,1)S(1)}, bf16[512,256]{1,0:T(8,128)(2,1)S(1)}, u32[]{:S(2)}, u32[]{:S(2)}) collective-permute-start(bf16[512,256]{1,0:T(8,128)(2,1)S(1)} %add_convert_fusion.2), channel_id=1, source_target_pairs={{3,4},{7,5},{11,12},{15,13},{19,20},{23,21},{27,28},{31,29},{35,38... | collective-permute-start | bytes 786440 | tf_op jit(solution)/shard_map/ppermute | solution.py:285
  172.6 1.7 collective-permute-start.30
  174.3 3.4 %collective-permute-start.21 = (bf16[512,256]{1,0:T(8,128)(2,1)S(1)}, bf16[512,256]{1,0:T(8,128)(2,1)S(1)}, u32[]{:S(2)}, u32[]{:S(2)}) collective-permute-start(bf16[512,256]{1,0:T(8,128)(2,1)S(1)} %add_convert_fusion.2), channel_id=1, source_target_pairs={{0,1},{2,3},{4,5},{6,7},{8,9},{10,11},{12,13},{14,15},{32,33},{34,... | collective-permute-start | bytes 786440 | tf_op jit(solution)/shard_map/ppermute | solution.py:290
  175.6 6.7 %collective-permute-start.31 = (f32[256,256]{1,0:T(8,128)S(1)}, f32[256,256]{1,0:T(8,128)S(1)}, u32[]{:S(2)}, u32[]{:S(2)}) collective-permute-start(f32[256,256]{1,0:T(8,128)S(1)} %add.469), channel_id=1, source_target_pairs={{0,2},{1,3},{2,0},{3,1},{4,6},{5,7},{6,4},{7,5},{8,10},{9,11},{10,... | collective-permute-start | bytes 786440 | tf_op jit(solution)/shard_map/ppermute | solution.py:61
  182.4 7.3 %collective-permute-start.32 = (f32[256,256]{1,0:T(8,128)S(1)}, f32[256,256]{1,0:T(8,128)S(1)}, u32[]{:S(2)}, u32[]{:S(2)}) collective-permute-start(f32[256,256]{1,0:T(8,128)S(1)} %add.470), channel_id=1, source_target_pairs={{0,4},{1,5},{2,6},{3,7},{4,0},{5,1},{6,2},{7,3},{8,12},{9,13},{10,... | collective-permute-start | bytes 786440 | tf_op jit(solution)/shard_map/ppermute | solution.py:62
  (7 other events, 19.8 us)

commit v8 on v7

--- a/solution.py
+++ b/solution.py
@@ -342,7 +342,8 @@
     back_part = lax.dot_general(up_b, grad_cols, cols_by_cols, preferred_element_type=f32)
     totals = jnp.concatenate([low_part, back_part], axis=0)
     lines[1], totals = lax.optimization_barrier((lines[1], totals))
-    blocks = [ring_gather(lines[h], 1, h) for h in range(2)]
+    below = [shift(line, 1, 1) for line in lines]
+    above = [shift(line, 1, -1) for line in lines]
     totals = over_tensor(totals).astype(bf16)
     low_bf, back_bf = totals[:rank], totals[rank:]
 
@@ -354,13 +355,19 @@
     beside = [[(3, 0), (1, 1)], [(1, 0), (3, 1)]]
     across = [(2, 0), (2, 1)]
 
+    sent_here = forward(turned, wide, lines)
+    slots_here = exchange(sent_here, "tensor", LANES)
+    grown = backward(after(spots_of(here), sent_here), None, out_grad, lines)
+    below[0], above[1], grown, totals = lax.optimization_barrier(
+        (below[0], above[1], grown, totals)
+    )
+    corner = [shift(below[0], 1, 1), shift(above[1], 1, -1)]
+    blocks = [[lines[h], above[h], corner[h], below[h]] for h in range(2)]
+
     def take(chunks):
         return [blocks[h][i] for i, h in chunks]
 
-    sent_here = forward(turned, wide, take(here))
-    slots_here = exchange(sent_here, "tensor", LANES)
-    grown = backward(after(spots_of(here), sent_here), None, out_grad, take(here))
-    sent_first = forward(after(turned, grown), wide, take(beside[0]))
+    sent_first = forward(turned, wide, take(beside[0]))
     slots_here, sent_first = lax.optimization_barrier((slots_here, sent_first))
     slots_first = exchange(sent_first, "tensor", LANES)
     sent_second = forward(after(turned, sent_first), wide, take(beside[1]))
@@ -369,24 +376,26 @@
     both_parts = over_side(both, 0)
     chunks = beside[0] + beside[1]
     grown = backward(after(spots_of(chunks), sent_second), grown, out_grad, take(chunks))
+    both = total_of(lax.optimization_barrier((*both_parts, grown))[:SIDE])
     slots = arrange(
-        far.astype(jnp.int32).reshape(1), slots_here, slots_first, after(slots_second, grown)
-    )
+        far.astype(jnp.int32).reshape(1), slots_here, slots_first, after(slots_second, grown, both)
+    )
+    both = with_partner(both, 1, slots)
     moved = exchange(slots, "tensor", LANES)
-    sent = forward(after(turned_here, slots), wide, take(across), apart=True)
+    sent = forward(after(turned_here, slots, both), wide, take(across), apart=True)
     arrived = [sent[0]]
     for step in range(1, SIDE):
         turns = [(t, (t + 2 * step) % 8) for t in range(8)]
         arrived.append(lax.ppermute(sent[step], "tensor", turns))
     piece = total_of([a.astype(f32) for a in arrived]).astype(bf16)
-    both = total_of(lax.optimization_barrier((*both_parts, *sent))[:SIDE])
-    grown, other = backward(
-        after(spots_of(across), *sent), grown, out_grad, take(across), last=True
-    )
-    both = with_partner(with_partner(both, 1, grown), 2)
+    both = with_partner(both, 2, *sent)
     bank_a, logit_grad_a = compose_back(both[:rank], weights_a, picked_a, mixing_a, vector_bank)
     bank_b, logit_grad_b = compose_back(both[rank:], weights_b, picked_b, mixing_b, vector_bank)
-    bank_grad = over_tensor(bank_a + bank_b)
+    bank_part = bank_a + bank_b
+    grown, other = backward(
+        after(spots_of(across), *sent, bank_part), grown, out_grad, take(across), last=True
+    )
+    bank_grad = over_tensor(bank_part)
     crossed = lax.ppermute(jnp.where(core == 0, slots[2:], moved[:2]), "tensor", SWAP)
     firsts = jnp.where(core == 0, slots[:2], crossed)
     seconds = jnp.where(core == 0, crossed, moved[2:])

time: 194 us -> 194 us (level)
  the two profiles are of different devices: /device:TPU:1 before, /device:TPU:58 now
where the time goes in v8:
time: 194 us; the launch traced here: 193 us
  starting transfers between devices  67 us (35%)
  Pallas kernels  47.2 us (24%)
  waiting for transfers between devices  45.3 us (23%)
  other arithmetic  18.5 us (10%)
  matrix products  9.88 us (5%)
  local copies, waits for them, and re-layouts  3.5 us (2%)
    pallas_call x3, Pallas kernels, backward(): pl.pallas_call(functools.partial(backward_kernel, count, first, last), ou...  24.7 us
    all_to_all x4, starting transfers between devices, exchange(): lax.all_to_all(value, axis, split_axis=0, concat_axis=0, tiled=True, axis...  22.9 us
    pallas_call x4, Pallas kernels, forward(): pl.pallas_call(functools.partial(forward_kernel, count, many), out_shape=...  19.8 us
    ppermute x12, waiting for transfers between devices, shift(): return lax.ppermute(value, BOTH, ring(stage, step))  15.6 us
    ppermute x12, starting transfers between devices, shift(): return lax.ppermute(value, BOTH, ring(stage, step))  13.4 us
    ppermute x2, waiting for transfers between devices, over_tensor(): lax.ppermute(value, 'tensor', [(t, t ^ 2) for t in range(8)])  12.5 us
    ppermute x2, waiting for transfers between devices, from_second(): return lax.ppermute(piece, BOTH, pairs(move))  9.18 us
    ppermute x2, starting transfers between devices, with_partner(): other = lax.ppermute(value, 'dp', [(d, d ^ bit) for d in range(16)])  7.26 us
  transfers between devices with their start and end apart: 37, of which 10 were waited for; matrix products, arithmetic and copies ran while one was open for 14% of the time, Pallas kernels for 24%

profile of v8, /device:TPU:58, one launch (start us, length us, event | category | flops | bytes accessed | tf_op | source)
XLA Modules:
  0.0 192.6 jit_solution(18267708004300655738)
XLA Ops:
  0.7 1.3 broadcast_select_fusion.1
  2.2 1.9 collective-permute-done.1
  5.2 1.6 collective-permute-start.3
  7.3 1.5 collective-permute-start.7
  10.9 10.8 %collective-permute-done.5 = bf16[2048,128]{1,0:T(8,128)(2,1)} collective-permute-done((bf16[2048,128]{1,0:T(8,128)(2,1)S(1)}, bf16[2048,128]{1,0:T(8,128)(2,1)}, u32[]{:S(2)}, u32[]{:S(2)}) %collective-permute-start.5) | collective-permute-done | bytes 524320 | tf_op jit(solution)/shard_map/ppermute | solution.py:43
  22.6 1.5 collective-permute-start.4
  24.1 1.6 fusion.11
  26.4 4.7 %collective-permute-done.6 = bf16[2048,128]{1,0:T(8,128)(2,1)S(1)} collective-permute-done((bf16[2048,128]{1,0:T(8,128)(2,1)}, bf16[2048,128]{1,0:T(8,128)(2,1)S(1)}, u32[]{:S(2)}, u32[]{:S(2)}) %collective-permute-start.6) | collective-permute-done | bytes 524320 | tf_op jit(solution)/shard_map/ppermute | solution.py:43
  31.1 2.8 %pad_maximum_fusion.1.refs_1_ = bf16[4,2048,128]{2,1,0:T(8,128)(2,1)} fusion(bf16[1,2048,128]{2,1,0:T(8,128)(2,1)} %bitcast.9, bf16[1,2048,128]{2,1,0:T(8,128)(2,1)S(1)} %bitcast.111, bf16[1,2048,128]{2,1,0:T(8,128)(2,1)} %bitcast.7, bf16[1,2048,128]{2,1,0:T(8,128)(2,1)S(1)} %bitcast.103), kind=kLoop, calls=%fused_computation.3 | loop fusion | flops 3145728 | bytes 4194304 | tf_op jit(solution)/shard_map/stack | solution.py:318
  34.0 1.6 pad_maximum_fusion.refs_0_
  35.6 1.9 collective-permute-start.8
  37.5 1.9 collective-permute-start.14
  40.5 1.3 constant_dynamic-update-slice_fusion.wide_ref
  41.8 5.0 %forward.4 = bf16[4,512,256]{2,1,0:T(8,128)(2,1)} custom-call(s32[1]{0:T(128)} %bitcast.1.start_ref, bf16[512,2048]{1,0:T(8,128)(2,1)S(1)} %constant_dynamic-update-slice_fusion.wide_ref, bf16[4,2048,128]{2,1,0:T(8,128)(2,1)} %pad_maximum_fusion.refs_0_, bf16[4,2048,128]{2,1,0:T(8,128)(2,1)} %pad_maximum_fusion.1.refs_1_), custom_call_target="tpu_custom_call" | custom-call | flops 268435456 | bytes 524288 | tf_op jit(solution)/shard_map/forward/pallas_call | solution.py:131
  46.8 4.7 %all-to-all-start = ((bf16[4,512,256]{2,1,0:T(8,128)(2,1)}), bf16[4,512,256]{2,1,0:T(8,128)(2,1)S(1)}, u32[]{:S(2)}, u32[]{:S(2)}) async-start(bf16[4,512,256]{2,1,0:T(8,128)(2,1)} %forward.4), calls=%async_computation | async-start | bytes 2097152 | tf_op jit(solution)/shard_map/all_to_all | solution.py:54
  53.3 12.5 %collective-permute-done.11 = f32[32,512]{1,0:T(8,128)S(1)} collective-permute-done((f32[32,512]{1,0:T(8,128)S(1)}, f32[32,512]{1,0:T(8,128)S(1)}, u32[]{:S(2)}, u32[]{:S(2)}) %collective-permute-start.11) | collective-permute-done | bytes 65568 | tf_op jit(solution)/shard_map/ppermute | solution.py:61
  67.5 7.1 %backward.3.refs_20_ = f32[512,2048]{1,0:T(8,128)} custom-call(s32[8]{0:T(128)S(1)} %stack.153.spots_ref, bf16[4,2048,128]{2,1,0:T(8,128)(2,1)} %pad_maximum_fusion.refs_0_, bf16[4,2048,128]{2,1,0:T(8,128)(2,1)} %pad_maximum_fusion.1.refs_1_, bf16[512,8192]{1,0:T(8,128)(2,1)} %refs_9_.5, bf16[512,8192]{1,0:T(8,128)(2,1)} %refs_9_.5, ...), custom_call_target="tpu_custom_call" | custom-call | flops 268435456 | bytes 524288 | tf_op jit(solution)/shard_map/backward/pallas_call | solution.py:237
  74.6 1.5 add_convert_fusion.3
  76.1 2.2 %collective-permute-start.20 = (bf16[4,2048,128]{2,1,0:T(8,128)(2,1)}, bf16[4,2048,128]{2,1,0:T(8,128)(2,1)}, u32[]{:S(2)}, u32[]{:S(2)}) collective-permute-start(bf16[4,2048,128]{2,1,0:T(8,128)(2,1)} %collective-permute-done.8.refs_0_), channel_id=1, source_target_pairs={{0,8},{1,33},{2,10},{3,35},{4,12},{5,37},{6,14},{7,39},{8,16},{9,4... | collective-permute-start | bytes 6291464 | tf_op jit(solution)/shard_map/ppermute | solution.py:43
  79.1 4.9 %forward.5 = bf16[4,512,256]{2,1,0:T(8,128)(2,1)} custom-call(s32[1]{0:T(128)} %bitcast.1.start_ref, bf16[512,2048]{1,0:T(8,128)(2,1)S(1)} %constant_dynamic-update-slice_fusion.wide_ref, bf16[4,2048,128]{2,1,0:T(8,128)(2,1)} %collective-permute-done.8.refs_0_, bf16[4,2048,128]{2,1,0:T(8,128)(2,1)} %collective-permute-done.9.refs_1_), custom_call_target="tpu_custom_call" | custom-call | flops 268435456 | bytes 524288 | tf_op jit(solution)/shard_map/forward/pallas_call | solution.py:131
  84.1 7.1 %all-to-all-start.1 = ((bf16[4,512,256]{2,1,0:T(8,128)(2,1)}), bf16[4,512,256]{2,1,0:T(8,128)(2,1)}, u32[]{:S(2)}, u32[]{:S(2)}) async-start(bf16[4,512,256]{2,1,0:T(8,128)(2,1)} %forward.5), calls=%async_computation.1 | async-start | bytes 2097152 | tf_op jit(solution)/shard_map/all_to_all | solution.py:54
  91.2 1.5 fusion.9
  92.7 1.5 fusion.34
  94.9 4.9 %forward.6 = bf16[4,512,256]{2,1,0:T(8,128)(2,1)} custom-call(s32[1]{0:T(128)} %bitcast.1.start_ref, bf16[512,2048]{1,0:T(8,128)(2,1)S(1)} %constant_dynamic-update-slice_fusion.wide_ref, bf16[4,2048,128]{2,1,0:T(8,128)(2,1)} %collective-permute-done.13.refs_0_.refs_2_, bf16[4,2048,128]{2,1,0:T(8,128)(2,1)} %collective-permute-done.14.refs_1_.refs_3_), custom_call_target="tpu_custom_call" | custom-call | flops 268435456 | bytes 524288 | tf_op jit(solution)/shard_map/forward/pallas_call | solution.py:131
  99.8 2.6 %all-to-all-done.1.refs_0_ = bf16[4,512,256]{2,1,0:T(8,128)(2,1)} async-done(((bf16[4,512,256]{2,1,0:T(8,128)(2,1)}), bf16[4,512,256]{2,1,0:T(8,128)(2,1)}, u32[]{:S(2)}, u32[]{:S(2)}) %all-to-all-start.1) | async-done | bytes 1048608 | tf_op jit(solution)/shard_map/all_to_all | solution.py:54
  102.5 6.3 %all-to-all-start.2 = ((bf16[4,512,256]{2,1,0:T(8,128)(2,1)}), bf16[4,512,256]{2,1,0:T(8,128)(2,1)}, u32[]{:S(2)}, u32[]{:S(2)}) async-start(bf16[4,512,256]{2,1,0:T(8,128)(2,1)} %forward.6), calls=%async_computation.2 | async-start | bytes 2097152 | tf_op jit(solution)/shard_map/all_to_all | solution.py:54
  108.7 3.0 %collective-permute-start.17 = (f32[32,1024]{1,0:T(8,128)}, f32[32,1024]{1,0:T(8,128)}, u32[]{:S(2)}, u32[]{:S(2)}) collective-permute-start(f32[32,1024]{1,0:T(8,128)} %maximum_multiply_fusion), channel_id=1, source_target_pairs={{0,96},{1,97},{2,98},{3,99},{4,100},{5,101},{6,102},{7,103},{8,104... | collective-permute-start | bytes 393224 | tf_op jit(solution)/shard_map/ppermute | solution.py:72
  112.4 2.3 %collective-permute-start.15 = (f32[32,1024]{1,0:T(8,128)}, f32[32,1024]{1,0:T(8,128)}, u32[]{:S(2)}, u32[]{:S(2)}) collective-permute-start(f32[32,1024]{1,0:T(8,128)} %maximum_multiply_fusion), channel_id=1, source_target_pairs={{0,32},{1,33},{2,34},{3,35},{4,36},{5,37},{6,38},{7,39},{8,40},{9,... | collective-permute-start | bytes 393224 | tf_op jit(solution)/shard_map/ppermute | solution.py:72
  114.8 10.6 %backward.4.refs_10_ = f32[512,2048]{1,0:T(8,128)} custom-call(s32[16]{0:T(128)S(1)} %stack.170.spots_ref, bf16[4,2048,128]{2,1,0:T(8,128)(2,1)} %collective-permute-done.8.refs_0_, bf16[4,2048,128]{2,1,0:T(8,128)(2,1)} %collective-permute-done.9.refs_1_, ...), custom_call_target="tpu_custom_call", output_to_operand_aliasing={{}: (21, {})} | custom-call | flops 536870912 | bytes 1048576 | tf_op jit(solution)/shard_map/backward/pallas_call | solution.py:237
  125.5 1.7 add_add_fusion
  127.2 2.9 %collective-permute-start.19 = (f32[32,1024]{1,0:T(8,128)}, f32[32,1024]{1,0:T(8,128)}, u32[]{:S(2)}, u32[]{:S(2)}) collective-permute-start(f32[32,1024]{1,0:T(8,128)} %add_add_fusion), channel_id=1, source_target_pairs={{0,8},{8,0},{16,24},{24,16},{32,40},{40,32},{48,56},{56,48},{64,72... | collective-permute-start | bytes 393224 | tf_op jit(solution)/shard_map/ppermute | solution.py:82
  130.2 2.6 %arrange.1 = bf16[4,512,256]{2,1,0:T(8,128)(2,1)} custom-call(s32[1]{0:T(128)} %bitcast.far_ref, bf16[4,512,256]{2,1,0:T(8,128)(2,1)S(1)} %all-to-all-done.here_ref, bf16[4,512,256]{2,1,0:T(8,128)(2,1)} %all-to-all-done.1.refs_0_, bf16[4,512,256]{2,1,0:T(8,128)(2,1)} %all-to-all-done.2.refs_1_), custom_call_target="tpu_custom_call" | custom-call | flops 2097152 | bytes 4194304 | tf_op jit(solution)/shard_map/arrange/pallas_call | solution.py:178
  133.4 1.6 add.442
  135.1 4.3 %collective-permute-start.28 = (f32[32,1024]{1,0:T(8,128)}, f32[32,1024]{1,0:T(8,128)}, u32[]{:S(2)}, u32[]{:S(2)}) collective-permute-start(f32[32,1024]{1,0:T(8,128)} %add.442), channel_id=1, source_target_pairs={{0,16},{8,24},{16,0},{24,8},{32,48},{40,56},{48,32},{56,40},{64,80... | collective-permute-start | bytes 393224 | tf_op jit(solution)/shard_map/ppermute | solution.py:82
  139.5 4.8 %all-to-all-start.3 = ((bf16[4,512,256]{2,1,0:T(8,128)(2,1)}), bf16[4,512,256]{2,1,0:T(8,128)(2,1)S(1)}, u32[]{:S(2)}, u32[]{:S(2)}) async-start(bf16[4,512,256]{2,1,0:T(8,128)(2,1)} %arrange.1), calls=%async_computation.3 | async-start | bytes 2097152 | tf_op jit(solution)/shard_map/all_to_all | solution.py:54
  144.3 5.0 %forward.7 = (bf16[512,256]{1,0:T(8,128)(2,1)}, bf16[512,256]{1,0:T(8,128)(2,1)}, bf16[512,256]{1,0:T(8,128)(2,1)}, bf16[512,256]{1,0:T(8,128)(2,1)}) custom-call(s32[1]{0:T(128)} %bitcast.36.start_ref, bf16[512,2048]{1,0:T(8,128)(2,1)S(1)} %constant_dynamic-update-slice_fusion.wide_ref, bf16[4,2048,128]{2,1,0:T(8,128)(2,1)} %collective-permute-done.20.refs_0_, ...), custom_call_target="tpu_custom_call" | custom-call | flops 268435456 | bytes 524288 | tf_op jit(solution)/shard_map/forward/pallas_call | solution.py:131
  149.3 1.5 collective-permute-start.22
  150.8 2.1 %collective-permute-start.23 = (bf16[512,256]{1,0:T(8,128)(2,1)}, bf16[512,256]{1,0:T(8,128)(2,1)}, u32[]{:S(2)}, u32[]{:S(2)}) collective-permute-start(bf16[512,256]{1,0:T(8,128)(2,1)} %get-tuple-element.63), channel_id=1, source_target_pairs={{0,2},{1,3},{2,4},{3,5},{4,6},{5,7},{6,0},{7,1},{8,10},{9,11},{10,... | collective-permute-start | bytes 786440 | tf_op jit(solution)/shard_map/ppermute | solution.py:389
  156.4 2.2 %all-to-all-done.3 = bf16[4,512,256]{2,1,0:T(8,128)(2,1)S(1)} async-done(((bf16[4,512,256]{2,1,0:T(8,128)(2,1)}), bf16[4,512,256]{2,1,0:T(8,128)(2,1)S(1)}, u32[]{:S(2)}, u32[]{:S(2)}) %all-to-all-start.3) | async-done | bytes 1048608 | tf_op jit(solution)/shard_map/all_to_all | solution.py:54
  159.6 3.1 %collective-permute-start.31 = (f32[256,256]{1,0:T(8,128)S(1)}, f32[256,256]{1,0:T(8,128)S(1)}, u32[]{:S(2)}, u32[]{:S(2)}) collective-permute-start(f32[256,256]{1,0:T(8,128)S(1)} %add.469), channel_id=1, source_target_pairs={{0,2},{1,3},{2,0},{3,1},{4,6},{5,7},{6,4},{7,5},{8,10},{9,11},{10,... | collective-permute-start | bytes 786440 | tf_op jit(solution)/shard_map/ppermute | solution.py:61
  162.6 7.0 %backward.5 = (f32[512,1024]{1,0:T(8,128)S(1)}, bf16[512,1024]{1,0:T(8,128)(2,1)S(1)}) custom-call(s32[8]{0:T(128)S(1)} %stack.179.spots_ref, bf16[4,2048,128]{2,1,0:T(8,128)(2,1)} %collective-permute-done.20.refs_0_, bf16[4,2048,128]{2,1,0:T(8,128)(2,1)} %collective-permute-done.21.refs_1_, bf16[512,8192]{1,0:T(8,128)(2,1)} %refs_9_.5, ...), custom_call_target="tpu_custom_call" | custom-call | flops 268435456 | bytes 524288 | tf_op jit(solution)/shard_map/backward/pallas_call | solution.py:237
  171.2 1.3 collective-permute-start.27
  172.5 1.3 collective-permute-start.26
  173.8 1.6 collective-permute-start.25
  175.5 4.1 %collective-permute-start.32 = (f32[256,256]{1,0:T(8,128)S(1)}, f32[256,256]{1,0:T(8,128)S(1)}, u32[]{:S(2)}, u32[]{:S(2)}) collective-permute-start(f32[256,256]{1,0:T(8,128)S(1)} %add.470), channel_id=1, source_target_pairs={{0,4},{1,5},{2,6},{3,7},{4,0},{5,1},{6,2},{7,3},{8,12},{9,13},{10,... | collective-permute-start | bytes 786440 | tf_op jit(solution)/shard_map/ppermute | solution.py:62
  180.5 8.3 %collective-permute-done.26 = bf16[512,256]{1,0:T(8,128)(2,1)S(1)} collective-permute-done((bf16[512,256]{1,0:T(8,128)(2,1)S(1)}, bf16[512,256]{1,0:T(8,128)(2,1)S(1)}, u32[]{:S(2)}, u32[]{:S(2)}) %collective-permute-start.26) | collective-permute-done | bytes 262176 | tf_op jit(solution)/shard_map/ppermute | solution.py:285
  189.0 1.4 add_convert_fusion.1
  191.2 1.4 add_convert_fusion
  (118 shorter events, 20.8 us)
Async XLA Ops:
  0.6 9.5 %copy-start = (f32[256,256]{1,0:T(8,128)S(1)}, f32[256,256]{1,0:T(8,128)}, u32[]{:S(2)}) copy-start(f32[256,256]{1,0:T(8,128)} %param.10) | copy-start | bytes 786436
  2.0 2.1 %collective-permute-start.1 = (bf16[1024,256]{1,0:T(8,128)(2,1)S(1)}, bf16[1024,256]{1,0:T(8,128)(2,1)}, u32[]{:S(2)}, u32[]{:S(2)}) collective-permute-start(bf16[1024,256]{1,0:T(8,128)(2,1)S(1)} %get-tuple-element.72), channel_id=1, source_target_pairs={{0,1},{1,0},{2,3},{3,2},{4,5},{5,4},{6,7},{7,6},{8,9},{9,8},{10,11... | collective-permute-start | bytes 1572872 | tf_op jit(solution)/shard_map/ppermute | solution.py:312
  2.1 8.0 %copy-start.10 = (s32[16,4,2]{0,2,1:T(2,128)S(1)}, s32[16,4,2]{0,2,1:T(2,128)}, u32[]{:S(2)}) copy-start(s32[16,4,2]{0,2,1:T(2,128)} %param.14) | copy-start | bytes 1540
  2.2 8.3 %copy-start.11 = (s32[16,4,2]{0,2,1:T(2,128)S(1)}, s32[16,4,2]{0,2,1:T(2,128)}, u32[]{:S(2)}) copy-start(s32[16,4,2]{0,2,1:T(2,128)} %param.12) | copy-start | bytes 1540
  2.2 20.1 %copy-start.2 = (bf16[512,1024]{1,0:T(8,128)(2,1)S(1)}, bf16[512,1024]{1,0:T(8,128)(2,1)}, u32[]{:S(2)}) copy-start(bf16[512,1024]{1,0:T(8,128)(2,1)} %param.8) | copy-start | bytes 3145732
  5.2 17.4 %collective-permute-start.3 = (bf16[2048,128]{1,0:T(8,128)(2,1)S(1)}, bf16[2048,128]{1,0:T(8,128)(2,1)S(1)}, u32[]{:S(2)}, u32[]{:S(2)}) collective-permute-start(bf16[2048,128]{1,0:T(8,128)(2,1)S(1)} %get-tuple-element.37), channel_id=1, source_target_pairs={{0,32},{1,9},{2,34},{3,11},{4,36},{5,13},{6,38},{7,15},{8,40},{9,1... | collective-permute-start | bytes 1572872 | tf_op jit(solution)/shard_map/ppermute | solution.py:43
  6.8 27.2 %collective-permute-start.2 = (bf16[2048,128]{1,0:T(8,128)(2,1)S(1)}, bf16[2048,128]{1,0:T(8,128)(2,1)S(1)}, u32[]{:S(2)}, u32[]{:S(2)}) collective-permute-start(bf16[2048,128]{1,0:T(8,128)(2,1)S(1)} %get-tuple-element.37), channel_id=1, source_target_pairs={{0,96},{1,25},{2,98},{3,27},{4,100},{5,29},{6,102},{7,31},{8,104},... | collective-permute-start | bytes 1572872 | tf_op jit(solution)/shard_map/ppermute | solution.py:43
  7.3 19.0 %collective-permute-start.7 = (bf16[2048,128]{1,0:T(8,128)(2,1)S(1)}, bf16[2048,128]{1,0:T(8,128)(2,1)}, u32[]{:S(2)}, u32[]{:S(2)}) collective-permute-start(bf16[2048,128]{1,0:T(8,128)(2,1)S(1)} %get-tuple-element.38), channel_id=1, source_target_pairs={{0,32},{1,9},{2,34},{3,11},{4,36},{5,13},{6,38},{7,15},{8,40},{9,1... | collective-permute-start | bytes 1572872 | tf_op jit(solution)/shard_map/ppermute | solution.py:43
  8.8 12.9 %collective-permute-start.5 = (bf16[2048,128]{1,0:T(8,128)(2,1)S(1)}, bf16[2048,128]{1,0:T(8,128)(2,1)}, u32[]{:S(2)}, u32[]{:S(2)}) collective-permute-start(bf16[2048,128]{1,0:T(8,128)(2,1)S(1)} %get-tuple-element.38), channel_id=1, source_target_pairs={{0,96},{1,25},{2,98},{3,27},{4,100},{5,29},{6,102},{7,31},{8,104},... | collective-permute-start | bytes 1572872 | tf_op jit(solution)/shard_map/ppermute | solution.py:43
  10.5 20.6 %copy-start.8 = (bf16[4,2,8,256]{3,2,0,1:T(8,128)(2,1)}, bf16[4,2,8,256]{3,2,0,1:T(8,128)(2,1)S(1)}, u32[]{:S(2)}) copy-start(bf16[4,2,8,256]{3,2,0,1:T(8,128)(2,1)S(1)} %copy.45) | copy-start | bytes 98308
  10.8 20.3 %copy-start.4 = (bf16[4,2,8,256]{3,2,0,1:T(8,128)(2,1)}, bf16[4,2,8,256]{3,2,0,1:T(8,128)(2,1)S(1)}, u32[]{:S(2)}) copy-start(bf16[4,2,8,256]{3,2,0,1:T(8,128)(2,1)S(1)} %copy.44) | copy-start | bytes 98308
  21.7 9.4 %collective-permute-start.6 = (bf16[2048,128]{1,0:T(8,128)(2,1)}, bf16[2048,128]{1,0:T(8,128)(2,1)S(1)}, u32[]{:S(2)}, u32[]{:S(2)}) collective-permute-start(bf16[2048,128]{1,0:T(8,128)(2,1)} %collective-permute-done.5), channel_id=1, source_target_pairs={{0,96},{1,25},{2,98},{3,27},{4,100},{5,29},{6,102},{7,31},{8,104},... | collective-permute-start | bytes 1572872 | tf_op jit(solution)/shard_map/ppermute | solution.py:43
  22.6 11.4 %collective-permute-start.4 = (bf16[2048,128]{1,0:T(8,128)(2,1)S(1)}, bf16[2048,128]{1,0:T(8,128)(2,1)S(1)}, u32[]{:S(2)}, u32[]{:S(2)}) collective-permute-start(bf16[2048,128]{1,0:T(8,128)(2,1)S(1)} %collective-permute-done.3), channel_id=1, source_target_pairs={{0,32},{1,9},{2,34},{3,11},{4,36},{5,13},{6,38},{7,15},{8,40},{9,1... | collective-permute-start | bytes 1572872 | tf_op jit(solution)/shard_map/ppermute | solution.py:43
  33.9 42.2 %collective-permute-start.9 = (bf16[4,2048,128]{2,1,0:T(8,128)(2,1)}, bf16[4,2048,128]{2,1,0:T(8,128)(2,1)}, u32[]{:S(2)}, u32[]{:S(2)}) collective-permute-start(bf16[4,2048,128]{2,1,0:T(8,128)(2,1)} %pad_maximum_fusion.1.refs_1_), channel_id=1, source_target_pairs={{0,24},{1,97},{2,26},{3,99},{4,28},{5,101},{6,30},{7,103},{8,0},{9... | collective-permute-start | bytes 6291464 | tf_op jit(solution)/shard_map/ppermute | solution.py:43
  35.6 40.5 %collective-permute-start.8 = (bf16[4,2048,128]{2,1,0:T(8,128)(2,1)}, bf16[4,2048,128]{2,1,0:T(8,128)(2,1)}, u32[]{:S(2)}, u32[]{:S(2)}) collective-permute-start(bf16[4,2048,128]{2,1,0:T(8,128)(2,1)} %pad_maximum_fusion.refs_0_), channel_id=1, source_target_pairs={{0,8},{1,33},{2,10},{3,35},{4,12},{5,37},{6,14},{7,39},{8,16},{9,4... | collective-permute-start | bytes 6291464 | tf_op jit(solution)/shard_map/ppermute | solution.py:43
  37.5 2.8 %collective-permute-start = (bf16[512,1024]{1,0:T(8,128)(2,1)S(1)}, bf16[512,1024]{1,0:T(8,128)(2,1)}, u32[]{:S(2)}, u32[]{:S(2)}) collective-permute-start(bf16[512,1024]{1,0:T(8,128)(2,1)S(1)} %copy-done.2), channel_id=1, source_target_pairs={{0,1},{1,0},{2,3},{3,2},{4,5},{5,4},{6,7},{7,6},{8,9},{9,8},{10,11... | collective-permute-start | bytes 3145736 | tf_op jit(solution)/shard_map/ppermute | solution.py:332
  37.5 57.3 %collective-permute-start.14 = (bf16[4,2048,128]{2,1,0:T(8,128)(2,1)}, bf16[4,2048,128]{2,1,0:T(8,128)(2,1)}, u32[]{:S(2)}, u32[]{:S(2)}) collective-permute-start(bf16[4,2048,128]{2,1,0:T(8,128)(2,1)} %pad_maximum_fusion.1.refs_1_), channel_id=1, source_target_pairs={{0,8},{1,33},{2,10},{3,35},{4,12},{5,37},{6,14},{7,39},{8,16},{9,4... | collective-permute-start | bytes 6291464 | tf_op jit(solution)/shard_map/ppermute | solution.py:43
  39.4 55.4 %collective-permute-start.13 = (bf16[4,2048,128]{2,1,0:T(8,128)(2,1)}, bf16[4,2048,128]{2,1,0:T(8,128)(2,1)}, u32[]{:S(2)}, u32[]{:S(2)}) collective-permute-start(bf16[4,2048,128]{2,1,0:T(8,128)(2,1)} %pad_maximum_fusion.refs_0_), channel_id=1, source_target_pairs={{0,24},{1,97},{2,26},{3,99},{4,28},{5,101},{6,30},{7,103},{8,0},{9... | collective-permute-start | bytes 6291464 | tf_op jit(solution)/shard_map/ppermute | solution.py:43
  40.3 11.2 %collective-permute-start.10 = (f32[32,512]{1,0:T(8,128)}, f32[32,512]{1,0:T(8,128)}, u32[]{:S(2)}, u32[]{:S(2)}) collective-permute-start(f32[32,512]{1,0:T(8,128)} %pad_maximum_fusion.4), channel_id=1, source_target_pairs={{0,1},{1,0},{2,3},{3,2},{4,5},{5,4},{6,7},{7,6},{8,9},{9,8},{10,11... | collective-permute-start | bytes 196616 | tf_op jit(solution)/shard_map/ppermute | solution.py:60
  46.8 37.3 %all-to-all-start = ((bf16[4,512,256]{2,1,0:T(8,128)(2,1)}), bf16[4,512,256]{2,1,0:T(8,128)(2,1)S(1)}, u32[]{:S(2)}, u32[]{:S(2)}) async-start(bf16[4,512,256]{2,1,0:T(8,128)(2,1)} %forward.4), calls=%async_computation | async-start | bytes 2097152 | tf_op jit(solution)/shard_map/all_to_all | solution.py:54
  52.4 13.5 %collective-permute-start.11 = (f32[32,512]{1,0:T(8,128)S(1)}, f32[32,512]{1,0:T(8,128)S(1)}, u32[]{:S(2)}, u32[]{:S(2)}) collective-permute-start(f32[32,512]{1,0:T(8,128)S(1)} %add.403), channel_id=1, source_target_pairs={{0,2},{1,3},{2,0},{3,1},{4,6},{5,7},{6,4},{7,5},{8,10},{9,11},{10,... | collective-permute-start | bytes 196616 | tf_op jit(solution)/shard_map/ppermute | solution.py:61
  66.5 8.1 %collective-permute-start.12 = (f32[32,512]{1,0:T(8,128)}, f32[32,512]{1,0:T(8,128)}, u32[]{:S(2)}, u32[]{:S(2)}) collective-permute-start(f32[32,512]{1,0:T(8,128)} %add.404), channel_id=1, source_target_pairs={{0,4},{1,5},{2,6},{3,7},{4,0},{5,1},{6,2},{7,3},{8,12},{9,13},{10,... | collective-permute-start | bytes 196616 | tf_op jit(solution)/shard_map/ppermute | solution.py:62
  76.1 68.2 %collective-permute-start.20 = (bf16[4,2048,128]{2,1,0:T(8,128)(2,1)}, bf16[4,2048,128]{2,1,0:T(8,128)(2,1)}, u32[]{:S(2)}, u32[]{:S(2)}) collective-permute-start(bf16[4,2048,128]{2,1,0:T(8,128)(2,1)} %collective-permute-done.8.refs_0_), channel_id=1, source_target_pairs={{0,8},{1,33},{2,10},{3,35},{4,12},{5,37},{6,14},{7,39},{8,16},{9,4... | collective-permute-start | bytes 6291464 | tf_op jit(solution)/shard_map/ppermute | solution.py:43
  78.2 66.0 %collective-permute-start.21 = (bf16[4,2048,128]{2,1,0:T(8,128)(2,1)}, bf16[4,2048,128]{2,1,0:T(8,128)(2,1)}, u32[]{:S(2)}, u32[]{:S(2)}) collective-permute-start(bf16[4,2048,128]{2,1,0:T(8,128)(2,1)} %collective-permute-done.9.refs_1_), channel_id=1, source_target_pairs={{0,24},{1,97},{2,26},{3,99},{4,28},{5,101},{6,30},{7,103},{8,0},{9... | collective-permute-start | bytes 6291464 | tf_op jit(solution)/shard_map/ppermute | solution.py:43
  84.1 18.4 %all-to-all-start.1 = ((bf16[4,512,256]{2,1,0:T(8,128)(2,1)}), bf16[4,512,256]{2,1,0:T(8,128)(2,1)}, u32[]{:S(2)}, u32[]{:S(2)}) async-start(bf16[4,512,256]{2,1,0:T(8,128)(2,1)} %forward.5), calls=%async_computation.1 | async-start | bytes 2097152 | tf_op jit(solution)/shard_map/all_to_all | solution.py:54
  102.5 27.7 %all-to-all-start.2 = ((bf16[4,512,256]{2,1,0:T(8,128)(2,1)}), bf16[4,512,256]{2,1,0:T(8,128)(2,1)}, u32[]{:S(2)}, u32[]{:S(2)}) async-start(bf16[4,512,256]{2,1,0:T(8,128)(2,1)} %forward.6), calls=%async_computation.2 | async-start | bytes 2097152 | tf_op jit(solution)/shard_map/all_to_all | solution.py:54
  108.7 16.7 %collective-permute-start.17 = (f32[32,1024]{1,0:T(8,128)}, f32[32,1024]{1,0:T(8,128)}, u32[]{:S(2)}, u32[]{:S(2)}) collective-permute-start(f32[32,1024]{1,0:T(8,128)} %maximum_multiply_fusion), channel_id=1, source_target_pairs={{0,96},{1,97},{2,98},{3,99},{4,100},{5,101},{6,102},{7,103},{8,104... | collective-permute-start | bytes 393224 | tf_op jit(solution)/shard_map/ppermute | solution.py:72
  111.8 13.7 %collective-permute-start.16 = (f32[32,1024]{1,0:T(8,128)}, f32[32,1024]{1,0:T(8,128)}, u32[]{:S(2)}, u32[]{:S(2)}) collective-permute-start(f32[32,1024]{1,0:T(8,128)} %maximum_multiply_fusion), channel_id=1, source_target_pairs={{0,64},{1,65},{2,66},{3,67},{4,68},{5,69},{6,70},{7,71},{8,72},{9,... | collective-permute-start | bytes 393224 | tf_op jit(solution)/shard_map/ppermute | solution.py:72
  112.4 13.1 %collective-permute-start.15 = (f32[32,1024]{1,0:T(8,128)}, f32[32,1024]{1,0:T(8,128)}, u32[]{:S(2)}, u32[]{:S(2)}) collective-permute-start(f32[32,1024]{1,0:T(8,128)} %maximum_multiply_fusion), channel_id=1, source_target_pairs={{0,32},{1,33},{2,34},{3,35},{4,36},{5,37},{6,38},{7,39},{8,40},{9,... | collective-permute-start | bytes 393224 | tf_op jit(solution)/shard_map/ppermute | solution.py:72
  114.8 10.7 %copy-start.3 = (f32[32,1024]{1,0:T(8,128)S(1)}, f32[32,1024]{1,0:T(8,128)}, u32[]{:S(2)}) copy-start(f32[32,1024]{1,0:T(8,128)} %maximum_multiply_fusion) | copy-start | bytes 393220
  127.2 6.2 %collective-permute-start.19 = (f32[32,1024]{1,0:T(8,128)}, f32[32,1024]{1,0:T(8,128)}, u32[]{:S(2)}, u32[]{:S(2)}) collective-permute-start(f32[32,1024]{1,0:T(8,128)} %add_add_fusion), channel_id=1, source_target_pairs={{0,8},{8,0},{16,24},{24,16},{32,40},{40,32},{48,56},{56,48},{64,72... | collective-permute-start | bytes 393224 | tf_op jit(solution)/shard_map/ppermute | solution.py:82
  135.1 17.8 %collective-permute-start.28 = (f32[32,1024]{1,0:T(8,128)}, f32[32,1024]{1,0:T(8,128)}, u32[]{:S(2)}, u32[]{:S(2)}) collective-permute-start(f32[32,1024]{1,0:T(8,128)} %add.442), channel_id=1, source_target_pairs={{0,16},{8,24},{16,0},{24,8},{32,48},{40,56},{48,32},{56,40},{64,80... | collective-permute-start | bytes 393224 | tf_op jit(solution)/shard_map/ppermute | solution.py:82
  139.5 19.1 %all-to-all-start.3 = ((bf16[4,512,256]{2,1,0:T(8,128)(2,1)}), bf16[4,512,256]{2,1,0:T(8,128)(2,1)S(1)}, u32[]{:S(2)}, u32[]{:S(2)}) async-start(bf16[4,512,256]{2,1,0:T(8,128)(2,1)} %arrange.1), calls=%async_computation.3 | async-start | bytes 2097152 | tf_op jit(solution)/shard_map/all_to_all | solution.py:54
  149.3 9.3 %copy-start.1 = (bf16[4,512,256]{2,1,0:T(8,128)(2,1)S(1)}, bf16[4,512,256]{2,1,0:T(8,128)(2,1)}, u32[]{:S(2)}) copy-start(bf16[4,512,256]{2,1,0:T(8,128)(2,1)} %arrange.1) | copy-start | bytes 3145732
  149.3 20.3 %collective-permute-start.22 = (bf16[512,256]{1,0:T(8,128)(2,1)}, bf16[512,256]{1,0:T(8,128)(2,1)}, u32[]{:S(2)}, u32[]{:S(2)}) collective-permute-start(bf16[512,256]{1,0:T(8,128)(2,1)} %get-tuple-element.62), channel_id=1, source_target_pairs={{0,4},{1,5},{2,6},{3,7},{4,0},{5,1},{6,2},{7,3},{8,12},{9,13},{10,... | collective-permute-start | bytes 786440 | tf_op jit(solution)/shard_map/ppermute | solution.py:389
  150.8 19.1 %collective-permute-start.23 = (bf16[512,256]{1,0:T(8,128)(2,1)}, bf16[512,256]{1,0:T(8,128)(2,1)}, u32[]{:S(2)}, u32[]{:S(2)}) collective-permute-start(bf16[512,256]{1,0:T(8,128)(2,1)} %get-tuple-element.63), channel_id=1, source_target_pairs={{0,2},{1,3},{2,4},{3,5},{4,6},{5,7},{6,0},{7,1},{8,10},{9,11},{10,... | collective-permute-start | bytes 786440 | tf_op jit(solution)/shard_map/ppermute | solution.py:389
  152.9 17.0 %collective-permute-start.24 = (bf16[512,256]{1,0:T(8,128)(2,1)}, bf16[512,256]{1,0:T(8,128)(2,1)}, u32[]{:S(2)}, u32[]{:S(2)}) collective-permute-start(bf16[512,256]{1,0:T(8,128)(2,1)} %get-tuple-element.64), channel_id=1, source_target_pairs={{0,6},{1,7},{2,0},{3,1},{4,2},{5,3},{6,4},{7,5},{8,14},{9,15},{10,... | collective-permute-start | bytes 786440 | tf_op jit(solution)/shard_map/ppermute | solution.py:389
  154.8 4.8 %collective-permute-start.30 = (f32[256,256]{1,0:T(8,128)S(1)}, f32[256,256]{1,0:T(8,128)S(1)}, u32[]{:S(2)}, u32[]{:S(2)}) collective-permute-start(f32[256,256]{1,0:T(8,128)S(1)} %fusion.2), channel_id=1, source_target_pairs={{0,1},{1,0},{2,3},{3,2},{4,5},{5,4},{6,7},{7,6},{8,9},{9,8},{10,11... | collective-permute-start | bytes 786440 | tf_op jit(solution)/shard_map/ppermute | solution.py:60
  158.6 16.8 %collective-permute-start.18 = (bf16[2,512,256]{2,1,0:T(8,128)(2,1)S(1)}, bf16[2,512,256]{2,1,0:T(8,128)(2,1)S(1)}, u32[]{:S(2)}, u32[]{:S(2)}) collective-permute-start(bf16[2,512,256]{2,1,0:T(8,128)(2,1)S(1)} %slice_select_fusion.1), channel_id=1, source_target_pairs={{0,1},{1,0},{2,3},{3,2},{4,5},{5,4},{6,7},{7,6},{8,9},{9,8},{10,11... | collective-permute-start | bytes 1572872 | tf_op jit(solution)/shard_map/ppermute | solution.py:399
  159.6 10.4 %copy-start.6 = (bf16[512,256]{1,0:T(8,128)(2,1)S(1)}, bf16[512,256]{1,0:T(8,128)(2,1)}, u32[]{:S(2)}) copy-start(bf16[512,256]{1,0:T(8,128)(2,1)} %get-tuple-element.61) | copy-start | bytes 786436
  159.6 14.2 %collective-permute-start.31 = (f32[256,256]{1,0:T(8,128)S(1)}, f32[256,256]{1,0:T(8,128)S(1)}, u32[]{:S(2)}, u32[]{:S(2)}) collective-permute-start(f32[256,256]{1,0:T(8,128)S(1)} %add.469), channel_id=1, source_target_pairs={{0,2},{1,3},{2,0},{3,1},{4,6},{5,7},{6,4},{7,5},{8,10},{9,11},{10,... | collective-permute-start | bytes 786440 | tf_op jit(solution)/shard_map/ppermute | solution.py:61
  169.6 21.5 %collective-permute-start.29 = (bf16[512,1024]{1,0:T(8,128)(2,1)S(1)}, bf16[512,1024]{1,0:T(8,128)(2,1)S(1)}, u32[]{:S(2)}, u32[]{:S(2)}) collective-permute-start(bf16[512,1024]{1,0:T(8,128)(2,1)S(1)} %get-tuple-element.68), channel_id=1, source_target_pairs={{0,1},{1,0},{2,3},{3,2},{4,5},{5,4},{6,7},{7,6},{8,9},{9,8},{10,11... | collective-permute-start | bytes 3145736 | tf_op jit(solution)/shard_map/ppermute | solution.py:413
  171.2 9.3 %collective-permute-start.27 = (bf16[512,256]{1,0:T(8,128)(2,1)S(1)}, bf16[512,256]{1,0:T(8,128)(2,1)S(1)}, u32[]{:S(2)}, u32[]{:S(2)}) collective-permute-start(bf16[512,256]{1,0:T(8,128)(2,1)S(1)} %add_convert_fusion.2), channel_id=1, source_target_pairs={{3,4},{7,5},{11,12},{15,13},{19,20},{23,21},{27,28},{31,29},{35,38... | collective-permute-start | bytes 786440 | tf_op jit(solution)/shard_map/ppermute | solution.py:285
  172.5 16.3 %collective-permute-start.26 = (bf16[512,256]{1,0:T(8,128)(2,1)S(1)}, bf16[512,256]{1,0:T(8,128)(2,1)S(1)}, u32[]{:S(2)}, u32[]{:S(2)}) collective-permute-start(bf16[512,256]{1,0:T(8,128)(2,1)S(1)} %add_convert_fusion.2), channel_id=1, source_target_pairs={{1,4},{5,5},{9,12},{13,13},{17,20},{21,21},{25,28},{29,29},{33,38}... | collective-permute-start | bytes 786440 | tf_op jit(solution)/shard_map/ppermute | solution.py:285
  173.8 15.1 %collective-permute-start.25 = (bf16[512,256]{1,0:T(8,128)(2,1)S(1)}, bf16[512,256]{1,0:T(8,128)(2,1)S(1)}, u32[]{:S(2)}, u32[]{:S(2)}) collective-permute-start(bf16[512,256]{1,0:T(8,128)(2,1)S(1)} %add_convert_fusion.2), channel_id=1, source_target_pairs={{0,1},{2,3},{4,5},{6,7},{8,9},{10,11},{12,13},{14,15},{32,33},{34,... | collective-permute-start | bytes 786440 | tf_op jit(solution)/shard_map/ppermute | solution.py:290
  175.5 15.0 %collective-permute-start.32 = (f32[256,256]{1,0:T(8,128)S(1)}, f32[256,256]{1,0:T(8,128)S(1)}, u32[]{:S(2)}, u32[]{:S(2)}) collective-permute-start(f32[256,256]{1,0:T(8,128)S(1)} %add.470), channel_id=1, source_target_pairs={{0,4},{1,5},{2,6},{3,7},{4,0},{5,1},{6,2},{7,3},{8,12},{9,13},{10,... | collective-permute-start | bytes 786440 | tf_op jit(solution)/shard_map/ppermute | solution.py:62
  179.6 9.3 %copy-start.7 = (bf16[32,512]{1,0:T(8,128)(2,1)S(1)}, bf16[32,512]{1,0:T(8,128)(2,1)}, u32[]{:S(2)}) copy-start(bf16[32,512]{1,0:T(8,128)(2,1)} %add_convert_fusion.3) | copy-start | bytes 98308
  179.6 9.3 %copy-start.9 = (bf16[4,2,8,256]{3,2,0,1:T(8,128)(2,1)S(1)}, bf16[4,2,8,256]{3,2,0,1:T(8,128)(2,1)}, u32[]{:S(2)}) copy-start(bf16[4,2,8,256]{3,2,0,1:T(8,128)(2,1)} %copy-done.8) | copy-start | bytes 98308
  (5 other events, 23.6 us)

commit v9 on v8

--- a/solution.py
+++ b/solution.py
@@ -56,10 +56,10 @@
     )
 
 
-def over_tensor(value):
-    value = value + lax.ppermute(value, "tensor", SWAP)
-    value = value + lax.ppermute(value, "tensor", [(t, t ^ 2) for t in range(8)])
-    return value + lax.ppermute(value, "tensor", [(t, t ^ 4) for t in range(8)])
+def over_tensor(value, bits=(1, 2, 4)):
+    for bit in bits:
+        value = value + lax.ppermute(value, "tensor", [(t, t ^ bit) for t in range(8)])
+    return value
 
 
 def over_side(value, axis):
@@ -197,11 +197,11 @@
         cols, weights, (((1,), (1,)), ((), ())), preferred_element_type=jnp.float32
     )
     if first:
-        refs[-1][...] = product
+        refs[-1][...] = product.astype(jnp.bfloat16)
     elif not last:
-        refs[-1][...] = refs[-2][...] + product
+        refs[-1][...] = (refs[-2][...].astype(jnp.float32) + product).astype(jnp.bfloat16)
     else:
-        total = refs[-3][...] + product
+        total = refs[-3][...].astype(jnp.float32) + product
 
         @pl.when(pl.program_id(0) < 2)
         def _():
@@ -224,7 +224,7 @@
         return pl.BlockSpec((tokens, part), lambda i, n: (0, n[j]))
 
     total = pl.BlockSpec((tokens, block), lambda i, n: (0, (i + 2) % 4))
-    outs, specs = [pltpu.HBM((tokens, depth), jnp.float32)], [total]
+    outs, specs = [pltpu.HBM((tokens, depth), jnp.bfloat16)], [total]
     if last:
         outs = [
             jax.ShapeDtypeStruct((tokens, depth // 2), jnp.float32),
@@ -356,6 +356,8 @@
     across = [(2, 0), (2, 1)]
 
     sent_here = forward(turned, wide, lines)
+    sent_here, totals = lax.optimization_barrier((sent_here, totals))
+    low_bf, back_bf = totals[:rank], totals[rank:]
     slots_here = exchange(sent_here, "tensor", LANES)
     grown = backward(after(spots_of(here), sent_here), None, out_grad, lines)
     below[0], above[1], grown, totals = lax.optimization_barrier(
@@ -391,11 +393,11 @@
     both = with_partner(both, 2, *sent)
     bank_a, logit_grad_a = compose_back(both[:rank], weights_a, picked_a, mixing_a, vector_bank)
     bank_b, logit_grad_b = compose_back(both[rank:], weights_b, picked_b, mixing_b, vector_bank)
-    bank_part = bank_a + bank_b
+    bank_part = over_tensor(bank_a + bank_b, (1, 2))
     grown, other = backward(
         after(spots_of(across), *sent, bank_part), grown, out_grad, take(across), last=True
     )
-    bank_grad = over_tensor(bank_part)
+    bank_grad = over_tensor(bank_part, (4,))
     crossed = lax.ppermute(jnp.where(core == 0, slots[2:], moved[:2]), "tensor", SWAP)
     firsts = jnp.where(core == 0, slots[:2], crossed)
     seconds = jnp.where(core == 0, crossed, moved[2:])

time: 194 us -> 181 us (0.933)
  the two profiles are of different devices: /device:TPU:58 before, /device:TPU:1 now
where the time goes in v9:
time: 181 us; the launch traced here: 180 us
  starting transfers between devices  68.4 us (38%)
  Pallas kernels  45.6 us (25%)
  waiting for transfers between devices  33.7 us (19%)
  other arithmetic  16.4 us (9%)
  matrix products  9.9 us (5%)
  local copies, waits for them, and re-layouts  4.86 us (3%)
    pallas_call x3, Pallas kernels, backward(): pl.pallas_call(functools.partial(backward_kernel, count, first, last), ou...  23.2 us
    pallas_call x4, Pallas kernels, forward(): pl.pallas_call(functools.partial(forward_kernel, count, many), out_shape=...  19.8 us
    ppermute x12, starting transfers between devices, shift(): return lax.ppermute(value, BOTH, ring(stage, step))  19.1 us
    all_to_all x4, starting transfers between devices, exchange(): lax.all_to_all(value, axis, split_axis=0, concat_axis=0, tiled=True, axis...  16.4 us
    ppermute x12, waiting for transfers between devices, shift(): return lax.ppermute(value, BOTH, ring(stage, step))  12.4 us
    ppermute x6, starting transfers between devices, over_tensor(): lax.ppermute(value, 'tensor', [(t, t ^ bit) for t in range(8)])  7.54 us
    ppermute x3, waiting for transfers between devices, local(): arrived.append(lax.ppermute(sent[step], 'tensor', turns))  6.43 us
    ppermute x2, starting transfers between devices, from_second(): return lax.ppermute(piece, BOTH, pairs(move))  6.14 us
  transfers between devices with their start and end apart: 37, of which 10 were waited for; matrix products, arithmetic and copies ran while one was open for 14% of the time, Pallas kernels for 25%

profile of v9, /device:TPU:1, one launch (start us, length us, event | category | flops | bytes accessed | tf_op | source)
XLA Modules:
  0.0 180.4 jit_solution(10509441189147780218)
XLA Ops:
  2.0 1.5 collective-permute-start.1
  3.5 1.6 collective-permute-done.1
  6.3 1.8 collective-permute-start.3
  8.1 2.2 %collective-permute-start.2 = (bf16[2048,128]{1,0:T(8,128)(2,1)S(1)}, bf16[2048,128]{1,0:T(8,128)(2,1)S(1)}, u32[]{:S(2)}, u32[]{:S(2)}) collective-permute-start(bf16[2048,128]{1,0:T(8,128)(2,1)S(1)} %get-tuple-element.39), channel_id=1, source_target_pairs={{0,96},{1,25},{2,98},{3,27},{4,100},{5,29},{6,102},{7,31},{8,104},... | collective-permute-start | bytes 1572872 | tf_op jit(solution)/shard_map/ppermute | solution.py:43
  10.3 2.7 %collective-permute-start.5 = (bf16[2048,128]{1,0:T(8,128)(2,1)S(1)}, bf16[2048,128]{1,0:T(8,128)(2,1)}, u32[]{:S(2)}, u32[]{:S(2)}) collective-permute-start(bf16[2048,128]{1,0:T(8,128)(2,1)S(1)} %get-tuple-element.40), channel_id=1, source_target_pairs={{0,96},{1,25},{2,98},{3,27},{4,100},{5,29},{6,102},{7,31},{8,104},... | collective-permute-start | bytes 1572872 | tf_op jit(solution)/shard_map/ppermute | solution.py:43
  14.5 7.9 %collective-permute-done.5 = bf16[2048,128]{1,0:T(8,128)(2,1)} collective-permute-done((bf16[2048,128]{1,0:T(8,128)(2,1)S(1)}, bf16[2048,128]{1,0:T(8,128)(2,1)}, u32[]{:S(2)}, u32[]{:S(2)}) %collective-permute-start.5) | collective-permute-done | bytes 524320 | tf_op jit(solution)/shard_map/ppermute | solution.py:43
  22.3 3.2 %collective-permute-start.6 = (bf16[2048,128]{1,0:T(8,128)(2,1)}, bf16[2048,128]{1,0:T(8,128)(2,1)S(1)}, u32[]{:S(2)}, u32[]{:S(2)}) collective-permute-start(bf16[2048,128]{1,0:T(8,128)(2,1)} %collective-permute-done.5), channel_id=1, source_target_pairs={{0,96},{1,25},{2,98},{3,27},{4,100},{5,29},{6,102},{7,31},{8,104},... | collective-permute-start | bytes 1572872 | tf_op jit(solution)/shard_map/ppermute | solution.py:43
  25.9 1.6 fusion.11
  27.6 4.4 %collective-permute-done.6 = bf16[2048,128]{1,0:T(8,128)(2,1)S(1)} collective-permute-done((bf16[2048,128]{1,0:T(8,128)(2,1)}, bf16[2048,128]{1,0:T(8,128)(2,1)S(1)}, u32[]{:S(2)}, u32[]{:S(2)}) %collective-permute-start.6) | collective-permute-done | bytes 524320 | tf_op jit(solution)/shard_map/ppermute | solution.py:43
  32.0 2.8 %pad_maximum_fusion.1.refs_1_ = bf16[4,2048,128]{2,1,0:T(8,128)(2,1)} fusion(bf16[1,2048,128]{2,1,0:T(8,128)(2,1)} %bitcast.9, bf16[1,2048,128]{2,1,0:T(8,128)(2,1)S(1)} %bitcast.111, bf16[1,2048,128]{2,1,0:T(8,128)(2,1)} %bitcast.7, bf16[1,2048,128]{2,1,0:T(8,128)(2,1)S(1)} %bitcast.103), kind=kLoop, calls=%fused_computation.3 | loop fusion | flops 3145728 | bytes 4194304 | tf_op jit(solution)/shard_map/stack | solution.py:318
  34.8 2.5 %collective-permute-start.12 = (bf16[4,2048,128]{2,1,0:T(8,128)(2,1)}, bf16[4,2048,128]{2,1,0:T(8,128)(2,1)}, u32[]{:S(2)}, u32[]{:S(2)}) collective-permute-start(bf16[4,2048,128]{2,1,0:T(8,128)(2,1)} %pad_maximum_fusion.1.refs_1_), channel_id=1, source_target_pairs={{0,24},{1,97},{2,26},{3,99},{4,28},{5,101},{6,30},{7,103},{8,0},{9... | collective-permute-start | bytes 6291464 | tf_op jit(solution)/shard_map/ppermute | solution.py:43
  37.2 1.6 pad_maximum_fusion.refs_0_
  38.8 2.8 %collective-permute-start = (bf16[512,1024]{1,0:T(8,128)(2,1)S(1)}, bf16[512,1024]{1,0:T(8,128)(2,1)}, u32[]{:S(2)}, u32[]{:S(2)}) collective-permute-start(bf16[512,1024]{1,0:T(8,128)(2,1)S(1)} %copy-done.2), channel_id=1, source_target_pairs={{0,1},{1,0},{2,3},{3,2},{4,5},{5,4},{6,7},{7,6},{8,9},{9,8},{10,11... | collective-permute-start | bytes 3145736 | tf_op jit(solution)/shard_map/ppermute | solution.py:332
  41.6 2.2 %collective-permute-done.8 = f32[32,512]{1,0:T(8,128)S(1)} collective-permute-done((f32[32,512]{1,0:T(8,128)S(1)}, f32[32,512]{1,0:T(8,128)S(1)}, u32[]{:S(2)}, u32[]{:S(2)}) %collective-permute-start.8) | collective-permute-done | bytes 65568 | tf_op jit(solution)/shard_map/ppermute | solution.py:61
  43.9 1.4 collective-permute-start.9
  45.9 1.7 collective-permute-done.9
  47.6 3.3 %collective-permute-start.13 = (bf16[4,2048,128]{2,1,0:T(8,128)(2,1)}, bf16[4,2048,128]{2,1,0:T(8,128)(2,1)}, u32[]{:S(2)}, u32[]{:S(2)}) collective-permute-start(bf16[4,2048,128]{2,1,0:T(8,128)(2,1)} %pad_maximum_fusion.refs_0_), channel_id=1, source_target_pairs={{0,24},{1,97},{2,26},{3,99},{4,28},{5,101},{6,30},{7,103},{8,0},{9... | collective-permute-start | bytes 6291464 | tf_op jit(solution)/shard_map/ppermute | solution.py:43
  51.8 3.0 %collective-permute-start.10 = (f32[32,512]{1,0:T(8,128)S(1)}, f32[32,512]{1,0:T(8,128)S(1)}, u32[]{:S(2)}, u32[]{:S(2)}) collective-permute-start(f32[32,512]{1,0:T(8,128)S(1)} %add.384), channel_id=1, source_target_pairs={{0,4},{1,5},{2,6},{3,7},{4,0},{5,1},{6,2},{7,3},{8,12},{9,13},{10,... | collective-permute-start | bytes 196616 | tf_op jit(solution)/shard_map/ppermute | solution.py:61
  56.1 5.0 %forward.4 = bf16[4,512,256]{2,1,0:T(8,128)(2,1)} custom-call(s32[1]{0:T(128)} %bitcast.1.start_ref, bf16[512,2048]{1,0:T(8,128)(2,1)S(1)} %constant_dynamic-update-slice_fusion.wide_ref, bf16[4,2048,128]{2,1,0:T(8,128)(2,1)} %pad_maximum_fusion.refs_0_, bf16[4,2048,128]{2,1,0:T(8,128)(2,1)} %pad_maximum_fusion.1.refs_1_), custom_call_target="tpu_custom_call" | custom-call | flops 268435456 | bytes 524288 | tf_op jit(solution)/shard_map/forward/pallas_call | solution.py:131
  61.7 3.5 %all-to-all-start = ((bf16[4,512,256]{2,1,0:T(8,128)(2,1)}), bf16[4,512,256]{2,1,0:T(8,128)(2,1)S(1)}, u32[]{:S(2)}, u32[]{:S(2)}) async-start(bf16[4,512,256]{2,1,0:T(8,128)(2,1)} %forward.4), calls=%async_computation | async-start | bytes 2097152 | tf_op jit(solution)/shard_map/all_to_all | solution.py:54
  65.5 6.7 %backward.3.refs_20_ = bf16[512,2048]{1,0:T(8,128)(2,1)} custom-call(s32[8]{0:T(128)S(1)} %stack.153.spots_ref, bf16[4,2048,128]{2,1,0:T(8,128)(2,1)} %pad_maximum_fusion.refs_0_, bf16[4,2048,128]{2,1,0:T(8,128)(2,1)} %pad_maximum_fusion.1.refs_1_, bf16[512,8192]{1,0:T(8,128)(2,1)} %refs_9_.5, bf16[512,8192]{1,0:T(8,128)(2,1)} %refs_9_.5, ...), custom_call_target="tpu_custom_call" | custom-call | flops 268435456 | bytes 524288 | tf_op jit(solution)/shard_map/backward/pallas_call | solution.py:237
  72.3 2.7 %collective-permute-start.21 = (bf16[4,2048,128]{2,1,0:T(8,128)(2,1)}, bf16[4,2048,128]{2,1,0:T(8,128)(2,1)}, u32[]{:S(2)}, u32[]{:S(2)}) collective-permute-start(bf16[4,2048,128]{2,1,0:T(8,128)(2,1)} %collective-permute-done.12.refs_1_), channel_id=1, source_target_pairs={{0,24},{1,97},{2,26},{3,99},{4,28},{5,101},{6,30},{7,103},{8,0},{9... | collective-permute-start | bytes 6291464 | tf_op jit(solution)/shard_map/ppermute | solution.py:43
  75.0 4.9 %forward.5 = bf16[4,512,256]{2,1,0:T(8,128)(2,1)} custom-call(s32[1]{0:T(128)} %bitcast.1.start_ref, bf16[512,2048]{1,0:T(8,128)(2,1)S(1)} %constant_dynamic-update-slice_fusion.wide_ref, bf16[4,2048,128]{2,1,0:T(8,128)(2,1)} %collective-permute-done.11.refs_0_, bf16[4,2048,128]{2,1,0:T(8,128)(2,1)} %collective-permute-done.12.refs_1_), custom_call_target="tpu_custom_call" | custom-call | flops 268435456 | bytes 524288 | tf_op jit(solution)/shard_map/forward/pallas_call | solution.py:131
  79.9 4.3 %all-to-all-start.1 = ((bf16[4,512,256]{2,1,0:T(8,128)(2,1)}), bf16[4,512,256]{2,1,0:T(8,128)(2,1)}, u32[]{:S(2)}, u32[]{:S(2)}) async-start(bf16[4,512,256]{2,1,0:T(8,128)(2,1)} %forward.5), calls=%async_computation.1 | async-start | bytes 2097152 | tf_op jit(solution)/shard_map/all_to_all | solution.py:54
  84.2 1.5 fusion.9
  85.7 1.5 fusion.32
  88.0 4.9 %forward.6 = bf16[4,512,256]{2,1,0:T(8,128)(2,1)} custom-call(s32[1]{0:T(128)} %bitcast.1.start_ref, bf16[512,2048]{1,0:T(8,128)(2,1)S(1)} %constant_dynamic-update-slice_fusion.wide_ref, bf16[4,2048,128]{2,1,0:T(8,128)(2,1)} %collective-permute-done.13.refs_0_.refs_2_, bf16[4,2048,128]{2,1,0:T(8,128)(2,1)} %collective-permute-done.14.refs_1_.refs_3_), custom_call_target="tpu_custom_call" | custom-call | flops 268435456 | bytes 524288 | tf_op jit(solution)/shard_map/forward/pallas_call | solution.py:131
  93.0 4.4 %all-to-all-done.1.refs_0_ = bf16[4,512,256]{2,1,0:T(8,128)(2,1)} async-done(((bf16[4,512,256]{2,1,0:T(8,128)(2,1)}), bf16[4,512,256]{2,1,0:T(8,128)(2,1)}, u32[]{:S(2)}, u32[]{:S(2)}) %all-to-all-start.1) | async-done | bytes 1048608 | tf_op jit(solution)/shard_map/all_to_all | solution.py:54
  97.3 4.3 %all-to-all-start.2 = ((bf16[4,512,256]{2,1,0:T(8,128)(2,1)}), bf16[4,512,256]{2,1,0:T(8,128)(2,1)}, u32[]{:S(2)}, u32[]{:S(2)}) async-start(bf16[4,512,256]{2,1,0:T(8,128)(2,1)} %forward.6), calls=%async_computation.2 | async-start | bytes 2097152 | tf_op jit(solution)/shard_map/all_to_all | solution.py:54
  101.8 1.4 collective-permute-start.15
  103.2 9.8 %backward.4.refs_10_ = bf16[512,2048]{1,0:T(8,128)(2,1)} custom-call(s32[16]{0:T(128)S(1)} %stack.170.spots_ref, bf16[4,2048,128]{2,1,0:T(8,128)(2,1)} %collective-permute-done.11.refs_0_, bf16[4,2048,128]{2,1,0:T(8,128)(2,1)} %collective-permute-done.12.refs_1_, ...), custom_call_target="tpu_custom_call", output_to_operand_aliasing={{}: (21, {})} | custom-call | flops 536870912 | bytes 1048576 | tf_op jit(solution)/shard_map/backward/pallas_call | solution.py:237
  113.1 3.0 %collective-permute-done.15 = f32[32,1024]{1,0:T(8,128)} collective-permute-done((f32[32,1024]{1,0:T(8,128)}, f32[32,1024]{1,0:T(8,128)}, u32[]{:S(2)}, u32[]{:S(2)}) %collective-permute-start.15) | collective-permute-done | bytes 131104 | tf_op jit(solution)/shard_map/ppermute | solution.py:72
  116.1 1.7 add_add_fusion
  118.1 2.6 %arrange.1 = bf16[4,512,256]{2,1,0:T(8,128)(2,1)} custom-call(s32[1]{0:T(128)} %bitcast.far_ref, bf16[4,512,256]{2,1,0:T(8,128)(2,1)S(1)} %all-to-all-done.here_ref, bf16[4,512,256]{2,1,0:T(8,128)(2,1)} %all-to-all-done.1.refs_0_, bf16[4,512,256]{2,1,0:T(8,128)(2,1)} %all-to-all-done.2.refs_1_), custom_call_target="tpu_custom_call" | custom-call | flops 2097152 | bytes 4194304 | tf_op jit(solution)/shard_map/arrange/pallas_call | solution.py:178
  120.7 1.9 %collective-permute-done.19 = f32[32,1024]{1,0:T(8,128)} collective-permute-done((f32[32,1024]{1,0:T(8,128)}, f32[32,1024]{1,0:T(8,128)}, u32[]{:S(2)}, u32[]{:S(2)}) %collective-permute-start.19) | collective-permute-done | bytes 131104 | tf_op jit(solution)/shard_map/ppermute | solution.py:82
  122.6 1.6 add.442
  124.3 3.6 %collective-permute-start.28 = (f32[32,1024]{1,0:T(8,128)}, f32[32,1024]{1,0:T(8,128)}, u32[]{:S(2)}, u32[]{:S(2)}) collective-permute-start(f32[32,1024]{1,0:T(8,128)} %add.442), channel_id=1, source_target_pairs={{0,16},{8,24},{16,0},{24,8},{32,48},{40,56},{48,32},{56,40},{64,80... | collective-permute-start | bytes 393224 | tf_op jit(solution)/shard_map/ppermute | solution.py:82
  127.9 4.3 %all-to-all-start.3 = ((bf16[4,512,256]{2,1,0:T(8,128)(2,1)}), bf16[4,512,256]{2,1,0:T(8,128)(2,1)S(1)}, u32[]{:S(2)}, u32[]{:S(2)}) async-start(bf16[4,512,256]{2,1,0:T(8,128)(2,1)} %arrange.1), calls=%async_computation.3 | async-start | bytes 2097152 | tf_op jit(solution)/shard_map/all_to_all | solution.py:54
  132.3 5.0 %forward.7 = (bf16[512,256]{1,0:T(8,128)(2,1)}, bf16[512,256]{1,0:T(8,128)(2,1)}, bf16[512,256]{1,0:T(8,128)(2,1)}, bf16[512,256]{1,0:T(8,128)(2,1)}) custom-call(s32[1]{0:T(128)} %bitcast.36.start_ref, bf16[512,2048]{1,0:T(8,128)(2,1)S(1)} %constant_dynamic-update-slice_fusion.wide_ref, bf16[4,2048,128]{2,1,0:T(8,128)(2,1)} %collective-permute-done.20.refs_0_, ...), custom_call_target="tpu_custom_call" | custom-call | flops 268435456 | bytes 524288 | tf_op jit(solution)/shard_map/forward/pallas_call | solution.py:131
  137.3 3.0 %collective-permute-start.22 = (bf16[512,256]{1,0:T(8,128)(2,1)}, bf16[512,256]{1,0:T(8,128)(2,1)}, u32[]{:S(2)}, u32[]{:S(2)}) collective-permute-start(bf16[512,256]{1,0:T(8,128)(2,1)} %get-tuple-element.66), channel_id=1, source_target_pairs={{0,4},{1,5},{2,6},{3,7},{4,0},{5,1},{6,2},{7,3},{8,12},{9,13},{10,... | collective-permute-start | bytes 786440 | tf_op jit(solution)/shard_map/ppermute | solution.py:391
  140.6 2.4 %collective-permute-start.24 = (bf16[512,256]{1,0:T(8,128)(2,1)}, bf16[512,256]{1,0:T(8,128)(2,1)}, u32[]{:S(2)}, u32[]{:S(2)}) collective-permute-start(bf16[512,256]{1,0:T(8,128)(2,1)} %get-tuple-element.68), channel_id=1, source_target_pairs={{0,6},{1,7},{2,0},{3,1},{4,2},{5,3},{6,4},{7,5},{8,14},{9,15},{10,... | collective-permute-start | bytes 786440 | tf_op jit(solution)/shard_map/ppermute | solution.py:391
  144.9 2.3 %collective-permute-start.29 = (f32[256,256]{1,0:T(8,128)S(1)}, f32[256,256]{1,0:T(8,128)}, u32[]{:S(2)}, u32[]{:S(2)}) collective-permute-start(f32[256,256]{1,0:T(8,128)S(1)} %fusion.2), channel_id=1, source_target_pairs={{0,1},{1,0},{2,3},{3,2},{4,5},{5,4},{6,7},{7,6},{8,9},{9,8},{10,11... | collective-permute-start | bytes 786440 | tf_op jit(solution)/shard_map/ppermute | solution.py:61
  148.8 1.4 collective-permute-start.18
  152.8 6.4 %collective-permute-done.23 = bf16[512,256]{1,0:T(8,128)(2,1)} collective-permute-done((bf16[512,256]{1,0:T(8,128)(2,1)}, bf16[512,256]{1,0:T(8,128)(2,1)}, u32[]{:S(2)}, u32[]{:S(2)}) %collective-permute-start.23) | collective-permute-done | bytes 262176 | tf_op jit(solution)/shard_map/ppermute | solution.py:391
  161.1 5.5 %collective-permute-start.26 = (bf16[512,256]{1,0:T(8,128)(2,1)S(1)}, bf16[512,256]{1,0:T(8,128)(2,1)S(1)}, u32[]{:S(2)}, u32[]{:S(2)}) collective-permute-start(bf16[512,256]{1,0:T(8,128)(2,1)S(1)} %add_convert_fusion.2), channel_id=1, source_target_pairs={{1,4},{5,5},{9,12},{13,13},{17,20},{21,21},{25,28},{29,29},{33,38}... | collective-permute-start | bytes 786440 | tf_op jit(solution)/shard_map/ppermute | solution.py:285
  168.0 6.6 %backward.5 = (f32[512,1024]{1,0:T(8,128)S(1)}, bf16[512,1024]{1,0:T(8,128)(2,1)S(1)}) custom-call(s32[8]{0:T(128)S(1)} %stack.179.spots_ref, bf16[4,2048,128]{2,1,0:T(8,128)(2,1)} %collective-permute-done.20.refs_0_, bf16[4,2048,128]{2,1,0:T(8,128)(2,1)} %collective-permute-done.21.refs_1_, bf16[512,8192]{1,0:T(8,128)(2,1)} %refs_9_.5, ...), custom_call_target="tpu_custom_call" | custom-call | flops 268435456 | bytes 524288 | tf_op jit(solution)/shard_map/backward/pallas_call | solution.py:237
  176.8 1.4 add_convert_fusion.1
  178.9 1.4 add_convert_fusion
  (126 shorter events, 21.8 us)
Async XLA Ops:
  0.6 13.1 %copy-start = (f32[256,256]{1,0:T(8,128)S(1)}, f32[256,256]{1,0:T(8,128)}, u32[]{:S(2)}) copy-start(f32[256,256]{1,0:T(8,128)} %param.10) | copy-start | bytes 786436
  2.0 3.2 %collective-permute-start.1 = (bf16[1024,256]{1,0:T(8,128)(2,1)S(1)}, bf16[1024,256]{1,0:T(8,128)(2,1)}, u32[]{:S(2)}, u32[]{:S(2)}) collective-permute-start(bf16[1024,256]{1,0:T(8,128)(2,1)S(1)} %get-tuple-element.76), channel_id=1, source_target_pairs={{0,1},{1,0},{2,3},{3,2},{4,5},{5,4},{6,7},{7,6},{8,9},{9,8},{10,11... | collective-permute-start | bytes 1572872 | tf_op jit(solution)/shard_map/ppermute | solution.py:312
  3.5 9.5 %copy-start.19 = (f32[16,4,2]{0,2,1:T(2,128)S(1)}, f32[16,4,2]{0,2,1:T(2,128)}, u32[]{:S(2)}) copy-start(f32[16,4,2]{0,2,1:T(2,128)} %param.13) | copy-start | bytes 1540
  3.5 10.2 %copy-start.14 = (s32[16,4,2]{0,2,1:T(2,128)S(1)}, s32[16,4,2]{0,2,1:T(2,128)}, u32[]{:S(2)}) copy-start(s32[16,4,2]{0,2,1:T(2,128)} %param.14) | copy-start | bytes 1540
  3.5 10.5 %copy-start.15 = (s32[16,4,2]{0,2,1:T(2,128)S(1)}, s32[16,4,2]{0,2,1:T(2,128)}, u32[]{:S(2)}) copy-start(s32[16,4,2]{0,2,1:T(2,128)} %param.12) | copy-start | bytes 1540
  3.5 22.0 %copy-start.2 = (bf16[512,1024]{1,0:T(8,128)(2,1)S(1)}, bf16[512,1024]{1,0:T(8,128)(2,1)}, u32[]{:S(2)}) copy-start(bf16[512,1024]{1,0:T(8,128)(2,1)} %param.8) | copy-start | bytes 3145732
  6.3 19.6 %collective-permute-start.3 = (bf16[2048,128]{1,0:T(8,128)(2,1)S(1)}, bf16[2048,128]{1,0:T(8,128)(2,1)S(1)}, u32[]{:S(2)}, u32[]{:S(2)}) collective-permute-start(bf16[2048,128]{1,0:T(8,128)(2,1)S(1)} %get-tuple-element.39), channel_id=1, source_target_pairs={{0,32},{1,9},{2,34},{3,11},{4,36},{5,13},{6,38},{7,15},{8,40},{9,1... | collective-permute-start | bytes 1572872 | tf_op jit(solution)/shard_map/ppermute | solution.py:43
  8.1 29.2 %collective-permute-start.2 = (bf16[2048,128]{1,0:T(8,128)(2,1)S(1)}, bf16[2048,128]{1,0:T(8,128)(2,1)S(1)}, u32[]{:S(2)}, u32[]{:S(2)}) collective-permute-start(bf16[2048,128]{1,0:T(8,128)(2,1)S(1)} %get-tuple-element.39), channel_id=1, source_target_pairs={{0,96},{1,25},{2,98},{3,27},{4,100},{5,29},{6,102},{7,31},{8,104},... | collective-permute-start | bytes 1572872 | tf_op jit(solution)/shard_map/ppermute | solution.py:43
  10.3 17.3 %collective-permute-start.7 = (bf16[2048,128]{1,0:T(8,128)(2,1)S(1)}, bf16[2048,128]{1,0:T(8,128)(2,1)}, u32[]{:S(2)}, u32[]{:S(2)}) collective-permute-start(bf16[2048,128]{1,0:T(8,128)(2,1)S(1)} %get-tuple-element.40), channel_id=1, source_target_pairs={{0,32},{1,9},{2,34},{3,11},{4,36},{5,13},{6,38},{7,15},{8,40},{9,1... | collective-permute-start | bytes 1572872 | tf_op jit(solution)/shard_map/ppermute | solution.py:43
  10.3 12.0 %collective-permute-start.5 = (bf16[2048,128]{1,0:T(8,128)(2,1)S(1)}, bf16[2048,128]{1,0:T(8,128)(2,1)}, u32[]{:S(2)}, u32[]{:S(2)}) collective-permute-start(bf16[2048,128]{1,0:T(8,128)(2,1)S(1)} %get-tuple-element.40), channel_id=1, source_target_pairs={{0,96},{1,25},{2,98},{3,27},{4,100},{5,29},{6,102},{7,31},{8,104},... | collective-permute-start | bytes 1572872 | tf_op jit(solution)/shard_map/ppermute | solution.py:43
  14.1 17.9 %copy-start.10 = (bf16[4,2,8,256]{3,2,0,1:T(8,128)(2,1)}, bf16[4,2,8,256]{3,2,0,1:T(8,128)(2,1)S(1)}, u32[]{:S(2)}) copy-start(bf16[4,2,8,256]{3,2,0,1:T(8,128)(2,1)S(1)} %copy.45) | copy-start | bytes 98308
  14.4 17.5 %copy-start.4 = (bf16[4,2,8,256]{3,2,0,1:T(8,128)(2,1)}, bf16[4,2,8,256]{3,2,0,1:T(8,128)(2,1)S(1)}, u32[]{:S(2)}) copy-start(bf16[4,2,8,256]{3,2,0,1:T(8,128)(2,1)S(1)} %copy.44) | copy-start | bytes 98308
  22.3 9.7 %collective-permute-start.6 = (bf16[2048,128]{1,0:T(8,128)(2,1)}, bf16[2048,128]{1,0:T(8,128)(2,1)S(1)}, u32[]{:S(2)}, u32[]{:S(2)}) collective-permute-start(bf16[2048,128]{1,0:T(8,128)(2,1)} %collective-permute-done.5), channel_id=1, source_target_pairs={{0,96},{1,25},{2,98},{3,27},{4,100},{5,29},{6,102},{7,31},{8,104},... | collective-permute-start | bytes 1572872 | tf_op jit(solution)/shard_map/ppermute | solution.py:43
  25.9 11.3 %collective-permute-start.4 = (bf16[2048,128]{1,0:T(8,128)(2,1)S(1)}, bf16[2048,128]{1,0:T(8,128)(2,1)S(1)}, u32[]{:S(2)}, u32[]{:S(2)}) collective-permute-start(bf16[2048,128]{1,0:T(8,128)(2,1)S(1)} %collective-permute-done.3), channel_id=1, source_target_pairs={{0,32},{1,9},{2,34},{3,11},{4,36},{5,13},{6,38},{7,15},{8,40},{9,1... | collective-permute-start | bytes 1572872 | tf_op jit(solution)/shard_map/ppermute | solution.py:43
  34.8 37.5 %collective-permute-start.12 = (bf16[4,2048,128]{2,1,0:T(8,128)(2,1)}, bf16[4,2048,128]{2,1,0:T(8,128)(2,1)}, u32[]{:S(2)}, u32[]{:S(2)}) collective-permute-start(bf16[4,2048,128]{2,1,0:T(8,128)(2,1)} %pad_maximum_fusion.1.refs_1_), channel_id=1, source_target_pairs={{0,24},{1,97},{2,26},{3,99},{4,28},{5,101},{6,30},{7,103},{8,0},{9... | collective-permute-start | bytes 6291464 | tf_op jit(solution)/shard_map/ppermute | solution.py:43
  38.8 33.4 %collective-permute-start.11 = (bf16[4,2048,128]{2,1,0:T(8,128)(2,1)}, bf16[4,2048,128]{2,1,0:T(8,128)(2,1)}, u32[]{:S(2)}, u32[]{:S(2)}) collective-permute-start(bf16[4,2048,128]{2,1,0:T(8,128)(2,1)} %pad_maximum_fusion.refs_0_), channel_id=1, source_target_pairs={{0,8},{1,33},{2,10},{3,35},{4,12},{5,37},{6,14},{7,39},{8,16},{9,4... | collective-permute-start | bytes 6291464 | tf_op jit(solution)/shard_map/ppermute | solution.py:43
  38.8 13.0 %collective-permute-start = (bf16[512,1024]{1,0:T(8,128)(2,1)S(1)}, bf16[512,1024]{1,0:T(8,128)(2,1)}, u32[]{:S(2)}, u32[]{:S(2)}) collective-permute-start(bf16[512,1024]{1,0:T(8,128)(2,1)S(1)} %copy-done.2), channel_id=1, source_target_pairs={{0,1},{1,0},{2,3},{3,2},{4,5},{5,4},{6,7},{7,6},{8,9},{9,8},{10,11... | collective-permute-start | bytes 3145736 | tf_op jit(solution)/shard_map/ppermute | solution.py:332
  41.6 2.2 %collective-permute-start.8 = (f32[32,512]{1,0:T(8,128)S(1)}, f32[32,512]{1,0:T(8,128)S(1)}, u32[]{:S(2)}, u32[]{:S(2)}) collective-permute-start(f32[32,512]{1,0:T(8,128)S(1)} %pad_maximum_fusion.4), channel_id=1, source_target_pairs={{0,1},{1,0},{2,3},{3,2},{4,5},{5,4},{6,7},{7,6},{8,9},{9,8},{10,11... | collective-permute-start | bytes 196616 | tf_op jit(solution)/shard_map/ppermute | solution.py:61
  43.9 3.7 %collective-permute-start.9 = (f32[32,512]{1,0:T(8,128)S(1)}, f32[32,512]{1,0:T(8,128)S(1)}, u32[]{:S(2)}, u32[]{:S(2)}) collective-permute-start(f32[32,512]{1,0:T(8,128)S(1)} %add.383), channel_id=1, source_target_pairs={{0,2},{1,3},{2,0},{3,1},{4,6},{5,7},{6,4},{7,5},{8,10},{9,11},{10,... | collective-permute-start | bytes 196616 | tf_op jit(solution)/shard_map/ppermute | solution.py:61
  45.2 42.8 %collective-permute-start.14 = (bf16[4,2048,128]{2,1,0:T(8,128)(2,1)}, bf16[4,2048,128]{2,1,0:T(8,128)(2,1)}, u32[]{:S(2)}, u32[]{:S(2)}) collective-permute-start(bf16[4,2048,128]{2,1,0:T(8,128)(2,1)} %pad_maximum_fusion.1.refs_1_), channel_id=1, source_target_pairs={{0,8},{1,33},{2,10},{3,35},{4,12},{5,37},{6,14},{7,39},{8,16},{9,4... | collective-permute-start | bytes 6291464 | tf_op jit(solution)/shard_map/ppermute | solution.py:43
  47.6 40.4 %collective-permute-start.13 = (bf16[4,2048,128]{2,1,0:T(8,128)(2,1)}, bf16[4,2048,128]{2,1,0:T(8,128)(2,1)}, u32[]{:S(2)}, u32[]{:S(2)}) collective-permute-start(bf16[4,2048,128]{2,1,0:T(8,128)(2,1)} %pad_maximum_fusion.refs_0_), channel_id=1, source_target_pairs={{0,24},{1,97},{2,26},{3,99},{4,28},{5,101},{6,30},{7,103},{8,0},{9... | collective-permute-start | bytes 6291464 | tf_op jit(solution)/shard_map/ppermute | solution.py:43
  51.8 9.3 %collective-permute-start.10 = (f32[32,512]{1,0:T(8,128)S(1)}, f32[32,512]{1,0:T(8,128)S(1)}, u32[]{:S(2)}, u32[]{:S(2)}) collective-permute-start(f32[32,512]{1,0:T(8,128)S(1)} %add.384), channel_id=1, source_target_pairs={{0,4},{1,5},{2,6},{3,7},{4,0},{5,1},{6,2},{7,3},{8,12},{9,13},{10,... | collective-permute-start | bytes 196616 | tf_op jit(solution)/shard_map/ppermute | solution.py:61
  61.7 18.2 %all-to-all-start = ((bf16[4,512,256]{2,1,0:T(8,128)(2,1)}), bf16[4,512,256]{2,1,0:T(8,128)(2,1)S(1)}, u32[]{:S(2)}, u32[]{:S(2)}) async-start(bf16[4,512,256]{2,1,0:T(8,128)(2,1)} %forward.4), calls=%async_computation | async-start | bytes 2097152 | tf_op jit(solution)/shard_map/all_to_all | solution.py:54
  72.2 60.1 %collective-permute-start.20 = (bf16[4,2048,128]{2,1,0:T(8,128)(2,1)}, bf16[4,2048,128]{2,1,0:T(8,128)(2,1)}, u32[]{:S(2)}, u32[]{:S(2)}) collective-permute-start(bf16[4,2048,128]{2,1,0:T(8,128)(2,1)} %collective-permute-done.11.refs_0_), channel_id=1, source_target_pairs={{0,8},{1,33},{2,10},{3,35},{4,12},{5,37},{6,14},{7,39},{8,16},{9,4... | collective-permute-start | bytes 6291464 | tf_op jit(solution)/shard_map/ppermute | solution.py:43
  72.3 60.0 %collective-permute-start.21 = (bf16[4,2048,128]{2,1,0:T(8,128)(2,1)}, bf16[4,2048,128]{2,1,0:T(8,128)(2,1)}, u32[]{:S(2)}, u32[]{:S(2)}) collective-permute-start(bf16[4,2048,128]{2,1,0:T(8,128)(2,1)} %collective-permute-done.12.refs_1_), channel_id=1, source_target_pairs={{0,24},{1,97},{2,26},{3,99},{4,28},{5,101},{6,30},{7,103},{8,0},{9... | collective-permute-start | bytes 6291464 | tf_op jit(solution)/shard_map/ppermute | solution.py:43
  79.9 17.4 %all-to-all-start.1 = ((bf16[4,512,256]{2,1,0:T(8,128)(2,1)}), bf16[4,512,256]{2,1,0:T(8,128)(2,1)}, u32[]{:S(2)}, u32[]{:S(2)}) async-start(bf16[4,512,256]{2,1,0:T(8,128)(2,1)} %forward.5), calls=%async_computation.1 | async-start | bytes 2097152 | tf_op jit(solution)/shard_map/all_to_all | solution.py:54
  97.3 20.8 %all-to-all-start.2 = ((bf16[4,512,256]{2,1,0:T(8,128)(2,1)}), bf16[4,512,256]{2,1,0:T(8,128)(2,1)}, u32[]{:S(2)}, u32[]{:S(2)}) async-start(bf16[4,512,256]{2,1,0:T(8,128)(2,1)} %forward.6), calls=%async_computation.2 | async-start | bytes 2097152 | tf_op jit(solution)/shard_map/all_to_all | solution.py:54
  101.6 11.5 %collective-permute-start.17 = (f32[32,1024]{1,0:T(8,128)}, f32[32,1024]{1,0:T(8,128)}, u32[]{:S(2)}, u32[]{:S(2)}) collective-permute-start(f32[32,1024]{1,0:T(8,128)} %maximum_multiply_fusion), channel_id=1, source_target_pairs={{0,96},{1,97},{2,98},{3,99},{4,100},{5,101},{6,102},{7,103},{8,104... | collective-permute-start | bytes 393224 | tf_op jit(solution)/shard_map/ppermute | solution.py:72
  101.7 11.4 %collective-permute-start.16 = (f32[32,1024]{1,0:T(8,128)}, f32[32,1024]{1,0:T(8,128)}, u32[]{:S(2)}, u32[]{:S(2)}) collective-permute-start(f32[32,1024]{1,0:T(8,128)} %maximum_multiply_fusion), channel_id=1, source_target_pairs={{0,64},{1,65},{2,66},{3,67},{4,68},{5,69},{6,70},{7,71},{8,72},{9,... | collective-permute-start | bytes 393224 | tf_op jit(solution)/shard_map/ppermute | solution.py:72
  101.8 14.3 %collective-permute-start.15 = (f32[32,1024]{1,0:T(8,128)}, f32[32,1024]{1,0:T(8,128)}, u32[]{:S(2)}, u32[]{:S(2)}) collective-permute-start(f32[32,1024]{1,0:T(8,128)} %maximum_multiply_fusion), channel_id=1, source_target_pairs={{0,32},{1,33},{2,34},{3,35},{4,36},{5,37},{6,38},{7,39},{8,40},{9,... | collective-permute-start | bytes 393224 | tf_op jit(solution)/shard_map/ppermute | solution.py:72
  103.2 12.9 %copy-start.3 = (f32[32,1024]{1,0:T(8,128)S(1)}, f32[32,1024]{1,0:T(8,128)}, u32[]{:S(2)}) copy-start(f32[32,1024]{1,0:T(8,128)} %maximum_multiply_fusion) | copy-start | bytes 393220
  117.8 4.8 %collective-permute-start.19 = (f32[32,1024]{1,0:T(8,128)}, f32[32,1024]{1,0:T(8,128)}, u32[]{:S(2)}, u32[]{:S(2)}) collective-permute-start(f32[32,1024]{1,0:T(8,128)} %add_add_fusion), channel_id=1, source_target_pairs={{0,8},{8,0},{16,24},{24,16},{32,40},{40,32},{48,56},{56,48},{64,72... | collective-permute-start | bytes 393224 | tf_op jit(solution)/shard_map/ppermute | solution.py:82
  124.3 18.8 %collective-permute-start.28 = (f32[32,1024]{1,0:T(8,128)}, f32[32,1024]{1,0:T(8,128)}, u32[]{:S(2)}, u32[]{:S(2)}) collective-permute-start(f32[32,1024]{1,0:T(8,128)} %add.442), channel_id=1, source_target_pairs={{0,16},{8,24},{16,0},{24,8},{32,48},{40,56},{48,32},{56,40},{64,80... | collective-permute-start | bytes 393224 | tf_op jit(solution)/shard_map/ppermute | solution.py:82
  127.9 20.8 %all-to-all-start.3 = ((bf16[4,512,256]{2,1,0:T(8,128)(2,1)}), bf16[4,512,256]{2,1,0:T(8,128)(2,1)S(1)}, u32[]{:S(2)}, u32[]{:S(2)}) async-start(bf16[4,512,256]{2,1,0:T(8,128)(2,1)} %arrange.1), calls=%async_computation.3 | async-start | bytes 2097152 | tf_op jit(solution)/shard_map/all_to_all | solution.py:54
  137.3 10.5 %copy-start.17 = (f32[16,4,2]{0,2,1:T(2,128)S(1)}, f32[16,4,2]{0,2,1:T(2,128)}, u32[]{:S(2)}) copy-start(f32[16,4,2]{0,2,1:T(2,128)} %copy-done.16) | copy-start | bytes 1540
  137.3 11.4 %copy-start.1 = (bf16[4,512,256]{2,1,0:T(8,128)(2,1)S(1)}, bf16[4,512,256]{2,1,0:T(8,128)(2,1)}, u32[]{:S(2)}) copy-start(bf16[4,512,256]{2,1,0:T(8,128)(2,1)} %arrange.1) | copy-start | bytes 3145732
  137.3 15.4 %collective-permute-start.22 = (bf16[512,256]{1,0:T(8,128)(2,1)}, bf16[512,256]{1,0:T(8,128)(2,1)}, u32[]{:S(2)}, u32[]{:S(2)}) collective-permute-start(bf16[512,256]{1,0:T(8,128)(2,1)} %get-tuple-element.66), channel_id=1, source_target_pairs={{0,4},{1,5},{2,6},{3,7},{4,0},{5,1},{6,2},{7,3},{8,12},{9,13},{10,... | collective-permute-start | bytes 786440 | tf_op jit(solution)/shard_map/ppermute | solution.py:391
  140.4 18.8 %collective-permute-start.23 = (bf16[512,256]{1,0:T(8,128)(2,1)}, bf16[512,256]{1,0:T(8,128)(2,1)}, u32[]{:S(2)}, u32[]{:S(2)}) collective-permute-start(bf16[512,256]{1,0:T(8,128)(2,1)} %get-tuple-element.67), channel_id=1, source_target_pairs={{0,2},{1,3},{2,4},{3,5},{4,6},{5,7},{6,0},{7,1},{8,10},{9,11},{10,... | collective-permute-start | bytes 786440 | tf_op jit(solution)/shard_map/ppermute | solution.py:391
  140.6 18.5 %collective-permute-start.24 = (bf16[512,256]{1,0:T(8,128)(2,1)}, bf16[512,256]{1,0:T(8,128)(2,1)}, u32[]{:S(2)}, u32[]{:S(2)}) collective-permute-start(bf16[512,256]{1,0:T(8,128)(2,1)} %get-tuple-element.68), channel_id=1, source_target_pairs={{0,6},{1,7},{2,0},{3,1},{4,2},{5,3},{6,4},{7,5},{8,14},{9,15},{10,... | collective-permute-start | bytes 786440 | tf_op jit(solution)/shard_map/ppermute | solution.py:391
  144.5 14.7 %copy-start.6 = (bf16[512,256]{1,0:T(8,128)(2,1)S(1)}, bf16[512,256]{1,0:T(8,128)(2,1)}, u32[]{:S(2)}) copy-start(bf16[512,256]{1,0:T(8,128)(2,1)} %get-tuple-element.65) | copy-start | bytes 786436
  144.9 5.5 %collective-permute-start.29 = (f32[256,256]{1,0:T(8,128)S(1)}, f32[256,256]{1,0:T(8,128)}, u32[]{:S(2)}, u32[]{:S(2)}) collective-permute-start(f32[256,256]{1,0:T(8,128)S(1)} %fusion.2), channel_id=1, source_target_pairs={{0,1},{1,0},{2,3},{3,2},{4,5},{5,4},{6,7},{7,6},{8,9},{9,8},{10,11... | collective-permute-start | bytes 786440 | tf_op jit(solution)/shard_map/ppermute | solution.py:61
  148.8 25.8 %collective-permute-start.18 = (bf16[2,512,256]{2,1,0:T(8,128)(2,1)S(1)}, bf16[2,512,256]{2,1,0:T(8,128)(2,1)S(1)}, u32[]{:S(2)}, u32[]{:S(2)}) collective-permute-start(bf16[2,512,256]{2,1,0:T(8,128)(2,1)S(1)} %slice_select_fusion.1), channel_id=1, source_target_pairs={{0,1},{1,0},{2,3},{3,2},{4,5},{5,4},{6,7},{7,6},{8,9},{9,8},{10,11... | collective-permute-start | bytes 1572872 | tf_op jit(solution)/shard_map/ppermute | solution.py:401
  151.4 16.5 %collective-permute-start.30 = (f32[256,256]{1,0:T(8,128)S(1)}, f32[256,256]{1,0:T(8,128)S(1)}, u32[]{:S(2)}, u32[]{:S(2)}) collective-permute-start(f32[256,256]{1,0:T(8,128)S(1)} %add.467), channel_id=1, source_target_pairs={{0,2},{1,3},{2,0},{3,1},{4,6},{5,7},{6,4},{7,5},{8,10},{9,11},{10,... | collective-permute-start | bytes 786440 | tf_op jit(solution)/shard_map/ppermute | solution.py:61
  160.4 15.6 %collective-permute-start.27 = (bf16[512,256]{1,0:T(8,128)(2,1)S(1)}, bf16[512,256]{1,0:T(8,128)(2,1)S(1)}, u32[]{:S(2)}, u32[]{:S(2)}) collective-permute-start(bf16[512,256]{1,0:T(8,128)(2,1)S(1)} %add_convert_fusion.2), channel_id=1, source_target_pairs={{3,4},{7,5},{11,12},{15,13},{19,20},{23,21},{27,28},{31,29},{35,38... | collective-permute-start | bytes 786440 | tf_op jit(solution)/shard_map/ppermute | solution.py:285
  161.1 14.9 %collective-permute-start.26 = (bf16[512,256]{1,0:T(8,128)(2,1)S(1)}, bf16[512,256]{1,0:T(8,128)(2,1)S(1)}, u32[]{:S(2)}, u32[]{:S(2)}) collective-permute-start(bf16[512,256]{1,0:T(8,128)(2,1)S(1)} %add_convert_fusion.2), channel_id=1, source_target_pairs={{1,4},{5,5},{9,12},{13,13},{17,20},{21,21},{25,28},{29,29},{33,38}... | collective-permute-start | bytes 786440 | tf_op jit(solution)/shard_map/ppermute | solution.py:285
  166.6 9.5 %collective-permute-start.25 = (bf16[512,256]{1,0:T(8,128)(2,1)S(1)}, bf16[512,256]{1,0:T(8,128)(2,1)S(1)}, u32[]{:S(2)}, u32[]{:S(2)}) collective-permute-start(bf16[512,256]{1,0:T(8,128)(2,1)S(1)} %add_convert_fusion.2), channel_id=1, source_target_pairs={{0,1},{2,3},{4,5},{6,7},{8,9},{10,11},{12,13},{14,15},{32,33},{34,... | collective-permute-start | bytes 786440 | tf_op jit(solution)/shard_map/ppermute | solution.py:290
  167.9 10.3 %collective-permute-start.32 = (f32[256,256]{1,0:T(8,128)S(1)}, f32[256,256]{1,0:T(8,128)S(1)}, u32[]{:S(2)}, u32[]{:S(2)}) collective-permute-start(f32[256,256]{1,0:T(8,128)S(1)} %add.468), channel_id=1, source_target_pairs={{0,4},{1,5},{2,6},{3,7},{4,0},{5,1},{6,2},{7,3},{8,12},{9,13},{10,... | collective-permute-start | bytes 786440 | tf_op jit(solution)/shard_map/ppermute | solution.py:61
  174.7 4.3 %collective-permute-start.31 = (bf16[512,1024]{1,0:T(8,128)(2,1)S(1)}, bf16[512,1024]{1,0:T(8,128)(2,1)S(1)}, u32[]{:S(2)}, u32[]{:S(2)}) collective-permute-start(bf16[512,1024]{1,0:T(8,128)(2,1)S(1)} %get-tuple-element.72), channel_id=1, source_target_pairs={{0,1},{1,0},{2,3},{3,2},{4,5},{5,4},{6,7},{7,6},{8,9},{9,8},{10,11... | collective-permute-start | bytes 3145736 | tf_op jit(solution)/shard_map/ppermute | solution.py:415
  (9 other events, 25.9 us)

commit v10 on v9

--- a/solution.py
+++ b/solution.py
@@ -382,22 +382,22 @@
     slots = arrange(
         far.astype(jnp.int32).reshape(1), slots_here, slots_first, after(slots_second, grown, both)
     )
-    both = with_partner(both, 1, slots)
     moved = exchange(slots, "tensor", LANES)
-    sent = forward(after(turned_here, slots, both), wide, take(across), apart=True)
+    sent = forward(after(turned_here, slots), wide, take(across), apart=True)
     arrived = [sent[0]]
     for step in range(1, SIDE):
         turns = [(t, (t + 2 * step) % 8) for t in range(8)]
         arrived.append(lax.ppermute(sent[step], "tensor", turns))
+    both = with_partner(both, 1, *sent)
+    grown, other = backward(
+        after(spots_of(across), *sent), grown, out_grad, take(across), last=True
+    )
+    both = with_partner(both, 2, other)
+    arrived = lax.optimization_barrier((*arrived, other))[:SIDE]
     piece = total_of([a.astype(f32) for a in arrived]).astype(bf16)
-    both = with_partner(both, 2, *sent)
     bank_a, logit_grad_a = compose_back(both[:rank], weights_a, picked_a, mixing_a, vector_bank)
     bank_b, logit_grad_b = compose_back(both[rank:], weights_b, picked_b, mixing_b, vector_bank)
-    bank_part = over_tensor(bank_a + bank_b, (1, 2))
-    grown, other = backward(
-        after(spots_of(across), *sent, bank_part), grown, out_grad, take(across), last=True
-    )
-    bank_grad = over_tensor(bank_part, (4,))
+    bank_grad = over_tensor(bank_a + bank_b)
     crossed = lax.ppermute(jnp.where(core == 0, slots[2:], moved[:2]), "tensor", SWAP)
     firsts = jnp.where(core == 0, slots[:2], crossed)
     seconds = jnp.where(core == 0, crossed, moved[2:])

time: 181 us -> 185 us (1.022)
  the two profiles are of different devices: /device:TPU:1 before, /device:TPU:5 now
where the time goes in v10:
time: 185 us; the launch traced here: 184 us
  starting transfers between devices  76.3 us (41%)
  Pallas kernels  45.7 us (25%)
  waiting for transfers between devices  25.4 us (14%)
  other arithmetic  19 us (10%)
  matrix products  10.6 us (6%)
  local copies, waits for them, and re-layouts  5.52 us (3%)
    pallas_call x3, Pallas kernels, backward(): pl.pallas_call(functools.partial(backward_kernel, count, first, last), ou...  23.2 us
    pallas_call x4, Pallas kernels, forward(): pl.pallas_call(functools.partial(forward_kernel, count, many), out_shape=...  19.9 us
    all_to_all x4, starting transfers between devices, exchange(): lax.all_to_all(value, axis, split_axis=0, concat_axis=0, tiled=True, axis...  16.3 us
    ppermute x12, starting transfers between devices, shift(): return lax.ppermute(value, BOTH, ring(stage, step))  16.1 us
    ppermute x6, starting transfers between devices, over_tensor(): lax.ppermute(value, 'tensor', [(t, t ^ bit) for t in range(8)])  13.5 us
    ppermute x12, waiting for transfers between devices, shift(): return lax.ppermute(value, BOTH, ring(stage, step))  12.4 us
    ppermute x3, starting transfers between devices, from_step(): return lax.ppermute(value, BOTH, pairs(move))  9.93 us
    ppermute x2, waiting for transfers between devices, from_second(): return lax.ppermute(piece, BOTH, pairs(move))  7.79 us
  transfers between devices with their start and end apart: 37, of which 8 were waited for; matrix products, arithmetic and copies ran while one was open for 15% of the time, Pallas kernels for 25%

profile of v10, /device:TPU:5, one launch (start us, length us, event | category | flops | bytes accessed | tf_op | source)
XLA Modules:
  0.0 184.0 jit_solution(10617469847420475979)
XLA Ops:
  0.7 1.3 broadcast_select_fusion.1
  2.8 1.6 collective-permute-done.1
  5.5 1.7 collective-permute-start.3
  7.3 2.2 %collective-permute-start.2 = (bf16[2048,128]{1,0:T(8,128)(2,1)S(1)}, bf16[2048,128]{1,0:T(8,128)(2,1)S(1)}, u32[]{:S(2)}, u32[]{:S(2)}) collective-permute-start(bf16[2048,128]{1,0:T(8,128)(2,1)S(1)} %get-tuple-element.43), channel_id=1, source_target_pairs={{0,96},{1,25},{2,98},{3,27},{4,100},{5,29},{6,102},{7,31},{8,104},... | collective-permute-start | bytes 1572872 | tf_op jit(solution)/shard_map/ppermute | solution.py:43
  9.5 2.7 %collective-permute-start.5 = (bf16[2048,128]{1,0:T(8,128)(2,1)S(1)}, bf16[2048,128]{1,0:T(8,128)(2,1)}, u32[]{:S(2)}, u32[]{:S(2)}) collective-permute-start(bf16[2048,128]{1,0:T(8,128)(2,1)S(1)} %get-tuple-element.44), channel_id=1, source_target_pairs={{0,96},{1,25},{2,98},{3,27},{4,100},{5,29},{6,102},{7,31},{8,104},... | collective-permute-start | bytes 1572872 | tf_op jit(solution)/shard_map/ppermute | solution.py:43
  13.6 7.9 %collective-permute-done.5 = bf16[2048,128]{1,0:T(8,128)(2,1)} collective-permute-done((bf16[2048,128]{1,0:T(8,128)(2,1)S(1)}, bf16[2048,128]{1,0:T(8,128)(2,1)}, u32[]{:S(2)}, u32[]{:S(2)}) %collective-permute-start.5) | collective-permute-done | bytes 524320 | tf_op jit(solution)/shard_map/ppermute | solution.py:43
  21.5 2.9 %collective-permute-start.6 = (bf16[2048,128]{1,0:T(8,128)(2,1)}, bf16[2048,128]{1,0:T(8,128)(2,1)S(1)}, u32[]{:S(2)}, u32[]{:S(2)}) collective-permute-start(bf16[2048,128]{1,0:T(8,128)(2,1)} %collective-permute-done.5), channel_id=1, source_target_pairs={{0,96},{1,25},{2,98},{3,27},{4,100},{5,29},{6,102},{7,31},{8,104},... | collective-permute-start | bytes 1572872 | tf_op jit(solution)/shard_map/ppermute | solution.py:43
  24.8 1.6 fusion.11
  26.5 4.4 %collective-permute-done.6 = bf16[2048,128]{1,0:T(8,128)(2,1)S(1)} collective-permute-done((bf16[2048,128]{1,0:T(8,128)(2,1)}, bf16[2048,128]{1,0:T(8,128)(2,1)S(1)}, u32[]{:S(2)}, u32[]{:S(2)}) %collective-permute-start.6) | collective-permute-done | bytes 524320 | tf_op jit(solution)/shard_map/ppermute | solution.py:43
  30.9 2.8 %pad_maximum_fusion.1.refs_1_ = bf16[4,2048,128]{2,1,0:T(8,128)(2,1)} fusion(bf16[1,2048,128]{2,1,0:T(8,128)(2,1)} %bitcast.9, bf16[1,2048,128]{2,1,0:T(8,128)(2,1)S(1)} %bitcast.111, bf16[1,2048,128]{2,1,0:T(8,128)(2,1)} %bitcast.7, bf16[1,2048,128]{2,1,0:T(8,128)(2,1)S(1)} %bitcast.103), kind=kLoop, calls=%fused_computation.3 | loop fusion | flops 3145728 | bytes 4194304 | tf_op jit(solution)/shard_map/stack | solution.py:318
  34.1 1.6 pad_maximum_fusion.refs_0_
  36.9 3.0 %collective-permute-start = (bf16[512,1024]{1,0:T(8,128)(2,1)S(1)}, bf16[512,1024]{1,0:T(8,128)(2,1)}, u32[]{:S(2)}, u32[]{:S(2)}) collective-permute-start(bf16[512,1024]{1,0:T(8,128)(2,1)S(1)} %copy-done.1), channel_id=1, source_target_pairs={{0,1},{1,0},{2,3},{3,2},{4,5},{5,4},{6,7},{7,6},{8,9},{9,8},{10,11... | collective-permute-start | bytes 3145736 | tf_op jit(solution)/shard_map/ppermute | solution.py:332
  39.9 2.2 %collective-permute-done.8 = f32[32,512]{1,0:T(8,128)S(1)} collective-permute-done((f32[32,512]{1,0:T(8,128)S(1)}, f32[32,512]{1,0:T(8,128)S(1)}, u32[]{:S(2)}, u32[]{:S(2)}) %collective-permute-start.8) | collective-permute-done | bytes 65568 | tf_op jit(solution)/shard_map/ppermute | solution.py:61
  44.1 2.6 %collective-permute-start.14 = (bf16[4,2048,128]{2,1,0:T(8,128)(2,1)}, bf16[4,2048,128]{2,1,0:T(8,128)(2,1)}, u32[]{:S(2)}, u32[]{:S(2)}) collective-permute-start(bf16[4,2048,128]{2,1,0:T(8,128)(2,1)} %pad_maximum_fusion.1.refs_1_), channel_id=1, source_target_pairs={{0,8},{1,33},{2,10},{3,35},{4,12},{5,37},{6,14},{7,39},{8,16},{9,4... | collective-permute-start | bytes 6291464 | tf_op jit(solution)/shard_map/ppermute | solution.py:43
  48.5 3.0 %collective-permute-start.10 = (f32[32,512]{1,0:T(8,128)S(1)}, f32[32,512]{1,0:T(8,128)S(1)}, u32[]{:S(2)}, u32[]{:S(2)}) collective-permute-start(f32[32,512]{1,0:T(8,128)S(1)} %add.384), channel_id=1, source_target_pairs={{0,4},{1,5},{2,6},{3,7},{4,0},{5,1},{6,2},{7,3},{8,12},{9,13},{10,... | collective-permute-start | bytes 196616 | tf_op jit(solution)/shard_map/ppermute | solution.py:61
  51.5 1.3 constant_dynamic-update-slice_fusion.wide_ref
  52.8 5.0 %forward.4 = bf16[4,512,256]{2,1,0:T(8,128)(2,1)} custom-call(s32[1]{0:T(128)} %bitcast.1.start_ref, bf16[512,2048]{1,0:T(8,128)(2,1)S(1)} %constant_dynamic-update-slice_fusion.wide_ref, bf16[4,2048,128]{2,1,0:T(8,128)(2,1)} %pad_maximum_fusion.refs_0_, bf16[4,2048,128]{2,1,0:T(8,128)(2,1)} %pad_maximum_fusion.1.refs_1_), custom_call_target="tpu_custom_call" | custom-call | flops 268435456 | bytes 524288 | tf_op jit(solution)/shard_map/forward/pallas_call | solution.py:131
  58.5 3.5 %all-to-all-start = ((bf16[4,512,256]{2,1,0:T(8,128)(2,1)}), bf16[4,512,256]{2,1,0:T(8,128)(2,1)S(1)}, u32[]{:S(2)}, u32[]{:S(2)}) async-start(bf16[4,512,256]{2,1,0:T(8,128)(2,1)} %forward.4), calls=%async_computation | async-start | bytes 2097152 | tf_op jit(solution)/shard_map/all_to_all | solution.py:54
  62.2 6.8 %backward.3.refs_20_ = bf16[512,2048]{1,0:T(8,128)(2,1)} custom-call(s32[8]{0:T(128)S(1)} %stack.153.spots_ref, bf16[4,2048,128]{2,1,0:T(8,128)(2,1)} %pad_maximum_fusion.refs_0_, bf16[4,2048,128]{2,1,0:T(8,128)(2,1)} %pad_maximum_fusion.1.refs_1_, bf16[512,8192]{1,0:T(8,128)(2,1)} %refs_9_.5, bf16[512,8192]{1,0:T(8,128)(2,1)} %refs_9_.5, ...), custom_call_target="tpu_custom_call" | custom-call | flops 268435456 | bytes 524288 | tf_op jit(solution)/shard_map/backward/pallas_call | solution.py:237
  69.0 2.1 %collective-permute-start.19 = (bf16[4,2048,128]{2,1,0:T(8,128)(2,1)}, bf16[4,2048,128]{2,1,0:T(8,128)(2,1)}, u32[]{:S(2)}, u32[]{:S(2)}) collective-permute-start(bf16[4,2048,128]{2,1,0:T(8,128)(2,1)} %collective-permute-done.11.refs_0_), channel_id=1, source_target_pairs={{0,8},{1,33},{2,10},{3,35},{4,12},{5,37},{6,14},{7,39},{8,16},{9,4... | collective-permute-start | bytes 6291464 | tf_op jit(solution)/shard_map/ppermute | solution.py:43
  71.1 5.0 %forward.5 = bf16[4,512,256]{2,1,0:T(8,128)(2,1)} custom-call(s32[1]{0:T(128)} %bitcast.1.start_ref, bf16[512,2048]{1,0:T(8,128)(2,1)S(1)} %constant_dynamic-update-slice_fusion.wide_ref, bf16[4,2048,128]{2,1,0:T(8,128)(2,1)} %collective-permute-done.11.refs_0_, bf16[4,2048,128]{2,1,0:T(8,128)(2,1)} %collective-permute-done.12.refs_1_), custom_call_target="tpu_custom_call" | custom-call | flops 268435456 | bytes 524288 | tf_op jit(solution)/shard_map/forward/pallas_call | solution.py:131
  76.1 4.3 %all-to-all-start.1 = ((bf16[4,512,256]{2,1,0:T(8,128)(2,1)}), bf16[4,512,256]{2,1,0:T(8,128)(2,1)}, u32[]{:S(2)}, u32[]{:S(2)}) async-start(bf16[4,512,256]{2,1,0:T(8,128)(2,1)} %forward.5), calls=%async_computation.1 | async-start | bytes 2097152 | tf_op jit(solution)/shard_map/all_to_all | solution.py:54
  80.4 1.5 fusion.9
  81.9 1.5 fusion.32
  84.1 4.9 %forward.6 = bf16[4,512,256]{2,1,0:T(8,128)(2,1)} custom-call(s32[1]{0:T(128)} %bitcast.1.start_ref, bf16[512,2048]{1,0:T(8,128)(2,1)S(1)} %constant_dynamic-update-slice_fusion.wide_ref, bf16[4,2048,128]{2,1,0:T(8,128)(2,1)} %collective-permute-done.13.refs_0_.refs_2_, bf16[4,2048,128]{2,1,0:T(8,128)(2,1)} %collective-permute-done.14.refs_1_.refs_3_), custom_call_target="tpu_custom_call" | custom-call | flops 268435456 | bytes 524288 | tf_op jit(solution)/shard_map/forward/pallas_call | solution.py:131
  90.2 4.2 %all-to-all-start.2 = ((bf16[4,512,256]{2,1,0:T(8,128)(2,1)}), bf16[4,512,256]{2,1,0:T(8,128)(2,1)}, u32[]{:S(2)}, u32[]{:S(2)}) async-start(bf16[4,512,256]{2,1,0:T(8,128)(2,1)} %forward.6), calls=%async_computation.2 | async-start | bytes 2097152 | tf_op jit(solution)/shard_map/all_to_all | solution.py:54
  94.5 3.9 %collective-permute-start.17 = (f32[32,1024]{1,0:T(8,128)}, f32[32,1024]{1,0:T(8,128)}, u32[]{:S(2)}, u32[]{:S(2)}) collective-permute-start(f32[32,1024]{1,0:T(8,128)} %maximum_multiply_fusion), channel_id=1, source_target_pairs={{0,96},{1,97},{2,98},{3,99},{4,100},{5,101},{6,102},{7,103},{8,104... | collective-permute-start | bytes 393224 | tf_op jit(solution)/shard_map/ppermute | solution.py:72
  98.3 4.1 %collective-permute-start.16 = (f32[32,1024]{1,0:T(8,128)}, f32[32,1024]{1,0:T(8,128)}, u32[]{:S(2)}, u32[]{:S(2)}) collective-permute-start(f32[32,1024]{1,0:T(8,128)} %maximum_multiply_fusion), channel_id=1, source_target_pairs={{0,64},{1,65},{2,66},{3,67},{4,68},{5,69},{6,70},{7,71},{8,72},{9,... | collective-permute-start | bytes 393224 | tf_op jit(solution)/shard_map/ppermute | solution.py:72
  102.4 2.0 %collective-permute-start.15 = (f32[32,1024]{1,0:T(8,128)}, f32[32,1024]{1,0:T(8,128)}, u32[]{:S(2)}, u32[]{:S(2)}) collective-permute-start(f32[32,1024]{1,0:T(8,128)} %maximum_multiply_fusion), channel_id=1, source_target_pairs={{0,32},{1,33},{2,34},{3,35},{4,36},{5,37},{6,38},{7,39},{8,40},{9,... | collective-permute-start | bytes 393224 | tf_op jit(solution)/shard_map/ppermute | solution.py:72
  104.5 9.9 %backward.4.refs_10_ = bf16[512,2048]{1,0:T(8,128)(2,1)} custom-call(s32[16]{0:T(128)S(1)} %stack.170.spots_ref, bf16[4,2048,128]{2,1,0:T(8,128)(2,1)} %collective-permute-done.11.refs_0_, bf16[4,2048,128]{2,1,0:T(8,128)(2,1)} %collective-permute-done.12.refs_1_, ...), custom_call_target="tpu_custom_call", output_to_operand_aliasing={{}: (21, {})} | custom-call | flops 536870912 | bytes 1048576 | tf_op jit(solution)/shard_map/backward/pallas_call | solution.py:237
  114.4 1.7 add_add_fusion
  116.1 1.6 collective-permute-start.28
  117.7 2.6 %arrange.1 = bf16[4,512,256]{2,1,0:T(8,128)(2,1)} custom-call(s32[1]{0:T(128)} %bitcast.far_ref, bf16[4,512,256]{2,1,0:T(8,128)(2,1)S(1)} %all-to-all-done.here_ref, bf16[4,512,256]{2,1,0:T(8,128)(2,1)} %all-to-all-done.1.refs_0_, bf16[4,512,256]{2,1,0:T(8,128)(2,1)} %all-to-all-done.2.refs_1_), custom_call_target="tpu_custom_call" | custom-call | flops 2097152 | bytes 4194304 | tf_op jit(solution)/shard_map/arrange/pallas_call | solution.py:178
  120.3 5.0 %forward.7 = (bf16[512,256]{1,0:T(8,128)(2,1)}, bf16[512,256]{1,0:T(8,128)(2,1)}, bf16[512,256]{1,0:T(8,128)(2,1)}, bf16[512,256]{1,0:T(8,128)(2,1)}) custom-call(s32[1]{0:T(128)} %bitcast.36.start_ref, bf16[512,2048]{1,0:T(8,128)(2,1)S(1)} %constant_dynamic-update-slice_fusion.wide_ref, bf16[4,2048,128]{2,1,0:T(8,128)(2,1)} %collective-permute-done.19.refs_0_, ...), custom_call_target="tpu_custom_call" | custom-call | flops 268435456 | bytes 524288 | tf_op jit(solution)/shard_map/forward/pallas_call | solution.py:131
  125.3 1.6 add.466
  127.0 4.1 %collective-permute-start.29 = (f32[32,1024]{1,0:T(8,128)}, f32[32,1024]{1,0:T(8,128)}, u32[]{:S(2)}, u32[]{:S(2)}) collective-permute-start(f32[32,1024]{1,0:T(8,128)} %add.466), channel_id=1, source_target_pairs={{0,16},{8,24},{16,0},{24,8},{32,48},{40,56},{48,32},{56,40},{64,80... | collective-permute-start | bytes 393224 | tf_op jit(solution)/shard_map/ppermute | solution.py:82
  131.1 4.3 %all-to-all-start.3 = ((bf16[4,512,256]{2,1,0:T(8,128)(2,1)}), bf16[4,512,256]{2,1,0:T(8,128)(2,1)}, u32[]{:S(2)}, u32[]{:S(2)}) async-start(bf16[4,512,256]{2,1,0:T(8,128)(2,1)} %arrange.1), calls=%async_computation.3 | async-start | bytes 2097152 | tf_op jit(solution)/shard_map/all_to_all | solution.py:54
  135.4 1.4 collective-permute-start.21
  136.8 2.4 %collective-permute-start.22 = (bf16[512,256]{1,0:T(8,128)(2,1)}, bf16[512,256]{1,0:T(8,128)(2,1)}, u32[]{:S(2)}, u32[]{:S(2)}) collective-permute-start(bf16[512,256]{1,0:T(8,128)(2,1)} %get-tuple-element.70), channel_id=1, source_target_pairs={{0,4},{1,5},{2,6},{3,7},{4,0},{5,1},{6,2},{7,3},{8,12},{9,13},{10,... | collective-permute-start | bytes 786440 | tf_op jit(solution)/shard_map/ppermute | solution.py:390
  140.4 6.6 %backward.5 = (f32[512,1024]{1,0:T(8,128)S(1)}, bf16[512,1024]{1,0:T(8,128)(2,1)S(1)}) custom-call(s32[8]{0:T(128)S(1)} %stack.179.spots_ref, bf16[4,2048,128]{2,1,0:T(8,128)(2,1)} %collective-permute-done.19.refs_0_, bf16[4,2048,128]{2,1,0:T(8,128)(2,1)} %collective-permute-done.20.refs_1_, bf16[512,8192]{1,0:T(8,128)(2,1)} %refs_9_.5, ...), custom_call_target="tpu_custom_call" | custom-call | flops 268435456 | bytes 524288 | tf_op jit(solution)/shard_map/backward/pallas_call | solution.py:237
  149.6 3.0 %collective-permute-start.30 = (f32[256,256]{1,0:T(8,128)}, f32[256,256]{1,0:T(8,128)}, u32[]{:S(2)}, u32[]{:S(2)}) collective-permute-start(f32[256,256]{1,0:T(8,128)} %fusion.2), channel_id=1, source_target_pairs={{0,1},{1,0},{2,3},{3,2},{4,5},{5,4},{6,7},{7,6},{8,9},{9,8},{10,11... | collective-permute-start | bytes 786440 | tf_op jit(solution)/shard_map/ppermute | solution.py:61
  156.8 4.5 %collective-permute-start.31 = (f32[256,256]{1,0:T(8,128)S(1)}, f32[256,256]{1,0:T(8,128)S(1)}, u32[]{:S(2)}, u32[]{:S(2)}) collective-permute-start(f32[256,256]{1,0:T(8,128)S(1)} %add.469), channel_id=1, source_target_pairs={{0,2},{1,3},{2,0},{3,1},{4,6},{5,7},{6,4},{7,5},{8,10},{9,11},{10,... | collective-permute-start | bytes 786440 | tf_op jit(solution)/shard_map/ppermute | solution.py:61
  164.7 3.1 %collective-permute-start.25 = (bf16[512,256]{1,0:T(8,128)(2,1)S(1)}, bf16[512,256]{1,0:T(8,128)(2,1)S(1)}, u32[]{:S(2)}, u32[]{:S(2)}) collective-permute-start(bf16[512,256]{1,0:T(8,128)(2,1)S(1)} %add_convert_fusion.2), channel_id=1, source_target_pairs={{1,4},{5,5},{9,12},{13,13},{17,20},{21,21},{25,28},{29,29},{33,38}... | collective-permute-start | bytes 786440 | tf_op jit(solution)/shard_map/ppermute | solution.py:285
  169.3 1.8 collective-permute-start.32
  171.1 1.3 slice_select_fusion.2
  172.4 7.8 %collective-permute-done.26 = bf16[512,256]{1,0:T(8,128)(2,1)S(1)} collective-permute-done((bf16[512,256]{1,0:T(8,128)(2,1)S(1)}, bf16[512,256]{1,0:T(8,128)(2,1)S(1)}, u32[]{:S(2)}, u32[]{:S(2)}) %collective-permute-start.26) | collective-permute-done | bytes 262176 | tf_op jit(solution)/shard_map/ppermute | solution.py:285
  180.4 1.4 add_convert_fusion.1
  182.6 1.5 add_convert_fusion
  (124 shorter events, 25.6 us)
Async XLA Ops:
  0.6 12.3 %copy-start = (f32[256,256]{1,0:T(8,128)S(1)}, f32[256,256]{1,0:T(8,128)}, u32[]{:S(2)}) copy-start(f32[256,256]{1,0:T(8,128)} %param.10) | copy-start | bytes 786436
  2.0 2.4 %collective-permute-start.1 = (bf16[1024,256]{1,0:T(8,128)(2,1)S(1)}, bf16[1024,256]{1,0:T(8,128)(2,1)}, u32[]{:S(2)}, u32[]{:S(2)}) collective-permute-start(bf16[1024,256]{1,0:T(8,128)(2,1)S(1)} %get-tuple-element.84), channel_id=1, source_target_pairs={{0,1},{1,0},{2,3},{3,2},{4,5},{5,4},{6,7},{7,6},{8,9},{9,8},{10,11... | collective-permute-start | bytes 1572872 | tf_op jit(solution)/shard_map/ppermute | solution.py:312
  2.7 9.4 %copy-start.17 = (f32[16,4,2]{0,2,1:T(2,128)S(1)}, f32[16,4,2]{0,2,1:T(2,128)}, u32[]{:S(2)}) copy-start(f32[16,4,2]{0,2,1:T(2,128)} %param.11) | copy-start | bytes 1540
  2.7 9.5 %copy-start.18 = (f32[16,4,2]{0,2,1:T(2,128)S(1)}, f32[16,4,2]{0,2,1:T(2,128)}, u32[]{:S(2)}) copy-start(f32[16,4,2]{0,2,1:T(2,128)} %param.13) | copy-start | bytes 1540
  2.7 10.1 %copy-start.13 = (s32[16,4,2]{0,2,1:T(2,128)S(1)}, s32[16,4,2]{0,2,1:T(2,128)}, u32[]{:S(2)}) copy-start(s32[16,4,2]{0,2,1:T(2,128)} %param.14) | copy-start | bytes 1540
  2.8 10.4 %copy-start.14 = (s32[16,4,2]{0,2,1:T(2,128)S(1)}, s32[16,4,2]{0,2,1:T(2,128)}, u32[]{:S(2)}) copy-start(s32[16,4,2]{0,2,1:T(2,128)} %param.12) | copy-start | bytes 1540
  2.8 21.6 %copy-start.1 = (bf16[512,1024]{1,0:T(8,128)(2,1)S(1)}, bf16[512,1024]{1,0:T(8,128)(2,1)}, u32[]{:S(2)}) copy-start(bf16[512,1024]{1,0:T(8,128)(2,1)} %param.8) | copy-start | bytes 3145732
  5.5 19.3 %collective-permute-start.3 = (bf16[2048,128]{1,0:T(8,128)(2,1)S(1)}, bf16[2048,128]{1,0:T(8,128)(2,1)S(1)}, u32[]{:S(2)}, u32[]{:S(2)}) collective-permute-start(bf16[2048,128]{1,0:T(8,128)(2,1)S(1)} %get-tuple-element.43), channel_id=1, source_target_pairs={{0,32},{1,9},{2,34},{3,11},{4,36},{5,13},{6,38},{7,15},{8,40},{9,1... | collective-permute-start | bytes 1572872 | tf_op jit(solution)/shard_map/ppermute | solution.py:43
  7.3 26.6 %collective-permute-start.2 = (bf16[2048,128]{1,0:T(8,128)(2,1)S(1)}, bf16[2048,128]{1,0:T(8,128)(2,1)S(1)}, u32[]{:S(2)}, u32[]{:S(2)}) collective-permute-start(bf16[2048,128]{1,0:T(8,128)(2,1)S(1)} %get-tuple-element.43), channel_id=1, source_target_pairs={{0,96},{1,25},{2,98},{3,27},{4,100},{5,29},{6,102},{7,31},{8,104},... | collective-permute-start | bytes 1572872 | tf_op jit(solution)/shard_map/ppermute | solution.py:43
  9.5 17.0 %collective-permute-start.7 = (bf16[2048,128]{1,0:T(8,128)(2,1)S(1)}, bf16[2048,128]{1,0:T(8,128)(2,1)}, u32[]{:S(2)}, u32[]{:S(2)}) collective-permute-start(bf16[2048,128]{1,0:T(8,128)(2,1)S(1)} %get-tuple-element.44), channel_id=1, source_target_pairs={{0,32},{1,9},{2,34},{3,11},{4,36},{5,13},{6,38},{7,15},{8,40},{9,1... | collective-permute-start | bytes 1572872 | tf_op jit(solution)/shard_map/ppermute | solution.py:43
  9.5 12.0 %collective-permute-start.5 = (bf16[2048,128]{1,0:T(8,128)(2,1)S(1)}, bf16[2048,128]{1,0:T(8,128)(2,1)}, u32[]{:S(2)}, u32[]{:S(2)}) collective-permute-start(bf16[2048,128]{1,0:T(8,128)(2,1)S(1)} %get-tuple-element.44), channel_id=1, source_target_pairs={{0,96},{1,25},{2,98},{3,27},{4,100},{5,29},{6,102},{7,31},{8,104},... | collective-permute-start | bytes 1572872 | tf_op jit(solution)/shard_map/ppermute | solution.py:43
  13.2 17.6 %copy-start.9 = (bf16[4,2,8,256]{3,2,0,1:T(8,128)(2,1)}, bf16[4,2,8,256]{3,2,0,1:T(8,128)(2,1)S(1)}, u32[]{:S(2)}) copy-start(bf16[4,2,8,256]{3,2,0,1:T(8,128)(2,1)S(1)} %copy.45) | copy-start | bytes 98308
  13.6 17.3 %copy-start.3 = (bf16[4,2,8,256]{3,2,0,1:T(8,128)(2,1)}, bf16[4,2,8,256]{3,2,0,1:T(8,128)(2,1)S(1)}, u32[]{:S(2)}) copy-start(bf16[4,2,8,256]{3,2,0,1:T(8,128)(2,1)S(1)} %copy.44) | copy-start | bytes 98308
  21.5 9.4 %collective-permute-start.6 = (bf16[2048,128]{1,0:T(8,128)(2,1)}, bf16[2048,128]{1,0:T(8,128)(2,1)S(1)}, u32[]{:S(2)}, u32[]{:S(2)}) collective-permute-start(bf16[2048,128]{1,0:T(8,128)(2,1)} %collective-permute-done.5), channel_id=1, source_target_pairs={{0,96},{1,25},{2,98},{3,27},{4,100},{5,29},{6,102},{7,31},{8,104},... | collective-permute-start | bytes 1572872 | tf_op jit(solution)/shard_map/ppermute | solution.py:43
  24.8 9.3 %collective-permute-start.4 = (bf16[2048,128]{1,0:T(8,128)(2,1)S(1)}, bf16[2048,128]{1,0:T(8,128)(2,1)S(1)}, u32[]{:S(2)}, u32[]{:S(2)}) collective-permute-start(bf16[2048,128]{1,0:T(8,128)(2,1)S(1)} %collective-permute-done.3), channel_id=1, source_target_pairs={{0,32},{1,9},{2,34},{3,11},{4,36},{5,13},{6,38},{7,15},{8,40},{9,1... | collective-permute-start | bytes 1572872 | tf_op jit(solution)/shard_map/ppermute | solution.py:43
  33.6 35.3 %collective-permute-start.12 = (bf16[4,2048,128]{2,1,0:T(8,128)(2,1)}, bf16[4,2048,128]{2,1,0:T(8,128)(2,1)}, u32[]{:S(2)}, u32[]{:S(2)}) collective-permute-start(bf16[4,2048,128]{2,1,0:T(8,128)(2,1)} %pad_maximum_fusion.1.refs_1_), channel_id=1, source_target_pairs={{0,24},{1,97},{2,26},{3,99},{4,28},{5,101},{6,30},{7,103},{8,0},{9... | collective-permute-start | bytes 6291464 | tf_op jit(solution)/shard_map/ppermute | solution.py:43
  35.7 33.3 %collective-permute-start.11 = (bf16[4,2048,128]{2,1,0:T(8,128)(2,1)}, bf16[4,2048,128]{2,1,0:T(8,128)(2,1)}, u32[]{:S(2)}, u32[]{:S(2)}) collective-permute-start(bf16[4,2048,128]{2,1,0:T(8,128)(2,1)} %pad_maximum_fusion.refs_0_), channel_id=1, source_target_pairs={{0,8},{1,33},{2,10},{3,35},{4,12},{5,37},{6,14},{7,39},{8,16},{9,4... | collective-permute-start | bytes 6291464 | tf_op jit(solution)/shard_map/ppermute | solution.py:43
  36.9 11.7 %collective-permute-start = (bf16[512,1024]{1,0:T(8,128)(2,1)S(1)}, bf16[512,1024]{1,0:T(8,128)(2,1)}, u32[]{:S(2)}, u32[]{:S(2)}) collective-permute-start(bf16[512,1024]{1,0:T(8,128)(2,1)S(1)} %copy-done.1), channel_id=1, source_target_pairs={{0,1},{1,0},{2,3},{3,2},{4,5},{5,4},{6,7},{7,6},{8,9},{9,8},{10,11... | collective-permute-start | bytes 3145736 | tf_op jit(solution)/shard_map/ppermute | solution.py:332
  39.9 2.2 %collective-permute-start.8 = (f32[32,512]{1,0:T(8,128)S(1)}, f32[32,512]{1,0:T(8,128)S(1)}, u32[]{:S(2)}, u32[]{:S(2)}) collective-permute-start(f32[32,512]{1,0:T(8,128)S(1)} %pad_maximum_fusion.4), channel_id=1, source_target_pairs={{0,1},{1,0},{2,3},{3,2},{4,5},{5,4},{6,7},{7,6},{8,9},{9,8},{10,11... | collective-permute-start | bytes 196616 | tf_op jit(solution)/shard_map/ppermute | solution.py:61
  42.8 3.9 %collective-permute-start.9 = (f32[32,512]{1,0:T(8,128)S(1)}, f32[32,512]{1,0:T(8,128)S(1)}, u32[]{:S(2)}, u32[]{:S(2)}) collective-permute-start(f32[32,512]{1,0:T(8,128)S(1)} %add.383), channel_id=1, source_target_pairs={{0,2},{1,3},{2,0},{3,1},{4,6},{5,7},{6,4},{7,5},{8,10},{9,11},{10,... | collective-permute-start | bytes 196616 | tf_op jit(solution)/shard_map/ppermute | solution.py:61
  44.1 40.0 %collective-permute-start.14 = (bf16[4,2048,128]{2,1,0:T(8,128)(2,1)}, bf16[4,2048,128]{2,1,0:T(8,128)(2,1)}, u32[]{:S(2)}, u32[]{:S(2)}) collective-permute-start(bf16[4,2048,128]{2,1,0:T(8,128)(2,1)} %pad_maximum_fusion.1.refs_1_), channel_id=1, source_target_pairs={{0,8},{1,33},{2,10},{3,35},{4,12},{5,37},{6,14},{7,39},{8,16},{9,4... | collective-permute-start | bytes 6291464 | tf_op jit(solution)/shard_map/ppermute | solution.py:43
  47.3 36.7 %collective-permute-start.13 = (bf16[4,2048,128]{2,1,0:T(8,128)(2,1)}, bf16[4,2048,128]{2,1,0:T(8,128)(2,1)}, u32[]{:S(2)}, u32[]{:S(2)}) collective-permute-start(bf16[4,2048,128]{2,1,0:T(8,128)(2,1)} %pad_maximum_fusion.refs_0_), channel_id=1, source_target_pairs={{0,24},{1,97},{2,26},{3,99},{4,28},{5,101},{6,30},{7,103},{8,0},{9... | collective-permute-start | bytes 6291464 | tf_op jit(solution)/shard_map/ppermute | solution.py:43
  48.5 9.3 %collective-permute-start.10 = (f32[32,512]{1,0:T(8,128)S(1)}, f32[32,512]{1,0:T(8,128)S(1)}, u32[]{:S(2)}, u32[]{:S(2)}) collective-permute-start(f32[32,512]{1,0:T(8,128)S(1)} %add.384), channel_id=1, source_target_pairs={{0,4},{1,5},{2,6},{3,7},{4,0},{5,1},{6,2},{7,3},{8,12},{9,13},{10,... | collective-permute-start | bytes 196616 | tf_op jit(solution)/shard_map/ppermute | solution.py:61
  58.5 17.6 %all-to-all-start = ((bf16[4,512,256]{2,1,0:T(8,128)(2,1)}), bf16[4,512,256]{2,1,0:T(8,128)(2,1)S(1)}, u32[]{:S(2)}, u32[]{:S(2)}) async-start(bf16[4,512,256]{2,1,0:T(8,128)(2,1)} %forward.4), calls=%async_computation | async-start | bytes 2097152 | tf_op jit(solution)/shard_map/all_to_all | solution.py:54
  69.0 51.3 %collective-permute-start.19 = (bf16[4,2048,128]{2,1,0:T(8,128)(2,1)}, bf16[4,2048,128]{2,1,0:T(8,128)(2,1)}, u32[]{:S(2)}, u32[]{:S(2)}) collective-permute-start(bf16[4,2048,128]{2,1,0:T(8,128)(2,1)} %collective-permute-done.11.refs_0_), channel_id=1, source_target_pairs={{0,8},{1,33},{2,10},{3,35},{4,12},{5,37},{6,14},{7,39},{8,16},{9,4... | collective-permute-start | bytes 6291464 | tf_op jit(solution)/shard_map/ppermute | solution.py:43
  71.1 49.2 %collective-permute-start.20 = (bf16[4,2048,128]{2,1,0:T(8,128)(2,1)}, bf16[4,2048,128]{2,1,0:T(8,128)(2,1)}, u32[]{:S(2)}, u32[]{:S(2)}) collective-permute-start(bf16[4,2048,128]{2,1,0:T(8,128)(2,1)} %collective-permute-done.12.refs_1_), channel_id=1, source_target_pairs={{0,24},{1,97},{2,26},{3,99},{4,28},{5,101},{6,30},{7,103},{8,0},{9... | collective-permute-start | bytes 6291464 | tf_op jit(solution)/shard_map/ppermute | solution.py:43
  76.1 14.1 %all-to-all-start.1 = ((bf16[4,512,256]{2,1,0:T(8,128)(2,1)}), bf16[4,512,256]{2,1,0:T(8,128)(2,1)}, u32[]{:S(2)}, u32[]{:S(2)}) async-start(bf16[4,512,256]{2,1,0:T(8,128)(2,1)} %forward.5), calls=%async_computation.1 | async-start | bytes 2097152 | tf_op jit(solution)/shard_map/all_to_all | solution.py:54
  90.2 27.5 %all-to-all-start.2 = ((bf16[4,512,256]{2,1,0:T(8,128)(2,1)}), bf16[4,512,256]{2,1,0:T(8,128)(2,1)}, u32[]{:S(2)}, u32[]{:S(2)}) async-start(bf16[4,512,256]{2,1,0:T(8,128)(2,1)} %forward.6), calls=%async_computation.2 | async-start | bytes 2097152 | tf_op jit(solution)/shard_map/all_to_all | solution.py:54
  94.5 19.9 %collective-permute-start.17 = (f32[32,1024]{1,0:T(8,128)}, f32[32,1024]{1,0:T(8,128)}, u32[]{:S(2)}, u32[]{:S(2)}) collective-permute-start(f32[32,1024]{1,0:T(8,128)} %maximum_multiply_fusion), channel_id=1, source_target_pairs={{0,96},{1,97},{2,98},{3,99},{4,100},{5,101},{6,102},{7,103},{8,104... | collective-permute-start | bytes 393224 | tf_op jit(solution)/shard_map/ppermute | solution.py:72
  98.3 16.1 %collective-permute-start.16 = (f32[32,1024]{1,0:T(8,128)}, f32[32,1024]{1,0:T(8,128)}, u32[]{:S(2)}, u32[]{:S(2)}) collective-permute-start(f32[32,1024]{1,0:T(8,128)} %maximum_multiply_fusion), channel_id=1, source_target_pairs={{0,64},{1,65},{2,66},{3,67},{4,68},{5,69},{6,70},{7,71},{8,72},{9,... | collective-permute-start | bytes 393224 | tf_op jit(solution)/shard_map/ppermute | solution.py:72
  102.4 12.0 %collective-permute-start.15 = (f32[32,1024]{1,0:T(8,128)}, f32[32,1024]{1,0:T(8,128)}, u32[]{:S(2)}, u32[]{:S(2)}) collective-permute-start(f32[32,1024]{1,0:T(8,128)} %maximum_multiply_fusion), channel_id=1, source_target_pairs={{0,32},{1,33},{2,34},{3,35},{4,36},{5,37},{6,38},{7,39},{8,40},{9,... | collective-permute-start | bytes 393224 | tf_op jit(solution)/shard_map/ppermute | solution.py:72
  104.5 9.9 %copy-start.2 = (f32[32,1024]{1,0:T(8,128)S(1)}, f32[32,1024]{1,0:T(8,128)}, u32[]{:S(2)}) copy-start(f32[32,1024]{1,0:T(8,128)} %maximum_multiply_fusion) | copy-start | bytes 393220
  116.1 9.2 %collective-permute-start.28 = (f32[32,1024]{1,0:T(8,128)}, f32[32,1024]{1,0:T(8,128)}, u32[]{:S(2)}, u32[]{:S(2)}) collective-permute-start(f32[32,1024]{1,0:T(8,128)} %add_add_fusion), channel_id=1, source_target_pairs={{0,8},{8,0},{16,24},{24,16},{32,40},{40,32},{48,56},{56,48},{64,72... | collective-permute-start | bytes 393224 | tf_op jit(solution)/shard_map/ppermute | solution.py:82
  127.0 20.1 %collective-permute-start.29 = (f32[32,1024]{1,0:T(8,128)}, f32[32,1024]{1,0:T(8,128)}, u32[]{:S(2)}, u32[]{:S(2)}) collective-permute-start(f32[32,1024]{1,0:T(8,128)} %add.466), channel_id=1, source_target_pairs={{0,16},{8,24},{16,0},{24,8},{32,48},{40,56},{48,32},{56,40},{64,80... | collective-permute-start | bytes 393224 | tf_op jit(solution)/shard_map/ppermute | solution.py:82
  131.1 23.0 %all-to-all-start.3 = ((bf16[4,512,256]{2,1,0:T(8,128)(2,1)}), bf16[4,512,256]{2,1,0:T(8,128)(2,1)}, u32[]{:S(2)}, u32[]{:S(2)}) async-start(bf16[4,512,256]{2,1,0:T(8,128)(2,1)} %arrange.1), calls=%async_computation.3 | async-start | bytes 2097152 | tf_op jit(solution)/shard_map/all_to_all | solution.py:54
  135.4 26.5 %collective-permute-start.21 = (bf16[512,256]{1,0:T(8,128)(2,1)}, bf16[512,256]{1,0:T(8,128)(2,1)}, u32[]{:S(2)}, u32[]{:S(2)}) collective-permute-start(bf16[512,256]{1,0:T(8,128)(2,1)} %get-tuple-element.69), channel_id=1, source_target_pairs={{0,2},{1,3},{2,4},{3,5},{4,6},{5,7},{6,0},{7,1},{8,10},{9,11},{10,... | collective-permute-start | bytes 786440 | tf_op jit(solution)/shard_map/ppermute | solution.py:390
  136.8 25.3 %collective-permute-start.22 = (bf16[512,256]{1,0:T(8,128)(2,1)}, bf16[512,256]{1,0:T(8,128)(2,1)}, u32[]{:S(2)}, u32[]{:S(2)}) collective-permute-start(bf16[512,256]{1,0:T(8,128)(2,1)} %get-tuple-element.70), channel_id=1, source_target_pairs={{0,4},{1,5},{2,6},{3,7},{4,0},{5,1},{6,2},{7,3},{8,12},{9,13},{10,... | collective-permute-start | bytes 786440 | tf_op jit(solution)/shard_map/ppermute | solution.py:390
  139.2 22.9 %collective-permute-start.23 = (bf16[512,256]{1,0:T(8,128)(2,1)}, bf16[512,256]{1,0:T(8,128)(2,1)}, u32[]{:S(2)}, u32[]{:S(2)}) collective-permute-start(bf16[512,256]{1,0:T(8,128)(2,1)} %get-tuple-element.71), channel_id=1, source_target_pairs={{0,6},{1,7},{2,0},{3,1},{4,2},{5,3},{6,4},{7,5},{8,14},{9,15},{10,... | collective-permute-start | bytes 786440 | tf_op jit(solution)/shard_map/ppermute | solution.py:390
  149.6 6.1 %collective-permute-start.30 = (f32[256,256]{1,0:T(8,128)}, f32[256,256]{1,0:T(8,128)}, u32[]{:S(2)}, u32[]{:S(2)}) collective-permute-start(f32[256,256]{1,0:T(8,128)} %fusion.2), channel_id=1, source_target_pairs={{0,1},{1,0},{2,3},{3,2},{4,5},{5,4},{6,7},{7,6},{8,9},{9,8},{10,11... | collective-permute-start | bytes 786440 | tf_op jit(solution)/shard_map/ppermute | solution.py:61
  154.1 8.1 %copy-start.5 = (bf16[512,256]{1,0:T(8,128)(2,1)S(1)}, bf16[512,256]{1,0:T(8,128)(2,1)}, u32[]{:S(2)}) copy-start(bf16[512,256]{1,0:T(8,128)(2,1)} %get-tuple-element.74) | copy-start | bytes 786436
  155.4 13.8 %collective-permute-start.18 = (bf16[2,512,256]{2,1,0:T(8,128)(2,1)S(1)}, bf16[2,512,256]{2,1,0:T(8,128)(2,1)S(1)}, u32[]{:S(2)}, u32[]{:S(2)}) collective-permute-start(bf16[2,512,256]{2,1,0:T(8,128)(2,1)S(1)} %slice_select_fusion.1), channel_id=1, source_target_pairs={{0,1},{1,0},{2,3},{3,2},{4,5},{5,4},{6,7},{7,6},{8,9},{9,8},{10,11... | collective-permute-start | bytes 1572872 | tf_op jit(solution)/shard_map/ppermute | solution.py:401
  156.8 11.2 %collective-permute-start.31 = (f32[256,256]{1,0:T(8,128)S(1)}, f32[256,256]{1,0:T(8,128)S(1)}, u32[]{:S(2)}, u32[]{:S(2)}) collective-permute-start(f32[256,256]{1,0:T(8,128)S(1)} %add.469), channel_id=1, source_target_pairs={{0,2},{1,3},{2,0},{3,1},{4,6},{5,7},{6,4},{7,5},{8,10},{9,11},{10,... | collective-permute-start | bytes 786440 | tf_op jit(solution)/shard_map/ppermute | solution.py:61
  161.9 20.7 %collective-permute-start.27 = (bf16[512,1024]{1,0:T(8,128)(2,1)S(1)}, bf16[512,1024]{1,0:T(8,128)(2,1)S(1)}, u32[]{:S(2)}, u32[]{:S(2)}) collective-permute-start(bf16[512,1024]{1,0:T(8,128)(2,1)S(1)} %get-tuple-element.73), channel_id=1, source_target_pairs={{0,1},{1,0},{2,3},{3,2},{4,5},{5,4},{6,7},{7,6},{8,9},{9,8},{10,11... | collective-permute-start | bytes 3145736 | tf_op jit(solution)/shard_map/ppermute | solution.py:415
  163.4 16.8 %collective-permute-start.26 = (bf16[512,256]{1,0:T(8,128)(2,1)S(1)}, bf16[512,256]{1,0:T(8,128)(2,1)S(1)}, u32[]{:S(2)}, u32[]{:S(2)}) collective-permute-start(bf16[512,256]{1,0:T(8,128)(2,1)S(1)} %add_convert_fusion.2), channel_id=1, source_target_pairs={{3,4},{7,5},{11,12},{15,13},{19,20},{23,21},{27,28},{31,29},{35,38... | collective-permute-start | bytes 786440 | tf_op jit(solution)/shard_map/ppermute | solution.py:285
  164.7 15.5 %collective-permute-start.25 = (bf16[512,256]{1,0:T(8,128)(2,1)S(1)}, bf16[512,256]{1,0:T(8,128)(2,1)S(1)}, u32[]{:S(2)}, u32[]{:S(2)}) collective-permute-start(bf16[512,256]{1,0:T(8,128)(2,1)S(1)} %add_convert_fusion.2), channel_id=1, source_target_pairs={{1,4},{5,5},{9,12},{13,13},{17,20},{21,21},{25,28},{29,29},{33,38}... | collective-permute-start | bytes 786440 | tf_op jit(solution)/shard_map/ppermute | solution.py:285
  167.9 12.3 %collective-permute-start.24 = (bf16[512,256]{1,0:T(8,128)(2,1)S(1)}, bf16[512,256]{1,0:T(8,128)(2,1)S(1)}, u32[]{:S(2)}, u32[]{:S(2)}) collective-permute-start(bf16[512,256]{1,0:T(8,128)(2,1)S(1)} %add_convert_fusion.2), channel_id=1, source_target_pairs={{0,1},{2,3},{4,5},{6,7},{8,9},{10,11},{12,13},{14,15},{32,33},{34,... | collective-permute-start | bytes 786440 | tf_op jit(solution)/shard_map/ppermute | solution.py:290
  169.3 12.5 %collective-permute-start.32 = (f32[256,256]{1,0:T(8,128)S(1)}, f32[256,256]{1,0:T(8,128)S(1)}, u32[]{:S(2)}, u32[]{:S(2)}) collective-permute-start(f32[256,256]{1,0:T(8,128)S(1)} %add.470), channel_id=1, source_target_pairs={{0,4},{1,5},{2,6},{3,7},{4,0},{5,1},{6,2},{7,3},{8,12},{9,13},{10,... | collective-permute-start | bytes 786440 | tf_op jit(solution)/shard_map/ppermute | solution.py:61
  172.4 8.0 %copy-start.8 = (bf16[32,512]{1,0:T(8,128)(2,1)S(1)}, bf16[32,512]{1,0:T(8,128)(2,1)}, u32[]{:S(2)}) copy-start(bf16[32,512]{1,0:T(8,128)(2,1)} %add_convert_fusion.3) | copy-start | bytes 98308
  (8 other events, 19.8 us)

commit v11 on v9

--- a/solution.py
+++ b/solution.py
@@ -382,22 +382,24 @@
     slots = arrange(
         far.astype(jnp.int32).reshape(1), slots_here, slots_first, after(slots_second, grown, both)
     )
-    both = with_partner(both, 1, slots)
     moved = exchange(slots, "tensor", LANES)
-    sent = forward(after(turned_here, slots, both), wide, take(across), apart=True)
+    sent = forward(after(turned_here, slots), wide, take(across), apart=True)
     arrived = [sent[0]]
     for step in range(1, SIDE):
         turns = [(t, (t + 2 * step) % 8) for t in range(8)]
         arrived.append(lax.ppermute(sent[step], "tensor", turns))
-    piece = total_of([a.astype(f32) for a in arrived]).astype(bf16)
-    both = with_partner(both, 2, *sent)
+    both = with_partner(both, 1, *sent)
+    both = with_partner(both, 2)
     bank_a, logit_grad_a = compose_back(both[:rank], weights_a, picked_a, mixing_a, vector_bank)
     bank_b, logit_grad_b = compose_back(both[rank:], weights_b, picked_b, mixing_b, vector_bank)
-    bank_part = over_tensor(bank_a + bank_b, (1, 2))
+    bank_part = bank_a + bank_b
     grown, other = backward(
         after(spots_of(across), *sent, bank_part), grown, out_grad, take(across), last=True
     )
-    bank_grad = over_tensor(bank_part, (4,))
+    moved, *arrived = lax.optimization_barrier((moved, *arrived, other))[: SIDE + 1]
+    piece = total_of([a.astype(f32) for a in arrived]).astype(bf16)
+    bank_part = bank_part + after(lax.ppermute(bank_part, "tensor", SWAP), other)
+    bank_grad = over_tensor(bank_part, (2, 4))
     crossed = lax.ppermute(jnp.where(core == 0, slots[2:], moved[:2]), "tensor", SWAP)
     firsts = jnp.where(core == 0, slots[:2], crossed)
     seconds = jnp.where(core == 0, crossed, moved[2:])

time: 181 us -> 189 us (1.044); the launches traced: 180 us -> 186 us
  waiting for transfers between devices: 33.7 us -> 36.5 us
  matrix products: 9.9 us -> 11.8 us
    ppermute x6 -> x5, waiting for transfers between devices: 3.98 us -> 9.48 us  [over_tensor(): lax.ppermute(value, 'tensor', [(t, t ^ bit) for t in range(8)])]
    ppermute x0 -> x1, starting transfers between devices: none -> 2.93 us  [local(): lax.ppermute(bank_part, 'tensor', SWAP)]
    ppermute x6 -> x5, starting transfers between devices: 7.54 us -> 5.41 us  [over_tensor(): lax.ppermute(value, 'tensor', [(t, t ^ bit) for t in range(8)])]
    ppermute x2, waiting for transfers between devices: 1.91 us -> 0.01 us  [with_partner(): other = lax.ppermute(value, 'dp', [(d, d ^ bit) for d in range(16)])]
  transfers between devices with their start and end apart: 37 -> 37, of which waited for: 10 -> 11; matrix products, arithmetic and copies ran while one was open for 14% -> 14% of each run, Pallas kernels for 25% -> 24%
where the time goes in v11:
time: 189 us; the launch traced here: 186 us
  starting transfers between devices  67.6 us (36%)
  Pallas kernels  45.7 us (24%)
  waiting for transfers between devices  36.5 us (19%)
  other arithmetic  17.3 us (9%)
  matrix products  11.8 us (6%)
  local copies, waits for them, and re-layouts  6.1 us (3%)
    pallas_call x3, Pallas kernels, backward(): pl.pallas_call(functools.partial(backward_kernel, count, first, last), ou...  23.2 us
    pallas_call x4, Pallas kernels, forward(): pl.pallas_call(functools.partial(forward_kernel, count, many), out_shape=...  19.9 us
    ppermute x12, starting transfers between devices, shift(): return lax.ppermute(value, BOTH, ring(stage, step))  19.1 us
    all_to_all x4, starting transfers between devices, exchange(): lax.all_to_all(value, axis, split_axis=0, concat_axis=0, tiled=True, axis...  16.5 us
    ppermute x12, waiting for transfers between devices, shift(): return lax.ppermute(value, BOTH, ring(stage, step))  12.3 us
    ppermute x5, waiting for transfers between devices, over_tensor(): lax.ppermute(value, 'tensor', [(t, t ^ bit) for t in range(8)])  9.48 us
    ppermute x3, waiting for transfers between devices, local(): arrived.append(lax.ppermute(sent[step], 'tensor', turns))  6.86 us
    ppermute x5, starting transfers between devices, over_tensor(): lax.ppermute(value, 'tensor', [(t, t ^ bit) for t in range(8)])  5.41 us
  transfers between devices with their start and end apart: 37, of which 11 were waited for; matrix products, arithmetic and copies ran while one was open for 14% of the time, Pallas kernels for 24%

profile of v11, /device:TPU:1, one launch (start us, length us, event | category | flops | bytes accessed | tf_op | source)
XLA Modules:
  0.0 186.5 jit_solution(17121416643553244444)
XLA Ops:
  0.7 1.3 broadcast_select_fusion.1
  2.0 1.5 collective-permute-start.1
  3.5 1.6 collective-permute-done.1
  6.3 1.8 collective-permute-start.3
  8.1 2.2 %collective-permute-start.2 = (bf16[2048,128]{1,0:T(8,128)(2,1)S(1)}, bf16[2048,128]{1,0:T(8,128)(2,1)S(1)}, u32[]{:S(2)}, u32[]{:S(2)}) collective-permute-start(bf16[2048,128]{1,0:T(8,128)(2,1)S(1)} %get-tuple-element.44), channel_id=1, source_target_pairs={{0,96},{1,25},{2,98},{3,27},{4,100},{5,29},{6,102},{7,31},{8,104},... | collective-permute-start | bytes 1572872 | tf_op jit(solution)/shard_map/ppermute | solution.py:43
  10.3 2.7 %collective-permute-start.5 = (bf16[2048,128]{1,0:T(8,128)(2,1)S(1)}, bf16[2048,128]{1,0:T(8,128)(2,1)}, u32[]{:S(2)}, u32[]{:S(2)}) collective-permute-start(bf16[2048,128]{1,0:T(8,128)(2,1)S(1)} %get-tuple-element.45), channel_id=1, source_target_pairs={{0,96},{1,25},{2,98},{3,27},{4,100},{5,29},{6,102},{7,31},{8,104},... | collective-permute-start | bytes 1572872 | tf_op jit(solution)/shard_map/ppermute | solution.py:43
  14.5 7.9 %collective-permute-done.5 = bf16[2048,128]{1,0:T(8,128)(2,1)} collective-permute-done((bf16[2048,128]{1,0:T(8,128)(2,1)S(1)}, bf16[2048,128]{1,0:T(8,128)(2,1)}, u32[]{:S(2)}, u32[]{:S(2)}) %collective-permute-start.5) | collective-permute-done | bytes 524320 | tf_op jit(solution)/shard_map/ppermute | solution.py:43
  22.3 3.2 %collective-permute-start.6 = (bf16[2048,128]{1,0:T(8,128)(2,1)}, bf16[2048,128]{1,0:T(8,128)(2,1)S(1)}, u32[]{:S(2)}, u32[]{:S(2)}) collective-permute-start(bf16[2048,128]{1,0:T(8,128)(2,1)} %collective-permute-done.5), channel_id=1, source_target_pairs={{0,96},{1,25},{2,98},{3,27},{4,100},{5,29},{6,102},{7,31},{8,104},... | collective-permute-start | bytes 1572872 | tf_op jit(solution)/shard_map/ppermute | solution.py:43
  25.9 1.6 fusion.11
  27.6 4.4 %collective-permute-done.6 = bf16[2048,128]{1,0:T(8,128)(2,1)S(1)} collective-permute-done((bf16[2048,128]{1,0:T(8,128)(2,1)}, bf16[2048,128]{1,0:T(8,128)(2,1)S(1)}, u32[]{:S(2)}, u32[]{:S(2)}) %collective-permute-start.6) | collective-permute-done | bytes 524320 | tf_op jit(solution)/shard_map/ppermute | solution.py:43
  32.0 2.8 %pad_maximum_fusion.1.refs_1_ = bf16[4,2048,128]{2,1,0:T(8,128)(2,1)} fusion(bf16[1,2048,128]{2,1,0:T(8,128)(2,1)} %bitcast.9, bf16[1,2048,128]{2,1,0:T(8,128)(2,1)S(1)} %bitcast.111, bf16[1,2048,128]{2,1,0:T(8,128)(2,1)} %bitcast.7, bf16[1,2048,128]{2,1,0:T(8,128)(2,1)S(1)} %bitcast.103), kind=kLoop, calls=%fused_computation.3 | loop fusion | flops 3145728 | bytes 4194304 | tf_op jit(solution)/shard_map/stack | solution.py:318
  34.8 2.5 %collective-permute-start.12 = (bf16[4,2048,128]{2,1,0:T(8,128)(2,1)}, bf16[4,2048,128]{2,1,0:T(8,128)(2,1)}, u32[]{:S(2)}, u32[]{:S(2)}) collective-permute-start(bf16[4,2048,128]{2,1,0:T(8,128)(2,1)} %pad_maximum_fusion.1.refs_1_), channel_id=1, source_target_pairs={{0,24},{1,97},{2,26},{3,99},{4,28},{5,101},{6,30},{7,103},{8,0},{9... | collective-permute-start | bytes 6291464 | tf_op jit(solution)/shard_map/ppermute | solution.py:43
  37.2 1.6 pad_maximum_fusion.refs_0_
  38.8 2.8 %collective-permute-start = (bf16[512,1024]{1,0:T(8,128)(2,1)S(1)}, bf16[512,1024]{1,0:T(8,128)(2,1)}, u32[]{:S(2)}, u32[]{:S(2)}) collective-permute-start(bf16[512,1024]{1,0:T(8,128)(2,1)S(1)} %copy-done.1), channel_id=1, source_target_pairs={{0,1},{1,0},{2,3},{3,2},{4,5},{5,4},{6,7},{7,6},{8,9},{9,8},{10,11... | collective-permute-start | bytes 3145736 | tf_op jit(solution)/shard_map/ppermute | solution.py:332
  41.6 2.2 %collective-permute-done.8 = f32[32,512]{1,0:T(8,128)S(1)} collective-permute-done((f32[32,512]{1,0:T(8,128)S(1)}, f32[32,512]{1,0:T(8,128)S(1)}, u32[]{:S(2)}, u32[]{:S(2)}) %collective-permute-start.8) | collective-permute-done | bytes 65568 | tf_op jit(solution)/shard_map/ppermute | solution.py:61
  46.4 1.7 collective-permute-done.9
  48.8 3.3 %collective-permute-start.13 = (bf16[4,2048,128]{2,1,0:T(8,128)(2,1)}, bf16[4,2048,128]{2,1,0:T(8,128)(2,1)}, u32[]{:S(2)}, u32[]{:S(2)}) collective-permute-start(bf16[4,2048,128]{2,1,0:T(8,128)(2,1)} %pad_maximum_fusion.refs_0_), channel_id=1, source_target_pairs={{0,24},{1,97},{2,26},{3,99},{4,28},{5,101},{6,30},{7,103},{8,0},{9... | collective-permute-start | bytes 6291464 | tf_op jit(solution)/shard_map/ppermute | solution.py:43
  53.0 3.0 %collective-permute-start.10 = (f32[32,512]{1,0:T(8,128)S(1)}, f32[32,512]{1,0:T(8,128)S(1)}, u32[]{:S(2)}, u32[]{:S(2)}) collective-permute-start(f32[32,512]{1,0:T(8,128)S(1)} %add.384), channel_id=1, source_target_pairs={{0,4},{1,5},{2,6},{3,7},{4,0},{5,1},{6,2},{7,3},{8,12},{9,13},{10,... | collective-permute-start | bytes 196616 | tf_op jit(solution)/shard_map/ppermute | solution.py:61
  57.3 5.0 %forward.4 = bf16[4,512,256]{2,1,0:T(8,128)(2,1)} custom-call(s32[1]{0:T(128)} %bitcast.1.start_ref, bf16[512,2048]{1,0:T(8,128)(2,1)S(1)} %constant_dynamic-update-slice_fusion.wide_ref, bf16[4,2048,128]{2,1,0:T(8,128)(2,1)} %pad_maximum_fusion.refs_0_, bf16[4,2048,128]{2,1,0:T(8,128)(2,1)} %pad_maximum_fusion.1.refs_1_), custom_call_target="tpu_custom_call" | custom-call | flops 268435456 | bytes 524288 | tf_op jit(solution)/shard_map/forward/pallas_call | solution.py:131
  62.9 3.5 %all-to-all-start = ((bf16[4,512,256]{2,1,0:T(8,128)(2,1)}), bf16[4,512,256]{2,1,0:T(8,128)(2,1)S(1)}, u32[]{:S(2)}, u32[]{:S(2)}) async-start(bf16[4,512,256]{2,1,0:T(8,128)(2,1)} %forward.4), calls=%async_computation | async-start | bytes 2097152 | tf_op jit(solution)/shard_map/all_to_all | solution.py:54
  66.7 6.8 %backward.3.refs_20_ = bf16[512,2048]{1,0:T(8,128)(2,1)} custom-call(s32[8]{0:T(128)S(1)} %stack.153.spots_ref, bf16[4,2048,128]{2,1,0:T(8,128)(2,1)} %pad_maximum_fusion.refs_0_, bf16[4,2048,128]{2,1,0:T(8,128)(2,1)} %pad_maximum_fusion.1.refs_1_, bf16[512,8192]{1,0:T(8,128)(2,1)} %refs_9_.5, bf16[512,8192]{1,0:T(8,128)(2,1)} %refs_9_.5, ...), custom_call_target="tpu_custom_call" | custom-call | flops 268435456 | bytes 524288 | tf_op jit(solution)/shard_map/backward/pallas_call | solution.py:237
  73.5 2.7 %collective-permute-start.19 = (bf16[4,2048,128]{2,1,0:T(8,128)(2,1)}, bf16[4,2048,128]{2,1,0:T(8,128)(2,1)}, u32[]{:S(2)}, u32[]{:S(2)}) collective-permute-start(bf16[4,2048,128]{2,1,0:T(8,128)(2,1)} %collective-permute-done.12.refs_1_), channel_id=1, source_target_pairs={{0,24},{1,97},{2,26},{3,99},{4,28},{5,101},{6,30},{7,103},{8,0},{9... | collective-permute-start | bytes 6291464 | tf_op jit(solution)/shard_map/ppermute | solution.py:43
  76.2 4.9 %forward.5 = bf16[4,512,256]{2,1,0:T(8,128)(2,1)} custom-call(s32[1]{0:T(128)} %bitcast.1.start_ref, bf16[512,2048]{1,0:T(8,128)(2,1)S(1)} %constant_dynamic-update-slice_fusion.wide_ref, bf16[4,2048,128]{2,1,0:T(8,128)(2,1)} %collective-permute-done.11.refs_0_, bf16[4,2048,128]{2,1,0:T(8,128)(2,1)} %collective-permute-done.12.refs_1_), custom_call_target="tpu_custom_call" | custom-call | flops 268435456 | bytes 524288 | tf_op jit(solution)/shard_map/forward/pallas_call | solution.py:131
  81.1 4.3 %all-to-all-start.1 = ((bf16[4,512,256]{2,1,0:T(8,128)(2,1)}), bf16[4,512,256]{2,1,0:T(8,128)(2,1)}, u32[]{:S(2)}, u32[]{:S(2)}) async-start(bf16[4,512,256]{2,1,0:T(8,128)(2,1)} %forward.5), calls=%async_computation.1 | async-start | bytes 2097152 | tf_op jit(solution)/shard_map/all_to_all | solution.py:54
  85.4 1.5 fusion.9
  86.9 1.5 fusion.32
  89.1 4.9 %forward.6 = bf16[4,512,256]{2,1,0:T(8,128)(2,1)} custom-call(s32[1]{0:T(128)} %bitcast.1.start_ref, bf16[512,2048]{1,0:T(8,128)(2,1)S(1)} %constant_dynamic-update-slice_fusion.wide_ref, bf16[4,2048,128]{2,1,0:T(8,128)(2,1)} %collective-permute-done.13.refs_0_.refs_2_, bf16[4,2048,128]{2,1,0:T(8,128)(2,1)} %collective-permute-done.14.refs_1_.refs_3_), custom_call_target="tpu_custom_call" | custom-call | flops 268435456 | bytes 524288 | tf_op jit(solution)/shard_map/forward/pallas_call | solution.py:131
  94.0 4.6 %all-to-all-done.1.refs_0_ = bf16[4,512,256]{2,1,0:T(8,128)(2,1)} async-done(((bf16[4,512,256]{2,1,0:T(8,128)(2,1)}), bf16[4,512,256]{2,1,0:T(8,128)(2,1)}, u32[]{:S(2)}, u32[]{:S(2)}) %all-to-all-start.1) | async-done | bytes 1048608 | tf_op jit(solution)/shard_map/all_to_all | solution.py:54
  98.6 4.2 %all-to-all-start.2 = ((bf16[4,512,256]{2,1,0:T(8,128)(2,1)}), bf16[4,512,256]{2,1,0:T(8,128)(2,1)}, u32[]{:S(2)}, u32[]{:S(2)}) async-start(bf16[4,512,256]{2,1,0:T(8,128)(2,1)} %forward.6), calls=%async_computation.2 | async-start | bytes 2097152 | tf_op jit(solution)/shard_map/all_to_all | solution.py:54
  103.0 1.4 collective-permute-start.15
  104.5 9.9 %backward.4.refs_10_ = bf16[512,2048]{1,0:T(8,128)(2,1)} custom-call(s32[16]{0:T(128)S(1)} %stack.170.spots_ref, bf16[4,2048,128]{2,1,0:T(8,128)(2,1)} %collective-permute-done.11.refs_0_, bf16[4,2048,128]{2,1,0:T(8,128)(2,1)} %collective-permute-done.12.refs_1_, ...), custom_call_target="tpu_custom_call", output_to_operand_aliasing={{}: (21, {})} | custom-call | flops 536870912 | bytes 1048576 | tf_op jit(solution)/shard_map/backward/pallas_call | solution.py:237
  114.4 1.7 collective-permute-done.15
  116.1 1.7 add_add_fusion
  117.9 2.6 %arrange.1 = bf16[4,512,256]{2,1,0:T(8,128)(2,1)} custom-call(s32[1]{0:T(128)} %bitcast.far_ref, bf16[4,512,256]{2,1,0:T(8,128)(2,1)S(1)} %all-to-all-done.here_ref, bf16[4,512,256]{2,1,0:T(8,128)(2,1)} %all-to-all-done.1.refs_0_, bf16[4,512,256]{2,1,0:T(8,128)(2,1)} %all-to-all-done.2.refs_1_), custom_call_target="tpu_custom_call" | custom-call | flops 2097152 | bytes 4194304 | tf_op jit(solution)/shard_map/arrange/pallas_call | solution.py:178
  120.5 5.0 %forward.7 = (bf16[512,256]{1,0:T(8,128)(2,1)}, bf16[512,256]{1,0:T(8,128)(2,1)}, bf16[512,256]{1,0:T(8,128)(2,1)}, bf16[512,256]{1,0:T(8,128)(2,1)}) custom-call(s32[1]{0:T(128)} %bitcast.35.start_ref, bf16[512,2048]{1,0:T(8,128)(2,1)S(1)} %constant_dynamic-update-slice_fusion.wide_ref, bf16[4,2048,128]{2,1,0:T(8,128)(2,1)} %collective-permute-done.18.refs_0_, ...), custom_call_target="tpu_custom_call" | custom-call | flops 268435456 | bytes 524288 | tf_op jit(solution)/shard_map/forward/pallas_call | solution.py:131
  126.5 4.5 %collective-permute-start.24 = (f32[32,1024]{1,0:T(8,128)S(1)}, f32[32,1024]{1,0:T(8,128)S(1)}, u32[]{:S(2)}, u32[]{:S(2)}) collective-permute-start(f32[32,1024]{1,0:T(8,128)S(1)} %add.453), channel_id=1, source_target_pairs={{0,16},{8,24},{16,0},{24,8},{32,48},{40,56},{48,32},{56,40},{64,80... | collective-permute-start | bytes 393224 | tf_op jit(solution)/shard_map/ppermute | solution.py:82
  131.1 4.4 %all-to-all-start.3 = ((bf16[4,512,256]{2,1,0:T(8,128)(2,1)}), bf16[4,512,256]{2,1,0:T(8,128)(2,1)}, u32[]{:S(2)}, u32[]{:S(2)}) async-start(bf16[4,512,256]{2,1,0:T(8,128)(2,1)} %arrange.1), calls=%async_computation.3 | async-start | bytes 2097152 | tf_op jit(solution)/shard_map/all_to_all | solution.py:54
  135.5 1.4 collective-permute-start.20
  136.9 2.5 %collective-permute-start.21 = (bf16[512,256]{1,0:T(8,128)(2,1)}, bf16[512,256]{1,0:T(8,128)(2,1)}, u32[]{:S(2)}, u32[]{:S(2)}) collective-permute-start(bf16[512,256]{1,0:T(8,128)(2,1)} %get-tuple-element.71), channel_id=1, source_target_pairs={{0,4},{1,5},{2,6},{3,7},{4,0},{5,1},{6,2},{7,3},{8,12},{9,13},{10,... | collective-permute-start | bytes 786440 | tf_op jit(solution)/shard_map/ppermute | solution.py:390
  143.3 2.9 %collective-permute-start.30 = (f32[256,256]{1,0:T(8,128)}, f32[256,256]{1,0:T(8,128)}, u32[]{:S(2)}, u32[]{:S(2)}) collective-permute-start(f32[256,256]{1,0:T(8,128)} %fusion.2), channel_id=1, source_target_pairs={{0,1},{1,0},{2,3},{3,2},{4,5},{5,4},{6,7},{7,6},{8,9},{9,8},{10,11... | collective-permute-start | bytes 786440 | tf_op jit(solution)/shard_map/ppermute | solution.py:401
  146.2 6.6 %backward.5 = (f32[512,1024]{1,0:T(8,128)S(1)}, bf16[512,1024]{1,0:T(8,128)(2,1)S(1)}) custom-call(s32[8]{0:T(128)S(1)} %stack.179.spots_ref, bf16[4,2048,128]{2,1,0:T(8,128)(2,1)} %collective-permute-done.18.refs_0_, bf16[4,2048,128]{2,1,0:T(8,128)(2,1)} %collective-permute-done.19.refs_1_, bf16[512,8192]{1,0:T(8,128)(2,1)} %refs_9_.5, ...), custom_call_target="tpu_custom_call" | custom-call | flops 268435456 | bytes 524288 | tf_op jit(solution)/shard_map/backward/pallas_call | solution.py:237
  154.3 5.9 %collective-permute-done.21 = bf16[512,256]{1,0:T(8,128)(2,1)} collective-permute-done((bf16[512,256]{1,0:T(8,128)(2,1)}, bf16[512,256]{1,0:T(8,128)(2,1)}, u32[]{:S(2)}, u32[]{:S(2)}) %collective-permute-start.21) | collective-permute-done | bytes 262176 | tf_op jit(solution)/shard_map/ppermute | solution.py:390
  161.4 2.8 %collective-permute-start.25 = (bf16[2,512,256]{2,1,0:T(8,128)(2,1)S(1)}, bf16[2,512,256]{2,1,0:T(8,128)(2,1)S(1)}, u32[]{:S(2)}, u32[]{:S(2)}) collective-permute-start(bf16[2,512,256]{2,1,0:T(8,128)(2,1)S(1)} %slice_select_fusion), channel_id=1, source_target_pairs={{0,1},{1,0},{2,3},{3,2},{4,5},{5,4},{6,7},{7,6},{8,9},{9,8},{10,11... | collective-permute-start | bytes 1572872 | tf_op jit(solution)/shard_map/ppermute | solution.py:403
  168.1 3.6 %collective-permute-start.27 = (bf16[512,256]{1,0:T(8,128)(2,1)S(1)}, bf16[512,256]{1,0:T(8,128)(2,1)S(1)}, u32[]{:S(2)}, u32[]{:S(2)}) collective-permute-start(bf16[512,256]{1,0:T(8,128)(2,1)S(1)} %add_convert_fusion.2), channel_id=1, source_target_pairs={{1,4},{5,5},{9,12},{13,13},{17,20},{21,21},{25,28},{29,29},{33,38}... | collective-permute-start | bytes 786440 | tf_op jit(solution)/shard_map/ppermute | solution.py:285
  171.7 1.8 collective-permute-done.31
  177.9 1.4 add_convert_fusion.1
  179.4 3.7 %collective-permute-done.32 = f32[256,256]{1,0:T(8,128)S(1)} collective-permute-done((f32[256,256]{1,0:T(8,128)S(1)}, f32[256,256]{1,0:T(8,128)S(1)}, u32[]{:S(2)}, u32[]{:S(2)}) %collective-permute-start.32) | collective-permute-done | bytes 262176 | tf_op jit(solution)/shard_map/ppermute | solution.py:61
  183.8 2.7 %add_convert_fusion = bf16[512,1024]{1,0:T(8,128)(2,1)} fusion(f32[512,1024]{1,0:T(8,128)S(1)} %get-tuple-element.81, bf16[512,1024]{1,0:T(8,128)(2,1)} %collective-permute-done.29, bf16[16,1024]{1,0:T(8,128)(2,1)S(1)} %bitcast.113, bf16[32,512]{1,0:T(8,128)(2,1)S(1)} %copy-done.8), kind=kOutput, calls=%fused_computation.4 | convolution fusion | flops 19398656 | bytes 4243456 | tf_op jit(solution)/shard_map/dot_general | solution.py:421
  (124 shorter events, 26.7 us)
Async XLA Ops:
  0.6 13.1 %copy-start = (f32[256,256]{1,0:T(8,128)S(1)}, f32[256,256]{1,0:T(8,128)}, u32[]{:S(2)}) copy-start(f32[256,256]{1,0:T(8,128)} %param.10) | copy-start | bytes 786436
  2.0 3.2 %collective-permute-start.1 = (bf16[1024,256]{1,0:T(8,128)(2,1)S(1)}, bf16[1024,256]{1,0:T(8,128)(2,1)}, u32[]{:S(2)}, u32[]{:S(2)}) collective-permute-start(bf16[1024,256]{1,0:T(8,128)(2,1)S(1)} %get-tuple-element.86), channel_id=1, source_target_pairs={{0,1},{1,0},{2,3},{3,2},{4,5},{5,4},{6,7},{7,6},{8,9},{9,8},{10,11... | collective-permute-start | bytes 1572872 | tf_op jit(solution)/shard_map/ppermute | solution.py:312
  3.5 9.5 %copy-start.17 = (f32[16,4,2]{0,2,1:T(2,128)S(1)}, f32[16,4,2]{0,2,1:T(2,128)}, u32[]{:S(2)}) copy-start(f32[16,4,2]{0,2,1:T(2,128)} %param.11) | copy-start | bytes 1540
  3.5 9.5 %copy-start.18 = (f32[16,4,2]{0,2,1:T(2,128)S(1)}, f32[16,4,2]{0,2,1:T(2,128)}, u32[]{:S(2)}) copy-start(f32[16,4,2]{0,2,1:T(2,128)} %param.13) | copy-start | bytes 1540
  3.5 10.2 %copy-start.13 = (s32[16,4,2]{0,2,1:T(2,128)S(1)}, s32[16,4,2]{0,2,1:T(2,128)}, u32[]{:S(2)}) copy-start(s32[16,4,2]{0,2,1:T(2,128)} %param.14) | copy-start | bytes 1540
  3.5 10.5 %copy-start.14 = (s32[16,4,2]{0,2,1:T(2,128)S(1)}, s32[16,4,2]{0,2,1:T(2,128)}, u32[]{:S(2)}) copy-start(s32[16,4,2]{0,2,1:T(2,128)} %param.12) | copy-start | bytes 1540
  3.5 22.0 %copy-start.1 = (bf16[512,1024]{1,0:T(8,128)(2,1)S(1)}, bf16[512,1024]{1,0:T(8,128)(2,1)}, u32[]{:S(2)}) copy-start(bf16[512,1024]{1,0:T(8,128)(2,1)} %param.8) | copy-start | bytes 3145732
  6.3 19.6 %collective-permute-start.3 = (bf16[2048,128]{1,0:T(8,128)(2,1)S(1)}, bf16[2048,128]{1,0:T(8,128)(2,1)S(1)}, u32[]{:S(2)}, u32[]{:S(2)}) collective-permute-start(bf16[2048,128]{1,0:T(8,128)(2,1)S(1)} %get-tuple-element.44), channel_id=1, source_target_pairs={{0,32},{1,9},{2,34},{3,11},{4,36},{5,13},{6,38},{7,15},{8,40},{9,1... | collective-permute-start | bytes 1572872 | tf_op jit(solution)/shard_map/ppermute | solution.py:43
  8.1 29.2 %collective-permute-start.2 = (bf16[2048,128]{1,0:T(8,128)(2,1)S(1)}, bf16[2048,128]{1,0:T(8,128)(2,1)S(1)}, u32[]{:S(2)}, u32[]{:S(2)}) collective-permute-start(bf16[2048,128]{1,0:T(8,128)(2,1)S(1)} %get-tuple-element.44), channel_id=1, source_target_pairs={{0,96},{1,25},{2,98},{3,27},{4,100},{5,29},{6,102},{7,31},{8,104},... | collective-permute-start | bytes 1572872 | tf_op jit(solution)/shard_map/ppermute | solution.py:43
  10.3 17.3 %collective-permute-start.7 = (bf16[2048,128]{1,0:T(8,128)(2,1)S(1)}, bf16[2048,128]{1,0:T(8,128)(2,1)}, u32[]{:S(2)}, u32[]{:S(2)}) collective-permute-start(bf16[2048,128]{1,0:T(8,128)(2,1)S(1)} %get-tuple-element.45), channel_id=1, source_target_pairs={{0,32},{1,9},{2,34},{3,11},{4,36},{5,13},{6,38},{7,15},{8,40},{9,1... | collective-permute-start | bytes 1572872 | tf_op jit(solution)/shard_map/ppermute | solution.py:43
  10.3 12.0 %collective-permute-start.5 = (bf16[2048,128]{1,0:T(8,128)(2,1)S(1)}, bf16[2048,128]{1,0:T(8,128)(2,1)}, u32[]{:S(2)}, u32[]{:S(2)}) collective-permute-start(bf16[2048,128]{1,0:T(8,128)(2,1)S(1)} %get-tuple-element.45), channel_id=1, source_target_pairs={{0,96},{1,25},{2,98},{3,27},{4,100},{5,29},{6,102},{7,31},{8,104},... | collective-permute-start | bytes 1572872 | tf_op jit(solution)/shard_map/ppermute | solution.py:43
  14.1 17.9 %copy-start.9 = (bf16[4,2,8,256]{3,2,0,1:T(8,128)(2,1)}, bf16[4,2,8,256]{3,2,0,1:T(8,128)(2,1)S(1)}, u32[]{:S(2)}) copy-start(bf16[4,2,8,256]{3,2,0,1:T(8,128)(2,1)S(1)} %copy.45) | copy-start | bytes 98308
  14.4 17.5 %copy-start.3 = (bf16[4,2,8,256]{3,2,0,1:T(8,128)(2,1)}, bf16[4,2,8,256]{3,2,0,1:T(8,128)(2,1)S(1)}, u32[]{:S(2)}) copy-start(bf16[4,2,8,256]{3,2,0,1:T(8,128)(2,1)S(1)} %copy.44) | copy-start | bytes 98308
  22.3 9.7 %collective-permute-start.6 = (bf16[2048,128]{1,0:T(8,128)(2,1)}, bf16[2048,128]{1,0:T(8,128)(2,1)S(1)}, u32[]{:S(2)}, u32[]{:S(2)}) collective-permute-start(bf16[2048,128]{1,0:T(8,128)(2,1)} %collective-permute-done.5), channel_id=1, source_target_pairs={{0,96},{1,25},{2,98},{3,27},{4,100},{5,29},{6,102},{7,31},{8,104},... | collective-permute-start | bytes 1572872 | tf_op jit(solution)/shard_map/ppermute | solution.py:43
  25.9 11.3 %collective-permute-start.4 = (bf16[2048,128]{1,0:T(8,128)(2,1)S(1)}, bf16[2048,128]{1,0:T(8,128)(2,1)S(1)}, u32[]{:S(2)}, u32[]{:S(2)}) collective-permute-start(bf16[2048,128]{1,0:T(8,128)(2,1)S(1)} %collective-permute-done.3), channel_id=1, source_target_pairs={{0,32},{1,9},{2,34},{3,11},{4,36},{5,13},{6,38},{7,15},{8,40},{9,1... | collective-permute-start | bytes 1572872 | tf_op jit(solution)/shard_map/ppermute | solution.py:43
  34.8 38.7 %collective-permute-start.12 = (bf16[4,2048,128]{2,1,0:T(8,128)(2,1)}, bf16[4,2048,128]{2,1,0:T(8,128)(2,1)}, u32[]{:S(2)}, u32[]{:S(2)}) collective-permute-start(bf16[4,2048,128]{2,1,0:T(8,128)(2,1)} %pad_maximum_fusion.1.refs_1_), channel_id=1, source_target_pairs={{0,24},{1,97},{2,26},{3,99},{4,28},{5,101},{6,30},{7,103},{8,0},{9... | collective-permute-start | bytes 6291464 | tf_op jit(solution)/shard_map/ppermute | solution.py:43
  38.8 34.6 %collective-permute-start.11 = (bf16[4,2048,128]{2,1,0:T(8,128)(2,1)}, bf16[4,2048,128]{2,1,0:T(8,128)(2,1)}, u32[]{:S(2)}, u32[]{:S(2)}) collective-permute-start(bf16[4,2048,128]{2,1,0:T(8,128)(2,1)} %pad_maximum_fusion.refs_0_), channel_id=1, source_target_pairs={{0,8},{1,33},{2,10},{3,35},{4,12},{5,37},{6,14},{7,39},{8,16},{9,4... | collective-permute-start | bytes 6291464 | tf_op jit(solution)/shard_map/ppermute | solution.py:43
  38.8 14.1 %collective-permute-start = (bf16[512,1024]{1,0:T(8,128)(2,1)S(1)}, bf16[512,1024]{1,0:T(8,128)(2,1)}, u32[]{:S(2)}, u32[]{:S(2)}) collective-permute-start(bf16[512,1024]{1,0:T(8,128)(2,1)S(1)} %copy-done.1), channel_id=1, source_target_pairs={{0,1},{1,0},{2,3},{3,2},{4,5},{5,4},{6,7},{7,6},{8,9},{9,8},{10,11... | collective-permute-start | bytes 3145736 | tf_op jit(solution)/shard_map/ppermute | solution.py:332
  41.6 2.2 %collective-permute-start.8 = (f32[32,512]{1,0:T(8,128)S(1)}, f32[32,512]{1,0:T(8,128)S(1)}, u32[]{:S(2)}, u32[]{:S(2)}) collective-permute-start(f32[32,512]{1,0:T(8,128)S(1)} %pad_maximum_fusion.4), channel_id=1, source_target_pairs={{0,1},{1,0},{2,3},{3,2},{4,5},{5,4},{6,7},{7,6},{8,9},{9,8},{10,11... | collective-permute-start | bytes 196616 | tf_op jit(solution)/shard_map/ppermute | solution.py:61
  44.5 3.7 %collective-permute-start.9 = (f32[32,512]{1,0:T(8,128)S(1)}, f32[32,512]{1,0:T(8,128)S(1)}, u32[]{:S(2)}, u32[]{:S(2)}) collective-permute-start(f32[32,512]{1,0:T(8,128)S(1)} %add.383), channel_id=1, source_target_pairs={{0,2},{1,3},{2,0},{3,1},{4,6},{5,7},{6,4},{7,5},{8,10},{9,11},{10,... | collective-permute-start | bytes 196616 | tf_op jit(solution)/shard_map/ppermute | solution.py:61
  45.8 43.3 %collective-permute-start.14 = (bf16[4,2048,128]{2,1,0:T(8,128)(2,1)}, bf16[4,2048,128]{2,1,0:T(8,128)(2,1)}, u32[]{:S(2)}, u32[]{:S(2)}) collective-permute-start(bf16[4,2048,128]{2,1,0:T(8,128)(2,1)} %pad_maximum_fusion.1.refs_1_), channel_id=1, source_target_pairs={{0,8},{1,33},{2,10},{3,35},{4,12},{5,37},{6,14},{7,39},{8,16},{9,4... | collective-permute-start | bytes 6291464 | tf_op jit(solution)/shard_map/ppermute | solution.py:43
  48.8 40.3 %collective-permute-start.13 = (bf16[4,2048,128]{2,1,0:T(8,128)(2,1)}, bf16[4,2048,128]{2,1,0:T(8,128)(2,1)}, u32[]{:S(2)}, u32[]{:S(2)}) collective-permute-start(bf16[4,2048,128]{2,1,0:T(8,128)(2,1)} %pad_maximum_fusion.refs_0_), channel_id=1, source_target_pairs={{0,24},{1,97},{2,26},{3,99},{4,28},{5,101},{6,30},{7,103},{8,0},{9... | collective-permute-start | bytes 6291464 | tf_op jit(solution)/shard_map/ppermute | solution.py:43
  53.0 9.3 %collective-permute-start.10 = (f32[32,512]{1,0:T(8,128)S(1)}, f32[32,512]{1,0:T(8,128)S(1)}, u32[]{:S(2)}, u32[]{:S(2)}) collective-permute-start(f32[32,512]{1,0:T(8,128)S(1)} %add.384), channel_id=1, source_target_pairs={{0,4},{1,5},{2,6},{3,7},{4,0},{5,1},{6,2},{7,3},{8,12},{9,13},{10,... | collective-permute-start | bytes 196616 | tf_op jit(solution)/shard_map/ppermute | solution.py:61
  62.9 18.2 %all-to-all-start = ((bf16[4,512,256]{2,1,0:T(8,128)(2,1)}), bf16[4,512,256]{2,1,0:T(8,128)(2,1)S(1)}, u32[]{:S(2)}, u32[]{:S(2)}) async-start(bf16[4,512,256]{2,1,0:T(8,128)(2,1)} %forward.4), calls=%async_computation | async-start | bytes 2097152 | tf_op jit(solution)/shard_map/all_to_all | solution.py:54
  73.4 47.0 %collective-permute-start.18 = (bf16[4,2048,128]{2,1,0:T(8,128)(2,1)}, bf16[4,2048,128]{2,1,0:T(8,128)(2,1)}, u32[]{:S(2)}, u32[]{:S(2)}) collective-permute-start(bf16[4,2048,128]{2,1,0:T(8,128)(2,1)} %collective-permute-done.11.refs_0_), channel_id=1, source_target_pairs={{0,8},{1,33},{2,10},{3,35},{4,12},{5,37},{6,14},{7,39},{8,16},{9,4... | collective-permute-start | bytes 6291464 | tf_op jit(solution)/shard_map/ppermute | solution.py:43
  73.5 46.9 %collective-permute-start.19 = (bf16[4,2048,128]{2,1,0:T(8,128)(2,1)}, bf16[4,2048,128]{2,1,0:T(8,128)(2,1)}, u32[]{:S(2)}, u32[]{:S(2)}) collective-permute-start(bf16[4,2048,128]{2,1,0:T(8,128)(2,1)} %collective-permute-done.12.refs_1_), channel_id=1, source_target_pairs={{0,24},{1,97},{2,26},{3,99},{4,28},{5,101},{6,30},{7,103},{8,0},{9... | collective-permute-start | bytes 6291464 | tf_op jit(solution)/shard_map/ppermute | solution.py:43
  81.1 17.5 %all-to-all-start.1 = ((bf16[4,512,256]{2,1,0:T(8,128)(2,1)}), bf16[4,512,256]{2,1,0:T(8,128)(2,1)}, u32[]{:S(2)}, u32[]{:S(2)}) async-start(bf16[4,512,256]{2,1,0:T(8,128)(2,1)} %forward.5), calls=%async_computation.1 | async-start | bytes 2097152 | tf_op jit(solution)/shard_map/all_to_all | solution.py:54
  98.6 19.3 %all-to-all-start.2 = ((bf16[4,512,256]{2,1,0:T(8,128)(2,1)}), bf16[4,512,256]{2,1,0:T(8,128)(2,1)}, u32[]{:S(2)}, u32[]{:S(2)}) async-start(bf16[4,512,256]{2,1,0:T(8,128)(2,1)} %forward.6), calls=%async_computation.2 | async-start | bytes 2097152 | tf_op jit(solution)/shard_map/all_to_all | solution.py:54
  102.9 11.5 %collective-permute-start.17 = (f32[32,1024]{1,0:T(8,128)}, f32[32,1024]{1,0:T(8,128)}, u32[]{:S(2)}, u32[]{:S(2)}) collective-permute-start(f32[32,1024]{1,0:T(8,128)} %maximum_multiply_fusion), channel_id=1, source_target_pairs={{0,96},{1,97},{2,98},{3,99},{4,100},{5,101},{6,102},{7,103},{8,104... | collective-permute-start | bytes 393224 | tf_op jit(solution)/shard_map/ppermute | solution.py:72
  102.9 11.4 %collective-permute-start.16 = (f32[32,1024]{1,0:T(8,128)}, f32[32,1024]{1,0:T(8,128)}, u32[]{:S(2)}, u32[]{:S(2)}) collective-permute-start(f32[32,1024]{1,0:T(8,128)} %maximum_multiply_fusion), channel_id=1, source_target_pairs={{0,64},{1,65},{2,66},{3,67},{4,68},{5,69},{6,70},{7,71},{8,72},{9,... | collective-permute-start | bytes 393224 | tf_op jit(solution)/shard_map/ppermute | solution.py:72
  103.0 13.1 %collective-permute-start.15 = (f32[32,1024]{1,0:T(8,128)}, f32[32,1024]{1,0:T(8,128)}, u32[]{:S(2)}, u32[]{:S(2)}) collective-permute-start(f32[32,1024]{1,0:T(8,128)} %maximum_multiply_fusion), channel_id=1, source_target_pairs={{0,32},{1,33},{2,34},{3,35},{4,36},{5,37},{6,38},{7,39},{8,40},{9,... | collective-permute-start | bytes 393224 | tf_op jit(solution)/shard_map/ppermute | solution.py:72
  104.5 11.6 %copy-start.2 = (f32[32,1024]{1,0:T(8,128)S(1)}, f32[32,1024]{1,0:T(8,128)}, u32[]{:S(2)}) copy-start(f32[32,1024]{1,0:T(8,128)} %maximum_multiply_fusion) | copy-start | bytes 393220
  117.8 7.6 %collective-permute-start.23 = (f32[32,1024]{1,0:T(8,128)}, f32[32,1024]{1,0:T(8,128)}, u32[]{:S(2)}, u32[]{:S(2)}) collective-permute-start(f32[32,1024]{1,0:T(8,128)} %add_add_fusion), channel_id=1, source_target_pairs={{0,8},{8,0},{16,24},{24,16},{32,40},{40,32},{48,56},{56,48},{64,72... | collective-permute-start | bytes 393224 | tf_op jit(solution)/shard_map/ppermute | solution.py:82
  126.5 14.0 %collective-permute-start.24 = (f32[32,1024]{1,0:T(8,128)S(1)}, f32[32,1024]{1,0:T(8,128)S(1)}, u32[]{:S(2)}, u32[]{:S(2)}) collective-permute-start(f32[32,1024]{1,0:T(8,128)S(1)} %add.453), channel_id=1, source_target_pairs={{0,16},{8,24},{16,0},{24,8},{32,48},{40,56},{48,32},{56,40},{64,80... | collective-permute-start | bytes 393224 | tf_op jit(solution)/shard_map/ppermute | solution.py:82
  131.1 11.6 %copy-start.16 = (f32[16,4,2]{0,2,1:T(2,128)S(1)}, f32[16,4,2]{0,2,1:T(2,128)}, u32[]{:S(2)}) copy-start(f32[16,4,2]{0,2,1:T(2,128)} %copy-done.15) | copy-start | bytes 1540
  131.1 22.2 %all-to-all-start.3 = ((bf16[4,512,256]{2,1,0:T(8,128)(2,1)}), bf16[4,512,256]{2,1,0:T(8,128)(2,1)}, u32[]{:S(2)}, u32[]{:S(2)}) async-start(bf16[4,512,256]{2,1,0:T(8,128)(2,1)} %arrange.1), calls=%async_computation.3 | async-start | bytes 2097152 | tf_op jit(solution)/shard_map/all_to_all | solution.py:54
  135.5 18.8 %collective-permute-start.20 = (bf16[512,256]{1,0:T(8,128)(2,1)}, bf16[512,256]{1,0:T(8,128)(2,1)}, u32[]{:S(2)}, u32[]{:S(2)}) collective-permute-start(bf16[512,256]{1,0:T(8,128)(2,1)} %get-tuple-element.70), channel_id=1, source_target_pairs={{0,2},{1,3},{2,4},{3,5},{4,6},{5,7},{6,0},{7,1},{8,10},{9,11},{10,... | collective-permute-start | bytes 786440 | tf_op jit(solution)/shard_map/ppermute | solution.py:390
  136.9 23.2 %collective-permute-start.21 = (bf16[512,256]{1,0:T(8,128)(2,1)}, bf16[512,256]{1,0:T(8,128)(2,1)}, u32[]{:S(2)}, u32[]{:S(2)}) collective-permute-start(bf16[512,256]{1,0:T(8,128)(2,1)} %get-tuple-element.71), channel_id=1, source_target_pairs={{0,4},{1,5},{2,6},{3,7},{4,0},{5,1},{6,2},{7,3},{8,12},{9,13},{10,... | collective-permute-start | bytes 786440 | tf_op jit(solution)/shard_map/ppermute | solution.py:390
  139.5 20.7 %collective-permute-start.22 = (bf16[512,256]{1,0:T(8,128)(2,1)}, bf16[512,256]{1,0:T(8,128)(2,1)}, u32[]{:S(2)}, u32[]{:S(2)}) collective-permute-start(bf16[512,256]{1,0:T(8,128)(2,1)} %get-tuple-element.72), channel_id=1, source_target_pairs={{0,6},{1,7},{2,0},{3,1},{4,2},{5,3},{6,4},{7,5},{8,14},{9,15},{10,... | collective-permute-start | bytes 786440 | tf_op jit(solution)/shard_map/ppermute | solution.py:390
  143.3 21.1 %collective-permute-start.30 = (f32[256,256]{1,0:T(8,128)}, f32[256,256]{1,0:T(8,128)}, u32[]{:S(2)}, u32[]{:S(2)}) collective-permute-start(f32[256,256]{1,0:T(8,128)} %fusion.2), channel_id=1, source_target_pairs={{0,1},{1,0},{2,3},{3,2},{4,5},{5,4},{6,7},{7,6},{8,9},{9,8},{10,11... | collective-permute-start | bytes 786440 | tf_op jit(solution)/shard_map/ppermute | solution.py:401
  152.8 31.0 %collective-permute-start.29 = (bf16[512,1024]{1,0:T(8,128)(2,1)S(1)}, bf16[512,1024]{1,0:T(8,128)(2,1)}, u32[]{:S(2)}, u32[]{:S(2)}) collective-permute-start(bf16[512,1024]{1,0:T(8,128)(2,1)S(1)} %get-tuple-element.75), channel_id=1, source_target_pairs={{0,1},{1,0},{2,3},{3,2},{4,5},{5,4},{6,7},{7,6},{8,9},{9,8},{10,11... | collective-permute-start | bytes 3145736 | tf_op jit(solution)/shard_map/ppermute | solution.py:417
  153.3 12.9 %copy-start.5 = (bf16[512,256]{1,0:T(8,128)(2,1)S(1)}, bf16[512,256]{1,0:T(8,128)(2,1)}, u32[]{:S(2)}) copy-start(bf16[512,256]{1,0:T(8,128)(2,1)} %get-tuple-element.77) | copy-start | bytes 786436
  161.4 13.4 %collective-permute-start.25 = (bf16[2,512,256]{2,1,0:T(8,128)(2,1)S(1)}, bf16[2,512,256]{2,1,0:T(8,128)(2,1)S(1)}, u32[]{:S(2)}, u32[]{:S(2)}) collective-permute-start(bf16[2,512,256]{2,1,0:T(8,128)(2,1)S(1)} %slice_select_fusion), channel_id=1, source_target_pairs={{0,1},{1,0},{2,3},{3,2},{4,5},{5,4},{6,7},{7,6},{8,9},{9,8},{10,11... | collective-permute-start | bytes 1572872 | tf_op jit(solution)/shard_map/ppermute | solution.py:403
  165.5 8.0 %collective-permute-start.31 = (f32[256,256]{1,0:T(8,128)S(1)}, f32[256,256]{1,0:T(8,128)S(1)}, u32[]{:S(2)}, u32[]{:S(2)}) collective-permute-start(f32[256,256]{1,0:T(8,128)S(1)} %add.469), channel_id=1, source_target_pairs={{0,2},{1,3},{2,0},{3,1},{4,6},{5,7},{6,4},{7,5},{8,10},{9,11},{10,... | collective-permute-start | bytes 786440 | tf_op jit(solution)/shard_map/ppermute | solution.py:61
  167.4 9.7 %collective-permute-start.28 = (bf16[512,256]{1,0:T(8,128)(2,1)S(1)}, bf16[512,256]{1,0:T(8,128)(2,1)S(1)}, u32[]{:S(2)}, u32[]{:S(2)}) collective-permute-start(bf16[512,256]{1,0:T(8,128)(2,1)S(1)} %add_convert_fusion.2), channel_id=1, source_target_pairs={{3,4},{7,5},{11,12},{15,13},{19,20},{23,21},{27,28},{31,29},{35,38... | collective-permute-start | bytes 786440 | tf_op jit(solution)/shard_map/ppermute | solution.py:285
  168.1 9.1 %collective-permute-start.27 = (bf16[512,256]{1,0:T(8,128)(2,1)S(1)}, bf16[512,256]{1,0:T(8,128)(2,1)S(1)}, u32[]{:S(2)}, u32[]{:S(2)}) collective-permute-start(bf16[512,256]{1,0:T(8,128)(2,1)S(1)} %add_convert_fusion.2), channel_id=1, source_target_pairs={{1,4},{5,5},{9,12},{13,13},{17,20},{21,21},{25,28},{29,29},{33,38}... | collective-permute-start | bytes 786440 | tf_op jit(solution)/shard_map/ppermute | solution.py:285
  173.5 3.8 %collective-permute-start.26 = (bf16[512,256]{1,0:T(8,128)(2,1)S(1)}, bf16[512,256]{1,0:T(8,128)(2,1)S(1)}, u32[]{:S(2)}, u32[]{:S(2)}) collective-permute-start(bf16[512,256]{1,0:T(8,128)(2,1)S(1)} %add_convert_fusion.2), channel_id=1, source_target_pairs={{0,1},{2,3},{4,5},{6,7},{8,9},{10,11},{12,13},{14,15},{32,33},{34,... | collective-permute-start | bytes 786440 | tf_op jit(solution)/shard_map/ppermute | solution.py:290
  174.8 8.2 %collective-permute-start.32 = (f32[256,256]{1,0:T(8,128)S(1)}, f32[256,256]{1,0:T(8,128)S(1)}, u32[]{:S(2)}, u32[]{:S(2)}) collective-permute-start(f32[256,256]{1,0:T(8,128)S(1)} %add.470), channel_id=1, source_target_pairs={{0,4},{1,5},{2,6},{3,7},{4,0},{5,1},{6,2},{7,3},{8,12},{9,13},{10,... | collective-permute-start | bytes 786440 | tf_op jit(solution)/shard_map/ppermute | solution.py:61
  (8 other events, 11.0 us)

commit v12 on v9

--- a/solution.py
+++ b/solution.py
@@ -382,15 +382,14 @@
     slots = arrange(
         far.astype(jnp.int32).reshape(1), slots_here, slots_first, after(slots_second, grown, both)
     )
-    both = with_partner(both, 1, slots)
     moved = exchange(slots, "tensor", LANES)
-    sent = forward(after(turned_here, slots, both), wide, take(across), apart=True)
+    sent = forward(after(turned_here, slots), wide, take(across), apart=True)
     arrived = [sent[0]]
     for step in range(1, SIDE):
         turns = [(t, (t + 2 * step) % 8) for t in range(8)]
         arrived.append(lax.ppermute(sent[step], "tensor", turns))
     piece = total_of([a.astype(f32) for a in arrived]).astype(bf16)
-    both = with_partner(both, 2, *sent)
+    both = with_partner(with_partner(both, 1, *sent), 2, *arrived)
     bank_a, logit_grad_a = compose_back(both[:rank], weights_a, picked_a, mixing_a, vector_bank)
     bank_b, logit_grad_b = compose_back(both[rank:], weights_b, picked_b, mixing_b, vector_bank)
     bank_part = over_tensor(bank_a + bank_b, (1, 2))

time: 181 us -> 191 us (1.055)
  waiting for transfers between devices: 33.7 us -> 46.3 us
    ppermute x6, waiting for transfers between devices: 3.98 us -> 17 us  [over_tensor(): lax.ppermute(value, 'tensor', [(t, t ^ bit) for t in range(8)])]
    ppermute x1, starting transfers between devices: 2.76 us -> 0.1 us  [local(): lax.ppermute(attn_out, 'tensor', SWAP)]
    ppermute x3, waiting for transfers between devices: 3 us -> 5.28 us  [from_step(): return lax.ppermute(value, BOTH, pairs(move))]
  transfers between devices with their start and end apart: 37 -> 37, of which waited for: 10 -> 14; matrix products, arithmetic and copies ran while one was open for 14% -> 13% of each run, Pallas kernels for 25% -> 24%
where the time goes in v12:
time: 191 us; the launch traced here: 190 us
  starting transfers between devices  67 us (35%)
  waiting for transfers between devices  46.3 us (24%)
  Pallas kernels  45.7 us (24%)
  other arithmetic  14.9 us (8%)
  matrix products  9.9 us (5%)
  local copies, waits for them, and re-layouts  4.76 us (2%)
    pallas_call x3, Pallas kernels, backward(): pl.pallas_call(functools.partial(backward_kernel, count, first, last), ou...  23.2 us
    pallas_call x4, Pallas kernels, forward(): pl.pallas_call(functools.partial(forward_kernel, count, many), out_shape=...  20 us
    ppermute x12, starting transfers between devices, shift(): return lax.ppermute(value, BOTH, ring(stage, step))  19.3 us
    ppermute x6, waiting for transfers between devices, over_tensor(): lax.ppermute(value, 'tensor', [(t, t ^ bit) for t in range(8)])  17 us
    all_to_all x4, starting transfers between devices, exchange(): lax.all_to_all(value, axis, split_axis=0, concat_axis=0, tiled=True, axis...  16.3 us
    ppermute x12, waiting for transfers between devices, shift(): return lax.ppermute(value, BOTH, ring(stage, step))  12.3 us
    ppermute x6, starting transfers between devices, over_tensor(): lax.ppermute(value, 'tensor', [(t, t ^ bit) for t in range(8)])  8.74 us
    ppermute x3, waiting for transfers between devices, local(): arrived.append(lax.ppermute(sent[step], 'tensor', turns))  7.02 us
  transfers between devices with their start and end apart: 37, of which 14 were waited for; matrix products, arithmetic and copies ran while one was open for 13% of the time, Pallas kernels for 24%

profile of v12, /device:TPU:1, one launch (start us, length us, event | category | flops | bytes accessed | tf_op | source)
XLA Modules:
  0.0 190.0 jit_solution(2934663536940768633)
XLA Ops:
  0.7 1.4 broadcast_select_fusion.1
  2.0 1.5 collective-permute-start.1
  3.7 1.5 collective-permute-done.1
  6.4 1.8 collective-permute-start.3
  8.2 2.2 %collective-permute-start.2 = (bf16[2048,128]{1,0:T(8,128)(2,1)S(1)}, bf16[2048,128]{1,0:T(8,128)(2,1)S(1)}, u32[]{:S(2)}, u32[]{:S(2)}) collective-permute-start(bf16[2048,128]{1,0:T(8,128)(2,1)S(1)} %get-tuple-element.39), channel_id=1, source_target_pairs={{0,96},{1,25},{2,98},{3,27},{4,100},{5,29},{6,102},{7,31},{8,104},... | collective-permute-start | bytes 1572872 | tf_op jit(solution)/shard_map/ppermute | solution.py:43
  10.4 2.7 %collective-permute-start.5 = (bf16[2048,128]{1,0:T(8,128)(2,1)S(1)}, bf16[2048,128]{1,0:T(8,128)(2,1)}, u32[]{:S(2)}, u32[]{:S(2)}) collective-permute-start(bf16[2048,128]{1,0:T(8,128)(2,1)S(1)} %get-tuple-element.40), channel_id=1, source_target_pairs={{0,96},{1,25},{2,98},{3,27},{4,100},{5,29},{6,102},{7,31},{8,104},... | collective-permute-start | bytes 1572872 | tf_op jit(solution)/shard_map/ppermute | solution.py:43
  14.5 7.9 %collective-permute-done.5 = bf16[2048,128]{1,0:T(8,128)(2,1)} collective-permute-done((bf16[2048,128]{1,0:T(8,128)(2,1)S(1)}, bf16[2048,128]{1,0:T(8,128)(2,1)}, u32[]{:S(2)}, u32[]{:S(2)}) %collective-permute-start.5) | collective-permute-done | bytes 524320 | tf_op jit(solution)/shard_map/ppermute | solution.py:43
  22.4 3.2 %collective-permute-start.6 = (bf16[2048,128]{1,0:T(8,128)(2,1)}, bf16[2048,128]{1,0:T(8,128)(2,1)S(1)}, u32[]{:S(2)}, u32[]{:S(2)}) collective-permute-start(bf16[2048,128]{1,0:T(8,128)(2,1)} %collective-permute-done.5), channel_id=1, source_target_pairs={{0,96},{1,25},{2,98},{3,27},{4,100},{5,29},{6,102},{7,31},{8,104},... | collective-permute-start | bytes 1572872 | tf_op jit(solution)/shard_map/ppermute | solution.py:43
  26.0 1.6 fusion.11
  27.7 4.4 %collective-permute-done.6 = bf16[2048,128]{1,0:T(8,128)(2,1)S(1)} collective-permute-done((bf16[2048,128]{1,0:T(8,128)(2,1)}, bf16[2048,128]{1,0:T(8,128)(2,1)S(1)}, u32[]{:S(2)}, u32[]{:S(2)}) %collective-permute-start.6) | collective-permute-done | bytes 524320 | tf_op jit(solution)/shard_map/ppermute | solution.py:43
  32.1 2.8 %pad_maximum_fusion.1.refs_1_ = bf16[4,2048,128]{2,1,0:T(8,128)(2,1)} fusion(bf16[1,2048,128]{2,1,0:T(8,128)(2,1)} %bitcast.9, bf16[1,2048,128]{2,1,0:T(8,128)(2,1)S(1)} %bitcast.111, bf16[1,2048,128]{2,1,0:T(8,128)(2,1)} %bitcast.7, bf16[1,2048,128]{2,1,0:T(8,128)(2,1)S(1)} %bitcast.103), kind=kLoop, calls=%fused_computation.3 | loop fusion | flops 3145728 | bytes 4194304 | tf_op jit(solution)/shard_map/stack | solution.py:318
  34.8 2.5 %collective-permute-start.12 = (bf16[4,2048,128]{2,1,0:T(8,128)(2,1)}, bf16[4,2048,128]{2,1,0:T(8,128)(2,1)}, u32[]{:S(2)}, u32[]{:S(2)}) collective-permute-start(bf16[4,2048,128]{2,1,0:T(8,128)(2,1)} %pad_maximum_fusion.1.refs_1_), channel_id=1, source_target_pairs={{0,24},{1,97},{2,26},{3,99},{4,28},{5,101},{6,30},{7,103},{8,0},{9... | collective-permute-start | bytes 6291464 | tf_op jit(solution)/shard_map/ppermute | solution.py:43
  37.3 1.6 pad_maximum_fusion.refs_0_
  38.9 2.8 %collective-permute-start.8 = (f32[32,512]{1,0:T(8,128)S(1)}, f32[32,512]{1,0:T(8,128)S(1)}, u32[]{:S(2)}, u32[]{:S(2)}) collective-permute-start(f32[32,512]{1,0:T(8,128)S(1)} %pad_maximum_fusion.4), channel_id=1, source_target_pairs={{0,1},{1,0},{2,3},{3,2},{4,5},{5,4},{6,7},{7,6},{8,9},{9,8},{10,11... | collective-permute-start | bytes 196616 | tf_op jit(solution)/shard_map/ppermute | solution.py:61
  42.6 1.4 collective-permute-start.9
  44.6 1.6 collective-permute-done.9
  46.2 3.3 %collective-permute-start.13 = (bf16[4,2048,128]{2,1,0:T(8,128)(2,1)}, bf16[4,2048,128]{2,1,0:T(8,128)(2,1)}, u32[]{:S(2)}, u32[]{:S(2)}) collective-permute-start(bf16[4,2048,128]{2,1,0:T(8,128)(2,1)} %pad_maximum_fusion.refs_0_), channel_id=1, source_target_pairs={{0,24},{1,97},{2,26},{3,99},{4,28},{5,101},{6,30},{7,103},{8,0},{9... | collective-permute-start | bytes 6291464 | tf_op jit(solution)/shard_map/ppermute | solution.py:43
  50.4 3.0 %collective-permute-start.10 = (f32[32,512]{1,0:T(8,128)S(1)}, f32[32,512]{1,0:T(8,128)S(1)}, u32[]{:S(2)}, u32[]{:S(2)}) collective-permute-start(f32[32,512]{1,0:T(8,128)S(1)} %add.384), channel_id=1, source_target_pairs={{0,4},{1,5},{2,6},{3,7},{4,0},{5,1},{6,2},{7,3},{8,12},{9,13},{10,... | collective-permute-start | bytes 196616 | tf_op jit(solution)/shard_map/ppermute | solution.py:61
  54.7 5.0 %forward.4 = bf16[4,512,256]{2,1,0:T(8,128)(2,1)} custom-call(s32[1]{0:T(128)} %bitcast.1.start_ref, bf16[512,2048]{1,0:T(8,128)(2,1)S(1)} %constant_dynamic-update-slice_fusion.wide_ref, bf16[4,2048,128]{2,1,0:T(8,128)(2,1)} %pad_maximum_fusion.refs_0_, bf16[4,2048,128]{2,1,0:T(8,128)(2,1)} %pad_maximum_fusion.1.refs_1_), custom_call_target="tpu_custom_call" | custom-call | flops 268435456 | bytes 524288 | tf_op jit(solution)/shard_map/forward/pallas_call | solution.py:131
  60.3 3.5 %all-to-all-start = ((bf16[4,512,256]{2,1,0:T(8,128)(2,1)}), bf16[4,512,256]{2,1,0:T(8,128)(2,1)S(1)}, u32[]{:S(2)}, u32[]{:S(2)}) async-start(bf16[4,512,256]{2,1,0:T(8,128)(2,1)} %forward.4), calls=%async_computation | async-start | bytes 2097152 | tf_op jit(solution)/shard_map/all_to_all | solution.py:54
  64.1 6.7 %backward.3.refs_20_ = bf16[512,2048]{1,0:T(8,128)(2,1)} custom-call(s32[8]{0:T(128)S(1)} %stack.153.spots_ref, bf16[4,2048,128]{2,1,0:T(8,128)(2,1)} %pad_maximum_fusion.refs_0_, bf16[4,2048,128]{2,1,0:T(8,128)(2,1)} %pad_maximum_fusion.1.refs_1_, bf16[512,8192]{1,0:T(8,128)(2,1)} %refs_9_.5, bf16[512,8192]{1,0:T(8,128)(2,1)} %refs_9_.5, ...), custom_call_target="tpu_custom_call" | custom-call | flops 268435456 | bytes 524288 | tf_op jit(solution)/shard_map/backward/pallas_call | solution.py:237
  70.8 5.0 %forward.5 = bf16[4,512,256]{2,1,0:T(8,128)(2,1)} custom-call(s32[1]{0:T(128)} %bitcast.1.start_ref, bf16[512,2048]{1,0:T(8,128)(2,1)S(1)} %constant_dynamic-update-slice_fusion.wide_ref, bf16[4,2048,128]{2,1,0:T(8,128)(2,1)} %collective-permute-done.11.refs_0_, bf16[4,2048,128]{2,1,0:T(8,128)(2,1)} %collective-permute-done.12.refs_1_), custom_call_target="tpu_custom_call" | custom-call | flops 268435456 | bytes 524288 | tf_op jit(solution)/shard_map/forward/pallas_call | solution.py:131
  75.8 1.8 all-to-all-done.here_ref
  77.6 4.3 %all-to-all-start.1 = ((bf16[4,512,256]{2,1,0:T(8,128)(2,1)}), bf16[4,512,256]{2,1,0:T(8,128)(2,1)}, u32[]{:S(2)}, u32[]{:S(2)}) async-start(bf16[4,512,256]{2,1,0:T(8,128)(2,1)} %forward.5), calls=%async_computation.1 | async-start | bytes 2097152 | tf_op jit(solution)/shard_map/all_to_all | solution.py:54
  82.2 2.7 %collective-permute-start.20 = (bf16[4,2048,128]{2,1,0:T(8,128)(2,1)}, bf16[4,2048,128]{2,1,0:T(8,128)(2,1)}, u32[]{:S(2)}, u32[]{:S(2)}) collective-permute-start(bf16[4,2048,128]{2,1,0:T(8,128)(2,1)} %collective-permute-done.12.refs_1_), channel_id=1, source_target_pairs={{0,24},{1,97},{2,26},{3,99},{4,28},{5,101},{6,30},{7,103},{8,0},{9... | collective-permute-start | bytes 6291464 | tf_op jit(solution)/shard_map/ppermute | solution.py:43
  84.8 1.5 fusion.9
  86.3 1.5 fusion.32
  88.5 4.9 %forward.6 = bf16[4,512,256]{2,1,0:T(8,128)(2,1)} custom-call(s32[1]{0:T(128)} %bitcast.1.start_ref, bf16[512,2048]{1,0:T(8,128)(2,1)S(1)} %constant_dynamic-update-slice_fusion.wide_ref, bf16[4,2048,128]{2,1,0:T(8,128)(2,1)} %collective-permute-done.13.refs_0_.refs_2_, bf16[4,2048,128]{2,1,0:T(8,128)(2,1)} %collective-permute-done.14.refs_1_.refs_3_), custom_call_target="tpu_custom_call" | custom-call | flops 268435456 | bytes 524288 | tf_op jit(solution)/shard_map/forward/pallas_call | solution.py:131
  93.4 1.4 all-to-all-done.1.refs_0_
  94.8 4.3 %all-to-all-start.2 = ((bf16[4,512,256]{2,1,0:T(8,128)(2,1)}), bf16[4,512,256]{2,1,0:T(8,128)(2,1)}, u32[]{:S(2)}, u32[]{:S(2)}) async-start(bf16[4,512,256]{2,1,0:T(8,128)(2,1)} %forward.6), calls=%async_computation.2 | async-start | bytes 2097152 | tf_op jit(solution)/shard_map/all_to_all | solution.py:54
  100.8 9.8 %backward.4.refs_10_ = bf16[512,2048]{1,0:T(8,128)(2,1)} custom-call(s32[16]{0:T(128)S(1)} %stack.170.spots_ref, bf16[4,2048,128]{2,1,0:T(8,128)(2,1)} %collective-permute-done.11.refs_0_, bf16[4,2048,128]{2,1,0:T(8,128)(2,1)} %collective-permute-done.12.refs_1_, ...), custom_call_target="tpu_custom_call", output_to_operand_aliasing={{}: (21, {})} | custom-call | flops 536870912 | bytes 1048576 | tf_op jit(solution)/shard_map/backward/pallas_call | solution.py:237
  110.6 3.1 %collective-permute-done.17 = f32[32,1024]{1,0:T(8,128)} collective-permute-done((f32[32,1024]{1,0:T(8,128)}, f32[32,1024]{1,0:T(8,128)}, u32[]{:S(2)}, u32[]{:S(2)}) %collective-permute-start.17) | collective-permute-done | bytes 131104 | tf_op jit(solution)/shard_map/ppermute | solution.py:72
  113.7 2.1 %collective-permute-done.15 = f32[32,1024]{1,0:T(8,128)} collective-permute-done((f32[32,1024]{1,0:T(8,128)}, f32[32,1024]{1,0:T(8,128)}, u32[]{:S(2)}, u32[]{:S(2)}) %collective-permute-start.15) | collective-permute-done | bytes 131104 | tf_op jit(solution)/shard_map/ppermute | solution.py:72
  115.9 1.7 add_add_fusion
  117.6 2.6 %arrange.1 = bf16[4,512,256]{2,1,0:T(8,128)(2,1)} custom-call(s32[1]{0:T(128)} %bitcast.far_ref, bf16[4,512,256]{2,1,0:T(8,128)(2,1)S(1)} %all-to-all-done.here_ref, bf16[4,512,256]{2,1,0:T(8,128)(2,1)} %all-to-all-done.1.refs_0_, bf16[4,512,256]{2,1,0:T(8,128)(2,1)} %all-to-all-done.2.refs_1_), custom_call_target="tpu_custom_call" | custom-call | flops 2097152 | bytes 4194304 | tf_op jit(solution)/shard_map/arrange/pallas_call | solution.py:178
  120.2 4.3 %all-to-all-start.3 = ((bf16[4,512,256]{2,1,0:T(8,128)(2,1)}), bf16[4,512,256]{2,1,0:T(8,128)(2,1)}, u32[]{:S(2)}, u32[]{:S(2)}) async-start(bf16[4,512,256]{2,1,0:T(8,128)(2,1)} %arrange.1), calls=%async_computation.3 | async-start | bytes 2097152 | tf_op jit(solution)/shard_map/all_to_all | solution.py:54
  125.3 5.1 %forward.7 = (bf16[512,256]{1,0:T(8,128)(2,1)}, bf16[512,256]{1,0:T(8,128)(2,1)}, bf16[512,256]{1,0:T(8,128)(2,1)}, bf16[512,256]{1,0:T(8,128)(2,1)}) custom-call(s32[1]{0:T(128)} %bitcast.36.start_ref, bf16[512,2048]{1,0:T(8,128)(2,1)S(1)} %constant_dynamic-update-slice_fusion.wide_ref, bf16[4,2048,128]{2,1,0:T(8,128)(2,1)} %collective-permute-done.19.refs_0_, ...), custom_call_target="tpu_custom_call" | custom-call | flops 268435456 | bytes 524288 | tf_op jit(solution)/shard_map/forward/pallas_call | solution.py:131
  130.3 2.9 %collective-permute-start.21 = (bf16[512,256]{1,0:T(8,128)(2,1)}, bf16[512,256]{1,0:T(8,128)(2,1)S(1)}, u32[]{:S(2)}, u32[]{:S(2)}) collective-permute-start(bf16[512,256]{1,0:T(8,128)(2,1)} %get-tuple-element.65), channel_id=1, source_target_pairs={{0,4},{1,5},{2,6},{3,7},{4,0},{5,1},{6,2},{7,3},{8,12},{9,13},{10,... | collective-permute-start | bytes 786440 | tf_op jit(solution)/shard_map/ppermute | solution.py:390
  133.6 2.4 %collective-permute-start.23 = (bf16[512,256]{1,0:T(8,128)(2,1)}, bf16[512,256]{1,0:T(8,128)(2,1)S(1)}, u32[]{:S(2)}, u32[]{:S(2)}) collective-permute-start(bf16[512,256]{1,0:T(8,128)(2,1)} %get-tuple-element.67), channel_id=1, source_target_pairs={{0,6},{1,7},{2,0},{3,1},{4,2},{5,3},{6,4},{7,5},{8,14},{9,15},{10,... | collective-permute-start | bytes 786440 | tf_op jit(solution)/shard_map/ppermute | solution.py:390
  136.9 4.2 %collective-permute-start.28 = (f32[32,1024]{1,0:T(8,128)S(1)}, f32[32,1024]{1,0:T(8,128)S(1)}, u32[]{:S(2)}, u32[]{:S(2)}) collective-permute-start(f32[32,1024]{1,0:T(8,128)S(1)} %add.464), channel_id=1, source_target_pairs={{0,16},{8,24},{16,0},{24,8},{32,48},{40,56},{48,32},{56,40},{64,80... | collective-permute-start | bytes 393224 | tf_op jit(solution)/shard_map/ppermute | solution.py:82
  142.3 1.9 %collective-permute-start.18 = (bf16[2,512,256]{2,1,0:T(8,128)(2,1)S(1)}, bf16[2,512,256]{2,1,0:T(8,128)(2,1)S(1)}, u32[]{:S(2)}, u32[]{:S(2)}) collective-permute-start(bf16[2,512,256]{2,1,0:T(8,128)(2,1)S(1)} %slice_select_fusion.1), channel_id=1, source_target_pairs={{0,1},{1,0},{2,3},{3,2},{4,5},{5,4},{6,7},{7,6},{8,9},{9,8},{10,11... | collective-permute-start | bytes 1572872 | tf_op jit(solution)/shard_map/ppermute | solution.py:400
  145.1 6.2 %collective-permute-done.22 = bf16[512,256]{1,0:T(8,128)(2,1)S(1)} collective-permute-done((bf16[512,256]{1,0:T(8,128)(2,1)}, bf16[512,256]{1,0:T(8,128)(2,1)S(1)}, u32[]{:S(2)}, u32[]{:S(2)}) %collective-permute-start.22) | collective-permute-done | bytes 262176 | tf_op jit(solution)/shard_map/ppermute | solution.py:390
  152.9 3.8 %collective-permute-start.25 = (bf16[512,256]{1,0:T(8,128)(2,1)S(1)}, bf16[512,256]{1,0:T(8,128)(2,1)S(1)}, u32[]{:S(2)}, u32[]{:S(2)}) collective-permute-start(bf16[512,256]{1,0:T(8,128)(2,1)S(1)} %add_convert_fusion.2), channel_id=1, source_target_pairs={{1,4},{5,5},{9,12},{13,13},{17,20},{21,21},{25,28},{29,29},{33,38}... | collective-permute-start | bytes 786440 | tf_op jit(solution)/shard_map/ppermute | solution.py:285
  162.4 6.7 %collective-permute-done.30 = f32[256,256]{1,0:T(8,128)S(1)} collective-permute-done((f32[256,256]{1,0:T(8,128)S(1)}, f32[256,256]{1,0:T(8,128)S(1)}, u32[]{:S(2)}, u32[]{:S(2)}) %collective-permute-start.30) | collective-permute-done | bytes 262176 | tf_op jit(solution)/shard_map/ppermute | solution.py:61
  169.1 6.6 %backward.5 = (f32[512,1024]{1,0:T(8,128)S(1)}, bf16[512,1024]{1,0:T(8,128)(2,1)S(1)}) custom-call(s32[8]{0:T(128)S(1)} %stack.179.spots_ref, bf16[4,2048,128]{2,1,0:T(8,128)(2,1)} %collective-permute-done.19.refs_0_, bf16[4,2048,128]{2,1,0:T(8,128)(2,1)} %collective-permute-done.20.refs_1_, bf16[512,8192]{1,0:T(8,128)(2,1)} %refs_9_.5, ...), custom_call_target="tpu_custom_call" | custom-call | flops 268435456 | bytes 524288 | tf_op jit(solution)/shard_map/backward/pallas_call | solution.py:237
  179.0 1.4 add_convert_fusion.1
  180.4 7.4 %collective-permute-done.32 = f32[256,256]{1,0:T(8,128)S(1)} collective-permute-done((f32[256,256]{1,0:T(8,128)S(1)}, f32[256,256]{1,0:T(8,128)S(1)}, u32[]{:S(2)}, u32[]{:S(2)}) %collective-permute-start.32) | collective-permute-done | bytes 262176 | tf_op jit(solution)/shard_map/ppermute | solution.py:61
  188.5 1.4 add_convert_fusion
  (126 shorter events, 25.2 us)
Async XLA Ops:
  0.6 13.2 %copy-start = (f32[256,256]{1,0:T(8,128)S(1)}, f32[256,256]{1,0:T(8,128)}, u32[]{:S(2)}) copy-start(f32[256,256]{1,0:T(8,128)} %param.10) | copy-start | bytes 786436
  2.0 3.2 %collective-permute-start.1 = (bf16[1024,256]{1,0:T(8,128)(2,1)S(1)}, bf16[1024,256]{1,0:T(8,128)(2,1)}, u32[]{:S(2)}, u32[]{:S(2)}) collective-permute-start(bf16[1024,256]{1,0:T(8,128)(2,1)S(1)} %get-tuple-element.76), channel_id=1, source_target_pairs={{0,1},{1,0},{2,3},{3,2},{4,5},{5,4},{6,7},{7,6},{8,9},{9,8},{10,11... | collective-permute-start | bytes 1572872 | tf_op jit(solution)/shard_map/ppermute | solution.py:312
  3.6 46.8 %collective-permute-start = (bf16[512,1024]{1,0:T(8,128)(2,1)S(1)}, bf16[512,1024]{1,0:T(8,128)(2,1)}, u32[]{:S(2)}, u32[]{:S(2)}) collective-permute-start(bf16[512,1024]{1,0:T(8,128)(2,1)S(1)} %copy-done.2), channel_id=1, source_target_pairs={{0,1},{1,0},{2,3},{3,2},{4,5},{5,4},{6,7},{7,6},{8,9},{9,8},{10,11... | collective-permute-start | bytes 3145736 | tf_op jit(solution)/shard_map/ppermute | solution.py:332
  3.7 9.4 %copy-start.19 = (f32[16,4,2]{0,2,1:T(2,128)S(1)}, f32[16,4,2]{0,2,1:T(2,128)}, u32[]{:S(2)}) copy-start(f32[16,4,2]{0,2,1:T(2,128)} %param.13) | copy-start | bytes 1540
  3.7 10.1 %copy-start.14 = (s32[16,4,2]{0,2,1:T(2,128)S(1)}, s32[16,4,2]{0,2,1:T(2,128)}, u32[]{:S(2)}) copy-start(s32[16,4,2]{0,2,1:T(2,128)} %param.14) | copy-start | bytes 1540
  3.7 10.4 %copy-start.15 = (s32[16,4,2]{0,2,1:T(2,128)S(1)}, s32[16,4,2]{0,2,1:T(2,128)}, u32[]{:S(2)}) copy-start(s32[16,4,2]{0,2,1:T(2,128)} %param.12) | copy-start | bytes 1540
  6.4 19.6 %collective-permute-start.3 = (bf16[2048,128]{1,0:T(8,128)(2,1)S(1)}, bf16[2048,128]{1,0:T(8,128)(2,1)S(1)}, u32[]{:S(2)}, u32[]{:S(2)}) collective-permute-start(bf16[2048,128]{1,0:T(8,128)(2,1)S(1)} %get-tuple-element.39), channel_id=1, source_target_pairs={{0,32},{1,9},{2,34},{3,11},{4,36},{5,13},{6,38},{7,15},{8,40},{9,1... | collective-permute-start | bytes 1572872 | tf_op jit(solution)/shard_map/ppermute | solution.py:43
  8.2 29.2 %collective-permute-start.2 = (bf16[2048,128]{1,0:T(8,128)(2,1)S(1)}, bf16[2048,128]{1,0:T(8,128)(2,1)S(1)}, u32[]{:S(2)}, u32[]{:S(2)}) collective-permute-start(bf16[2048,128]{1,0:T(8,128)(2,1)S(1)} %get-tuple-element.39), channel_id=1, source_target_pairs={{0,96},{1,25},{2,98},{3,27},{4,100},{5,29},{6,102},{7,31},{8,104},... | collective-permute-start | bytes 1572872 | tf_op jit(solution)/shard_map/ppermute | solution.py:43
  10.4 17.3 %collective-permute-start.7 = (bf16[2048,128]{1,0:T(8,128)(2,1)S(1)}, bf16[2048,128]{1,0:T(8,128)(2,1)}, u32[]{:S(2)}, u32[]{:S(2)}) collective-permute-start(bf16[2048,128]{1,0:T(8,128)(2,1)S(1)} %get-tuple-element.40), channel_id=1, source_target_pairs={{0,32},{1,9},{2,34},{3,11},{4,36},{5,13},{6,38},{7,15},{8,40},{9,1... | collective-permute-start | bytes 1572872 | tf_op jit(solution)/shard_map/ppermute | solution.py:43
  10.4 12.0 %collective-permute-start.5 = (bf16[2048,128]{1,0:T(8,128)(2,1)S(1)}, bf16[2048,128]{1,0:T(8,128)(2,1)}, u32[]{:S(2)}, u32[]{:S(2)}) collective-permute-start(bf16[2048,128]{1,0:T(8,128)(2,1)S(1)} %get-tuple-element.40), channel_id=1, source_target_pairs={{0,96},{1,25},{2,98},{3,27},{4,100},{5,29},{6,102},{7,31},{8,104},... | collective-permute-start | bytes 1572872 | tf_op jit(solution)/shard_map/ppermute | solution.py:43
  14.1 17.9 %copy-start.10 = (bf16[4,2,8,256]{3,2,0,1:T(8,128)(2,1)}, bf16[4,2,8,256]{3,2,0,1:T(8,128)(2,1)S(1)}, u32[]{:S(2)}) copy-start(bf16[4,2,8,256]{3,2,0,1:T(8,128)(2,1)S(1)} %copy.45) | copy-start | bytes 98308
  14.5 17.5 %copy-start.4 = (bf16[4,2,8,256]{3,2,0,1:T(8,128)(2,1)}, bf16[4,2,8,256]{3,2,0,1:T(8,128)(2,1)S(1)}, u32[]{:S(2)}) copy-start(bf16[4,2,8,256]{3,2,0,1:T(8,128)(2,1)S(1)} %copy.44) | copy-start | bytes 98308
  22.4 9.7 %collective-permute-start.6 = (bf16[2048,128]{1,0:T(8,128)(2,1)}, bf16[2048,128]{1,0:T(8,128)(2,1)S(1)}, u32[]{:S(2)}, u32[]{:S(2)}) collective-permute-start(bf16[2048,128]{1,0:T(8,128)(2,1)} %collective-permute-done.5), channel_id=1, source_target_pairs={{0,96},{1,25},{2,98},{3,27},{4,100},{5,29},{6,102},{7,31},{8,104},... | collective-permute-start | bytes 1572872 | tf_op jit(solution)/shard_map/ppermute | solution.py:43
  26.0 11.3 %collective-permute-start.4 = (bf16[2048,128]{1,0:T(8,128)(2,1)S(1)}, bf16[2048,128]{1,0:T(8,128)(2,1)S(1)}, u32[]{:S(2)}, u32[]{:S(2)}) collective-permute-start(bf16[2048,128]{1,0:T(8,128)(2,1)S(1)} %collective-permute-done.3), channel_id=1, source_target_pairs={{0,32},{1,9},{2,34},{3,11},{4,36},{5,13},{6,38},{7,15},{8,40},{9,1... | collective-permute-start | bytes 1572872 | tf_op jit(solution)/shard_map/ppermute | solution.py:43
  34.8 36.0 %collective-permute-start.12 = (bf16[4,2048,128]{2,1,0:T(8,128)(2,1)}, bf16[4,2048,128]{2,1,0:T(8,128)(2,1)}, u32[]{:S(2)}, u32[]{:S(2)}) collective-permute-start(bf16[4,2048,128]{2,1,0:T(8,128)(2,1)} %pad_maximum_fusion.1.refs_1_), channel_id=1, source_target_pairs={{0,24},{1,97},{2,26},{3,99},{4,28},{5,101},{6,30},{7,103},{8,0},{9... | collective-permute-start | bytes 6291464 | tf_op jit(solution)/shard_map/ppermute | solution.py:43
  38.9 31.9 %collective-permute-start.11 = (bf16[4,2048,128]{2,1,0:T(8,128)(2,1)}, bf16[4,2048,128]{2,1,0:T(8,128)(2,1)}, u32[]{:S(2)}, u32[]{:S(2)}) collective-permute-start(bf16[4,2048,128]{2,1,0:T(8,128)(2,1)} %pad_maximum_fusion.refs_0_), channel_id=1, source_target_pairs={{0,8},{1,33},{2,10},{3,35},{4,12},{5,37},{6,14},{7,39},{8,16},{9,4... | collective-permute-start | bytes 6291464 | tf_op jit(solution)/shard_map/ppermute | solution.py:43
  38.9 3.7 %collective-permute-start.8 = (f32[32,512]{1,0:T(8,128)S(1)}, f32[32,512]{1,0:T(8,128)S(1)}, u32[]{:S(2)}, u32[]{:S(2)}) collective-permute-start(f32[32,512]{1,0:T(8,128)S(1)} %pad_maximum_fusion.4), channel_id=1, source_target_pairs={{0,1},{1,0},{2,3},{3,2},{4,5},{5,4},{6,7},{7,6},{8,9},{9,8},{10,11... | collective-permute-start | bytes 196616 | tf_op jit(solution)/shard_map/ppermute | solution.py:61
  42.6 3.6 %collective-permute-start.9 = (f32[32,512]{1,0:T(8,128)S(1)}, f32[32,512]{1,0:T(8,128)S(1)}, u32[]{:S(2)}, u32[]{:S(2)}) collective-permute-start(f32[32,512]{1,0:T(8,128)S(1)} %add.383), channel_id=1, source_target_pairs={{0,2},{1,3},{2,0},{3,1},{4,6},{5,7},{6,4},{7,5},{8,10},{9,11},{10,... | collective-permute-start | bytes 196616 | tf_op jit(solution)/shard_map/ppermute | solution.py:61
  44.0 44.5 %collective-permute-start.14 = (bf16[4,2048,128]{2,1,0:T(8,128)(2,1)}, bf16[4,2048,128]{2,1,0:T(8,128)(2,1)}, u32[]{:S(2)}, u32[]{:S(2)}) collective-permute-start(bf16[4,2048,128]{2,1,0:T(8,128)(2,1)} %pad_maximum_fusion.1.refs_1_), channel_id=1, source_target_pairs={{0,8},{1,33},{2,10},{3,35},{4,12},{5,37},{6,14},{7,39},{8,16},{9,4... | collective-permute-start | bytes 6291464 | tf_op jit(solution)/shard_map/ppermute | solution.py:43
  46.2 42.3 %collective-permute-start.13 = (bf16[4,2048,128]{2,1,0:T(8,128)(2,1)}, bf16[4,2048,128]{2,1,0:T(8,128)(2,1)}, u32[]{:S(2)}, u32[]{:S(2)}) collective-permute-start(bf16[4,2048,128]{2,1,0:T(8,128)(2,1)} %pad_maximum_fusion.refs_0_), channel_id=1, source_target_pairs={{0,24},{1,97},{2,26},{3,99},{4,28},{5,101},{6,30},{7,103},{8,0},{9... | collective-permute-start | bytes 6291464 | tf_op jit(solution)/shard_map/ppermute | solution.py:43
  50.4 9.3 %collective-permute-start.10 = (f32[32,512]{1,0:T(8,128)S(1)}, f32[32,512]{1,0:T(8,128)S(1)}, u32[]{:S(2)}, u32[]{:S(2)}) collective-permute-start(f32[32,512]{1,0:T(8,128)S(1)} %add.384), channel_id=1, source_target_pairs={{0,4},{1,5},{2,6},{3,7},{4,0},{5,1},{6,2},{7,3},{8,12},{9,13},{10,... | collective-permute-start | bytes 196616 | tf_op jit(solution)/shard_map/ppermute | solution.py:61
  60.3 17.3 %all-to-all-start = ((bf16[4,512,256]{2,1,0:T(8,128)(2,1)}), bf16[4,512,256]{2,1,0:T(8,128)(2,1)S(1)}, u32[]{:S(2)}, u32[]{:S(2)}) async-start(bf16[4,512,256]{2,1,0:T(8,128)(2,1)} %forward.4), calls=%async_computation | async-start | bytes 2097152 | tf_op jit(solution)/shard_map/all_to_all | solution.py:54
  77.6 17.2 %all-to-all-start.1 = ((bf16[4,512,256]{2,1,0:T(8,128)(2,1)}), bf16[4,512,256]{2,1,0:T(8,128)(2,1)}, u32[]{:S(2)}, u32[]{:S(2)}) async-start(bf16[4,512,256]{2,1,0:T(8,128)(2,1)} %forward.5), calls=%async_computation.1 | async-start | bytes 2097152 | tf_op jit(solution)/shard_map/all_to_all | solution.py:54
  81.9 43.3 %collective-permute-start.19 = (bf16[4,2048,128]{2,1,0:T(8,128)(2,1)}, bf16[4,2048,128]{2,1,0:T(8,128)(2,1)}, u32[]{:S(2)}, u32[]{:S(2)}) collective-permute-start(bf16[4,2048,128]{2,1,0:T(8,128)(2,1)} %collective-permute-done.11.refs_0_), channel_id=1, source_target_pairs={{0,8},{1,33},{2,10},{3,35},{4,12},{5,37},{6,14},{7,39},{8,16},{9,4... | collective-permute-start | bytes 6291464 | tf_op jit(solution)/shard_map/ppermute | solution.py:43
  82.2 43.1 %collective-permute-start.20 = (bf16[4,2048,128]{2,1,0:T(8,128)(2,1)}, bf16[4,2048,128]{2,1,0:T(8,128)(2,1)}, u32[]{:S(2)}, u32[]{:S(2)}) collective-permute-start(bf16[4,2048,128]{2,1,0:T(8,128)(2,1)} %collective-permute-done.12.refs_1_), channel_id=1, source_target_pairs={{0,24},{1,97},{2,26},{3,99},{4,28},{5,101},{6,30},{7,103},{8,0},{9... | collective-permute-start | bytes 6291464 | tf_op jit(solution)/shard_map/ppermute | solution.py:43
  94.8 22.7 %all-to-all-start.2 = ((bf16[4,512,256]{2,1,0:T(8,128)(2,1)}), bf16[4,512,256]{2,1,0:T(8,128)(2,1)}, u32[]{:S(2)}, u32[]{:S(2)}) async-start(bf16[4,512,256]{2,1,0:T(8,128)(2,1)} %forward.6), calls=%async_computation.2 | async-start | bytes 2097152 | tf_op jit(solution)/shard_map/all_to_all | solution.py:54
  99.1 14.6 %collective-permute-start.17 = (f32[32,1024]{1,0:T(8,128)}, f32[32,1024]{1,0:T(8,128)}, u32[]{:S(2)}, u32[]{:S(2)}) collective-permute-start(f32[32,1024]{1,0:T(8,128)} %maximum_multiply_fusion), channel_id=1, source_target_pairs={{0,96},{1,97},{2,98},{3,99},{4,100},{5,101},{6,102},{7,103},{8,104... | collective-permute-start | bytes 393224 | tf_op jit(solution)/shard_map/ppermute | solution.py:72
  99.2 14.5 %collective-permute-start.16 = (f32[32,1024]{1,0:T(8,128)}, f32[32,1024]{1,0:T(8,128)}, u32[]{:S(2)}, u32[]{:S(2)}) collective-permute-start(f32[32,1024]{1,0:T(8,128)} %maximum_multiply_fusion), channel_id=1, source_target_pairs={{0,64},{1,65},{2,66},{3,67},{4,68},{5,69},{6,70},{7,71},{8,72},{9,... | collective-permute-start | bytes 393224 | tf_op jit(solution)/shard_map/ppermute | solution.py:72
  99.3 16.6 %collective-permute-start.15 = (f32[32,1024]{1,0:T(8,128)}, f32[32,1024]{1,0:T(8,128)}, u32[]{:S(2)}, u32[]{:S(2)}) collective-permute-start(f32[32,1024]{1,0:T(8,128)} %maximum_multiply_fusion), channel_id=1, source_target_pairs={{0,32},{1,33},{2,34},{3,35},{4,36},{5,37},{6,38},{7,39},{8,40},{9,... | collective-permute-start | bytes 393224 | tf_op jit(solution)/shard_map/ppermute | solution.py:72
  100.7 15.1 %copy-start.3 = (f32[32,1024]{1,0:T(8,128)S(1)}, f32[32,1024]{1,0:T(8,128)}, u32[]{:S(2)}) copy-start(f32[32,1024]{1,0:T(8,128)} %maximum_multiply_fusion) | copy-start | bytes 393220
  120.2 21.0 %all-to-all-start.3 = ((bf16[4,512,256]{2,1,0:T(8,128)(2,1)}), bf16[4,512,256]{2,1,0:T(8,128)(2,1)}, u32[]{:S(2)}, u32[]{:S(2)}) async-start(bf16[4,512,256]{2,1,0:T(8,128)(2,1)} %arrange.1), calls=%async_computation.3 | async-start | bytes 2097152 | tf_op jit(solution)/shard_map/all_to_all | solution.py:54
  124.5 11.5 %collective-permute-start.27 = (f32[32,1024]{1,0:T(8,128)}, f32[32,1024]{1,0:T(8,128)}, u32[]{:S(2)}, u32[]{:S(2)}) collective-permute-start(f32[32,1024]{1,0:T(8,128)} %add_add_fusion), channel_id=1, source_target_pairs={{0,8},{8,0},{16,24},{24,16},{32,40},{40,32},{48,56},{56,48},{64,72... | collective-permute-start | bytes 393224 | tf_op jit(solution)/shard_map/ppermute | solution.py:82
  125.2 16.0 %copy-start.1 = (bf16[4,512,256]{2,1,0:T(8,128)(2,1)S(1)}, bf16[4,512,256]{2,1,0:T(8,128)(2,1)}, u32[]{:S(2)}) copy-start(bf16[4,512,256]{2,1,0:T(8,128)(2,1)} %arrange.1) | copy-start | bytes 3145732
  130.3 21.7 %copy-start.6 = (bf16[512,256]{1,0:T(8,128)(2,1)S(1)}, bf16[512,256]{1,0:T(8,128)(2,1)}, u32[]{:S(2)}) copy-start(bf16[512,256]{1,0:T(8,128)(2,1)} %get-tuple-element.64) | copy-start | bytes 786436
  130.3 14.7 %collective-permute-start.21 = (bf16[512,256]{1,0:T(8,128)(2,1)}, bf16[512,256]{1,0:T(8,128)(2,1)S(1)}, u32[]{:S(2)}, u32[]{:S(2)}) collective-permute-start(bf16[512,256]{1,0:T(8,128)(2,1)} %get-tuple-element.65), channel_id=1, source_target_pairs={{0,4},{1,5},{2,6},{3,7},{4,0},{5,1},{6,2},{7,3},{8,12},{9,13},{10,... | collective-permute-start | bytes 786440 | tf_op jit(solution)/shard_map/ppermute | solution.py:390
  133.3 18.0 %collective-permute-start.22 = (bf16[512,256]{1,0:T(8,128)(2,1)}, bf16[512,256]{1,0:T(8,128)(2,1)S(1)}, u32[]{:S(2)}, u32[]{:S(2)}) collective-permute-start(bf16[512,256]{1,0:T(8,128)(2,1)} %get-tuple-element.66), channel_id=1, source_target_pairs={{0,2},{1,3},{2,4},{3,5},{4,6},{5,7},{6,0},{7,1},{8,10},{9,11},{10,... | collective-permute-start | bytes 786440 | tf_op jit(solution)/shard_map/ppermute | solution.py:390
  133.6 17.7 %collective-permute-start.23 = (bf16[512,256]{1,0:T(8,128)(2,1)}, bf16[512,256]{1,0:T(8,128)(2,1)S(1)}, u32[]{:S(2)}, u32[]{:S(2)}) collective-permute-start(bf16[512,256]{1,0:T(8,128)(2,1)} %get-tuple-element.67), channel_id=1, source_target_pairs={{0,6},{1,7},{2,0},{3,1},{4,2},{5,3},{6,4},{7,5},{8,14},{9,15},{10,... | collective-permute-start | bytes 786440 | tf_op jit(solution)/shard_map/ppermute | solution.py:390
  136.9 7.3 %collective-permute-start.28 = (f32[32,1024]{1,0:T(8,128)S(1)}, f32[32,1024]{1,0:T(8,128)S(1)}, u32[]{:S(2)}, u32[]{:S(2)}) collective-permute-start(f32[32,1024]{1,0:T(8,128)S(1)} %add.464), channel_id=1, source_target_pairs={{0,16},{8,24},{16,0},{24,8},{32,48},{40,56},{48,32},{56,40},{64,80... | collective-permute-start | bytes 393224 | tf_op jit(solution)/shard_map/ppermute | solution.py:82
  142.3 18.0 %copy-start.17 = (f32[16,4,2]{0,2,1:T(2,128)S(1)}, f32[16,4,2]{0,2,1:T(2,128)}, u32[]{:S(2)}) copy-start(f32[16,4,2]{0,2,1:T(2,128)} %copy-done.16) | copy-start | bytes 1540
  142.3 34.8 %collective-permute-start.18 = (bf16[2,512,256]{2,1,0:T(8,128)(2,1)S(1)}, bf16[2,512,256]{2,1,0:T(8,128)(2,1)S(1)}, u32[]{:S(2)}, u32[]{:S(2)}) collective-permute-start(bf16[2,512,256]{2,1,0:T(8,128)(2,1)S(1)} %slice_select_fusion.1), channel_id=1, source_target_pairs={{0,1},{1,0},{2,3},{3,2},{4,5},{5,4},{6,7},{7,6},{8,9},{9,8},{10,11... | collective-permute-start | bytes 1572872 | tf_op jit(solution)/shard_map/ppermute | solution.py:400
  152.2 26.0 %collective-permute-start.26 = (bf16[512,256]{1,0:T(8,128)(2,1)S(1)}, bf16[512,256]{1,0:T(8,128)(2,1)S(1)}, u32[]{:S(2)}, u32[]{:S(2)}) collective-permute-start(bf16[512,256]{1,0:T(8,128)(2,1)S(1)} %add_convert_fusion.2), channel_id=1, source_target_pairs={{3,4},{7,5},{11,12},{15,13},{19,20},{23,21},{27,28},{31,29},{35,38... | collective-permute-start | bytes 786440 | tf_op jit(solution)/shard_map/ppermute | solution.py:285
  152.9 25.3 %collective-permute-start.25 = (bf16[512,256]{1,0:T(8,128)(2,1)S(1)}, bf16[512,256]{1,0:T(8,128)(2,1)S(1)}, u32[]{:S(2)}, u32[]{:S(2)}) collective-permute-start(bf16[512,256]{1,0:T(8,128)(2,1)S(1)} %add_convert_fusion.2), channel_id=1, source_target_pairs={{1,4},{5,5},{9,12},{13,13},{17,20},{21,21},{25,28},{29,29},{33,38}... | collective-permute-start | bytes 786440 | tf_op jit(solution)/shard_map/ppermute | solution.py:285
  156.8 21.6 %collective-permute-start.24 = (bf16[512,256]{1,0:T(8,128)(2,1)S(1)}, bf16[512,256]{1,0:T(8,128)(2,1)S(1)}, u32[]{:S(2)}, u32[]{:S(2)}) collective-permute-start(bf16[512,256]{1,0:T(8,128)(2,1)S(1)} %add_convert_fusion.2), channel_id=1, source_target_pairs={{0,1},{2,3},{4,5},{6,7},{8,9},{10,11},{12,13},{14,15},{32,33},{34,... | collective-permute-start | bytes 786440 | tf_op jit(solution)/shard_map/ppermute | solution.py:290
  158.9 2.4 %collective-permute-start.29 = (f32[256,256]{1,0:T(8,128)S(1)}, f32[256,256]{1,0:T(8,128)S(1)}, u32[]{:S(2)}, u32[]{:S(2)}) collective-permute-start(f32[256,256]{1,0:T(8,128)S(1)} %fusion.2), channel_id=1, source_target_pairs={{0,1},{1,0},{2,3},{3,2},{4,5},{5,4},{6,7},{7,6},{8,9},{9,8},{10,11... | collective-permute-start | bytes 786440 | tf_op jit(solution)/shard_map/ppermute | solution.py:61
  161.3 7.8 %collective-permute-start.30 = (f32[256,256]{1,0:T(8,128)S(1)}, f32[256,256]{1,0:T(8,128)S(1)}, u32[]{:S(2)}, u32[]{:S(2)}) collective-permute-start(f32[256,256]{1,0:T(8,128)S(1)} %add.467), channel_id=1, source_target_pairs={{0,2},{1,3},{2,0},{3,1},{4,6},{5,7},{6,4},{7,5},{8,10},{9,11},{10,... | collective-permute-start | bytes 786440 | tf_op jit(solution)/shard_map/ppermute | solution.py:61
  175.8 12.8 %collective-permute-start.31 = (bf16[512,1024]{1,0:T(8,128)(2,1)S(1)}, bf16[512,1024]{1,0:T(8,128)(2,1)S(1)}, u32[]{:S(2)}, u32[]{:S(2)}) collective-permute-start(bf16[512,1024]{1,0:T(8,128)(2,1)S(1)} %get-tuple-element.72), channel_id=1, source_target_pairs={{0,1},{1,0},{2,3},{3,2},{4,5},{5,4},{6,7},{7,6},{8,9},{9,8},{10,11... | collective-permute-start | bytes 3145736 | tf_op jit(solution)/shard_map/ppermute | solution.py:414
  178.3 9.5 %collective-permute-start.32 = (f32[256,256]{1,0:T(8,128)S(1)}, f32[256,256]{1,0:T(8,128)S(1)}, u32[]{:S(2)}, u32[]{:S(2)}) collective-permute-start(f32[256,256]{1,0:T(8,128)S(1)} %add.468), channel_id=1, source_target_pairs={{0,4},{1,5},{2,6},{3,7},{4,0},{5,1},{6,2},{7,3},{8,12},{9,13},{10,... | collective-permute-start | bytes 786440 | tf_op jit(solution)/shard_map/ppermute | solution.py:61
  179.0 9.6 %copy-start.5 = (bf16[4,2,8,256]{3,2,0,1:T(8,128)(2,1)S(1)}, bf16[4,2,8,256]{3,2,0,1:T(8,128)(2,1)}, u32[]{:S(2)}) copy-start(bf16[4,2,8,256]{3,2,0,1:T(8,128)(2,1)} %copy-done.4) | copy-start | bytes 98308
  (9 other events, 26.4 us)

commit v13 on v9

--- a/solution.py
+++ b/solution.py
@@ -393,11 +393,11 @@
     both = with_partner(both, 2, *sent)
     bank_a, logit_grad_a = compose_back(both[:rank], weights_a, picked_a, mixing_a, vector_bank)
     bank_b, logit_grad_b = compose_back(both[rank:], weights_b, picked_b, mixing_b, vector_bank)
-    bank_part = over_tensor(bank_a + bank_b, (1, 2))
+    bank_part = over_tensor(bank_a + bank_b, (1,))
     grown, other = backward(
         after(spots_of(across), *sent, bank_part), grown, out_grad, take(across), last=True
     )
-    bank_grad = over_tensor(bank_part, (4,))
+    bank_grad = over_tensor(bank_part, (2, 4))
     crossed = lax.ppermute(jnp.where(core == 0, slots[2:], moved[:2]), "tensor", SWAP)
     firsts = jnp.where(core == 0, slots[:2], crossed)
     seconds = jnp.where(core == 0, crossed, moved[2:])

time: 181 us -> 189 us (1.044)
  waiting for transfers between devices: 33.7 us -> 41.8 us
    ppermute x6, waiting for transfers between devices: 3.98 us -> 11.1 us  [over_tensor(): lax.ppermute(value, 'tensor', [(t, t ^ bit) for t in range(8)])]
  transfers between devices with their start and end apart: 37 -> 37, of which waited for: 10 -> 12; matrix products, arithmetic and copies ran while one was open for 14% -> 13% of each run, Pallas kernels for 25% -> 24%
where the time goes in v13:
time: 189 us; the launch traced here: 187 us
  starting transfers between devices  68.4 us (36%)
  Pallas kernels  45.6 us (24%)
  waiting for transfers between devices  41.8 us (22%)
  other arithmetic  15.5 us (8%)
  matrix products  9.9 us (5%)
  local copies, waits for them, and re-layouts  4.86 us (3%)
    pallas_call x3, Pallas kernels, backward(): pl.pallas_call(functools.partial(backward_kernel, count, first, last), ou...  23.2 us
    pallas_call x4, Pallas kernels, forward(): pl.pallas_call(functools.partial(forward_kernel, count, many), out_shape=...  19.8 us
    ppermute x12, starting transfers between devices, shift(): return lax.ppermute(value, BOTH, ring(stage, step))  19.1 us
    all_to_all x4, starting transfers between devices, exchange(): lax.all_to_all(value, axis, split_axis=0, concat_axis=0, tiled=True, axis...  16.4 us
    ppermute x12, waiting for transfers between devices, shift(): return lax.ppermute(value, BOTH, ring(stage, step))  12.4 us
    ppermute x6, waiting for transfers between devices, over_tensor(): lax.ppermute(value, 'tensor', [(t, t ^ bit) for t in range(8)])  11.1 us
    ppermute x6, starting transfers between devices, over_tensor(): lax.ppermute(value, 'tensor', [(t, t ^ bit) for t in range(8)])  7.54 us
    ppermute x3, waiting for transfers between devices, local(): arrived.append(lax.ppermute(sent[step], 'tensor', turns))  7.37 us
  transfers between devices with their start and end apart: 37, of which 12 were waited for; matrix products, arithmetic and copies ran while one was open for 13% of the time, Pallas kernels for 24%

profile of v13, /device:TPU:1, one launch (start us, length us, event | category | flops | bytes accessed | tf_op | source)
XLA Modules:
  0.0 187.5 jit_solution(14251037870202513494)
XLA Ops:
  2.0 1.5 collective-permute-start.1
  3.5 1.6 collective-permute-done.1
  6.3 1.8 collective-permute-start.3
  8.1 2.2 %collective-permute-start.2 = (bf16[2048,128]{1,0:T(8,128)(2,1)S(1)}, bf16[2048,128]{1,0:T(8,128)(2,1)S(1)}, u32[]{:S(2)}, u32[]{:S(2)}) collective-permute-start(bf16[2048,128]{1,0:T(8,128)(2,1)S(1)} %get-tuple-element.39), channel_id=1, source_target_pairs={{0,96},{1,25},{2,98},{3,27},{4,100},{5,29},{6,102},{7,31},{8,104},... | collective-permute-start | bytes 1572872 | tf_op jit(solution)/shard_map/ppermute | solution.py:43
  10.3 2.7 %collective-permute-start.5 = (bf16[2048,128]{1,0:T(8,128)(2,1)S(1)}, bf16[2048,128]{1,0:T(8,128)(2,1)}, u32[]{:S(2)}, u32[]{:S(2)}) collective-permute-start(bf16[2048,128]{1,0:T(8,128)(2,1)S(1)} %get-tuple-element.40), channel_id=1, source_target_pairs={{0,96},{1,25},{2,98},{3,27},{4,100},{5,29},{6,102},{7,31},{8,104},... | collective-permute-start | bytes 1572872 | tf_op jit(solution)/shard_map/ppermute | solution.py:43
  14.5 7.9 %collective-permute-done.5 = bf16[2048,128]{1,0:T(8,128)(2,1)} collective-permute-done((bf16[2048,128]{1,0:T(8,128)(2,1)S(1)}, bf16[2048,128]{1,0:T(8,128)(2,1)}, u32[]{:S(2)}, u32[]{:S(2)}) %collective-permute-start.5) | collective-permute-done | bytes 524320 | tf_op jit(solution)/shard_map/ppermute | solution.py:43
  22.3 3.2 %collective-permute-start.6 = (bf16[2048,128]{1,0:T(8,128)(2,1)}, bf16[2048,128]{1,0:T(8,128)(2,1)S(1)}, u32[]{:S(2)}, u32[]{:S(2)}) collective-permute-start(bf16[2048,128]{1,0:T(8,128)(2,1)} %collective-permute-done.5), channel_id=1, source_target_pairs={{0,96},{1,25},{2,98},{3,27},{4,100},{5,29},{6,102},{7,31},{8,104},... | collective-permute-start | bytes 1572872 | tf_op jit(solution)/shard_map/ppermute | solution.py:43
  25.9 1.6 fusion.11
  27.6 4.4 %collective-permute-done.6 = bf16[2048,128]{1,0:T(8,128)(2,1)S(1)} collective-permute-done((bf16[2048,128]{1,0:T(8,128)(2,1)}, bf16[2048,128]{1,0:T(8,128)(2,1)S(1)}, u32[]{:S(2)}, u32[]{:S(2)}) %collective-permute-start.6) | collective-permute-done | bytes 524320 | tf_op jit(solution)/shard_map/ppermute | solution.py:43
  32.0 2.8 %pad_maximum_fusion.1.refs_1_ = bf16[4,2048,128]{2,1,0:T(8,128)(2,1)} fusion(bf16[1,2048,128]{2,1,0:T(8,128)(2,1)} %bitcast.9, bf16[1,2048,128]{2,1,0:T(8,128)(2,1)S(1)} %bitcast.111, bf16[1,2048,128]{2,1,0:T(8,128)(2,1)} %bitcast.7, bf16[1,2048,128]{2,1,0:T(8,128)(2,1)S(1)} %bitcast.103), kind=kLoop, calls=%fused_computation.3 | loop fusion | flops 3145728 | bytes 4194304 | tf_op jit(solution)/shard_map/stack | solution.py:318
  34.8 2.5 %collective-permute-start.12 = (bf16[4,2048,128]{2,1,0:T(8,128)(2,1)}, bf16[4,2048,128]{2,1,0:T(8,128)(2,1)}, u32[]{:S(2)}, u32[]{:S(2)}) collective-permute-start(bf16[4,2048,128]{2,1,0:T(8,128)(2,1)} %pad_maximum_fusion.1.refs_1_), channel_id=1, source_target_pairs={{0,24},{1,97},{2,26},{3,99},{4,28},{5,101},{6,30},{7,103},{8,0},{9... | collective-permute-start | bytes 6291464 | tf_op jit(solution)/shard_map/ppermute | solution.py:43
  37.2 1.6 pad_maximum_fusion.refs_0_
  38.8 2.8 %collective-permute-start = (bf16[512,1024]{1,0:T(8,128)(2,1)S(1)}, bf16[512,1024]{1,0:T(8,128)(2,1)}, u32[]{:S(2)}, u32[]{:S(2)}) collective-permute-start(bf16[512,1024]{1,0:T(8,128)(2,1)S(1)} %copy-done.2), channel_id=1, source_target_pairs={{0,1},{1,0},{2,3},{3,2},{4,5},{5,4},{6,7},{7,6},{8,9},{9,8},{10,11... | collective-permute-start | bytes 3145736 | tf_op jit(solution)/shard_map/ppermute | solution.py:332
  41.6 2.2 %collective-permute-done.8 = f32[32,512]{1,0:T(8,128)S(1)} collective-permute-done((f32[32,512]{1,0:T(8,128)S(1)}, f32[32,512]{1,0:T(8,128)S(1)}, u32[]{:S(2)}, u32[]{:S(2)}) %collective-permute-start.8) | collective-permute-done | bytes 65568 | tf_op jit(solution)/shard_map/ppermute | solution.py:61
  43.9 1.4 collective-permute-start.9
  45.9 1.7 collective-permute-done.9
  47.6 3.3 %collective-permute-start.13 = (bf16[4,2048,128]{2,1,0:T(8,128)(2,1)}, bf16[4,2048,128]{2,1,0:T(8,128)(2,1)}, u32[]{:S(2)}, u32[]{:S(2)}) collective-permute-start(bf16[4,2048,128]{2,1,0:T(8,128)(2,1)} %pad_maximum_fusion.refs_0_), channel_id=1, source_target_pairs={{0,24},{1,97},{2,26},{3,99},{4,28},{5,101},{6,30},{7,103},{8,0},{9... | collective-permute-start | bytes 6291464 | tf_op jit(solution)/shard_map/ppermute | solution.py:43
  51.8 3.0 %collective-permute-start.10 = (f32[32,512]{1,0:T(8,128)S(1)}, f32[32,512]{1,0:T(8,128)S(1)}, u32[]{:S(2)}, u32[]{:S(2)}) collective-permute-start(f32[32,512]{1,0:T(8,128)S(1)} %add.384), channel_id=1, source_target_pairs={{0,4},{1,5},{2,6},{3,7},{4,0},{5,1},{6,2},{7,3},{8,12},{9,13},{10,... | collective-permute-start | bytes 196616 | tf_op jit(solution)/shard_map/ppermute | solution.py:61
  56.1 5.0 %forward.4 = bf16[4,512,256]{2,1,0:T(8,128)(2,1)} custom-call(s32[1]{0:T(128)} %bitcast.1.start_ref, bf16[512,2048]{1,0:T(8,128)(2,1)S(1)} %constant_dynamic-update-slice_fusion.wide_ref, bf16[4,2048,128]{2,1,0:T(8,128)(2,1)} %pad_maximum_fusion.refs_0_, bf16[4,2048,128]{2,1,0:T(8,128)(2,1)} %pad_maximum_fusion.1.refs_1_), custom_call_target="tpu_custom_call" | custom-call | flops 268435456 | bytes 524288 | tf_op jit(solution)/shard_map/forward/pallas_call | solution.py:131
  61.7 3.5 %all-to-all-start = ((bf16[4,512,256]{2,1,0:T(8,128)(2,1)}), bf16[4,512,256]{2,1,0:T(8,128)(2,1)S(1)}, u32[]{:S(2)}, u32[]{:S(2)}) async-start(bf16[4,512,256]{2,1,0:T(8,128)(2,1)} %forward.4), calls=%async_computation | async-start | bytes 2097152 | tf_op jit(solution)/shard_map/all_to_all | solution.py:54
  65.5 6.7 %backward.3.refs_20_ = bf16[512,2048]{1,0:T(8,128)(2,1)} custom-call(s32[8]{0:T(128)S(1)} %stack.153.spots_ref, bf16[4,2048,128]{2,1,0:T(8,128)(2,1)} %pad_maximum_fusion.refs_0_, bf16[4,2048,128]{2,1,0:T(8,128)(2,1)} %pad_maximum_fusion.1.refs_1_, bf16[512,8192]{1,0:T(8,128)(2,1)} %refs_9_.5, bf16[512,8192]{1,0:T(8,128)(2,1)} %refs_9_.5, ...), custom_call_target="tpu_custom_call" | custom-call | flops 268435456 | bytes 524288 | tf_op jit(solution)/shard_map/backward/pallas_call | solution.py:237
  72.3 2.7 %collective-permute-start.21 = (bf16[4,2048,128]{2,1,0:T(8,128)(2,1)}, bf16[4,2048,128]{2,1,0:T(8,128)(2,1)}, u32[]{:S(2)}, u32[]{:S(2)}) collective-permute-start(bf16[4,2048,128]{2,1,0:T(8,128)(2,1)} %collective-permute-done.12.refs_1_), channel_id=1, source_target_pairs={{0,24},{1,97},{2,26},{3,99},{4,28},{5,101},{6,30},{7,103},{8,0},{9... | collective-permute-start | bytes 6291464 | tf_op jit(solution)/shard_map/ppermute | solution.py:43
  75.0 4.9 %forward.5 = bf16[4,512,256]{2,1,0:T(8,128)(2,1)} custom-call(s32[1]{0:T(128)} %bitcast.1.start_ref, bf16[512,2048]{1,0:T(8,128)(2,1)S(1)} %constant_dynamic-update-slice_fusion.wide_ref, bf16[4,2048,128]{2,1,0:T(8,128)(2,1)} %collective-permute-done.11.refs_0_, bf16[4,2048,128]{2,1,0:T(8,128)(2,1)} %collective-permute-done.12.refs_1_), custom_call_target="tpu_custom_call" | custom-call | flops 268435456 | bytes 524288 | tf_op jit(solution)/shard_map/forward/pallas_call | solution.py:131
  79.9 4.3 %all-to-all-start.1 = ((bf16[4,512,256]{2,1,0:T(8,128)(2,1)}), bf16[4,512,256]{2,1,0:T(8,128)(2,1)}, u32[]{:S(2)}, u32[]{:S(2)}) async-start(bf16[4,512,256]{2,1,0:T(8,128)(2,1)} %forward.5), calls=%async_computation.1 | async-start | bytes 2097152 | tf_op jit(solution)/shard_map/all_to_all | solution.py:54
  84.2 1.5 fusion.9
  85.7 1.5 fusion.32
  88.0 4.9 %forward.6 = bf16[4,512,256]{2,1,0:T(8,128)(2,1)} custom-call(s32[1]{0:T(128)} %bitcast.1.start_ref, bf16[512,2048]{1,0:T(8,128)(2,1)S(1)} %constant_dynamic-update-slice_fusion.wide_ref, bf16[4,2048,128]{2,1,0:T(8,128)(2,1)} %collective-permute-done.13.refs_0_.refs_2_, bf16[4,2048,128]{2,1,0:T(8,128)(2,1)} %collective-permute-done.14.refs_1_.refs_3_), custom_call_target="tpu_custom_call" | custom-call | flops 268435456 | bytes 524288 | tf_op jit(solution)/shard_map/forward/pallas_call | solution.py:131
  93.0 4.4 %all-to-all-done.1.refs_0_ = bf16[4,512,256]{2,1,0:T(8,128)(2,1)} async-done(((bf16[4,512,256]{2,1,0:T(8,128)(2,1)}), bf16[4,512,256]{2,1,0:T(8,128)(2,1)}, u32[]{:S(2)}, u32[]{:S(2)}) %all-to-all-start.1) | async-done | bytes 1048608 | tf_op jit(solution)/shard_map/all_to_all | solution.py:54
  97.3 4.3 %all-to-all-start.2 = ((bf16[4,512,256]{2,1,0:T(8,128)(2,1)}), bf16[4,512,256]{2,1,0:T(8,128)(2,1)}, u32[]{:S(2)}, u32[]{:S(2)}) async-start(bf16[4,512,256]{2,1,0:T(8,128)(2,1)} %forward.6), calls=%async_computation.2 | async-start | bytes 2097152 | tf_op jit(solution)/shard_map/all_to_all | solution.py:54
  103.2 9.8 %backward.4.refs_10_ = bf16[512,2048]{1,0:T(8,128)(2,1)} custom-call(s32[16]{0:T(128)S(1)} %stack.170.spots_ref, bf16[4,2048,128]{2,1,0:T(8,128)(2,1)} %collective-permute-done.11.refs_0_, bf16[4,2048,128]{2,1,0:T(8,128)(2,1)} %collective-permute-done.12.refs_1_, ...), custom_call_target="tpu_custom_call", output_to_operand_aliasing={{}: (21, {})} | custom-call | flops 536870912 | bytes 1048576 | tf_op jit(solution)/shard_map/backward/pallas_call | solution.py:237
  113.1 3.0 %collective-permute-done.15 = f32[32,1024]{1,0:T(8,128)} collective-permute-done((f32[32,1024]{1,0:T(8,128)}, f32[32,1024]{1,0:T(8,128)}, u32[]{:S(2)}, u32[]{:S(2)}) %collective-permute-start.15) | collective-permute-done | bytes 131104 | tf_op jit(solution)/shard_map/ppermute | solution.py:72
  116.1 1.7 add_add_fusion
  118.1 2.6 %arrange.1 = bf16[4,512,256]{2,1,0:T(8,128)(2,1)} custom-call(s32[1]{0:T(128)} %bitcast.far_ref, bf16[4,512,256]{2,1,0:T(8,128)(2,1)S(1)} %all-to-all-done.here_ref, bf16[4,512,256]{2,1,0:T(8,128)(2,1)} %all-to-all-done.1.refs_0_, bf16[4,512,256]{2,1,0:T(8,128)(2,1)} %all-to-all-done.2.refs_1_), custom_call_target="tpu_custom_call" | custom-call | flops 2097152 | bytes 4194304 | tf_op jit(solution)/shard_map/arrange/pallas_call | solution.py:178
  120.7 1.9 %collective-permute-done.19 = f32[32,1024]{1,0:T(8,128)} collective-permute-done((f32[32,1024]{1,0:T(8,128)}, f32[32,1024]{1,0:T(8,128)}, u32[]{:S(2)}, u32[]{:S(2)}) %collective-permute-start.19) | collective-permute-done | bytes 131104 | tf_op jit(solution)/shard_map/ppermute | solution.py:82
  122.6 1.6 add.442
  124.3 3.6 %collective-permute-start.28 = (f32[32,1024]{1,0:T(8,128)}, f32[32,1024]{1,0:T(8,128)}, u32[]{:S(2)}, u32[]{:S(2)}) collective-permute-start(f32[32,1024]{1,0:T(8,128)} %add.442), channel_id=1, source_target_pairs={{0,16},{8,24},{16,0},{24,8},{32,48},{40,56},{48,32},{56,40},{64,80... | collective-permute-start | bytes 393224 | tf_op jit(solution)/shard_map/ppermute | solution.py:82
  127.9 4.3 %all-to-all-start.3 = ((bf16[4,512,256]{2,1,0:T(8,128)(2,1)}), bf16[4,512,256]{2,1,0:T(8,128)(2,1)S(1)}, u32[]{:S(2)}, u32[]{:S(2)}) async-start(bf16[4,512,256]{2,1,0:T(8,128)(2,1)} %arrange.1), calls=%async_computation.3 | async-start | bytes 2097152 | tf_op jit(solution)/shard_map/all_to_all | solution.py:54
  132.3 5.0 %forward.7 = (bf16[512,256]{1,0:T(8,128)(2,1)}, bf16[512,256]{1,0:T(8,128)(2,1)}, bf16[512,256]{1,0:T(8,128)(2,1)}, bf16[512,256]{1,0:T(8,128)(2,1)}) custom-call(s32[1]{0:T(128)} %bitcast.36.start_ref, bf16[512,2048]{1,0:T(8,128)(2,1)S(1)} %constant_dynamic-update-slice_fusion.wide_ref, bf16[4,2048,128]{2,1,0:T(8,128)(2,1)} %collective-permute-done.20.refs_0_, ...), custom_call_target="tpu_custom_call" | custom-call | flops 268435456 | bytes 524288 | tf_op jit(solution)/shard_map/forward/pallas_call | solution.py:131
  137.3 3.0 %collective-permute-start.22 = (bf16[512,256]{1,0:T(8,128)(2,1)}, bf16[512,256]{1,0:T(8,128)(2,1)}, u32[]{:S(2)}, u32[]{:S(2)}) collective-permute-start(bf16[512,256]{1,0:T(8,128)(2,1)} %get-tuple-element.66), channel_id=1, source_target_pairs={{0,4},{1,5},{2,6},{3,7},{4,0},{5,1},{6,2},{7,3},{8,12},{9,13},{10,... | collective-permute-start | bytes 786440 | tf_op jit(solution)/shard_map/ppermute | solution.py:391
  140.6 2.4 %collective-permute-start.24 = (bf16[512,256]{1,0:T(8,128)(2,1)}, bf16[512,256]{1,0:T(8,128)(2,1)}, u32[]{:S(2)}, u32[]{:S(2)}) collective-permute-start(bf16[512,256]{1,0:T(8,128)(2,1)} %get-tuple-element.68), channel_id=1, source_target_pairs={{0,6},{1,7},{2,0},{3,1},{4,2},{5,3},{6,4},{7,5},{8,14},{9,15},{10,... | collective-permute-start | bytes 786440 | tf_op jit(solution)/shard_map/ppermute | solution.py:391
  144.9 2.3 %collective-permute-start.29 = (f32[256,256]{1,0:T(8,128)S(1)}, f32[256,256]{1,0:T(8,128)S(1)}, u32[]{:S(2)}, u32[]{:S(2)}) collective-permute-start(f32[256,256]{1,0:T(8,128)S(1)} %fusion.2), channel_id=1, source_target_pairs={{0,1},{1,0},{2,3},{3,2},{4,5},{5,4},{6,7},{7,6},{8,9},{9,8},{10,11... | collective-permute-start | bytes 786440 | tf_op jit(solution)/shard_map/ppermute | solution.py:61
  148.8 1.4 collective-permute-start.18
  152.1 7.1 %collective-permute-done.23 = bf16[512,256]{1,0:T(8,128)(2,1)} collective-permute-done((bf16[512,256]{1,0:T(8,128)(2,1)}, bf16[512,256]{1,0:T(8,128)(2,1)}, u32[]{:S(2)}, u32[]{:S(2)}) %collective-permute-start.23) | collective-permute-done | bytes 262176 | tf_op jit(solution)/shard_map/ppermute | solution.py:391
  161.1 5.5 %collective-permute-start.26 = (bf16[512,256]{1,0:T(8,128)(2,1)S(1)}, bf16[512,256]{1,0:T(8,128)(2,1)S(1)}, u32[]{:S(2)}, u32[]{:S(2)}) collective-permute-start(bf16[512,256]{1,0:T(8,128)(2,1)S(1)} %add_convert_fusion.2), channel_id=1, source_target_pairs={{1,4},{5,5},{9,12},{13,13},{17,20},{21,21},{25,28},{29,29},{33,38}... | collective-permute-start | bytes 786440 | tf_op jit(solution)/shard_map/ppermute | solution.py:285
  167.9 6.6 %backward.5 = (f32[512,1024]{1,0:T(8,128)S(1)}, bf16[512,1024]{1,0:T(8,128)(2,1)S(1)}) custom-call(s32[8]{0:T(128)S(1)} %stack.179.spots_ref, bf16[4,2048,128]{2,1,0:T(8,128)(2,1)} %collective-permute-done.20.refs_0_, bf16[4,2048,128]{2,1,0:T(8,128)(2,1)} %collective-permute-done.21.refs_1_, bf16[512,8192]{1,0:T(8,128)(2,1)} %refs_9_.5, ...), custom_call_target="tpu_custom_call" | custom-call | flops 268435456 | bytes 524288 | tf_op jit(solution)/shard_map/backward/pallas_call | solution.py:237
  176.8 1.4 add_convert_fusion.1
  178.2 7.1 %collective-permute-done.32 = f32[256,256]{1,0:T(8,128)S(1)} collective-permute-done((f32[256,256]{1,0:T(8,128)S(1)}, f32[256,256]{1,0:T(8,128)S(1)}, u32[]{:S(2)}, u32[]{:S(2)}) %collective-permute-start.32) | collective-permute-done | bytes 262176 | tf_op jit(solution)/shard_map/ppermute | solution.py:61
  186.0 1.4 add_convert_fusion
  (126 shorter events, 22.5 us)
Async XLA Ops:
  0.6 13.1 %copy-start = (f32[256,256]{1,0:T(8,128)S(1)}, f32[256,256]{1,0:T(8,128)}, u32[]{:S(2)}) copy-start(f32[256,256]{1,0:T(8,128)} %param.10) | copy-start | bytes 786436
  2.0 3.2 %collective-permute-start.1 = (bf16[1024,256]{1,0:T(8,128)(2,1)S(1)}, bf16[1024,256]{1,0:T(8,128)(2,1)}, u32[]{:S(2)}, u32[]{:S(2)}) collective-permute-start(bf16[1024,256]{1,0:T(8,128)(2,1)S(1)} %get-tuple-element.76), channel_id=1, source_target_pairs={{0,1},{1,0},{2,3},{3,2},{4,5},{5,4},{6,7},{7,6},{8,9},{9,8},{10,11... | collective-permute-start | bytes 1572872 | tf_op jit(solution)/shard_map/ppermute | solution.py:312
  3.5 9.5 %copy-start.19 = (f32[16,4,2]{0,2,1:T(2,128)S(1)}, f32[16,4,2]{0,2,1:T(2,128)}, u32[]{:S(2)}) copy-start(f32[16,4,2]{0,2,1:T(2,128)} %param.13) | copy-start | bytes 1540
  3.5 10.2 %copy-start.14 = (s32[16,4,2]{0,2,1:T(2,128)S(1)}, s32[16,4,2]{0,2,1:T(2,128)}, u32[]{:S(2)}) copy-start(s32[16,4,2]{0,2,1:T(2,128)} %param.14) | copy-start | bytes 1540
  3.5 10.5 %copy-start.15 = (s32[16,4,2]{0,2,1:T(2,128)S(1)}, s32[16,4,2]{0,2,1:T(2,128)}, u32[]{:S(2)}) copy-start(s32[16,4,2]{0,2,1:T(2,128)} %param.12) | copy-start | bytes 1540
  3.5 22.0 %copy-start.2 = (bf16[512,1024]{1,0:T(8,128)(2,1)S(1)}, bf16[512,1024]{1,0:T(8,128)(2,1)}, u32[]{:S(2)}) copy-start(bf16[512,1024]{1,0:T(8,128)(2,1)} %param.8) | copy-start | bytes 3145732
  6.3 19.6 %collective-permute-start.3 = (bf16[2048,128]{1,0:T(8,128)(2,1)S(1)}, bf16[2048,128]{1,0:T(8,128)(2,1)S(1)}, u32[]{:S(2)}, u32[]{:S(2)}) collective-permute-start(bf16[2048,128]{1,0:T(8,128)(2,1)S(1)} %get-tuple-element.39), channel_id=1, source_target_pairs={{0,32},{1,9},{2,34},{3,11},{4,36},{5,13},{6,38},{7,15},{8,40},{9,1... | collective-permute-start | bytes 1572872 | tf_op jit(solution)/shard_map/ppermute | solution.py:43
  8.1 29.2 %collective-permute-start.2 = (bf16[2048,128]{1,0:T(8,128)(2,1)S(1)}, bf16[2048,128]{1,0:T(8,128)(2,1)S(1)}, u32[]{:S(2)}, u32[]{:S(2)}) collective-permute-start(bf16[2048,128]{1,0:T(8,128)(2,1)S(1)} %get-tuple-element.39), channel_id=1, source_target_pairs={{0,96},{1,25},{2,98},{3,27},{4,100},{5,29},{6,102},{7,31},{8,104},... | collective-permute-start | bytes 1572872 | tf_op jit(solution)/shard_map/ppermute | solution.py:43
  10.3 17.3 %collective-permute-start.7 = (bf16[2048,128]{1,0:T(8,128)(2,1)S(1)}, bf16[2048,128]{1,0:T(8,128)(2,1)}, u32[]{:S(2)}, u32[]{:S(2)}) collective-permute-start(bf16[2048,128]{1,0:T(8,128)(2,1)S(1)} %get-tuple-element.40), channel_id=1, source_target_pairs={{0,32},{1,9},{2,34},{3,11},{4,36},{5,13},{6,38},{7,15},{8,40},{9,1... | collective-permute-start | bytes 1572872 | tf_op jit(solution)/shard_map/ppermute | solution.py:43
  10.3 12.0 %collective-permute-start.5 = (bf16[2048,128]{1,0:T(8,128)(2,1)S(1)}, bf16[2048,128]{1,0:T(8,128)(2,1)}, u32[]{:S(2)}, u32[]{:S(2)}) collective-permute-start(bf16[2048,128]{1,0:T(8,128)(2,1)S(1)} %get-tuple-element.40), channel_id=1, source_target_pairs={{0,96},{1,25},{2,98},{3,27},{4,100},{5,29},{6,102},{7,31},{8,104},... | collective-permute-start | bytes 1572872 | tf_op jit(solution)/shard_map/ppermute | solution.py:43
  14.1 17.9 %copy-start.10 = (bf16[4,2,8,256]{3,2,0,1:T(8,128)(2,1)}, bf16[4,2,8,256]{3,2,0,1:T(8,128)(2,1)S(1)}, u32[]{:S(2)}) copy-start(bf16[4,2,8,256]{3,2,0,1:T(8,128)(2,1)S(1)} %copy.45) | copy-start | bytes 98308
  14.4 17.5 %copy-start.4 = (bf16[4,2,8,256]{3,2,0,1:T(8,128)(2,1)}, bf16[4,2,8,256]{3,2,0,1:T(8,128)(2,1)S(1)}, u32[]{:S(2)}) copy-start(bf16[4,2,8,256]{3,2,0,1:T(8,128)(2,1)S(1)} %copy.44) | copy-start | bytes 98308
  22.3 9.7 %collective-permute-start.6 = (bf16[2048,128]{1,0:T(8,128)(2,1)}, bf16[2048,128]{1,0:T(8,128)(2,1)S(1)}, u32[]{:S(2)}, u32[]{:S(2)}) collective-permute-start(bf16[2048,128]{1,0:T(8,128)(2,1)} %collective-permute-done.5), channel_id=1, source_target_pairs={{0,96},{1,25},{2,98},{3,27},{4,100},{5,29},{6,102},{7,31},{8,104},... | collective-permute-start | bytes 1572872 | tf_op jit(solution)/shard_map/ppermute | solution.py:43
  25.9 11.3 %collective-permute-start.4 = (bf16[2048,128]{1,0:T(8,128)(2,1)S(1)}, bf16[2048,128]{1,0:T(8,128)(2,1)S(1)}, u32[]{:S(2)}, u32[]{:S(2)}) collective-permute-start(bf16[2048,128]{1,0:T(8,128)(2,1)S(1)} %collective-permute-done.3), channel_id=1, source_target_pairs={{0,32},{1,9},{2,34},{3,11},{4,36},{5,13},{6,38},{7,15},{8,40},{9,1... | collective-permute-start | bytes 1572872 | tf_op jit(solution)/shard_map/ppermute | solution.py:43
  34.8 37.5 %collective-permute-start.12 = (bf16[4,2048,128]{2,1,0:T(8,128)(2,1)}, bf16[4,2048,128]{2,1,0:T(8,128)(2,1)}, u32[]{:S(2)}, u32[]{:S(2)}) collective-permute-start(bf16[4,2048,128]{2,1,0:T(8,128)(2,1)} %pad_maximum_fusion.1.refs_1_), channel_id=1, source_target_pairs={{0,24},{1,97},{2,26},{3,99},{4,28},{5,101},{6,30},{7,103},{8,0},{9... | collective-permute-start | bytes 6291464 | tf_op jit(solution)/shard_map/ppermute | solution.py:43
  38.8 33.4 %collective-permute-start.11 = (bf16[4,2048,128]{2,1,0:T(8,128)(2,1)}, bf16[4,2048,128]{2,1,0:T(8,128)(2,1)}, u32[]{:S(2)}, u32[]{:S(2)}) collective-permute-start(bf16[4,2048,128]{2,1,0:T(8,128)(2,1)} %pad_maximum_fusion.refs_0_), channel_id=1, source_target_pairs={{0,8},{1,33},{2,10},{3,35},{4,12},{5,37},{6,14},{7,39},{8,16},{9,4... | collective-permute-start | bytes 6291464 | tf_op jit(solution)/shard_map/ppermute | solution.py:43
  38.8 13.0 %collective-permute-start = (bf16[512,1024]{1,0:T(8,128)(2,1)S(1)}, bf16[512,1024]{1,0:T(8,128)(2,1)}, u32[]{:S(2)}, u32[]{:S(2)}) collective-permute-start(bf16[512,1024]{1,0:T(8,128)(2,1)S(1)} %copy-done.2), channel_id=1, source_target_pairs={{0,1},{1,0},{2,3},{3,2},{4,5},{5,4},{6,7},{7,6},{8,9},{9,8},{10,11... | collective-permute-start | bytes 3145736 | tf_op jit(solution)/shard_map/ppermute | solution.py:332
  41.6 2.2 %collective-permute-start.8 = (f32[32,512]{1,0:T(8,128)S(1)}, f32[32,512]{1,0:T(8,128)S(1)}, u32[]{:S(2)}, u32[]{:S(2)}) collective-permute-start(f32[32,512]{1,0:T(8,128)S(1)} %pad_maximum_fusion.4), channel_id=1, source_target_pairs={{0,1},{1,0},{2,3},{3,2},{4,5},{5,4},{6,7},{7,6},{8,9},{9,8},{10,11... | collective-permute-start | bytes 196616 | tf_op jit(solution)/shard_map/ppermute | solution.py:61
  43.9 3.7 %collective-permute-start.9 = (f32[32,512]{1,0:T(8,128)S(1)}, f32[32,512]{1,0:T(8,128)S(1)}, u32[]{:S(2)}, u32[]{:S(2)}) collective-permute-start(f32[32,512]{1,0:T(8,128)S(1)} %add.383), channel_id=1, source_target_pairs={{0,2},{1,3},{2,0},{3,1},{4,6},{5,7},{6,4},{7,5},{8,10},{9,11},{10,... | collective-permute-start | bytes 196616 | tf_op jit(solution)/shard_map/ppermute | solution.py:61
  45.2 42.8 %collective-permute-start.14 = (bf16[4,2048,128]{2,1,0:T(8,128)(2,1)}, bf16[4,2048,128]{2,1,0:T(8,128)(2,1)}, u32[]{:S(2)}, u32[]{:S(2)}) collective-permute-start(bf16[4,2048,128]{2,1,0:T(8,128)(2,1)} %pad_maximum_fusion.1.refs_1_), channel_id=1, source_target_pairs={{0,8},{1,33},{2,10},{3,35},{4,12},{5,37},{6,14},{7,39},{8,16},{9,4... | collective-permute-start | bytes 6291464 | tf_op jit(solution)/shard_map/ppermute | solution.py:43
  47.6 40.4 %collective-permute-start.13 = (bf16[4,2048,128]{2,1,0:T(8,128)(2,1)}, bf16[4,2048,128]{2,1,0:T(8,128)(2,1)}, u32[]{:S(2)}, u32[]{:S(2)}) collective-permute-start(bf16[4,2048,128]{2,1,0:T(8,128)(2,1)} %pad_maximum_fusion.refs_0_), channel_id=1, source_target_pairs={{0,24},{1,97},{2,26},{3,99},{4,28},{5,101},{6,30},{7,103},{8,0},{9... | collective-permute-start | bytes 6291464 | tf_op jit(solution)/shard_map/ppermute | solution.py:43
  51.8 9.3 %collective-permute-start.10 = (f32[32,512]{1,0:T(8,128)S(1)}, f32[32,512]{1,0:T(8,128)S(1)}, u32[]{:S(2)}, u32[]{:S(2)}) collective-permute-start(f32[32,512]{1,0:T(8,128)S(1)} %add.384), channel_id=1, source_target_pairs={{0,4},{1,5},{2,6},{3,7},{4,0},{5,1},{6,2},{7,3},{8,12},{9,13},{10,... | collective-permute-start | bytes 196616 | tf_op jit(solution)/shard_map/ppermute | solution.py:61
  61.7 18.2 %all-to-all-start = ((bf16[4,512,256]{2,1,0:T(8,128)(2,1)}), bf16[4,512,256]{2,1,0:T(8,128)(2,1)S(1)}, u32[]{:S(2)}, u32[]{:S(2)}) async-start(bf16[4,512,256]{2,1,0:T(8,128)(2,1)} %forward.4), calls=%async_computation | async-start | bytes 2097152 | tf_op jit(solution)/shard_map/all_to_all | solution.py:54
  72.2 60.1 %collective-permute-start.20 = (bf16[4,2048,128]{2,1,0:T(8,128)(2,1)}, bf16[4,2048,128]{2,1,0:T(8,128)(2,1)}, u32[]{:S(2)}, u32[]{:S(2)}) collective-permute-start(bf16[4,2048,128]{2,1,0:T(8,128)(2,1)} %collective-permute-done.11.refs_0_), channel_id=1, source_target_pairs={{0,8},{1,33},{2,10},{3,35},{4,12},{5,37},{6,14},{7,39},{8,16},{9,4... | collective-permute-start | bytes 6291464 | tf_op jit(solution)/shard_map/ppermute | solution.py:43
  72.3 60.0 %collective-permute-start.21 = (bf16[4,2048,128]{2,1,0:T(8,128)(2,1)}, bf16[4,2048,128]{2,1,0:T(8,128)(2,1)}, u32[]{:S(2)}, u32[]{:S(2)}) collective-permute-start(bf16[4,2048,128]{2,1,0:T(8,128)(2,1)} %collective-permute-done.12.refs_1_), channel_id=1, source_target_pairs={{0,24},{1,97},{2,26},{3,99},{4,28},{5,101},{6,30},{7,103},{8,0},{9... | collective-permute-start | bytes 6291464 | tf_op jit(solution)/shard_map/ppermute | solution.py:43
  79.9 17.4 %all-to-all-start.1 = ((bf16[4,512,256]{2,1,0:T(8,128)(2,1)}), bf16[4,512,256]{2,1,0:T(8,128)(2,1)}, u32[]{:S(2)}, u32[]{:S(2)}) async-start(bf16[4,512,256]{2,1,0:T(8,128)(2,1)} %forward.5), calls=%async_computation.1 | async-start | bytes 2097152 | tf_op jit(solution)/shard_map/all_to_all | solution.py:54
  97.3 20.8 %all-to-all-start.2 = ((bf16[4,512,256]{2,1,0:T(8,128)(2,1)}), bf16[4,512,256]{2,1,0:T(8,128)(2,1)}, u32[]{:S(2)}, u32[]{:S(2)}) async-start(bf16[4,512,256]{2,1,0:T(8,128)(2,1)} %forward.6), calls=%async_computation.2 | async-start | bytes 2097152 | tf_op jit(solution)/shard_map/all_to_all | solution.py:54
  101.6 11.5 %collective-permute-start.17 = (f32[32,1024]{1,0:T(8,128)}, f32[32,1024]{1,0:T(8,128)}, u32[]{:S(2)}, u32[]{:S(2)}) collective-permute-start(f32[32,1024]{1,0:T(8,128)} %maximum_multiply_fusion), channel_id=1, source_target_pairs={{0,96},{1,97},{2,98},{3,99},{4,100},{5,101},{6,102},{7,103},{8,104... | collective-permute-start | bytes 393224 | tf_op jit(solution)/shard_map/ppermute | solution.py:72
  101.7 11.4 %collective-permute-start.16 = (f32[32,1024]{1,0:T(8,128)}, f32[32,1024]{1,0:T(8,128)}, u32[]{:S(2)}, u32[]{:S(2)}) collective-permute-start(f32[32,1024]{1,0:T(8,128)} %maximum_multiply_fusion), channel_id=1, source_target_pairs={{0,64},{1,65},{2,66},{3,67},{4,68},{5,69},{6,70},{7,71},{8,72},{9,... | collective-permute-start | bytes 393224 | tf_op jit(solution)/shard_map/ppermute | solution.py:72
  101.8 14.3 %collective-permute-start.15 = (f32[32,1024]{1,0:T(8,128)}, f32[32,1024]{1,0:T(8,128)}, u32[]{:S(2)}, u32[]{:S(2)}) collective-permute-start(f32[32,1024]{1,0:T(8,128)} %maximum_multiply_fusion), channel_id=1, source_target_pairs={{0,32},{1,33},{2,34},{3,35},{4,36},{5,37},{6,38},{7,39},{8,40},{9,... | collective-permute-start | bytes 393224 | tf_op jit(solution)/shard_map/ppermute | solution.py:72
  103.2 12.9 %copy-start.3 = (f32[32,1024]{1,0:T(8,128)S(1)}, f32[32,1024]{1,0:T(8,128)}, u32[]{:S(2)}) copy-start(f32[32,1024]{1,0:T(8,128)} %maximum_multiply_fusion) | copy-start | bytes 393220
  117.8 4.8 %collective-permute-start.19 = (f32[32,1024]{1,0:T(8,128)}, f32[32,1024]{1,0:T(8,128)}, u32[]{:S(2)}, u32[]{:S(2)}) collective-permute-start(f32[32,1024]{1,0:T(8,128)} %add_add_fusion), channel_id=1, source_target_pairs={{0,8},{8,0},{16,24},{24,16},{32,40},{40,32},{48,56},{56,48},{64,72... | collective-permute-start | bytes 393224 | tf_op jit(solution)/shard_map/ppermute | solution.py:82
  124.3 18.8 %collective-permute-start.28 = (f32[32,1024]{1,0:T(8,128)}, f32[32,1024]{1,0:T(8,128)}, u32[]{:S(2)}, u32[]{:S(2)}) collective-permute-start(f32[32,1024]{1,0:T(8,128)} %add.442), channel_id=1, source_target_pairs={{0,16},{8,24},{16,0},{24,8},{32,48},{40,56},{48,32},{56,40},{64,80... | collective-permute-start | bytes 393224 | tf_op jit(solution)/shard_map/ppermute | solution.py:82
  127.9 20.8 %all-to-all-start.3 = ((bf16[4,512,256]{2,1,0:T(8,128)(2,1)}), bf16[4,512,256]{2,1,0:T(8,128)(2,1)S(1)}, u32[]{:S(2)}, u32[]{:S(2)}) async-start(bf16[4,512,256]{2,1,0:T(8,128)(2,1)} %arrange.1), calls=%async_computation.3 | async-start | bytes 2097152 | tf_op jit(solution)/shard_map/all_to_all | solution.py:54
  137.3 10.5 %copy-start.17 = (f32[16,4,2]{0,2,1:T(2,128)S(1)}, f32[16,4,2]{0,2,1:T(2,128)}, u32[]{:S(2)}) copy-start(f32[16,4,2]{0,2,1:T(2,128)} %copy-done.16) | copy-start | bytes 1540
  137.3 11.4 %copy-start.1 = (bf16[4,512,256]{2,1,0:T(8,128)(2,1)S(1)}, bf16[4,512,256]{2,1,0:T(8,128)(2,1)}, u32[]{:S(2)}) copy-start(bf16[4,512,256]{2,1,0:T(8,128)(2,1)} %arrange.1) | copy-start | bytes 3145732
  137.3 14.8 %collective-permute-start.22 = (bf16[512,256]{1,0:T(8,128)(2,1)}, bf16[512,256]{1,0:T(8,128)(2,1)}, u32[]{:S(2)}, u32[]{:S(2)}) collective-permute-start(bf16[512,256]{1,0:T(8,128)(2,1)} %get-tuple-element.66), channel_id=1, source_target_pairs={{0,4},{1,5},{2,6},{3,7},{4,0},{5,1},{6,2},{7,3},{8,12},{9,13},{10,... | collective-permute-start | bytes 786440 | tf_op jit(solution)/shard_map/ppermute | solution.py:391
  140.4 18.8 %collective-permute-start.23 = (bf16[512,256]{1,0:T(8,128)(2,1)}, bf16[512,256]{1,0:T(8,128)(2,1)}, u32[]{:S(2)}, u32[]{:S(2)}) collective-permute-start(bf16[512,256]{1,0:T(8,128)(2,1)} %get-tuple-element.67), channel_id=1, source_target_pairs={{0,2},{1,3},{2,4},{3,5},{4,6},{5,7},{6,0},{7,1},{8,10},{9,11},{10,... | collective-permute-start | bytes 786440 | tf_op jit(solution)/shard_map/ppermute | solution.py:391
  140.6 18.5 %collective-permute-start.24 = (bf16[512,256]{1,0:T(8,128)(2,1)}, bf16[512,256]{1,0:T(8,128)(2,1)}, u32[]{:S(2)}, u32[]{:S(2)}) collective-permute-start(bf16[512,256]{1,0:T(8,128)(2,1)} %get-tuple-element.68), channel_id=1, source_target_pairs={{0,6},{1,7},{2,0},{3,1},{4,2},{5,3},{6,4},{7,5},{8,14},{9,15},{10,... | collective-permute-start | bytes 786440 | tf_op jit(solution)/shard_map/ppermute | solution.py:391
  144.5 14.7 %copy-start.6 = (bf16[512,256]{1,0:T(8,128)(2,1)S(1)}, bf16[512,256]{1,0:T(8,128)(2,1)}, u32[]{:S(2)}) copy-start(bf16[512,256]{1,0:T(8,128)(2,1)} %get-tuple-element.65) | copy-start | bytes 786436
  144.9 6.1 %collective-permute-start.29 = (f32[256,256]{1,0:T(8,128)S(1)}, f32[256,256]{1,0:T(8,128)S(1)}, u32[]{:S(2)}, u32[]{:S(2)}) collective-permute-start(f32[256,256]{1,0:T(8,128)S(1)} %fusion.2), channel_id=1, source_target_pairs={{0,1},{1,0},{2,3},{3,2},{4,5},{5,4},{6,7},{7,6},{8,9},{9,8},{10,11... | collective-permute-start | bytes 786440 | tf_op jit(solution)/shard_map/ppermute | solution.py:61
  148.8 27.0 %collective-permute-start.18 = (bf16[2,512,256]{2,1,0:T(8,128)(2,1)S(1)}, bf16[2,512,256]{2,1,0:T(8,128)(2,1)S(1)}, u32[]{:S(2)}, u32[]{:S(2)}) collective-permute-start(bf16[2,512,256]{2,1,0:T(8,128)(2,1)S(1)} %slice_select_fusion.1), channel_id=1, source_target_pairs={{0,1},{1,0},{2,3},{3,2},{4,5},{5,4},{6,7},{7,6},{8,9},{9,8},{10,11... | collective-permute-start | bytes 1572872 | tf_op jit(solution)/shard_map/ppermute | solution.py:401
  151.0 23.5 %collective-permute-start.31 = (f32[256,256]{1,0:T(8,128)S(1)}, f32[256,256]{1,0:T(8,128)S(1)}, u32[]{:S(2)}, u32[]{:S(2)}) collective-permute-start(f32[256,256]{1,0:T(8,128)S(1)} %add.467), channel_id=1, source_target_pairs={{0,2},{1,3},{2,0},{3,1},{4,6},{5,7},{6,4},{7,5},{8,10},{9,11},{10,... | collective-permute-start | bytes 786440 | tf_op jit(solution)/shard_map/ppermute | solution.py:61
  160.4 15.6 %collective-permute-start.27 = (bf16[512,256]{1,0:T(8,128)(2,1)S(1)}, bf16[512,256]{1,0:T(8,128)(2,1)S(1)}, u32[]{:S(2)}, u32[]{:S(2)}) collective-permute-start(bf16[512,256]{1,0:T(8,128)(2,1)S(1)} %add_convert_fusion.2), channel_id=1, source_target_pairs={{3,4},{7,5},{11,12},{15,13},{19,20},{23,21},{27,28},{31,29},{35,38... | collective-permute-start | bytes 786440 | tf_op jit(solution)/shard_map/ppermute | solution.py:285
  161.1 14.9 %collective-permute-start.26 = (bf16[512,256]{1,0:T(8,128)(2,1)S(1)}, bf16[512,256]{1,0:T(8,128)(2,1)S(1)}, u32[]{:S(2)}, u32[]{:S(2)}) collective-permute-start(bf16[512,256]{1,0:T(8,128)(2,1)S(1)} %add_convert_fusion.2), channel_id=1, source_target_pairs={{1,4},{5,5},{9,12},{13,13},{17,20},{21,21},{25,28},{29,29},{33,38}... | collective-permute-start | bytes 786440 | tf_op jit(solution)/shard_map/ppermute | solution.py:285
  166.6 9.5 %collective-permute-start.25 = (bf16[512,256]{1,0:T(8,128)(2,1)S(1)}, bf16[512,256]{1,0:T(8,128)(2,1)S(1)}, u32[]{:S(2)}, u32[]{:S(2)}) collective-permute-start(bf16[512,256]{1,0:T(8,128)(2,1)S(1)} %add_convert_fusion.2), channel_id=1, source_target_pairs={{0,1},{2,3},{4,5},{6,7},{8,9},{10,11},{12,13},{14,15},{32,33},{34,... | collective-permute-start | bytes 786440 | tf_op jit(solution)/shard_map/ppermute | solution.py:290
  174.5 11.5 %collective-permute-start.30 = (bf16[512,1024]{1,0:T(8,128)(2,1)S(1)}, bf16[512,1024]{1,0:T(8,128)(2,1)S(1)}, u32[]{:S(2)}, u32[]{:S(2)}) collective-permute-start(bf16[512,1024]{1,0:T(8,128)(2,1)S(1)} %get-tuple-element.72), channel_id=1, source_target_pairs={{0,1},{1,0},{2,3},{3,2},{4,5},{5,4},{6,7},{7,6},{8,9},{9,8},{10,11... | collective-permute-start | bytes 3145736 | tf_op jit(solution)/shard_map/ppermute | solution.py:415
  175.8 9.5 %collective-permute-start.32 = (f32[256,256]{1,0:T(8,128)S(1)}, f32[256,256]{1,0:T(8,128)S(1)}, u32[]{:S(2)}, u32[]{:S(2)}) collective-permute-start(f32[256,256]{1,0:T(8,128)S(1)} %add.470), channel_id=1, source_target_pairs={{0,4},{1,5},{2,6},{3,7},{4,0},{5,1},{6,2},{7,3},{8,12},{9,13},{10,... | collective-permute-start | bytes 786440 | tf_op jit(solution)/shard_map/ppermute | solution.py:61
  (9 other events, 33.0 us)
